TPU v7x, 512 devices: a whole 4x4x16 slice. The times are simulated.
512 devices in a mesh: ctx: 64 (over y, z_lo, core), exp: 8 (over z_hi, x).
Axes of the slice: x: 4, y: 4, z: 16 (z_hi: 2, z_lo: 8; z = z_hi * 8 + z_lo), core: 2. Of those that a mesh axis runs over, the one named last changes fastest.
Arguments:
- queries: bfloat16 [8192, 32, 128], P('ctx', 'exp'), may hold values from -100 to 100
- keys: bfloat16 [8192, 2, 128], P('ctx'), may hold values from -4 to 4
- values: bfloat16 [8192, 2, 128], P('ctx'), may hold values from -4 to 4
- resid: bfloat16 [8192, 4096], P('ctx', 'exp'), may hold values from -20 to 20
- gain: float32 [4096], P('exp'), may hold values from 0.1 to 1.9
- expert_ids: int32 [8192, 8], P('ctx'), may hold values from 0 to 127, all different within a row; in each aligned block of 128 rows (0 to 127, 128 to 255, ...) at most 10 rows name the same one
- gate_scores: float32 [8192, 8], P('ctx'), may hold values from 0.05 to 1
- w_gate_up: bfloat16 [64, 4096, 2, 768], P('ctx', 'exp'), may hold values from -0.09375 to 0.09375
- w_down: bfloat16 [64, 768, 4096], P('ctx', None, 'exp'), may hold values from -0.625 to 0.625
- w_out: bfloat16 [32, 128, 4096], P('exp', 'ctx'), may hold values from -0.5 to 0.5
Outputs:
- context: bfloat16 [8192, 32, 128], P('ctx', 'exp')
- mixed: bfloat16 [8192, 4096], P('ctx', 'exp')
Inputs may be any that keep to these rules, and one draw needn't show every extreme that they name: `expert_ids`: each row names 8 different experts; within the 128 rows of one index of ctx no expert is named more than 10 times.
All inputs are finite; a program needn't handle non-finite values.
Results may differ from a plain program's by a relative error of at most 0.02.
Values may be sent and summed in bfloat16 or wider, within the bound.
No kernel may reach another device: no remote copies, remote signals or barrier semaphores. Data moves between devices by JAX's collectives and lax.ppermute only.
A program may use at most 64 MiB of HBM per device.

v0:
```python
import math

import jax
import jax.numpy as jnp
from jax import lax
from jax.sharding import PartitionSpec as P

D = 4096
HQ = 32
KVH = 2
EXPERTS = 128
TOPK = 8


masked_score = -1e30
epsilon = 1e-06


def attend_piece(state_now, pair_piece, offset, query_rows, query_pos, last_pos, scaling):
    key_piece, value_piece = pair_piece
    length = key_piece.shape[0]

    def compute(state_in):
        running, denominator, numerator = state_in
        scores = (
            jnp.einsum("rd,kd->rk", query_rows, key_piece, preferred_element_type=jnp.float32)
            * scaling
        )
        key_pos = jnp.arange(length, dtype=jnp.int32)
        visible = key_pos[None, :] <= query_pos[:, None]
        masked = jnp.where(visible, scores, masked_score)
        highest = jnp.maximum(running, jnp.max(masked, axis=1))
        weights_exp = jnp.where(visible, jnp.exp(masked - highest[:, None]), 0.0)
        rounded = weights_exp.astype(jnp.bfloat16)
        numerator = jnp.dot(rounded, value_piece, preferred_element_type=jnp.float32)
        denominator = jnp.sum(weights_exp, axis=1)
        return (highest, denominator, numerator)

    def untouched(state_in):
        return state_in

    return lax.cond(offset <= last_pos, compute, untouched, state_now)


def body(queries, keys, values, resid, gain, expert_ids, gate_scores, w_gate_up, w_down, w_out):
    tokens_here = queries.shape[0]
    heads_here = queries.shape[1]
    head_size = queries.shape[2]
    ctx_count = lax.axis_size("ctx")
    ctx_place = lax.axis_index("ctx")
    exp_place = lax.axis_index("exp")
    own_pos = ctx_place * tokens_here + jnp.arange(tokens_here, dtype=jnp.int32)
    query_sets = (queries, own_pos)
    group_index = exp_place * heads_here // (HQ // KVH)
    key_local = lax.dynamic_index_in_dim(keys, group_index, 1, keepdims=False)
    value_local = lax.dynamic_index_in_dim(values, group_index, 1, keepdims=False)
    scaling = 1.0 / math.sqrt(head_size)
    set_queries, set_pos = query_sets
    set_rows = set_queries.shape[0] * heads_here
    initial = [
        (
            jnp.full((set_rows,), masked_score, jnp.float32),
            jnp.zeros((set_rows,), jnp.float32),
            jnp.zeros((set_rows, head_size), jnp.float32),
        )
    ]
    rows_set = set_queries.reshape(set_rows, head_size)
    pos_set = jnp.repeat(set_pos, heads_here)
    last_set = jnp.max(set_pos)
    updated = [
        attend_piece(
            tuple(initial)[0],
            (
                lax.all_gather(key_local, "ctx", axis=0, tiled=True),
                lax.all_gather(value_local, "ctx", axis=0, tiled=True),
            ),
            jnp.int32(0),
            rows_set,
            pos_set,
            last_set,
            scaling,
        )
    ]
    folded = tuple(updated)
    pieces_out = []
    for state_set in folded:
        normalized = state_set[2] / state_set[1][:, None]
        pieces_out.append(normalized.reshape(-1, heads_here, head_size).astype(jnp.bfloat16))
    context = pieces_out[0]
    whole_out = lax.all_gather(w_out, "ctx", axis=1, tiled=True)
    projected = jnp.einsum("thp,hpd->td", context, whole_out, preferred_element_type=jnp.float32)
    attended = lax.psum_scatter(
        projected.astype(jnp.bfloat16), "exp", scatter_dimension=1, tiled=True
    ).astype(jnp.float32)
    hidden_state = resid.astype(jnp.float32) + attended
    square_sum = lax.psum(jnp.sum(hidden_state * hidden_state, axis=1), "exp")
    inverse = lax.rsqrt(square_sum / D + epsilon)
    normed = (hidden_state * inverse[:, None] * gain[None, :]).astype(jnp.bfloat16)
    capacity = max(2, 5 * tokens_here * TOPK // (4 * EXPERTS))
    flat_ids = expert_ids.reshape(-1)
    onehot = (flat_ids[:, None] == jnp.arange(ctx_count, dtype=jnp.int32)[None, :]).astype(
        jnp.int32
    )
    earlier = jnp.cumsum(onehot, axis=0) - onehot
    rank_of = jnp.sum(earlier * onehot, axis=1)
    active = flat_ids < ctx_count
    slot_of = jnp.where(active, flat_ids * capacity + rank_of, -1).reshape(tokens_here, TOPK)
    slot_range = jnp.arange(ctx_count * capacity, dtype=jnp.int32)
    dispatch_map = jnp.zeros((ctx_count * capacity, tokens_here), jnp.bfloat16)
    for column in range(TOPK):
        dispatch_map = dispatch_map + (slot_range[:, None] == slot_of[None, :, column]).astype(
            jnp.bfloat16
        )
    local_width = normed.shape[1]
    outgoing = jnp.dot(dispatch_map, normed, preferred_element_type=jnp.float32).astype(
        jnp.bfloat16
    )
    outgoing = outgoing.reshape(ctx_count, capacity, local_width)
    arrived = lax.all_to_all(outgoing, "ctx", split_axis=0, concat_axis=0, tiled=True)
    sources = arrived.shape[0]
    width_slots = arrived.shape[1]
    row_block = arrived.reshape(sources * width_slots, local_width)
    partial_sum = jnp.einsum(
        "rd,dgf->rgf", row_block, w_gate_up[0], preferred_element_type=jnp.float32
    )
    summed = lax.psum(partial_sum.astype(jnp.bfloat16), "exp").astype(jnp.float32)
    hidden_units = (jax.nn.silu(summed[:, 0]) * summed[:, 1]).astype(jnp.bfloat16)
    result = jnp.dot(hidden_units, w_down[0], preferred_element_type=jnp.float32).astype(
        jnp.bfloat16
    )
    result = result.reshape(sources, width_slots, local_width)
    returned = lax.all_to_all(result, "ctx", split_axis=0, concat_axis=0, tiled=True)
    back_rows = returned.reshape(ctx_count * capacity, local_width)
    picked = jnp.take(back_rows, jnp.maximum(slot_of, 0).reshape(-1), axis=0).reshape(
        tokens_here, TOPK, local_width
    )
    weight_now = gate_scores / jnp.sum(gate_scores, axis=1, keepdims=True)
    weight_now = jnp.where(active.reshape(tokens_here, TOPK), weight_now, 0.0)
    routed = jnp.zeros((tokens_here, local_width), jnp.float32)
    for column in range(TOPK):
        routed = routed + weight_now[:, column : column + 1] * picked[:, column].astype(jnp.float32)
    mixed = (hidden_state + routed).astype(jnp.bfloat16)
    return (context, mixed)


def solution(mesh):
    in_specs = (
        P("ctx", "exp", None),
        P("ctx", None, None),
        P("ctx", None, None),
        P("ctx", "exp"),
        P("exp"),
        P("ctx", None),
        P("ctx", None),
        P("ctx", "exp", None, None),
        P("ctx", None, "exp"),
        P("exp", "ctx", None),
    )
    out_specs = (P("ctx", "exp", None), P("ctx", "exp"))
    return jax.shard_map(body, mesh=mesh, in_specs=in_specs, out_specs=out_specs, check_vma=False)
```

profile of v0, /device:TPU:1, one launch (start us, length us, event | category | flops | bytes accessed | tf_op | source)
XLA Modules:
  0.0 894.8 jit_solution(3959203209659631209)
XLA Ops:
  7.2 1.0 constant_dynamic-slice_fusion.1
  8.3 0.6 copy.83
  9.0 0.9 constant_dynamic-slice_fusion
  9.9 0.6 copy.84
  10.6 1.5 copy.72
  12.2 0.6 fusion.63
  13.4 123.8 %all-gather.8.cloned.1.call-done = bf16[8192,1,128]{2,0,1:T(8,128)(2,1)} async-done(((bf16[128,1,128]{2,0,1:T(8,128)(2,1)}), bf16[8192,1,128]{2,0,1:T(8,128)(2,1)}) %all-gather.8.cloned.1.call-update) | async-done | bytes 2097168 | tf_op jit(solution)/shard_map/all_gather | solution.py:74
  137.2 118.7 %all-gather.10.cloned.1.call-done = bf16[8192,1,128]{2,0,1:T(8,128)(2,1)} async-done(((bf16[128,1,128]{2,0,1:T(8,128)(2,1)}), bf16[8192,1,128]{2,0,1:T(8,128)(2,1)}) %all-gather.10.cloned.1.call-update) | async-done | bytes 2097168 | tf_op jit(solution)/shard_map/all_gather | solution.py:75
  255.9 16.5 %conditional.1 = (f32[512]{0:T(512)S(1)}, f32[512,128]{1,0:T(8,128)S(1)}) conditional(s32[]{:T(128)} %convert_element_type.124, () %tuple.16, (s32[128]{0:T(128)S(1)}, bf16[128,4,128]{2,1,0:T(4,128)(2,1)}, bf16[8192,128]{1,0:T(8,128)(2,1)}, bf16[8192,128]{1,0:T(8,128)(2,1)}) %tuple.48), branch_computations={%region_1.2_spmd, %region_2.5_spmd} | conditional | flops 2214592000 | bytes 63332908 | solution.py:42
  255.9 0.1 broadcast_in_dim.27
  256.0 0.1 le.24
  256.1 5.0 fusion
  261.1 5.8 fusion.3
  266.9 5.5 fusion.2
  272.4 0.1 divide_convert_fusion
  272.6 104.4 %all-gather.6.cloned.1.call-done = bf16[4,128,4096]{2,0,1:T(4,128)(2,1)} async-done(((bf16[4,2,4096]{2,0,1:T(4,128)(2,1)}), bf16[4,128,4096]{2,0,1:T(4,128)(2,1)}) %all-gather.6.cloned.1.call-update) | async-done | bytes 4194320 | tf_op jit(solution)/shard_map/all_gather | solution.py:90
  377.0 8.0 fusion.8
  385.0 0.2 all-reduce.2.cloned.1.call-start
  385.3 0.1 copy.75
  385.4 0.1 eq.149
  385.5 0.1 eq.145
  385.6 18.0 %reduce-window.6 = s32[64,8,128]{2,1,0:T(8,128)S(1)} reduce-window(s32[64,8,128]{2,1,0:T(8,128)S(1)} %fusion.35, s32[]{:T(128)} %constant.71.clone.1), window={size=1x1x128 pad=0_0x0_0x127_0}, to_apply=%region_7.8 | reduce-window | flops 8323072 | bytes 524292 | tf_op jit(solution)/shard_map/reduce-window
  403.6 0.1 slice.114
  403.7 0.1 copy.77
  403.9 0.1 copy.78
  404.0 0.1 broadcast_add_fusion
  404.2 0.1 reduce_sum.40
  404.4 92.8 %reduce-scatter.2.cloned.1.call-done = bf16[128,512]{1,0:T(8,128)(2,1)} async-done(((bf16[128,4096]{1,0:T(8,128)(2,1)}), bf16[128,512]{1,0:T(8,128)(2,1)}) %reduce-scatter.2.cloned.1.call-update) | async-done | bytes 131088 | tf_op jit(solution)/shard_map/reduce_scatter | solution.py:92
  497.2 1.0 multiply_reduce_fusion
  498.3 31.1 %psum.14 = f32[128]{0:T(128)S(1)} all-reduce(f32[128]{0:T(128)S(1)} %multiply_reduce_fusion), channel_id=1, replica_groups=mesh['ctx'=64,'exp'=8] {'exp'}, use_global_device_ids=true, to_apply=%region_11.12 | all-reduce | flops 128 | bytes 1024 | tf_op jit(solution)/shard_map/psum | solution.py:96
  529.4 1.4 convolution_convert_fusion.1
  530.7 0.2 reshape.120
  531.0 68.8 %all_to_all.10 = bf16[64,10,512]{2,1,0:T(8,128)(2,1)} all-to-all(bf16[64,10,512]{2,1,0:T(8,128)(2,1)S(1)} %reshape.120), channel_id=1, replica_groups=mesh['ctx'=64,'exp'=8] {'ctx'}, dimensions={0} | all-to-all | bytes 1310720 | tf_op jit(solution)/shard_map/all_to_all | solution.py:119
  599.8 1.4 reshape.144
  601.2 2.5 convolution_convert_fusion
  603.7 216.9 %all-reduce.2.cloned.1.call-done = bf16[640,2,768]{2,0,1:T(8,128)(2,1)} async-done(((bf16[640,2,768]{2,0,1:T(8,128)(2,1)}), bf16[640,2,768]{2,0,1:T(8,128)(2,1)}) %all-reduce.2.cloned.1.call-update) | async-done | bytes 1966096 | tf_op jit(solution)/shard_map/psum | solution.py:126
  820.5 1.8 convert_element_type.143
  822.4 0.7 convolution_convert_fusion.2
  823.1 1.2 reshape.122
  824.3 6.1 all-to-all-start.1
  830.4 0.1 copy.81
  830.5 0.1 reshape.124
  830.7 0.6 slice_bitcast_fusion.23
  831.3 50.4 %all-to-all-done.1 = bf16[64,10,512]{2,1,0:T(8,128)(2,1)S(1)} async-done(((bf16[64,10,512]{2,1,0:T(8,128)(2,1)}), bf16[64,10,512]{2,1,0:T(8,128)(2,1)S(1)}, u32[]{:S(2)}, u32[]{:S(2)}) %all-to-all-start.1) | async-done | bytes 655392 | tf_op jit(solution)/shard_map/all_to_all | solution.py:132
  881.7 0.2 reshape.123
  882.0 4.0 gather_fusion
  885.9 0.7 copy_select_fusion
  886.6 1.6 fusion.28
  (42 shorter events, 0.6 us)
Async XLA Ops:
  7.2 594.0 %copy-start = (bf16[1,512,2,768]{3,2,1,0:T(2,128)(2,1)S(1)}, bf16[1,512,2,768]{3,2,1,0:T(2,128)(2,1)}, u32[]{:S(2)}) copy-start(bf16[1,512,2,768]{3,2,1,0:T(2,128)(2,1)} %param.19) | copy-start | bytes 4718596
  7.2 130.0 %all-gather.8.cloned.1.call-start = ((), (), s32[]{:S(2)}) async-start(), calls=%async_computation.6 | async-start | bytes 2129920 | tf_op jit(solution)/shard_map/all_gather | solution.py:74
  8.9 247.0 %all-gather.10.cloned.1.call-start = ((), (), s32[]{:S(2)}) async-start(), calls=%async_computation.7 | async-start | bytes 2129920 | tf_op jit(solution)/shard_map/all_gather | solution.py:75
  10.5 366.5 %all-gather.6.cloned.1.call-start = ((), (), s32[]{:S(2)}) async-start(), calls=%async_computation.3 | async-start | bytes 4259840 | tf_op jit(solution)/shard_map/all_gather | solution.py:90
  12.1 485.1 %reduce-scatter.2.cloned.1.call-start = ((), (), s32[]{:S(2)}) async-start(), calls=%async_computation.4 | async-start | bytes 1179648 | tf_op jit(solution)/shard_map/reduce_scatter | solution.py:92
  256.1 5.0 copy-start.6
  272.4 112.8 %copy-start.4 = (s32[128,8]{0,1:T(8,128)S(1)}, s32[128,8]{0,1:T(8,128)}, u32[]{:S(2)}) copy-start(s32[128,8]{0,1:T(8,128)} %param.17) | copy-start | bytes 12292
  272.6 113.0 %copy-start.3 = (bf16[512,128]{1,0:T(8,128)(2,1)}, bf16[512,128]{1,0:T(8,128)(2,1)S(1)}, u32[]{:S(2)}) copy-start(bf16[512,128]{1,0:T(8,128)(2,1)S(1)} %divide_convert_fusion) | copy-start | bytes 393220
  377.0 120.2 %copy-start.1 = (bf16[128,512]{1,0:T(8,128)(2,1)S(1)}, bf16[128,512]{1,0:T(8,128)(2,1)}, u32[]{:S(2)}) copy-start(bf16[128,512]{1,0:T(8,128)(2,1)} %param.15) | copy-start | bytes 393220
  377.0 152.4 %copy-start.8 = (f32[512]{0:T(512)S(1)}, f32[512]{0:T(512)}, u32[]{:S(2)}) copy-start(f32[512]{0:T(512)} %param.16) | copy-start | bytes 6148
  385.0 435.5 %all-reduce.2.cloned.1.call-start = ((), (), s32[]{:S(2)}) async-start(), calls=%async_computation.5 | async-start | bytes 3932160 | tf_op jit(solution)/shard_map/psum | solution.py:126
  603.6 218.8 %copy-start.7 = (bf16[1,768,512]{2,1,0:T(8,128)(2,1)S(1)}, bf16[1,768,512]{2,1,0:T(8,128)(2,1)}, u32[]{:S(2)}) copy-start(bf16[1,768,512]{2,1,0:T(8,128)(2,1)} %param.20) | copy-start | bytes 2359300
  822.4 8.2 copy-start.5
  824.3 57.4 %all-to-all-start.1 = ((bf16[64,10,512]{2,1,0:T(8,128)(2,1)}), bf16[64,10,512]{2,1,0:T(8,128)(2,1)S(1)}, u32[]{:S(2)}, u32[]{:S(2)}) async-start(bf16[64,10,512]{2,1,0:T(8,128)(2,1)} %reshape.122), calls=%async_computation.2 | async-start | bytes 2097152 | tf_op jit(solution)/shard_map/all_to_all | solution.py:132
  881.9 4.7 copy-start.2
Sparse Core Ops, SparseCore 0:
  10.7 126.4 all-gather.7
  139.3 116.4 all-gather.9
  258.6 118.3 all-gather.5
  385.2 112.0 reduce-scatter.1
  603.8 216.7 all-reduce.1
where the time goes:
time: 900 us; the launch traced here: 895 us
  waiting for transfers between devices  707 us (79%)
  blocking collectives  99.9 us (11%)
  other arithmetic  29.8 us (3%)
  matrix products  23.4 us (3%)
  between operations  14.7 us (2%)
  local copies, waits for them, and re-layouts  13.5 us (2%)
    psum x1, waiting for transfers between devices, body(): lax.psum(partial_sum.astype(jnp.bfloat16), 'exp').astype(jnp.float32)  217 us
    all_gather x1, waiting for transfers between devices, body(): lax.all_gather(key_local, 'ctx', axis=0, tiled=True)  124 us
    all_gather x1, waiting for transfers between devices, body(): lax.all_gather(value_local, 'ctx', axis=0, tiled=True)  119 us
    all_gather x1, waiting for transfers between devices, body(): whole_out = lax.all_gather(w_out, 'ctx', axis=1, tiled=True)  104 us
    reduce_scatter x1, waiting for transfers between devices, body(): lax.psum_scatter(projected.astype(jnp.bfloat16), 'exp', scatter_dimension...  92.8 us
    all_to_all x1, blocking collectives, body(): lax.all_to_all(outgoing, 'ctx', split_axis=0, concat_axis=0, tiled=True)  68.8 us
    all_to_all x1, waiting for transfers between devices, body(): lax.all_to_all(result, 'ctx', split_axis=0, concat_axis=0, tiled=True)  50.4 us
    psum x1, blocking collectives, body(): square_sum = lax.psum(jnp.sum(hidden_state * hidden_state, axis=1), 'exp')  31.1 us
  transfers between devices with their start and end apart: 6, of which 6 were waited for; matrix products, arithmetic and copies ran while one was open for 4% of the time, Pallas kernels for 0%

commit v1 on v0

v1 whole, which is shorter than its diff:
```python
import functools
import math

import jax
import jax.numpy as jnp
from jax import lax
from jax.experimental import pallas as pl
from jax.experimental.pallas import tpu as pltpu
from jax.sharding import Mesh, PartitionSpec as P

D = 4096
KVH = 2
TOPK = 8
MOST = 10
FLOOR = -1e20
EPSILON = 1e-06
CTX = ("y", "zl", "core")
EXP = ("zh", "x")
SIZES = {"y": 4, "zl": 8, "core": 2, "zh": 2, "x": 4}
F32 = jnp.float32
BF16 = jnp.bfloat16


def shift(value, axis, step):
    count = SIZES[axis]
    return lax.ppermute(value, axis, [(i, (i + step) % count) for i in range(count)])


def attend_kernel(place, q_ref, k_ref, v_ref, o_ref, *, heads, piece, tokens):
    rows = q_ref.shape[0]
    keys = k_ref.shape[0]
    half = keys // 2
    scores = lax.dot_general(
        k_ref[...], q_ref[...], (((1,), (1,)), ((), ())), preferred_element_type=F32
    )
    key = lax.broadcasted_iota(jnp.int32, (keys, rows), 0)
    row = lax.broadcasted_iota(jnp.int32, (keys, rows), 1) + pl.program_id(0) * rows
    core = jnp.where(key >= half, 1 - place[1], place[1])
    block = (key % half) // piece
    key_pos = (block * 2 + core) * tokens + place[2] * piece + key % piece
    row_pos = place[0] + row // heads
    factor = math.log2(math.e) / math.sqrt(q_ref.shape[1])
    masked = jnp.where(key_pos <= row_pos, scores * factor, -1e30)
    best = jnp.max(masked, axis=0, keepdims=True)
    best = jnp.maximum(best, FLOOR).astype(BF16)
    prob = jnp.exp2(masked - best.astype(F32))
    total = jnp.sum(prob, axis=0, keepdims=True)
    high = total.astype(BF16)
    low = (total - high.astype(F32)).astype(BF16)
    summed = lax.dot_general(
        v_ref[...], prob.astype(BF16), (((0,), (0,)), ((), ())), preferred_element_type=F32
    )
    size = v_ref.shape[1]
    o_ref[0:size, :] = summed.astype(BF16)
    line = lax.broadcasted_iota(jnp.int32, (16, rows), 0)
    extra = jnp.where(
        line == 0,
        best.astype(F32),
        jnp.where(line == 1, high.astype(F32), jnp.where(line == 2, low.astype(F32), 0.0)),
    )
    o_ref[size : size + 16, :] = extra.astype(BF16)


def attend(place, rows, keys, values, heads, piece, tokens):
    count, size = rows.shape
    step = 256
    return pl.pallas_call(
        functools.partial(attend_kernel, heads=heads, piece=piece, tokens=tokens),
        out_shape=jax.ShapeDtypeStruct((size + 16, count), BF16),
        grid=(count // step,),
        in_specs=[
            pl.BlockSpec(memory_space=pltpu.SMEM),
            pl.BlockSpec((step, size), lambda i: (i, 0)),
            pl.BlockSpec(keys.shape, lambda i: (0, 0)),
            pl.BlockSpec(values.shape, lambda i: (0, 0)),
        ],
        out_specs=pl.BlockSpec((size + 16, step), lambda i: (0, i)),
        compiler_params=pltpu.CompilerParams(vmem_limit_bytes=48 << 20),
        name="attend",
    )(place, rows, keys, values)


def body(queries, keys, values, resid, gain, expert_ids, gate_scores, w_gate_up, w_down, w_out):
    tokens, heads, size = queries.shape
    y, zl, core = lax.axis_index("y"), lax.axis_index("zl"), lax.axis_index("core")
    zh, x = lax.axis_index("zh"), lax.axis_index("x")
    ctx_place = (y * 8 + zl) * 2 + core
    ctx_count = 64
    width = resid.shape[1]

    whole_out = lax.all_gather(w_out, CTX, axis=1, tiled=True)

    piece = tokens // 4
    pair = jnp.stack([keys, values], axis=0)
    pair = lax.dynamic_index_in_dim(pair, zh, 2, keepdims=False)
    pair = lax.dynamic_slice_in_dim(pair, x * piece, piece, 1)
    pair = jnp.broadcast_to(pair[None], (8,) + pair.shape)
    pair = lax.all_to_all(pair, "zl", 0, 0, tiled=True)
    pair = jnp.broadcast_to(pair[None], (4,) + pair.shape)
    pair = lax.all_to_all(pair, "y", 0, 0, tiled=True)
    pair = jnp.stack([pair, shift(pair, "core", 1)], axis=0)
    all_keys = pair[:, :, :, 0].reshape(-1, size)
    all_values = pair[:, :, :, 1].reshape(-1, size)

    rows = queries.reshape(tokens * heads, size)
    place = jnp.stack([ctx_place * tokens, core, x]).astype(jnp.int32)
    asked = [shift(rows, "x", step) for step in (1, 2, 3)]
    parts = []
    for step in (2, 1, 3):
        found = attend(place, asked[step - 1], all_keys, all_values, heads, piece, tokens)
        parts.append(shift(found, "x", -step))
    parts.append(attend(place, rows, all_keys, all_values, heads, piece, tokens))

    bests = [part[size].astype(F32) for part in parts]
    best = functools.reduce(jnp.maximum, bests)
    above = jnp.zeros((size, tokens * heads), F32)
    below = jnp.zeros((tokens * heads,), F32)
    for part, top in zip(parts, bests):
        scale = jnp.exp2(top - best)
        above = above + part[:size].astype(F32) * scale[None, :]
        below = below + (part[size + 1].astype(F32) + part[size + 2].astype(F32)) * scale
    context = (above / below[None, :]).astype(BF16).T.reshape(tokens, heads, size)

    projected = jnp.dot(
        context.reshape(tokens, heads * size),
        whole_out.reshape(heads * size, D),
        preferred_element_type=F32,
    ).astype(BF16)
    projected = projected.reshape(tokens, 2, 4, width).transpose(2, 1, 0, 3)
    projected = lax.all_to_all(projected, "x", 0, 0, tiled=True)
    half = jnp.sum(projected.astype(F32), axis=0)
    theirs = lax.dynamic_index_in_dim(half, 1 - zh, 0, keepdims=False).astype(BF16)
    mine = lax.dynamic_index_in_dim(half, zh, 0, keepdims=False)
    attended = mine + shift(theirs, "zh", 1).astype(F32)
    state = resid.astype(F32) + attended
    scaled = (state * gain[None, :]).astype(BF16)

    slots = ctx_count * MOST
    ids = expert_ids.T
    expert = jnp.arange(ctx_count, dtype=jnp.int32)
    named = (ids[:, None, :] == expert[None, :, None]).astype(F32)
    weight = (gate_scores / jnp.sum(gate_scores, axis=1, keepdims=True)).T
    weight = jnp.sum(named * weight[:, None, :], axis=0)
    named = jnp.sum(named, axis=0).astype(BF16)
    token = jnp.arange(tokens, dtype=jnp.int32)
    before = (token[:, None] < token[None, :]).astype(BF16)
    rank = jnp.dot(named, before, preferred_element_type=F32)
    slot = jnp.arange(slots, dtype=jnp.int32)
    spread = (slot[:, None] // MOST == expert[None, :]).astype(BF16)
    weight_high = weight.astype(BF16)
    weight_low = (weight - weight_high.astype(F32)).astype(BF16)
    rank = jnp.where(named > 0, rank, -1.0).astype(BF16)
    tables = jnp.concatenate([rank, weight_high, weight_low], axis=1)
    tables = jnp.dot(spread, tables, preferred_element_type=F32)
    live = tables[:, :tokens] == (slot % MOST).astype(F32)[:, None]
    dispatch = live.astype(BF16)
    combine = jnp.concatenate(
        [
            jnp.where(live, tables[:, tokens : 2 * tokens], 0.0).astype(BF16),
            jnp.where(live, tables[:, 2 * tokens :], 0.0).astype(BF16),
        ],
        axis=1,
    )

    outgoing = jnp.dot(dispatch, scaled, preferred_element_type=F32).astype(BF16)
    outgoing = outgoing.reshape(ctx_count, MOST, width)
    arrived = lax.all_to_all(outgoing, CTX, 0, 0, tiled=True).reshape(slots, width)

    units = w_gate_up.shape[3]
    part = jnp.dot(
        arrived, w_gate_up.reshape(width, 2 * units), preferred_element_type=F32
    ).astype(BF16)
    plain = arrived.astype(F32) / gain[None, :]
    square = jnp.sum(plain * plain, axis=1, keepdims=True)
    high = square.astype(BF16)
    low = (square - high.astype(F32)).astype(BF16)
    lane = jnp.arange(128)[None, :]
    extra = jnp.where(lane == 0, high, jnp.where(lane == 1, low, jnp.zeros((), BF16)))
    part = jnp.concatenate([part, extra], axis=1)
    part = part.reshape(4, slots // 4, 2 * units + 128)
    part = lax.all_to_all(part, "x", 0, 0, tiled=True)
    part = jnp.sum(part.astype(F32), axis=0).reshape(2, slots // 8, 2 * units + 128)
    theirs = lax.dynamic_index_in_dim(part, 1 - zh, 0, keepdims=False).astype(BF16)
    mine = lax.dynamic_index_in_dim(part, zh, 0, keepdims=False)
    part = mine + shift(theirs, "zh", 1).astype(F32)
    square = part[:, 2 * units : 2 * units + 1] + part[:, 2 * units + 1 : 2 * units + 2]
    inverse = lax.rsqrt(square / D + EPSILON)
    hidden = (jax.nn.silu(part[:, :units] * inverse) * (part[:, units : 2 * units] * inverse)).astype(
        BF16
    )
    other = shift(hidden, "zh", 1)
    hidden = jnp.where(
        zh == 0, jnp.stack([hidden, other], axis=0), jnp.stack([other, hidden], axis=0)
    ).reshape(slots // 4, units)
    hidden = lax.all_gather(hidden, "x", axis=0, tiled=True)
    result = jnp.dot(hidden, w_down[0], preferred_element_type=F32).astype(BF16)
    result = result.reshape(ctx_count, MOST, width)
    returned = lax.all_to_all(result, CTX, 0, 0, tiled=True).reshape(slots, width)
    routed = lax.dot_general(
        combine, returned, (((0,), (0,)), ((), ())), preferred_element_type=F32
    )
    routed = routed[:tokens] + routed[tokens:]
    mixed = (state + routed).astype(BF16)
    return (context, mixed)


def solution(mesh):
    mesh = Mesh(mesh.devices.reshape(4, 8, 2, 2, 4), CTX + EXP)
    in_specs = (
        P(CTX, EXP, None),
        P(CTX, None, None),
        P(CTX, None, None),
        P(CTX, EXP),
        P(EXP),
        P(CTX, None),
        P(CTX, None),
        P(CTX, EXP, None, None),
        P(CTX, None, EXP),
        P(EXP, CTX, None),
    )
    out_specs = (P(CTX, EXP, None), P(CTX, EXP))
    return jax.shard_map(body, mesh=mesh, in_specs=in_specs, out_specs=out_specs, check_vma=False)
```

time: 900 us -> 426 us (0.47)
  waiting for transfers between devices: 707 us -> 198 us
  starting transfers between devices: 6.47 us -> 93.9 us
  other arithmetic: 29.8 us -> 5.37 us
  blocking collectives: 99.9 us -> 76.2 us
  matrix products: 23.4 us -> 6.47 us
  Pallas kernels: 0 us -> 13.7 us
    all_gather x3 -> x1, waiting for transfers between devices: 347 us -> 49.8 us  [body(): whole_out = lax.all_gather(w_out, CTX, axis=1, tiled=True)]
    psum x1 -> x0, waiting for transfers between devices: 217 us -> none  [body(): lax.psum(partial_sum.astype(jnp.bfloat16), 'exp').astype(jnp.float32)]
    reduce_scatter x1 -> x0, waiting for transfers between devices: 92.8 us -> none  [body(): lax.psum_scatter(projected.astype(jnp.bfloat16), 'exp', scatter_dimension...]
    all_to_all x1 -> x3, waiting for transfers between devices: 50.4 us -> 113 us  [the longest x1 50.6 us: body(): lax.all_to_all(result, CTX, 0, 0, tiled=True).reshape(slots, width)]
    ppermute x0 -> x10, starting transfers between devices: none -> 52.1 us  [shift(): lax.ppermute(value, axis, [(i, (i + step) % count) for i in range(count)])]
    all_to_all x1 -> x3, starting transfers between devices: 6.08 us -> 41.8 us  [the longest x1 21.3 us: body(): lax.all_to_all(result, CTX, 0, 0, tiled=True).reshape(slots, width)]
    ppermute x0 -> x10, waiting for transfers between devices: none -> 34.9 us  [shift(): lax.ppermute(value, axis, [(i, (i + step) % count) for i in range(count)])]
    psum x1 -> x0, blocking collectives: 31.1 us -> none  [body(): square_sum = lax.psum(jnp.sum(hidden_state * hidden_state, axis=1), 'exp')]
  transfers between devices with their start and end apart: 6 -> 14, of which waited for: 6 -> 9; matrix products, arithmetic and copies ran while one was open for 4% -> 2% of each run, Pallas kernels for 0% -> 3%
where the time goes in v1:
time: 426 us; the launch traced here: 425 us
  waiting for transfers between devices  198 us (46%)
  starting transfers between devices  93.9 us (22%)
  blocking collectives  76.2 us (18%)
  local copies, waits for them, and re-layouts  17.4 us (4%)
  between operations  14.5 us (3%)
  Pallas kernels  13.7 us (3%)
  matrix products  6.47 us (2%)
  other arithmetic  5.37 us (1%)
    ppermute x10, starting transfers between devices, shift(): lax.ppermute(value, axis, [(i, (i + step) % count) for i in range(count)])  52.1 us
    all_to_all x1, waiting for transfers between devices, body(): lax.all_to_all(result, CTX, 0, 0, tiled=True).reshape(slots, width)  50.6 us
    all_gather x1, waiting for transfers between devices, body(): whole_out = lax.all_gather(w_out, CTX, axis=1, tiled=True)  49.8 us
    all_to_all x1, waiting for transfers between devices, body(): lax.all_to_all(outgoing, CTX, 0, 0, tiled=True).reshape(slots, width)  48.5 us
    ppermute x10, waiting for transfers between devices, shift(): lax.ppermute(value, axis, [(i, (i + step) % count) for i in range(count)])  34.9 us
    all_to_all x1, blocking collectives, body(): part = lax.all_to_all(part, 'x', 0, 0, tiled=True)  28.7 us
    all_to_all x1, blocking collectives, body(): pair = lax.all_to_all(pair, 'zl', 0, 0, tiled=True)  23.2 us
    all_to_all x1, starting transfers between devices, body(): lax.all_to_all(result, CTX, 0, 0, tiled=True).reshape(slots, width)  21.3 us
  transfers between devices with their start and end apart: 14, of which 9 were waited for; matrix products, arithmetic and copies ran while one was open for 2% of the time, Pallas kernels for 3%

profile of v1, /device:TPU:1, one launch (start us, length us, event | category | flops | bytes accessed | tf_op | source)
XLA Modules:
  0.0 425.4 jit_solution(4636434207891985788)
XLA Ops:
  7.2 1.6 copy.58
  8.9 0.9 copy_bitcast_fusion.1
  9.8 23.2 %all_to_all.30 = bf16[8,2,32,128]{3,2,1,0:T(8,128)(2,1)S(1)} all-to-all(bf16[8,2,32,128]{3,2,1,0:T(8,128)(2,1)S(1)} %broadcast_in_dim.46), channel_id=1, replica_groups=mesh['y'=4,'zl'=8,'core'=2,'zh'=2,'x'=4] {'zl'}, dimensions={0} | all-to-all | bytes 262144 | tf_op jit(solution)/shard_map/all_to_all | solution.py:98
  33.1 12.6 %all_to_all.31 = bf16[4,8,2,32,128]{4,3,1,2,0:T(8,128)(2,1)S(1)} all-to-all(bf16[4,8,2,32,128]{4,3,1,2,0:T(8,128)(2,1)S(1)} %broadcast_in_dim.47), channel_id=1, replica_groups=mesh['y'=4,'zl'=8,'core'=2,'zh'=2,'x'=4] {'y'}, dimensions={0} | all-to-all | bytes 1048576 | tf_op jit(solution)/shard_map/all_to_all | solution.py:100
  45.7 5.4 %collective-permute-start.1 = (bf16[4,8,2,32,128]{4,3,1,2,0:T(8,128)(2,1)S(1)}, bf16[4,8,2,32,128]{4,3,1,2,0:T(8,128)(2,1)S(1)}, u32[]{:S(2)}, u32[]{:S(2)}) collective-permute-start(bf16[4,8,2,32,128]{4,3,1,2,0:T(8,128)(2,1)S(1)} %all_to_all.31), channel_id=1, source_target_pairs={{0,8},{8,0},{1,9},{9,1},{2,10},{10,2},{3,11},{11,3},{4,12},{12,4},... | collective-permute-start | bytes 1572872 | tf_op jit(solution)/shard_map/ppermute | solution.py:26
  51.1 4.4 %collective-permute-start.5 = (bf16[512,128]{1,0:T(8,128)(2,1)S(1)}, bf16[512,128]{1,0:T(8,128)(2,1)S(1)}, u32[]{:S(2)}, u32[]{:S(2)}) collective-permute-start(bf16[512,128]{1,0:T(8,128)(2,1)S(1)} %bitcast.72), channel_id=1, source_target_pairs={{0,3},{1,0},{2,1},{3,2},{4,7},{5,4},{6,5},{7,6},{8,11},{9,8},{10,9... | collective-permute-start | bytes 393224 | tf_op jit(solution)/shard_map/ppermute | solution.py:26
  55.5 1.9 collective-permute-start.3
  57.5 3.6 collective-permute-start
  61.3 4.4 %collective-permute-done.q_ref = bf16[512,128]{1,0:T(8,128)(2,1)S(1)} collective-permute-done((bf16[512,128]{1,0:T(8,128)(2,1)S(1)}, bf16[512,128]{1,0:T(8,128)(2,1)S(1)}, u32[]{:S(2)}, u32[]{:S(2)}) %collective-permute-start) | collective-permute-done | bytes 131104 | tf_op jit(solution)/shard_map/ppermute | solution.py:26
  65.7 3.4 attend.4
  69.1 3.3 collective-permute-start.2
  72.4 3.4 attend.5
  75.8 3.0 collective-permute-start.4
  78.8 3.4 attend.6
  82.3 2.4 collective-permute-start.6
  84.8 3.4 attend.7
  88.2 1.2 collective-permute-done.6
  89.8 49.8 %all-gather.2.cloned.1.call-done = bf16[4,128,4096]{2,0,1:T(4,128)(2,1)} async-done(((bf16[4,2,4096]{2,0,1:T(4,128)(2,1)}), bf16[4,128,4096]{2,0,1:T(4,128)(2,1)}) %all-gather.2.cloned.1.call-update) | async-done | bytes 4194320 | tf_op jit(solution)/shard_map/all_gather | solution.py:91
  139.5 4.5 %copy.59 = bf16[4,128,4096]{2,1,0:T(8,128)(2,1)S(1)} copy(bf16[4,128,4096]{2,0,1:T(4,128)(2,1)} %all-gather.2.cloned.1.call-done) | data formatting | bytes 8388608 | tf_op jit(solution)/shard_map/all_gather | solution.py:91
  144.0 0.7 convolution_convert_fusion
  144.7 0.8 reshape.120
  145.6 1.8 copy.74
  147.3 4.1 all-to-all-start.2
  152.0 14.1 %all-to-all-done.2 = bf16[4,2,128,512]{3,1,2,0:T(2,128)(2,1)S(1)} async-done(((bf16[4,2,128,512]{3,1,2,0:T(2,128)(2,1)}), bf16[4,2,128,512]{3,1,2,0:T(2,128)(2,1)S(1)}, u32[]{:S(2)}, u32[]{:S(2)}) %all-to-all-start.2) | async-done | bytes 1048608 | tf_op jit(solution)/shard_map/all_to_all | solution.py:130
  166.2 8.2 %collective-permute-start.7 = (bf16[128,512]{1,0:T(8,128)(2,1)S(1)}, bf16[128,512]{1,0:T(8,128)(2,1)S(1)}, u32[]{:S(2)}, u32[]{:S(2)}) collective-permute-start(bf16[128,512]{1,0:T(8,128)(2,1)S(1)} %fusion.17), channel_id=1, source_target_pairs={{0,4},{4,0},{1,5},{5,1},{2,6},{6,2},{3,7},{7,3},{8,12},{12,8},{9,1... | collective-permute-start | bytes 393224 | tf_op jit(solution)/shard_map/ppermute | solution.py:26
  174.4 0.7 fusion.4
  175.1 6.0 %collective-permute-done.7 = bf16[128,512]{1,0:T(8,128)(2,1)S(1)} collective-permute-done((bf16[128,512]{1,0:T(8,128)(2,1)S(1)}, bf16[128,512]{1,0:T(8,128)(2,1)S(1)}, u32[]{:S(2)}, u32[]{:S(2)}) %collective-permute-start.7) | collective-permute-done | bytes 131104 | tf_op jit(solution)/shard_map/ppermute | solution.py:26
  181.5 1.2 reshape.121
  182.8 16.4 %all-to-all-start.3 = ((bf16[64,10,512]{2,1,0:T(8,128)(2,1)}), bf16[64,10,512]{2,1,0:T(8,128)(2,1)S(1)}, u32[]{:S(2)}, u32[]{:S(2)}) async-start(bf16[64,10,512]{2,1,0:T(8,128)(2,1)} %reshape.121), calls=%async_computation.3 | async-start | bytes 2097152 | tf_op jit(solution)/shard_map/all_to_all | solution.py:167
  199.2 2.8 copy.69
  202.1 48.5 %all-to-all-done.3 = bf16[64,10,512]{2,1,0:T(8,128)(2,1)S(1)} async-done(((bf16[64,10,512]{2,1,0:T(8,128)(2,1)}), bf16[64,10,512]{2,1,0:T(8,128)(2,1)S(1)}, u32[]{:S(2)}, u32[]{:S(2)}) %all-to-all-start.3) | async-done | bytes 655392 | tf_op jit(solution)/shard_map/all_to_all | solution.py:167
  251.1 1.1 reshape.122
  252.1 2.8 convolution_convert_fusion.1
  255.3 28.7 %all_to_all.32 = bf16[4,160,1664]{2,1,0:T(8,128)(2,1)S(1)} all-to-all(bf16[4,160,1664]{2,1,0:T(8,128)(2,1)S(1)} %bitcast.77), channel_id=1, replica_groups=mesh['y'=4,'zl'=8,'core'=2,'zh'=2,'x'=4] {'x'}, dimensions={0} | all-to-all | bytes 4259840 | tf_op jit(solution)/shard_map/all_to_all | solution.py:181
  284.3 0.7 fusion.10
  285.1 9.2 %collective-permute-start.8 = (bf16[80,1664]{1,0:T(8,128)(2,1)}, bf16[80,1664]{1,0:T(8,128)(2,1)}, u32[]{:S(2)}, u32[]{:S(2)}) collective-permute-start(bf16[80,1664]{1,0:T(8,128)(2,1)} %fusion.10), channel_id=1, source_target_pairs={{0,4},{4,0},{1,5},{5,1},{2,6},{6,2},{3,7},{7,3},{8,12},{12,8},{9,1... | collective-permute-start | bytes 798728 | tf_op jit(solution)/shard_map/ppermute | solution.py:26
  294.3 17.4 %collective-permute-done.8 = bf16[80,1664]{1,0:T(8,128)(2,1)} collective-permute-done((bf16[80,1664]{1,0:T(8,128)(2,1)}, bf16[80,1664]{1,0:T(8,128)(2,1)}, u32[]{:S(2)}, u32[]{:S(2)}) %collective-permute-start.8) | collective-permute-done | bytes 266272 | tf_op jit(solution)/shard_map/ppermute | solution.py:26
  311.7 1.0 bitcast_add_fusion
  313.0 10.8 %collective-permute-start.9 = (bf16[80,768]{1,0:T(8,128)(2,1)S(1)}, bf16[80,768]{1,0:T(8,128)(2,1)S(1)}, u32[]{:S(2)}, u32[]{:S(2)}) collective-permute-start(bf16[80,768]{1,0:T(8,128)(2,1)S(1)} %fusion.15), channel_id=1, source_target_pairs={{0,4},{4,0},{1,5},{5,1},{2,6},{6,2},{3,7},{7,3},{8,12},{12,8},{9,1... | collective-permute-start | bytes 368648 | tf_op jit(solution)/shard_map/ppermute | solution.py:26
  324.0 6.0 %collective-permute-done.9 = bf16[80,768]{1,0:T(8,128)(2,1)S(1)} collective-permute-done((bf16[80,768]{1,0:T(8,128)(2,1)S(1)}, bf16[80,768]{1,0:T(8,128)(2,1)S(1)}, u32[]{:S(2)}, u32[]{:S(2)}) %collective-permute-start.9) | collective-permute-done | bytes 122912 | tf_op jit(solution)/shard_map/ppermute | solution.py:26
  330.0 11.7 %all_gather.7 = bf16[640,768]{1,0:T(8,128)(2,1)S(1)} all-gather(bf16[160,768]{1,0:T(8,128)(2,1)S(1)} %bitcast.83), channel_id=1, replica_groups=mesh['y'=4,'zl'=8,'core'=2,'zh'=2,'x'=4] {'x'}, dimensions={0}, use_global_device_ids=true | all-gather | bytes 1228800 | tf_op jit(solution)/shard_map/all_gather | solution.py:195
  341.7 0.7 convolution_convert_fusion.3
  342.4 1.2 reshape.126
  343.6 21.3 %all-to-all-start.5 = ((bf16[64,10,512]{2,1,0:T(8,128)(2,1)}), bf16[64,10,512]{2,1,0:T(8,128)(2,1)S(1)}, u32[]{:S(2)}, u32[]{:S(2)}) async-start(bf16[64,10,512]{2,1,0:T(8,128)(2,1)} %reshape.126), calls=%async_computation.5 | async-start | bytes 2097152 | tf_op jit(solution)/shard_map/all_to_all | solution.py:198
  364.9 0.7 fusion.3
  365.6 50.6 %all-to-all-done.5 = bf16[64,10,512]{2,1,0:T(8,128)(2,1)S(1)} async-done(((bf16[64,10,512]{2,1,0:T(8,128)(2,1)}), bf16[64,10,512]{2,1,0:T(8,128)(2,1)S(1)}, u32[]{:S(2)}, u32[]{:S(2)}) %all-to-all-start.5) | async-done | bytes 655392 | tf_op jit(solution)/shard_map/all_to_all | solution.py:198
  416.4 1.4 fusion.5
  417.8 0.8 fusion.12
  (60 shorter events, 3.9 us)
Async XLA Ops:
  7.2 334.6 %copy-start = (bf16[1,768,512]{2,1,0:T(8,128)(2,1)S(1)}, bf16[1,768,512]{2,1,0:T(8,128)(2,1)}, u32[]{:S(2)}) copy-start(bf16[1,768,512]{2,1,0:T(8,128)(2,1)} %param.18) | copy-start | bytes 2359300
  7.2 44.0 %copy-start.1 = (bf16[128,4,128]{2,1,0:T(4,128)(2,1)S(1)}, bf16[128,4,128]{2,1,0:T(4,128)(2,1)}, u32[]{:S(2)}) copy-start(bf16[128,4,128]{2,1,0:T(4,128)(2,1)} %param.10) | copy-start | bytes 393220
  7.2 53.9 %copy-start.7 = (f32[128,8]{0,1:T(8,128)S(1)}, f32[128,8]{0,1:T(8,128)}, u32[]{:S(2)}) copy-start(f32[128,8]{0,1:T(8,128)} %param.16) | copy-start | bytes 12292
  7.2 132.3 %all-gather.2.cloned.1.call-start = ((), (), s32[]{:S(2)}) async-start(), calls=%async_computation.6 | async-start | bytes 4259840 | tf_op jit(solution)/shard_map/all_gather | solution.py:91
  45.7 15.5 %collective-permute-start.1 = (bf16[4,8,2,32,128]{4,3,1,2,0:T(8,128)(2,1)S(1)}, bf16[4,8,2,32,128]{4,3,1,2,0:T(8,128)(2,1)S(1)}, u32[]{:S(2)}, u32[]{:S(2)}) collective-permute-start(bf16[4,8,2,32,128]{4,3,1,2,0:T(8,128)(2,1)S(1)} %all_to_all.31), channel_id=1, source_target_pairs={{0,8},{8,0},{1,9},{9,1},{2,10},{10,2},{3,11},{11,3},{4,12},{12,4},... | collective-permute-start | bytes 1572872 | tf_op jit(solution)/shard_map/ppermute | solution.py:26
  51.1 27.7 %collective-permute-start.5 = (bf16[512,128]{1,0:T(8,128)(2,1)S(1)}, bf16[512,128]{1,0:T(8,128)(2,1)S(1)}, u32[]{:S(2)}, u32[]{:S(2)}) collective-permute-start(bf16[512,128]{1,0:T(8,128)(2,1)S(1)} %bitcast.72), channel_id=1, source_target_pairs={{0,3},{1,0},{2,1},{3,2},{4,7},{5,4},{6,5},{7,6},{8,11},{9,8},{10,9... | collective-permute-start | bytes 393224 | tf_op jit(solution)/shard_map/ppermute | solution.py:26
  55.5 16.9 %collective-permute-start.3 = (bf16[512,128]{1,0:T(8,128)(2,1)S(1)}, bf16[512,128]{1,0:T(8,128)(2,1)S(1)}, u32[]{:S(2)}, u32[]{:S(2)}) collective-permute-start(bf16[512,128]{1,0:T(8,128)(2,1)S(1)} %bitcast.73), channel_id=1, source_target_pairs={{0,1},{1,2},{2,3},{3,0},{4,5},{5,6},{6,7},{7,4},{8,9},{9,10},{10,1... | collective-permute-start | bytes 393224 | tf_op jit(solution)/shard_map/ppermute | solution.py:26
  57.5 8.2 %collective-permute-start = (bf16[512,128]{1,0:T(8,128)(2,1)S(1)}, bf16[512,128]{1,0:T(8,128)(2,1)S(1)}, u32[]{:S(2)}, u32[]{:S(2)}) collective-permute-start(bf16[512,128]{1,0:T(8,128)(2,1)S(1)} %bitcast.74), channel_id=1, source_target_pairs={{0,2},{1,3},{2,0},{3,1},{4,6},{5,7},{6,4},{7,5},{8,10},{9,11},{10,... | collective-permute-start | bytes 393224 | tf_op jit(solution)/shard_map/ppermute | solution.py:26
  61.3 23.4 %copy-start.9 = (s32[128,8]{0,1:T(8,128)S(1)}, s32[128,8]{0,1:T(8,128)}, u32[]{:S(2)}) copy-start(s32[128,8]{0,1:T(8,128)} %param.15) | copy-start | bytes 12292
  69.1 19.1 %collective-permute-start.2 = (bf16[144,512]{1,0:T(8,128)(2,1)S(1)}, bf16[144,512]{1,0:T(8,128)(2,1)S(1)}, u32[]{:S(2)}, u32[]{:S(2)}) collective-permute-start(bf16[144,512]{1,0:T(8,128)(2,1)S(1)} %attend.4), channel_id=1, source_target_pairs={{0,2},{1,3},{2,0},{3,1},{4,6},{5,7},{6,4},{7,5},{8,10},{9,11},{10,... | collective-permute-start | bytes 442376 | tf_op jit(solution)/shard_map/ppermute | solution.py:26
  75.8 12.4 %collective-permute-start.4 = (bf16[144,512]{1,0:T(8,128)(2,1)S(1)}, bf16[144,512]{1,0:T(8,128)(2,1)S(1)}, u32[]{:S(2)}, u32[]{:S(2)}) collective-permute-start(bf16[144,512]{1,0:T(8,128)(2,1)S(1)} %attend.5), channel_id=1, source_target_pairs={{0,3},{1,0},{2,1},{3,2},{4,7},{5,4},{6,5},{7,6},{8,11},{9,8},{10,9... | collective-permute-start | bytes 442376 | tf_op jit(solution)/shard_map/ppermute | solution.py:26
  82.3 7.1 %collective-permute-start.6 = (bf16[144,512]{1,0:T(8,128)(2,1)S(1)}, bf16[144,512]{1,0:T(8,128)(2,1)S(1)}, u32[]{:S(2)}, u32[]{:S(2)}) collective-permute-start(bf16[144,512]{1,0:T(8,128)(2,1)S(1)} %attend.6), channel_id=1, source_target_pairs={{0,1},{1,2},{2,3},{3,0},{4,5},{5,6},{6,7},{7,4},{8,9},{9,10},{10,1... | collective-permute-start | bytes 442376 | tf_op jit(solution)/shard_map/ppermute | solution.py:26
  89.7 54.4 %copy-start.6 = (bf16[512,128]{1,0:T(8,128)(2,1)}, bf16[512,128]{1,0:T(8,128)(2,1)S(1)}, u32[]{:S(2)}) copy-start(bf16[512,128]{1,0:T(8,128)(2,1)S(1)} %copy.56) | copy-start | bytes 393220
  147.3 18.7 %all-to-all-start.2 = ((bf16[4,2,128,512]{3,1,2,0:T(2,128)(2,1)}), bf16[4,2,128,512]{3,1,2,0:T(2,128)(2,1)S(1)}, u32[]{:S(2)}, u32[]{:S(2)}) async-start(bf16[4,2,128,512]{3,1,2,0:T(2,128)(2,1)} %bitcast.63), calls=%async_computation.2 | async-start | bytes 2097152 | tf_op jit(solution)/shard_map/all_to_all | solution.py:130
  151.4 29.7 %copy-start.2 = (bf16[128,512]{1,0:T(8,128)(2,1)S(1)}, bf16[128,512]{1,0:T(8,128)(2,1)}, u32[]{:S(2)}) copy-start(bf16[128,512]{1,0:T(8,128)(2,1)} %param.13) | copy-start | bytes 393220
  151.4 29.7 %copy-start.8 = (f32[512]{0:T(512)S(1)}, f32[512]{0:T(512)}, u32[]{:S(2)}) copy-start(f32[512]{0:T(512)} %param.14) | copy-start | bytes 6148
  166.2 14.9 %collective-permute-start.7 = (bf16[128,512]{1,0:T(8,128)(2,1)S(1)}, bf16[128,512]{1,0:T(8,128)(2,1)S(1)}, u32[]{:S(2)}, u32[]{:S(2)}) collective-permute-start(bf16[128,512]{1,0:T(8,128)(2,1)S(1)} %fusion.17), channel_id=1, source_target_pairs={{0,4},{4,0},{1,5},{5,1},{2,6},{6,2},{3,7},{7,3},{8,12},{12,8},{9,1... | collective-permute-start | bytes 393224 | tf_op jit(solution)/shard_map/ppermute | solution.py:26
  181.1 1.6 copy-start.4
  182.8 67.8 %all-to-all-start.3 = ((bf16[64,10,512]{2,1,0:T(8,128)(2,1)}), bf16[64,10,512]{2,1,0:T(8,128)(2,1)S(1)}, u32[]{:S(2)}, u32[]{:S(2)}) async-start(bf16[64,10,512]{2,1,0:T(8,128)(2,1)} %reshape.121), calls=%async_computation.3 | async-start | bytes 2097152 | tf_op jit(solution)/shard_map/all_to_all | solution.py:167
  285.1 26.6 %collective-permute-start.8 = (bf16[80,1664]{1,0:T(8,128)(2,1)}, bf16[80,1664]{1,0:T(8,128)(2,1)}, u32[]{:S(2)}, u32[]{:S(2)}) collective-permute-start(bf16[80,1664]{1,0:T(8,128)(2,1)} %fusion.10), channel_id=1, source_target_pairs={{0,4},{4,0},{1,5},{5,1},{2,6},{6,2},{3,7},{7,3},{8,12},{12,8},{9,1... | collective-permute-start | bytes 798728 | tf_op jit(solution)/shard_map/ppermute | solution.py:26
  313.0 16.9 %collective-permute-start.9 = (bf16[80,768]{1,0:T(8,128)(2,1)S(1)}, bf16[80,768]{1,0:T(8,128)(2,1)S(1)}, u32[]{:S(2)}, u32[]{:S(2)}) collective-permute-start(bf16[80,768]{1,0:T(8,128)(2,1)S(1)} %fusion.15), channel_id=1, source_target_pairs={{0,4},{4,0},{1,5},{5,1},{2,6},{6,2},{3,7},{7,3},{8,12},{12,8},{9,1... | collective-permute-start | bytes 368648 | tf_op jit(solution)/shard_map/ppermute | solution.py:26
  343.6 72.6 %all-to-all-start.5 = ((bf16[64,10,512]{2,1,0:T(8,128)(2,1)}), bf16[64,10,512]{2,1,0:T(8,128)(2,1)S(1)}, u32[]{:S(2)}, u32[]{:S(2)}) async-start(bf16[64,10,512]{2,1,0:T(8,128)(2,1)} %reshape.126), calls=%async_computation.5 | async-start | bytes 2097152 | tf_op jit(solution)/shard_map/all_to_all | solution.py:198
  364.8 52.9 %copy-start.3 = (bf16[128,512]{1,0:T(8,128)(2,1)S(1)}, bf16[128,512]{1,0:T(8,128)(2,1)}, u32[]{:S(2)}) copy-start(bf16[128,512]{1,0:T(8,128)(2,1)} %param.13) | copy-start | bytes 393220
  365.6 52.2 %copy-start.5 = (bf16[128,512]{1,0:T(8,128)(2,1)S(1)}, bf16[128,512]{1,0:T(8,128)(2,1)}, u32[]{:S(2)}) copy-start(bf16[128,512]{1,0:T(8,128)(2,1)} %copy-done.4) | copy-start | bytes 393220
Sparse Core Ops, SparseCore 0:
  10.8 128.7 all-gather.1

commit v2 on v1

--- a/solution.py
+++ b/solution.py
@@ -24,6 +24,110 @@
 def shift(value, axis, step):
     count = SIZES[axis]
     return lax.ppermute(value, axis, [(i, (i + step) % count) for i in range(count)])
+
+
+def partner(value, axis, bit):
+    return lax.ppermute(value, axis, [(i, i ^ bit) for i in range(SIZES[axis])])
+
+
+def gather_out(w_out):
+    rows = w_out.reshape(-1, D)
+    for bit in (4, 2, 1):
+        rows = jnp.concatenate([rows, partner(rows, "zl", bit)], axis=0)
+    half = rows.shape[0] // 2
+    below = shift(rows, "y", 1)
+    above = shift(rows, "y", -1)
+    across = [shift(below[:half], "y", 1), shift(above[half:], "y", -1)]
+    near = jnp.concatenate([rows, below, above] + across, axis=0)
+    return near, shift(near, "core", 1)
+
+
+def feature_order(y, zl, core, heads, size):
+    place = lax.broadcasted_iota(jnp.int32, (heads * size, heads * size), 1)
+    source = lax.broadcasted_iota(jnp.int32, (heads * size, heads * size), 0)
+    inner = place % (2 * heads)
+    slot = place // (2 * heads)
+    bits = slot % 8
+    from_zl = zl ^ (bits // 4 + bits // 2 % 2 * 2 + bits % 2 * 4)
+    turn = slot // 8 % 4
+    from_y = (y + jnp.where(turn == 1, 3, jnp.where(turn == 2, 1, jnp.where(turn == 3, 2, 0)))) % 4
+    from_core = jnp.where(slot >= 32, 1 - core, core)
+    block = (from_y * 8 + from_zl) * 2 + from_core
+    return (source == inner // 2 * size + block * 2 + inner % 2).astype(BF16)
+
+
+def swap_order():
+    count = 16 * MOST
+    into = lax.broadcasted_iota(jnp.int32, (count, count), 0)
+    source = lax.broadcasted_iota(jnp.int32, (count, count), 1)
+    outer, inner, rank = into // (4 * MOST), into // MOST % 4, into % MOST
+    return (source == (inner * 4 + outer) * MOST + rank).astype(BF16)
+
+
+def gate_up_kernel(x_ref, order_ref, w_ref, gain_ref, o_ref, rows_ref):
+    step = order_ref.shape[0]
+    quarter = step // 4
+    lanes = x_ref.shape[1]
+    for b in range(x_ref.shape[0] // step):
+        moved = jnp.dot(
+            order_ref[...], x_ref[b * step : (b + 1) * step, :], preferred_element_type=F32
+        ).astype(BF16)
+        for c in range(4):
+            rows_ref[b * quarter : (b + 1) * quarter, c * lanes : (c + 1) * lanes] = moved[
+                c * quarter : (c + 1) * quarter
+            ]
+    wide = w_ref.shape[1]
+    inverse = 1.0 / gain_ref[...]
+    for b in range(rows_ref.shape[0] // step):
+        rows = rows_ref[b * step : (b + 1) * step, :]
+        part = jnp.dot(rows, w_ref[...], preferred_element_type=F32)
+        o_ref[b * step : (b + 1) * step, 0:wide] = part.astype(BF16)
+        plain = rows.astype(F32) * inverse
+        square = jnp.sum(plain * plain, axis=1, keepdims=True)
+        high = square.astype(BF16).astype(F32)
+        lane = lax.broadcasted_iota(jnp.int32, (step, 128), 1)
+        extra = jnp.where(lane == 0, high, jnp.where(lane == 1, square - high, 0.0))
+        o_ref[b * step : (b + 1) * step, wide : wide + 128] = extra.astype(BF16)
+
+
+def gate_up(arrived, weights, gain):
+    slots = arrived.shape[0] // 4
+    return pl.pallas_call(
+        gate_up_kernel,
+        out_shape=jax.ShapeDtypeStruct((slots, weights.shape[1] + 128), BF16),
+        scratch_shapes=[pltpu.VMEM((slots, weights.shape[0]), BF16)],
+        compiler_params=pltpu.CompilerParams(vmem_limit_bytes=48 << 20),
+        name="gate_up",
+    )(arrived, swap_order(), weights, gain[None, :])
+
+
+def down_kernel(h_ref, order_ref, w_ref, o_ref):
+    step = order_ref.shape[0]
+    quarter = step // 4
+    lanes = o_ref.shape[1]
+    for a in range(h_ref.shape[0] // step):
+        found = jnp.dot(
+            h_ref[a * step : (a + 1) * step, :], w_ref[...], preferred_element_type=F32
+        )
+        for e in range(4):
+            b = a * 4 + e
+            piece = found[e * quarter : (e + 1) * quarter]
+            piece = jnp.concatenate(
+                [piece[:, c * lanes : (c + 1) * lanes] for c in range(4)], axis=0
+            ).astype(BF16)
+            o_ref[b * step : (b + 1) * step, :] = jnp.dot(
+                order_ref[...], piece, preferred_element_type=F32
+            ).astype(BF16)
+
+
+def down(hidden, weights):
+    lanes = weights.shape[1] // 4
+    return pl.pallas_call(
+        down_kernel,
+        out_shape=jax.ShapeDtypeStruct((hidden.shape[0] * 4, lanes), BF16),
+        compiler_params=pltpu.CompilerParams(vmem_limit_bytes=48 << 20),
+        name="down",
+    )(hidden, swap_order(), weights)
 
 
 def attend_kernel(place, q_ref, k_ref, v_ref, o_ref, *, heads, piece, tokens):
@@ -88,7 +192,7 @@
     ctx_count = 64
     width = resid.shape[1]
 
-    whole_out = lax.all_gather(w_out, CTX, axis=1, tiled=True)
+    near, far = gather_out(w_out)
 
     piece = tokens // 4
     pair = jnp.stack([keys, values], axis=0)
@@ -121,11 +225,14 @@
         below = below + (part[size + 1].astype(F32) + part[size + 2].astype(F32)) * scale
     context = (above / below[None, :]).astype(BF16).T.reshape(tokens, heads, size)
 
-    projected = jnp.dot(
-        context.reshape(tokens, heads * size),
-        whole_out.reshape(heads * size, D),
-        preferred_element_type=F32,
+    order = feature_order(y, zl, core, heads, size)
+    ordered = jnp.dot(
+        context.reshape(tokens, heads * size), order, preferred_element_type=F32
     ).astype(BF16)
+    split = heads * size // 2
+    projected = jnp.dot(ordered[:, :split], near, preferred_element_type=F32)
+    projected = projected + jnp.dot(ordered[:, split:], far, preferred_element_type=F32)
+    projected = projected.astype(BF16)
     projected = projected.reshape(tokens, 2, 4, width).transpose(2, 1, 0, 3)
     projected = lax.all_to_all(projected, "x", 0, 0, tiled=True)
     half = jnp.sum(projected.astype(F32), axis=0)
@@ -145,38 +252,36 @@
     token = jnp.arange(tokens, dtype=jnp.int32)
     before = (token[:, None] < token[None, :]).astype(BF16)
     rank = jnp.dot(named, before, preferred_element_type=F32)
-    slot = jnp.arange(slots, dtype=jnp.int32)
-    spread = (slot[:, None] // MOST == expert[None, :]).astype(BF16)
+    line = jnp.arange(4 * slots, dtype=jnp.int32)
+    spread = (line[:, None] // (4 * MOST) == expert[None, :]).astype(BF16)
     weight_high = weight.astype(BF16)
     weight_low = (weight - weight_high.astype(F32)).astype(BF16)
     rank = jnp.where(named > 0, rank, -1.0).astype(BF16)
     tables = jnp.concatenate([rank, weight_high, weight_low], axis=1)
     tables = jnp.dot(spread, tables, preferred_element_type=F32)
-    live = tables[:, :tokens] == (slot % MOST).astype(F32)[:, None]
-    dispatch = live.astype(BF16)
+    live = tables[:, :tokens] == (line % MOST).astype(F32)[:, None]
+    chunk = line // MOST % 4
+
+    def by_chunk(table):
+        table = table.astype(BF16)
+        zero = jnp.zeros((), BF16)
+        return [jnp.where((chunk == c)[:, None], table, zero) for c in range(4)]
+
+    dispatch = jnp.concatenate(by_chunk(live), axis=1)
     combine = jnp.concatenate(
-        [
-            jnp.where(live, tables[:, tokens : 2 * tokens], 0.0).astype(BF16),
-            jnp.where(live, tables[:, 2 * tokens :], 0.0).astype(BF16),
-        ],
+        by_chunk(jnp.where(live, tables[:, tokens : 2 * tokens], 0.0))
+        + by_chunk(jnp.where(live, tables[:, 2 * tokens :], 0.0)),
         axis=1,
     )
 
-    outgoing = jnp.dot(dispatch, scaled, preferred_element_type=F32).astype(BF16)
-    outgoing = outgoing.reshape(ctx_count, MOST, width)
-    arrived = lax.all_to_all(outgoing, CTX, 0, 0, tiled=True).reshape(slots, width)
+    lanes = width // 4
+    stacked = jnp.concatenate([scaled[:, c * lanes : (c + 1) * lanes] for c in range(4)], axis=0)
+    outgoing = jnp.dot(dispatch, stacked, preferred_element_type=F32).astype(BF16)
+    outgoing = outgoing.reshape(ctx_count, 4 * MOST, lanes)
+    arrived = lax.all_to_all(outgoing, CTX, 0, 0, tiled=True).reshape(4 * slots, lanes)
 
     units = w_gate_up.shape[3]
-    part = jnp.dot(
-        arrived, w_gate_up.reshape(width, 2 * units), preferred_element_type=F32
-    ).astype(BF16)
-    plain = arrived.astype(F32) / gain[None, :]
-    square = jnp.sum(plain * plain, axis=1, keepdims=True)
-    high = square.astype(BF16)
-    low = (square - high.astype(F32)).astype(BF16)
-    lane = jnp.arange(128)[None, :]
-    extra = jnp.where(lane == 0, high, jnp.where(lane == 1, low, jnp.zeros((), BF16)))
-    part = jnp.concatenate([part, extra], axis=1)
+    part = gate_up(arrived, w_gate_up.reshape(width, 2 * units), gain)
     part = part.reshape(4, slots // 4, 2 * units + 128)
     part = lax.all_to_all(part, "x", 0, 0, tiled=True)
     part = jnp.sum(part.astype(F32), axis=0).reshape(2, slots // 8, 2 * units + 128)
@@ -193,13 +298,13 @@
         zh == 0, jnp.stack([hidden, other], axis=0), jnp.stack([other, hidden], axis=0)
     ).reshape(slots // 4, units)
     hidden = lax.all_gather(hidden, "x", axis=0, tiled=True)
-    result = jnp.dot(hidden, w_down[0], preferred_element_type=F32).astype(BF16)
-    result = result.reshape(ctx_count, MOST, width)
-    returned = lax.all_to_all(result, CTX, 0, 0, tiled=True).reshape(slots, width)
+    result = down(hidden, w_down[0]).reshape(ctx_count, 4 * MOST, lanes)
+    returned = lax.all_to_all(result, CTX, 0, 0, tiled=True).reshape(4 * slots, lanes)
     routed = lax.dot_general(
         combine, returned, (((0,), (0,)), ((), ())), preferred_element_type=F32
     )
-    routed = routed[:tokens] + routed[tokens:]
+    routed = routed[: 4 * tokens] + routed[4 * tokens :]
+    routed = jnp.concatenate([routed[c * tokens : (c + 1) * tokens] for c in range(4)], axis=1)
     mixed = (state + routed).astype(BF16)
     return (context, mixed)
 

time: 426 us -> 380 us (0.89)
  waiting for transfers between devices: 198 us -> 148 us
  blocking collectives: 76.2 us -> 40.3 us
  starting transfers between devices: 93.9 us -> 128 us
  between operations: 14.5 us -> 1.31 us
  other arithmetic: 5.37 us -> 15.5 us
  matrix products: 6.47 us -> 13.4 us
    all_gather x1 -> x0, waiting for transfers between devices: 49.8 us -> none  [body(): whole_out = lax.all_gather(w_out, CTX, axis=1, tiled=True)]
    all_to_all x2 -> x0, blocking collectives: 35.8 us -> none  [the longest x1 23.2 us: body(): pair = lax.all_to_all(pair, 'zl', 0, 0, tiled=True)]
    all_to_all x2 -> x4, waiting for transfers between devices: 99.1 us -> 64.7 us  [the longest x1 32.8 us: body(): lax.all_to_all(outgoing, CTX, 0, 0, tiled=True).reshape(4 * slots, lanes)]
    ppermute x10 -> x15, waiting for transfers between devices: 34.9 us -> 59.2 us  [shift(): lax.ppermute(value, axis, [(i, (i + step) % count) for i in range(count)])]
    ppermute x0 -> x3, waiting for transfers between devices: none -> 12.1 us  [partner(): return lax.ppermute(value, axis, [(i, i ^ bit) for i in range(SIZES[axis])])]
    all_to_all x2 -> x4, starting transfers between devices: 37.7 us -> 49.2 us  [the longest x1 19.8 us: body(): lax.all_to_all(result, CTX, 0, 0, tiled=True).reshape(4 * slots, lanes)]
    ppermute x10 -> x15, starting transfers between devices: 52.1 us -> 63.6 us  [shift(): lax.ppermute(value, axis, [(i, (i + step) % count) for i in range(count)])]
    ppermute x0 -> x3, starting transfers between devices: none -> 11.1 us  [partner(): return lax.ppermute(value, axis, [(i, i ^ bit) for i in range(SIZES[axis])])]
  transfers between devices with their start and end apart: 14 -> 23, of which waited for: 9 -> 13; matrix products, arithmetic and copies ran while one was open for 2% -> 7% of each run, Pallas kernels for 3% -> 4%
where the time goes in v2:
time: 380 us; the launch traced here: 379 us
  waiting for transfers between devices  148 us (39%)
  starting transfers between devices  128 us (34%)
  blocking collectives  40.3 us (11%)
  Pallas kernels  17.7 us (5%)
  other arithmetic  15.5 us (4%)
  local copies, waits for them, and re-layouts  15.2 us (4%)
  matrix products  13.4 us (4%)
    ppermute x15, starting transfers between devices, shift(): lax.ppermute(value, axis, [(i, (i + step) % count) for i in range(count)])  63.6 us
    ppermute x15, waiting for transfers between devices, shift(): lax.ppermute(value, axis, [(i, (i + step) % count) for i in range(count)])  59.2 us
    all_to_all x1, waiting for transfers between devices, body(): lax.all_to_all(outgoing, CTX, 0, 0, tiled=True).reshape(4 * slots, lanes)  32.8 us
    all_to_all x1, waiting for transfers between devices, body(): lax.all_to_all(result, CTX, 0, 0, tiled=True).reshape(4 * slots, lanes)  31.9 us
    all_to_all x1, blocking collectives, body(): part = lax.all_to_all(part, 'x', 0, 0, tiled=True)  27.8 us
    all_to_all x1, starting transfers between devices, body(): lax.all_to_all(result, CTX, 0, 0, tiled=True).reshape(4 * slots, lanes)  19.8 us
    pallas_call x4, Pallas kernels, attend(): pl.pallas_call(functools.partial(attend_kernel, heads=heads, piece=piece,...  13.7 us
    all_to_all x1, starting transfers between devices, body(): lax.all_to_all(outgoing, CTX, 0, 0, tiled=True).reshape(4 * slots, lanes)  13 us
  transfers between devices with their start and end apart: 23, of which 13 were waited for; matrix products, arithmetic and copies ran while one was open for 7% of the time, Pallas kernels for 4%

profile of v2, /device:TPU:1, one launch (start us, length us, event | category | flops | bytes accessed | tf_op | source)
XLA Modules:
  0.0 378.7 jit_solution(8609669859921692866)
XLA Ops:
  0.6 5.2 %collective-permute-start.5 = (bf16[512,128]{1,0:T(8,128)(2,1)}, bf16[512,128]{1,0:T(8,128)(2,1)S(1)}, u32[]{:S(2)}, u32[]{:S(2)}) collective-permute-start(bf16[512,128]{1,0:T(8,128)(2,1)} %bitcast.76), channel_id=1, source_target_pairs={{0,3},{1,0},{2,1},{3,2},{4,7},{5,4},{6,5},{7,6},{8,11},{9,8},{10,9... | collective-permute-start | bytes 393224 | tf_op jit(solution)/shard_map/ppermute | solution.py:26
  5.9 1.9 collective-permute-start.3
  7.8 3.6 collective-permute-start
  13.0 12.2 %all-to-all-start = ((bf16[8,2,32,128]{3,2,1,0:T(8,128)(2,1)}), bf16[8,2,32,128]{3,2,1,0:T(8,128)(2,1)S(1)}, u32[]{:S(2)}, u32[]{:S(2)}) async-start(bf16[8,2,32,128]{3,2,1,0:T(8,128)(2,1)} %broadcast_in_dim.147), calls=%async_computation | async-start | bytes 262144 | tf_op jit(solution)/shard_map/all_to_all | solution.py:202
  26.1 7.3 %collective-permute-start.7 = (bf16[8,4096]{1,0:T(8,128)(2,1)S(1)}, bf16[8,4096]{1,0:T(8,128)(2,1)S(1)}, u32[]{:S(2)}, u32[]{:S(2)}) collective-permute-start(bf16[8,4096]{1,0:T(8,128)(2,1)S(1)} %reshape.116), channel_id=1, source_target_pairs={{0,64},{16,80},{32,96},{48,112},{64,0},{80,16},{96,32},{112,48},{1... | collective-permute-start | bytes 196616 | tf_op jit(solution)/shard_map/ppermute | solution.py:30
  39.8 3.7 collective-permute-done.7
  43.5 1.9 collective-permute-start.8
  46.1 7.0 %collective-permute-done.8 = bf16[16,4096]{1,0:T(8,128)(2,1)S(1)} collective-permute-done((bf16[16,4096]{1,0:T(8,128)(2,1)S(1)}, bf16[16,4096]{1,0:T(8,128)(2,1)S(1)}, u32[]{:S(2)}, u32[]{:S(2)}) %collective-permute-start.8) | collective-permute-done | bytes 131104 | tf_op jit(solution)/shard_map/ppermute | solution.py:30
  53.1 1.9 collective-permute-start.9
  56.6 4.2 %all-to-all-start.1 = ((bf16[4,8,2,32,128]{4,3,1,2,0:T(8,128)(2,1)}), bf16[4,8,2,32,128]{4,3,1,2,0:T(8,128)(2,1)S(1)}, u32[]{:S(2)}, u32[]{:S(2)}) async-start(bf16[4,8,2,32,128]{4,3,1,2,0:T(8,128)(2,1)} %broadcast_in_dim.148), calls=%async_computation.1 | async-start | bytes 1048576 | tf_op jit(solution)/shard_map/all_to_all | solution.py:204
  63.1 3.2 collective-permute-start.10
  67.3 3.3 collective-permute-start.11
  70.7 10.8 %collective-permute-done.10 = bf16[64,4096]{1,0:T(8,128)(2,1)S(1)} collective-permute-done((bf16[64,4096]{1,0:T(8,128)(2,1)}, bf16[64,4096]{1,0:T(8,128)(2,1)S(1)}, u32[]{:S(2)}, u32[]{:S(2)}) %collective-permute-start.10) | collective-permute-done | bytes 524320 | tf_op jit(solution)/shard_map/ppermute | solution.py:26
  81.5 2.8 collective-permute-start.1
  85.2 1.9 collective-permute-start.12
  88.0 8.2 %collective-permute-done.12 = bf16[32,4096]{1,0:T(8,128)(2,1)S(1)} collective-permute-done((bf16[32,4096]{1,0:T(8,128)(2,1)S(1)}, bf16[32,4096]{1,0:T(8,128)(2,1)S(1)}, u32[]{:S(2)}, u32[]{:S(2)}) %collective-permute-start.12) | collective-permute-done | bytes 262176 | tf_op jit(solution)/shard_map/ppermute | solution.py:26
  96.2 1.9 collective-permute-start.13
  98.9 6.3 %collective-permute-done.13 = bf16[32,4096]{1,0:T(8,128)(2,1)S(1)} collective-permute-done((bf16[32,4096]{1,0:T(8,128)(2,1)S(1)}, bf16[32,4096]{1,0:T(8,128)(2,1)S(1)}, u32[]{:S(2)}, u32[]{:S(2)}) %collective-permute-start.13) | collective-permute-done | bytes 262176 | tf_op jit(solution)/shard_map/ppermute | solution.py:26
  105.9 3.6 collective-permute-start.14
  109.7 3.4 attend.6
  113.1 3.4 collective-permute-start.6
  116.6 3.4 attend.5
  120.0 3.1 collective-permute-start.4
  123.1 3.4 attend.4
  126.5 2.6 collective-permute-start.2
  129.1 3.4 attend.7
  132.6 2.2 collective-permute-done.2
  135.8 2.0 fusion.83
  137.9 2.1 fusion
  140.8 1.8 copy.77
  142.6 3.7 all-to-all-start.2
  148.2 11.6 %all-to-all-done.2 = bf16[4,2,128,512]{3,1,2,0:T(2,128)(2,1)S(1)} async-done(((bf16[4,2,128,512]{3,1,2,0:T(2,128)(2,1)}), bf16[4,2,128,512]{3,1,2,0:T(2,128)(2,1)S(1)}, u32[]{:S(2)}, u32[]{:S(2)}) %all-to-all-start.2) | async-done | bytes 1048608 | tf_op jit(solution)/shard_map/all_to_all | solution.py:237
  160.1 8.1 %collective-permute-start.15 = (bf16[128,512]{0,1:T(8,128)(2,1)S(1)}, bf16[128,512]{0,1:T(8,128)(2,1)S(1)}, u32[]{:S(2)}, u32[]{:S(2)}) collective-permute-start(bf16[128,512]{0,1:T(8,128)(2,1)S(1)} %bitcast.89), channel_id=1, source_target_pairs={{0,4},{4,0},{1,5},{5,1},{2,6},{6,2},{3,7},{7,3},{8,12},{12,8},{9,1... | collective-permute-start | bytes 393224 | tf_op jit(solution)/shard_map/ppermute | solution.py:26
  168.2 3.1 convert_select_fusion.2
  171.6 7.4 %collective-permute-done.15 = bf16[128,512]{0,1:T(8,128)(2,1)S(1)} collective-permute-done((bf16[128,512]{0,1:T(8,128)(2,1)S(1)}, bf16[128,512]{0,1:T(8,128)(2,1)S(1)}, u32[]{:S(2)}, u32[]{:S(2)}) %collective-permute-start.15) | collective-permute-done | bytes 131104 | tf_op jit(solution)/shard_map/ppermute | solution.py:26
  179.2 3.3 convolution_convert_fusion
  182.5 13.0 %all-to-all-start.3 = ((bf16[64,40,128]{2,1,0:T(8,128)(2,1)}), bf16[64,40,128]{2,1,0:T(8,128)(2,1)S(1)}, u32[]{:S(2)}, u32[]{:S(2)}) async-start(bf16[64,40,128]{2,1,0:T(8,128)(2,1)} %bitcast.23), calls=%async_computation.3 | async-start | bytes 1310720 | tf_op jit(solution)/shard_map/all_to_all | solution.py:281
  197.4 32.8 %all-to-all-done.3 = bf16[64,40,128]{2,1,0:T(8,128)(2,1)S(1)} async-done(((bf16[64,40,128]{2,1,0:T(8,128)(2,1)}), bf16[64,40,128]{2,1,0:T(8,128)(2,1)S(1)}, u32[]{:S(2)}, u32[]{:S(2)}) %all-to-all-start.3) | async-done | bytes 655392 | tf_op jit(solution)/shard_map/all_to_all | solution.py:281
  231.9 27.8 %all_to_all.30 = bf16[4,160,1664]{2,1,0:T(8,128)(2,1)S(1)} all-to-all(bf16[4,160,1664]{2,1,0:T(8,128)(2,1)S(1)} %bitcast.72), channel_id=1, replica_groups=mesh['y'=4,'zl'=8,'core'=2,'zh'=2,'x'=4] {'x'}, dimensions={0} | all-to-all | bytes 4259840 | tf_op jit(solution)/shard_map/all_to_all | solution.py:286
  260.0 8.2 %collective-permute-start.16 = (bf16[80,1664]{1,0:T(8,128)(2,1)S(1)}, bf16[80,1664]{1,0:T(8,128)(2,1)S(1)}, u32[]{:S(2)}, u32[]{:S(2)}) collective-permute-start(bf16[80,1664]{1,0:T(8,128)(2,1)S(1)} %fusion.63), channel_id=1, source_target_pairs={{0,4},{4,0},{1,5},{5,1},{2,6},{6,2},{3,7},{7,3},{8,12},{12,8},{9,1... | collective-permute-start | bytes 798728 | tf_op jit(solution)/shard_map/ppermute | solution.py:26
  268.2 18.5 %collective-permute-done.16 = bf16[80,1664]{1,0:T(8,128)(2,1)S(1)} collective-permute-done((bf16[80,1664]{1,0:T(8,128)(2,1)S(1)}, bf16[80,1664]{1,0:T(8,128)(2,1)S(1)}, u32[]{:S(2)}, u32[]{:S(2)}) %collective-permute-start.16) | collective-permute-done | bytes 266272 | tf_op jit(solution)/shard_map/ppermute | solution.py:26
  287.1 10.8 %collective-permute-start.17 = (bf16[80,768]{1,0:T(8,128)(2,1)S(1)}, bf16[80,768]{1,0:T(8,128)(2,1)S(1)}, u32[]{:S(2)}, u32[]{:S(2)}) collective-permute-start(bf16[80,768]{1,0:T(8,128)(2,1)S(1)} %fusion.67), channel_id=1, source_target_pairs={{0,4},{4,0},{1,5},{5,1},{2,6},{6,2},{3,7},{7,3},{8,12},{12,8},{9,1... | collective-permute-start | bytes 368648 | tf_op jit(solution)/shard_map/ppermute | solution.py:26
  298.1 5.8 %collective-permute-done.17 = bf16[80,768]{1,0:T(8,128)(2,1)S(1)} collective-permute-done((bf16[80,768]{1,0:T(8,128)(2,1)S(1)}, bf16[80,768]{1,0:T(8,128)(2,1)S(1)}, u32[]{:S(2)}, u32[]{:S(2)}) %collective-permute-start.17) | collective-permute-done | bytes 122912 | tf_op jit(solution)/shard_map/ppermute | solution.py:26
  303.9 12.5 %all_gather.3.h_ref = bf16[640,768]{1,0:T(8,128)(2,1)S(1)} all-gather(bf16[160,768]{1,0:T(8,128)(2,1)S(1)} %bitcast.86), channel_id=1, replica_groups=mesh['y'=4,'zl'=8,'core'=2,'zh'=2,'x'=4] {'x'}, dimensions={0}, use_global_device_ids=true | all-gather | bytes 1228800 | tf_op jit(solution)/shard_map/all_gather | solution.py:300
  316.4 2.4 down.1
  318.8 19.8 %all-to-all-start.5 = ((bf16[64,40,128]{2,1,0:T(8,128)(2,1)}), bf16[64,40,128]{2,1,0:T(8,128)(2,1)S(1)}, u32[]{:S(2)}, u32[]{:S(2)}) async-start(bf16[64,40,128]{2,1,0:T(8,128)(2,1)} %bitcast.34), calls=%async_computation.5 | async-start | bytes 1310720 | tf_op jit(solution)/shard_map/all_to_all | solution.py:302
  341.5 31.9 %all-to-all-done.5 = bf16[64,40,128]{2,1,0:T(8,128)(2,1)S(1)} async-done(((bf16[64,40,128]{2,1,0:T(8,128)(2,1)}), bf16[64,40,128]{2,1,0:T(8,128)(2,1)S(1)}, u32[]{:S(2)}, u32[]{:S(2)}) %all-to-all-start.5) | async-done | bytes 655392 | tf_op jit(solution)/shard_map/all_to_all | solution.py:302
  373.4 4.4 %fusion.146 = f32[1024,128]{0,1:T(8,128)S(1)} fusion(bf16[2560,1024]{0,1:T(8,128)(2,1)} %select_dynamic-update-slice_fusion, bf16[2560,128]{1,0:T(8,128)(2,1)S(1)} %bitcast.83), kind=kOutput, calls=%fused_computation.292 | convolution fusion | flops 671088640 | bytes 6422528 | tf_op jit(solution)/shard_map/dot_general | solution.py:303
  (103 shorter events, 30.6 us)
Async XLA Ops:
  0.6 109.0 %collective-permute-start.5 = (bf16[512,128]{1,0:T(8,128)(2,1)}, bf16[512,128]{1,0:T(8,128)(2,1)S(1)}, u32[]{:S(2)}, u32[]{:S(2)}) collective-permute-start(bf16[512,128]{1,0:T(8,128)(2,1)} %bitcast.76), channel_id=1, source_target_pairs={{0,3},{1,0},{2,1},{3,2},{4,7},{5,4},{6,5},{7,6},{8,11},{9,8},{10,9... | collective-permute-start | bytes 393224 | tf_op jit(solution)/shard_map/ppermute | solution.py:26
  5.9 110.7 %collective-permute-start.3 = (bf16[512,128]{1,0:T(8,128)(2,1)}, bf16[512,128]{1,0:T(8,128)(2,1)S(1)}, u32[]{:S(2)}, u32[]{:S(2)}) collective-permute-start(bf16[512,128]{1,0:T(8,128)(2,1)} %bitcast.77), channel_id=1, source_target_pairs={{0,1},{1,2},{2,3},{3,0},{4,5},{5,6},{6,7},{7,4},{8,9},{9,10},{10,1... | collective-permute-start | bytes 393224 | tf_op jit(solution)/shard_map/ppermute | solution.py:26
  7.8 115.3 %collective-permute-start = (bf16[512,128]{1,0:T(8,128)(2,1)}, bf16[512,128]{1,0:T(8,128)(2,1)S(1)}, u32[]{:S(2)}, u32[]{:S(2)}) collective-permute-start(bf16[512,128]{1,0:T(8,128)(2,1)} %bitcast.78), channel_id=1, source_target_pairs={{0,2},{1,3},{2,0},{3,1},{4,6},{5,7},{6,4},{7,5},{8,10},{9,11},{10,... | collective-permute-start | bytes 393224 | tf_op jit(solution)/shard_map/ppermute | solution.py:26
  13.0 42.7 %all-to-all-start = ((bf16[8,2,32,128]{3,2,1,0:T(8,128)(2,1)}), bf16[8,2,32,128]{3,2,1,0:T(8,128)(2,1)S(1)}, u32[]{:S(2)}, u32[]{:S(2)}) async-start(bf16[8,2,32,128]{3,2,1,0:T(8,128)(2,1)} %broadcast_in_dim.147), calls=%async_computation | async-start | bytes 262144 | tf_op jit(solution)/shard_map/all_to_all | solution.py:202
  26.1 17.3 %collective-permute-start.7 = (bf16[8,4096]{1,0:T(8,128)(2,1)S(1)}, bf16[8,4096]{1,0:T(8,128)(2,1)S(1)}, u32[]{:S(2)}, u32[]{:S(2)}) collective-permute-start(bf16[8,4096]{1,0:T(8,128)(2,1)S(1)} %reshape.116), channel_id=1, source_target_pairs={{0,64},{16,80},{32,96},{48,112},{64,0},{80,16},{96,32},{112,48},{1... | collective-permute-start | bytes 196616 | tf_op jit(solution)/shard_map/ppermute | solution.py:30
  36.6 2.5 copy-start.3
  43.5 9.6 %collective-permute-start.8 = (bf16[16,4096]{1,0:T(8,128)(2,1)S(1)}, bf16[16,4096]{1,0:T(8,128)(2,1)S(1)}, u32[]{:S(2)}, u32[]{:S(2)}) collective-permute-start(bf16[16,4096]{1,0:T(8,128)(2,1)S(1)} %pad_maximum_fusion.2), channel_id=1, source_target_pairs={{0,32},{16,48},{32,0},{48,16},{64,96},{80,112},{96,64},{112,80},{1... | collective-permute-start | bytes 393224 | tf_op jit(solution)/shard_map/ppermute | solution.py:30
  53.1 9.2 %collective-permute-start.9 = (bf16[32,4096]{1,0:T(8,128)(2,1)S(1)}, bf16[32,4096]{1,0:T(8,128)(2,1)S(1)}, u32[]{:S(2)}, u32[]{:S(2)}) collective-permute-start(bf16[32,4096]{1,0:T(8,128)(2,1)S(1)} %pad_maximum_fusion.1), channel_id=1, source_target_pairs={{0,16},{16,0},{32,48},{48,32},{64,80},{80,64},{96,112},{112,96},{1... | collective-permute-start | bytes 786440 | tf_op jit(solution)/shard_map/ppermute | solution.py:30
  56.6 14.0 %all-to-all-start.1 = ((bf16[4,8,2,32,128]{4,3,1,2,0:T(8,128)(2,1)}), bf16[4,8,2,32,128]{4,3,1,2,0:T(8,128)(2,1)S(1)}, u32[]{:S(2)}, u32[]{:S(2)}) async-start(bf16[4,8,2,32,128]{4,3,1,2,0:T(8,128)(2,1)} %broadcast_in_dim.148), calls=%async_computation.1 | async-start | bytes 1048576 | tf_op jit(solution)/shard_map/all_to_all | solution.py:204
  63.1 18.4 %collective-permute-start.10 = (bf16[64,4096]{1,0:T(8,128)(2,1)}, bf16[64,4096]{1,0:T(8,128)(2,1)S(1)}, u32[]{:S(2)}, u32[]{:S(2)}) collective-permute-start(bf16[64,4096]{1,0:T(8,128)(2,1)} %get-tuple-element.40), channel_id=1, source_target_pairs={{0,128},{128,256},{256,384},{384,0},{1,129},{129,257},{257,385},{3... | collective-permute-start | bytes 1572872 | tf_op jit(solution)/shard_map/ppermute | solution.py:26
  67.3 17.9 %collective-permute-start.11 = (bf16[64,4096]{1,0:T(8,128)(2,1)}, bf16[64,4096]{1,0:T(8,128)(2,1)S(1)}, u32[]{:S(2)}, u32[]{:S(2)}) collective-permute-start(bf16[64,4096]{1,0:T(8,128)(2,1)} %get-tuple-element.40), channel_id=1, source_target_pairs={{0,384},{128,0},{256,128},{384,256},{1,385},{129,1},{257,129},{385... | collective-permute-start | bytes 1572872 | tf_op jit(solution)/shard_map/ppermute | solution.py:26
  81.5 28.0 %collective-permute-start.1 = (bf16[4,8,2,32,128]{4,3,1,2,0:T(8,128)(2,1)S(1)}, bf16[4,8,2,32,128]{4,3,1,2,0:T(8,128)(2,1)S(1)}, u32[]{:S(2)}, u32[]{:S(2)}) collective-permute-start(bf16[4,8,2,32,128]{4,3,1,2,0:T(8,128)(2,1)S(1)} %all-to-all-done.1), channel_id=1, source_target_pairs={{0,8},{8,0},{1,9},{9,1},{2,10},{10,2},{3,11},{11,3},{4,12},{12,4},... | collective-permute-start | bytes 1572872 | tf_op jit(solution)/shard_map/ppermute | solution.py:26
  85.2 11.0 %collective-permute-start.12 = (bf16[32,4096]{1,0:T(8,128)(2,1)S(1)}, bf16[32,4096]{1,0:T(8,128)(2,1)S(1)}, u32[]{:S(2)}, u32[]{:S(2)}) collective-permute-start(bf16[32,4096]{1,0:T(8,128)(2,1)S(1)} %slice.175), channel_id=1, source_target_pairs={{0,128},{128,256},{256,384},{384,0},{1,129},{129,257},{257,385},{3... | collective-permute-start | bytes 786440 | tf_op jit(solution)/shard_map/ppermute | solution.py:26
  96.2 8.9 %collective-permute-start.13 = (bf16[32,4096]{1,0:T(8,128)(2,1)S(1)}, bf16[32,4096]{1,0:T(8,128)(2,1)S(1)}, u32[]{:S(2)}, u32[]{:S(2)}) collective-permute-start(bf16[32,4096]{1,0:T(8,128)(2,1)S(1)} %slice.176), channel_id=1, source_target_pairs={{0,384},{128,0},{256,128},{384,256},{1,385},{129,1},{257,129},{385... | collective-permute-start | bytes 786440 | tf_op jit(solution)/shard_map/ppermute | solution.py:26
  105.9 29.9 %collective-permute-start.14 = (bf16[256,4096]{1,0:T(8,128)(2,1)}, bf16[256,4096]{1,0:T(8,128)(2,1)}, u32[]{:S(2)}, u32[]{:S(2)}) collective-permute-start(bf16[256,4096]{1,0:T(8,128)(2,1)} %constant_dynamic-update-slice_fusion.4), channel_id=1, source_target_pairs={{0,8},{8,0},{1,9},{9,1},{2,10},{10,2},{3,11},{11,3},{4,12},{12,4},... | collective-permute-start | bytes 6291464 | tf_op jit(solution)/shard_map/ppermute | solution.py:26
  109.6 19.5 %copy-start.1 = (bf16[128,4,128]{2,1,0:T(4,128)(2,1)S(1)}, bf16[128,4,128]{2,1,0:T(4,128)(2,1)}, u32[]{:S(2)}) copy-start(bf16[128,4,128]{2,1,0:T(4,128)(2,1)} %param.10) | copy-start | bytes 393220
  113.1 19.5 %collective-permute-start.6 = (bf16[144,512]{1,0:T(8,128)(2,1)S(1)}, bf16[144,512]{1,0:T(8,128)(2,1)S(1)}, u32[]{:S(2)}, u32[]{:S(2)}) collective-permute-start(bf16[144,512]{1,0:T(8,128)(2,1)S(1)} %attend.6), channel_id=1, source_target_pairs={{0,1},{1,2},{2,3},{3,0},{4,5},{5,6},{6,7},{7,4},{8,9},{9,10},{10,1... | collective-permute-start | bytes 442376 | tf_op jit(solution)/shard_map/ppermute | solution.py:26
  120.0 12.6 %collective-permute-start.4 = (bf16[144,512]{1,0:T(8,128)(2,1)S(1)}, bf16[144,512]{1,0:T(8,128)(2,1)S(1)}, u32[]{:S(2)}, u32[]{:S(2)}) collective-permute-start(bf16[144,512]{1,0:T(8,128)(2,1)S(1)} %attend.5), channel_id=1, source_target_pairs={{0,3},{1,0},{2,1},{3,2},{4,7},{5,4},{6,5},{7,6},{8,11},{9,8},{10,9... | collective-permute-start | bytes 442376 | tf_op jit(solution)/shard_map/ppermute | solution.py:26
  126.5 8.2 %collective-permute-start.2 = (bf16[144,512]{1,0:T(8,128)(2,1)S(1)}, bf16[144,512]{1,0:T(8,128)(2,1)S(1)}, u32[]{:S(2)}, u32[]{:S(2)}) collective-permute-start(bf16[144,512]{1,0:T(8,128)(2,1)S(1)} %attend.4), channel_id=1, source_target_pairs={{0,2},{1,3},{2,0},{3,1},{4,6},{5,7},{6,4},{7,5},{8,10},{9,11},{10,... | collective-permute-start | bytes 442376 | tf_op jit(solution)/shard_map/ppermute | solution.py:26
  135.0 0.8 copy-start.7
  142.6 17.2 %all-to-all-start.2 = ((bf16[4,2,128,512]{3,1,2,0:T(2,128)(2,1)}), bf16[4,2,128,512]{3,1,2,0:T(2,128)(2,1)S(1)}, u32[]{:S(2)}, u32[]{:S(2)}) async-start(bf16[4,2,128,512]{3,1,2,0:T(2,128)(2,1)} %bitcast.63), calls=%async_computation.2 | async-start | bytes 2097152 | tf_op jit(solution)/shard_map/all_to_all | solution.py:237
  160.1 11.3 %copy-start.8 = (bf16[128,512]{1,0:T(8,128)(2,1)S(1)}, bf16[128,512]{1,0:T(8,128)(2,1)}, u32[]{:S(2)}) copy-start(bf16[128,512]{1,0:T(8,128)(2,1)} %param.13) | copy-start | bytes 393220
  160.1 18.9 %copy-start.2 = (f32[512]{0:T(512)S(1)}, f32[512]{0:T(512)}, u32[]{:S(2)}) copy-start(f32[512]{0:T(512)} %param.14) | copy-start | bytes 6148
  160.1 18.9 %collective-permute-start.15 = (bf16[128,512]{0,1:T(8,128)(2,1)S(1)}, bf16[128,512]{0,1:T(8,128)(2,1)S(1)}, u32[]{:S(2)}, u32[]{:S(2)}) collective-permute-start(bf16[128,512]{0,1:T(8,128)(2,1)S(1)} %bitcast.89), channel_id=1, source_target_pairs={{0,4},{4,0},{1,5},{5,1},{2,6},{6,2},{3,7},{7,3},{8,12},{12,8},{9,1... | collective-permute-start | bytes 393224 | tf_op jit(solution)/shard_map/ppermute | solution.py:26
  171.3 7.9 %copy-start.4 = (bf16[2560,128]{0,1:T(8,128)(2,1)S(1)}, bf16[2560,128]{0,1:T(8,128)(2,1)}, u32[]{:S(2)}) copy-start(bf16[2560,128]{0,1:T(8,128)(2,1)} %get-tuple-element.16) | copy-start | bytes 1966084
  179.0 3.4 copy-start.5
  182.5 47.8 %all-to-all-start.3 = ((bf16[64,40,128]{2,1,0:T(8,128)(2,1)}), bf16[64,40,128]{2,1,0:T(8,128)(2,1)S(1)}, u32[]{:S(2)}, u32[]{:S(2)}) async-start(bf16[64,40,128]{2,1,0:T(8,128)(2,1)} %bitcast.23), calls=%async_computation.3 | async-start | bytes 1310720 | tf_op jit(solution)/shard_map/all_to_all | solution.py:281
  260.0 26.7 %collective-permute-start.16 = (bf16[80,1664]{1,0:T(8,128)(2,1)S(1)}, bf16[80,1664]{1,0:T(8,128)(2,1)S(1)}, u32[]{:S(2)}, u32[]{:S(2)}) collective-permute-start(bf16[80,1664]{1,0:T(8,128)(2,1)S(1)} %fusion.63), channel_id=1, source_target_pairs={{0,4},{4,0},{1,5},{5,1},{2,6},{6,2},{3,7},{7,3},{8,12},{12,8},{9,1... | collective-permute-start | bytes 798728 | tf_op jit(solution)/shard_map/ppermute | solution.py:26
  268.2 48.2 %copy-start = (bf16[1,768,512]{2,1,0:T(8,128)(2,1)S(1)}, bf16[1,768,512]{2,1,0:T(8,128)(2,1)}, u32[]{:S(2)}) copy-start(bf16[1,768,512]{2,1,0:T(8,128)(2,1)} %param.18) | copy-start | bytes 2359300
  287.1 16.8 %collective-permute-start.17 = (bf16[80,768]{1,0:T(8,128)(2,1)S(1)}, bf16[80,768]{1,0:T(8,128)(2,1)S(1)}, u32[]{:S(2)}, u32[]{:S(2)}) collective-permute-start(bf16[80,768]{1,0:T(8,128)(2,1)S(1)} %fusion.67), channel_id=1, source_target_pairs={{0,4},{4,0},{1,5},{5,1},{2,6},{6,2},{3,7},{7,3},{8,12},{12,8},{9,1... | collective-permute-start | bytes 368648 | tf_op jit(solution)/shard_map/ppermute | solution.py:26
  318.8 54.6 %all-to-all-start.5 = ((bf16[64,40,128]{2,1,0:T(8,128)(2,1)}), bf16[64,40,128]{2,1,0:T(8,128)(2,1)S(1)}, u32[]{:S(2)}, u32[]{:S(2)}) async-start(bf16[64,40,128]{2,1,0:T(8,128)(2,1)} %bitcast.34), calls=%async_computation.5 | async-start | bytes 1310720 | tf_op jit(solution)/shard_map/all_to_all | solution.py:302
  373.4 4.4 %copy-start.6 = (bf16[128,512]{0,1:T(8,128)(2,1)S(1)}, bf16[128,512]{0,1:T(8,128)(2,1)}, u32[]{:S(2)}) copy-start(bf16[128,512]{0,1:T(8,128)(2,1)} %copy-done.5) | copy-start | bytes 393220

commit v3 on v2

--- a/solution.py
+++ b/solution.py
@@ -30,30 +30,59 @@
     return lax.ppermute(value, axis, [(i, i ^ bit) for i in range(SIZES[axis])])
 
 
-def gather_out(w_out):
+def after(value, earlier):
+    return lax.optimization_barrier((value, earlier))[0]
+
+
+def gather_line(w_out):
     rows = w_out.reshape(-1, D)
-    for bit in (4, 2, 1):
-        rows = jnp.concatenate([rows, partner(rows, "zl", bit)], axis=0)
-    half = rows.shape[0] // 2
-    below = shift(rows, "y", 1)
-    above = shift(rows, "y", -1)
-    across = [shift(below[:half], "y", 1), shift(above[half:], "y", -1)]
-    near = jnp.concatenate([rows, below, above] + across, axis=0)
-    return near, shift(near, "core", 1)
-
-
-def feature_order(y, zl, core, heads, size):
+    rows = jnp.concatenate([rows, partner(rows, "zl", 4)], axis=0)
+    return jnp.concatenate([rows, partner(rows, "zl", 2)], axis=0)
+
+
+def gather_rest(rows, first, second):
+    rows = after(rows, first)
+    rows = jnp.concatenate([rows, partner(rows, "zl", 1)], axis=0)
+    rows = after(rows, second)
+    rows = jnp.broadcast_to(rows[None], (4,) + rows.shape)
+    return lax.all_to_all(rows, "y", 0, 0, tiled=True).reshape(-1, D)
+
+
+def feature_order(zl, core, heads, size):
     place = lax.broadcasted_iota(jnp.int32, (heads * size, heads * size), 1)
     source = lax.broadcasted_iota(jnp.int32, (heads * size, heads * size), 0)
     inner = place % (2 * heads)
     slot = place // (2 * heads)
     bits = slot % 8
     from_zl = zl ^ (bits // 4 + bits // 2 % 2 * 2 + bits % 2 * 4)
-    turn = slot // 8 % 4
-    from_y = (y + jnp.where(turn == 1, 3, jnp.where(turn == 2, 1, jnp.where(turn == 3, 2, 0)))) % 4
     from_core = jnp.where(slot >= 32, 1 - core, core)
-    block = (from_y * 8 + from_zl) * 2 + from_core
+    block = (slot // 8 % 4 * 8 + from_zl) * 2 + from_core
     return (source == inner // 2 * size + block * 2 + inner % 2).astype(BF16)
+
+
+def project_kernel(c_ref, near_ref, far_ref, o_ref):
+    half = near_ref.shape[0]
+    part = jnp.dot(c_ref[:, :half], near_ref[...], preferred_element_type=F32)
+    part = part + jnp.dot(c_ref[:, half:], far_ref[...], preferred_element_type=F32)
+    o_ref[0, 0] = part.astype(BF16)
+
+
+def project(ordered, near, far):
+    tokens = ordered.shape[0]
+    width = D // 8
+    return pl.pallas_call(
+        project_kernel,
+        out_shape=jax.ShapeDtypeStruct((4, 2, tokens, width), BF16),
+        grid=(4, 2),
+        in_specs=[
+            pl.BlockSpec(ordered.shape, lambda i, j: (0, 0)),
+            pl.BlockSpec((near.shape[0], width), lambda i, j: (0, j * 4 + i)),
+            pl.BlockSpec((near.shape[0], width), lambda i, j: (0, j * 4 + i)),
+        ],
+        out_specs=pl.BlockSpec((1, 1, tokens, width), lambda i, j: (i, j, 0, 0)),
+        compiler_params=pltpu.CompilerParams(vmem_limit_bytes=32 << 20),
+        name="project",
+    )(ordered, near, far)
 
 
 def swap_order():
@@ -192,28 +221,33 @@
     ctx_count = 64
     width = resid.shape[1]
 
-    near, far = gather_out(w_out)
-
     piece = tokens // 4
     pair = jnp.stack([keys, values], axis=0)
     pair = lax.dynamic_index_in_dim(pair, zh, 2, keepdims=False)
     pair = lax.dynamic_slice_in_dim(pair, x * piece, piece, 1)
     pair = jnp.broadcast_to(pair[None], (8,) + pair.shape)
-    pair = lax.all_to_all(pair, "zl", 0, 0, tiled=True)
+    line = gather_line(w_out)
+    pair = first = lax.all_to_all(pair, "zl", 0, 0, tiled=True)
+    rows = queries.reshape(tokens * heads, size)
+    asked = [shift(rows, "x", step) for step in (1, 2, 3)]
+    pair = after(pair, asked)
     pair = jnp.broadcast_to(pair[None], (4,) + pair.shape)
-    pair = lax.all_to_all(pair, "y", 0, 0, tiled=True)
+    pair = second = lax.all_to_all(pair, "y", 0, 0, tiled=True)
+    near = gather_rest(line, first, second)
     pair = jnp.stack([pair, shift(pair, "core", 1)], axis=0)
     all_keys = pair[:, :, :, 0].reshape(-1, size)
     all_values = pair[:, :, :, 1].reshape(-1, size)
 
-    rows = queries.reshape(tokens * heads, size)
     place = jnp.stack([ctx_place * tokens, core, x]).astype(jnp.int32)
-    asked = [shift(rows, "x", step) for step in (1, 2, 3)]
-    parts = []
+    parts, found = [], place
     for step in (2, 1, 3):
-        found = attend(place, asked[step - 1], all_keys, all_values, heads, piece, tokens)
+        theirs = after(asked[step - 1], found)
+        found = attend(place, theirs, all_keys, all_values, heads, piece, tokens)
         parts.append(shift(found, "x", -step))
+    rows = after(rows, found)
     parts.append(attend(place, rows, all_keys, all_values, heads, piece, tokens))
+    near = after(near, parts)
+    far = shift(near, "core", 1)
 
     bests = [part[size].astype(F32) for part in parts]
     best = functools.reduce(jnp.maximum, bests)
@@ -225,15 +259,11 @@
         below = below + (part[size + 1].astype(F32) + part[size + 2].astype(F32)) * scale
     context = (above / below[None, :]).astype(BF16).T.reshape(tokens, heads, size)
 
-    order = feature_order(y, zl, core, heads, size)
+    order = feature_order(zl, core, heads, size)
     ordered = jnp.dot(
         context.reshape(tokens, heads * size), order, preferred_element_type=F32
     ).astype(BF16)
-    split = heads * size // 2
-    projected = jnp.dot(ordered[:, :split], near, preferred_element_type=F32)
-    projected = projected + jnp.dot(ordered[:, split:], far, preferred_element_type=F32)
-    projected = projected.astype(BF16)
-    projected = projected.reshape(tokens, 2, 4, width).transpose(2, 1, 0, 3)
+    projected = project(ordered, near, far)
     projected = lax.all_to_all(projected, "x", 0, 0, tiled=True)
     half = jnp.sum(projected.astype(F32), axis=0)
     theirs = lax.dynamic_index_in_dim(half, 1 - zh, 0, keepdims=False).astype(BF16)

time: 380 us -> 369 us (0.971)
  waiting for transfers between devices: 148 us -> 130 us
  other arithmetic: 15.5 us -> 23.1 us
  Pallas kernels: 17.7 us -> 25.2 us
  local copies, waits for them, and re-layouts: 15.2 us -> 10.6 us
    ppermute x15 -> x11, waiting for transfers between devices: 59.2 us -> 31.9 us  [shift(): lax.ppermute(value, axis, [(i, (i + step) % count) for i in range(count)])]
    ppermute x15 -> x11, starting transfers between devices: 63.6 us -> 52.7 us  [shift(): lax.ppermute(value, axis, [(i, (i + step) % count) for i in range(count)])]
    all_to_all x2 -> x3, waiting for transfers between devices: 0.01 us -> 7.23 us  [the longest x1 7.22 us: body(): pair = second = lax.all_to_all(pair, 'y', 0, 0, tiled=True)]
    pallas_call x0 -> x1, Pallas kernels: none -> 6.37 us  [project(): pl.pallas_call(project_kernel, out_shape=jax.ShapeDtypeStruct((4, 2, toke...]
    all_to_all x1, starting transfers between devices: 13 us -> 18.2 us  [body(): lax.all_to_all(outgoing, CTX, 0, 0, tiled=True).reshape(4 * slots, lanes)]
    dot_general x2 -> x0, matrix products: 4.14 us -> none  [the longest x1 2.1 us: body(): projected = jnp.dot(ordered[:, :split], near, preferred_element_type=F32)]
    all_to_all x2 -> x3, starting transfers between devices: 16.4 us -> 20 us  [the longest x1 12.2 us: body(): pair = first = lax.all_to_all(pair, 'zl', 0, 0, tiled=True)]
  transfers between devices with their start and end apart: 23 -> 20, of which waited for: 13 -> 11; matrix products, arithmetic and copies ran while one was open for 7% -> 9% of each run, Pallas kernels for 4% -> 4%
where the time goes in v3:
time: 369 us; the launch traced here: 367 us
  waiting for transfers between devices  130 us (35%)
  starting transfers between devices  125 us (34%)
  blocking collectives  40 us (11%)
  Pallas kernels  25.2 us (7%)
  other arithmetic  23.1 us (6%)
  matrix products  11.5 us (3%)
  local copies, waits for them, and re-layouts  10.6 us (3%)
    ppermute x11, starting transfers between devices, shift(): lax.ppermute(value, axis, [(i, (i + step) % count) for i in range(count)])  52.7 us
    all_to_all x1, waiting for transfers between devices, body(): lax.all_to_all(outgoing, CTX, 0, 0, tiled=True).reshape(4 * slots, lanes)  32.8 us
    all_to_all x1, waiting for transfers between devices, body(): lax.all_to_all(result, CTX, 0, 0, tiled=True).reshape(4 * slots, lanes)  31.9 us
    ppermute x11, waiting for transfers between devices, shift(): lax.ppermute(value, axis, [(i, (i + step) % count) for i in range(count)])  31.9 us
    all_to_all x1, blocking collectives, body(): part = lax.all_to_all(part, 'x', 0, 0, tiled=True)  27.9 us
    all_to_all x1, starting transfers between devices, body(): lax.all_to_all(result, CTX, 0, 0, tiled=True).reshape(4 * slots, lanes)  19.3 us
    all_to_all x1, starting transfers between devices, body(): lax.all_to_all(outgoing, CTX, 0, 0, tiled=True).reshape(4 * slots, lanes)  18.2 us
    pallas_call x4, Pallas kernels, attend(): pl.pallas_call(functools.partial(attend_kernel, heads=heads, piece=piece,...  14.9 us
  transfers between devices with their start and end apart: 20, of which 11 were waited for; matrix products, arithmetic and copies ran while one was open for 9% of the time, Pallas kernels for 4%

profile of v3, /device:TPU:1, one launch (start us, length us, event | category | flops | bytes accessed | tf_op | source)
XLA Modules:
  0.0 367.0 jit_solution(7388129238970002497)
XLA Ops:
  0.6 5.5 %collective-permute-start = (bf16[512,128]{1,0:T(8,128)(2,1)}, bf16[512,128]{1,0:T(8,128)(2,1)S(1)}, u32[]{:S(2)}, u32[]{:S(2)}) collective-permute-start(bf16[512,128]{1,0:T(8,128)(2,1)} %bitcast.74), channel_id=1, source_target_pairs={{0,2},{1,3},{2,0},{3,1},{4,6},{5,7},{6,4},{7,5},{8,10},{9,11},{10,... | collective-permute-start | bytes 393224 | tf_op jit(solution)/shard_map/ppermute | solution.py:26
  6.1 2.2 collective-permute-start.1
  8.4 4.3 %collective-permute-start.2 = (bf16[512,128]{1,0:T(8,128)(2,1)}, bf16[512,128]{1,0:T(8,128)(2,1)S(1)}, u32[]{:S(2)}, u32[]{:S(2)}) collective-permute-start(bf16[512,128]{1,0:T(8,128)(2,1)} %bitcast.76), channel_id=1, source_target_pairs={{0,3},{1,0},{2,1},{3,2},{4,7},{5,4},{6,5},{7,6},{8,11},{9,8},{10,9... | collective-permute-start | bytes 393224 | tf_op jit(solution)/shard_map/ppermute | solution.py:26
  14.2 12.2 %all-to-all-start = ((bf16[8,2,32,128]{3,2,1,0:T(8,128)(2,1)}), bf16[8,2,32,128]{3,2,1,0:T(8,128)(2,1)S(1)}, u32[]{:S(2)}, u32[]{:S(2)}) async-start(bf16[8,2,32,128]{3,2,1,0:T(8,128)(2,1)} %broadcast_in_dim.146), calls=%async_computation | async-start | bytes 262144 | tf_op jit(solution)/shard_map/all_to_all | solution.py:230
  27.4 7.3 %collective-permute-start.7 = (bf16[8,4096]{1,0:T(8,128)(2,1)S(1)}, bf16[8,4096]{1,0:T(8,128)(2,1)S(1)}, u32[]{:S(2)}, u32[]{:S(2)}) collective-permute-start(bf16[8,4096]{1,0:T(8,128)(2,1)S(1)} %reshape.117), channel_id=1, source_target_pairs={{0,64},{16,80},{32,96},{48,112},{64,0},{80,16},{96,32},{112,48},{1... | collective-permute-start | bytes 196616 | tf_op jit(solution)/shard_map/ppermute | solution.py:30
  37.0 3.1 fusion.9
  40.1 4.6 %collective-permute-done.7 = bf16[8,4096]{1,0:T(8,128)(2,1)S(1)} collective-permute-done((bf16[8,4096]{1,0:T(8,128)(2,1)S(1)}, bf16[8,4096]{1,0:T(8,128)(2,1)S(1)}, u32[]{:S(2)}, u32[]{:S(2)}) %collective-permute-start.7) | collective-permute-done | bytes 65568 | tf_op jit(solution)/shard_map/ppermute | solution.py:30
  44.7 1.9 collective-permute-start.8
  47.2 7.1 %collective-permute-done.8 = bf16[16,4096]{1,0:T(8,128)(2,1)S(1)} collective-permute-done((bf16[16,4096]{1,0:T(8,128)(2,1)S(1)}, bf16[16,4096]{1,0:T(8,128)(2,1)S(1)}, u32[]{:S(2)}, u32[]{:S(2)}) %collective-permute-start.8) | collective-permute-done | bytes 131104 | tf_op jit(solution)/shard_map/ppermute | solution.py:30
  54.3 1.9 collective-permute-start.9
  57.9 4.2 %all-to-all-start.1 = ((bf16[4,8,2,32,128]{4,3,1,2,0:T(8,128)(2,1)}), bf16[4,8,2,32,128]{4,3,1,2,0:T(8,128)(2,1)S(1)}, u32[]{:S(2)}, u32[]{:S(2)}) async-start(bf16[4,8,2,32,128]{4,3,1,2,0:T(8,128)(2,1)} %broadcast_in_dim.147), calls=%async_computation.1 | async-start | bytes 1048576 | tf_op jit(solution)/shard_map/all_to_all | solution.py:235
  63.5 7.2 %all-to-all-done.1 = bf16[4,8,2,32,128]{4,3,1,2,0:T(8,128)(2,1)S(1)} async-done(((bf16[4,8,2,32,128]{4,3,1,2,0:T(8,128)(2,1)}), bf16[4,8,2,32,128]{4,3,1,2,0:T(8,128)(2,1)S(1)}, u32[]{:S(2)}, u32[]{:S(2)}) %all-to-all-start.1) | async-done | bytes 524320 | tf_op jit(solution)/shard_map/all_to_all | solution.py:235
  70.8 1.6 broadcast_in_dim.150
  72.3 3.6 all-to-all-start.2
  75.9 2.5 convert_select_fusion.3
  78.4 3.6 collective-permute-start.3
  82.1 2.6 select_dynamic-update-slice_fusion.7
  86.8 3.4 attend.4
  90.2 1.9 collective-permute-start.4
  92.1 4.1 %attend.5 = bf16[144,512]{1,0:T(8,128)(2,1)} custom-call(s32[3]{0:T(128)S(1)} %pad_add_fusion.place, bf16[512,128]{1,0:T(8,128)(2,1)S(1)} %copy-done.3, bf16[2048,128]{1,0:T(8,128)(2,1)S(1)} %bitcast.65, bf16[2048,128]{1,0:T(8,128)(2,1)S(1)} %bitcast.61), custom_call_target="tpu_custom_call" | custom-call | tf_op jit(solution)/shard_map/attend/pallas_call | solution.py:200
  96.2 3.4 collective-permute-start.5
  99.6 4.0 %attend.6 = bf16[144,512]{1,0:T(8,128)(2,1)} custom-call(s32[3]{0:T(128)S(1)} %pad_add_fusion.place, bf16[512,128]{1,0:T(8,128)(2,1)S(1)} %collective-permute-done.2.q_ref, bf16[2048,128]{1,0:T(8,128)(2,1)S(1)} %bitcast.66, bf16[2048,128]{1,0:T(8,128)(2,1)S(1)} %bitcast.62), custom_call_target="tpu_custom_call" | custom-call | tf_op jit(solution)/shard_map/attend/pallas_call | solution.py:200
  103.6 1.9 collective-permute-start.6
  106.5 3.4 attend.7
  109.9 2.0 collective-permute-done.6
  111.9 3.3 collective-permute-start.10
  115.2 2.1 select_dynamic-update-slice_fusion.6
  120.3 6.4 %project.1 = bf16[4,2,128,512]{3,2,1,0:T(8,128)(2,1)} custom-call(bf16[128,512]{1,0:T(8,128)(2,1)S(1)} %convolution_convert_fusion.1.c_ref, bf16[256,4096]{1,0:T(8,128)(2,1)S(1)} %bitcast.70, bf16[256,4096]{1,0:T(8,128)(2,1)} %collective-permute-done.10.far_ref), custom_call_target="tpu_custom_call" | custom-call | tf_op jit(solution)/shard_map/project/pallas_call | solution.py:73
  126.7 3.6 all-to-all-start.3
  132.3 13.3 %all-to-all-done.3 = bf16[4,2,128,512]{3,2,1,0:T(8,128)(2,1)S(1)} async-done(((bf16[4,2,128,512]{3,2,1,0:T(8,128)(2,1)}), bf16[4,2,128,512]{3,2,1,0:T(8,128)(2,1)S(1)}, u32[]{:S(2)}, u32[]{:S(2)}) %all-to-all-start.3) | async-done | bytes 1048608 | tf_op jit(solution)/shard_map/all_to_all | solution.py:267
  145.9 8.1 %collective-permute-start.11 = (bf16[128,512]{0,1:T(8,128)(2,1)S(1)}, bf16[128,512]{0,1:T(8,128)(2,1)S(1)}, u32[]{:S(2)}, u32[]{:S(2)}) collective-permute-start(bf16[128,512]{0,1:T(8,128)(2,1)S(1)} %bitcast.87), channel_id=1, source_target_pairs={{0,4},{4,0},{1,5},{5,1},{2,6},{6,2},{3,7},{7,3},{8,12},{12,8},{9,1... | collective-permute-start | bytes 393224 | tf_op jit(solution)/shard_map/ppermute | solution.py:26
  154.0 2.9 convert_select_fusion.2
  157.2 3.5 collective-permute-done.11
  160.9 3.2 convolution_convert_fusion
  164.1 18.2 %all-to-all-start.4 = ((bf16[64,40,128]{2,1,0:T(8,128)(2,1)}), bf16[64,40,128]{2,1,0:T(8,128)(2,1)S(1)}, u32[]{:S(2)}, u32[]{:S(2)}) async-start(bf16[64,40,128]{2,1,0:T(8,128)(2,1)} %bitcast.23), calls=%async_computation.4 | async-start | bytes 1310720 | tf_op jit(solution)/shard_map/all_to_all | solution.py:311
  182.4 1.7 copy.50
  184.4 32.8 %all-to-all-done.4 = bf16[64,40,128]{2,1,0:T(8,128)(2,1)S(1)} async-done(((bf16[64,40,128]{2,1,0:T(8,128)(2,1)}), bf16[64,40,128]{2,1,0:T(8,128)(2,1)S(1)}, u32[]{:S(2)}, u32[]{:S(2)}) %all-to-all-start.4) | async-done | bytes 655392 | tf_op jit(solution)/shard_map/all_to_all | solution.py:311
  217.2 1.6 gate_up.1
  218.8 27.9 %all_to_all.35 = bf16[4,160,1664]{2,1,0:T(8,128)(2,1)S(1)} all-to-all(bf16[4,160,1664]{2,1,0:T(8,128)(2,1)S(1)} %bitcast.68), channel_id=1, replica_groups=mesh['y'=4,'zl'=8,'core'=2,'zh'=2,'x'=4] {'x'}, dimensions={0} | all-to-all | bytes 4259840 | tf_op jit(solution)/shard_map/all_to_all | solution.py:316
  247.8 7.9 %collective-permute-start.12 = (bf16[80,1664]{1,0:T(8,128)(2,1)}, bf16[80,1664]{1,0:T(8,128)(2,1)S(1)}, u32[]{:S(2)}, u32[]{:S(2)}) collective-permute-start(bf16[80,1664]{1,0:T(8,128)(2,1)} %fusion.60), channel_id=1, source_target_pairs={{0,4},{4,0},{1,5},{5,1},{2,6},{6,2},{3,7},{7,3},{8,12},{12,8},{9,1... | collective-permute-start | bytes 798728 | tf_op jit(solution)/shard_map/ppermute | solution.py:26
  255.7 19.5 %collective-permute-done.12 = bf16[80,1664]{1,0:T(8,128)(2,1)S(1)} collective-permute-done((bf16[80,1664]{1,0:T(8,128)(2,1)}, bf16[80,1664]{1,0:T(8,128)(2,1)S(1)}, u32[]{:S(2)}, u32[]{:S(2)}) %collective-permute-start.12) | collective-permute-done | bytes 266272 | tf_op jit(solution)/shard_map/ppermute | solution.py:26
  275.6 10.5 %collective-permute-start.13 = (bf16[80,768]{1,0:T(8,128)(2,1)S(1)}, bf16[80,768]{1,0:T(8,128)(2,1)S(1)}, u32[]{:S(2)}, u32[]{:S(2)}) collective-permute-start(bf16[80,768]{1,0:T(8,128)(2,1)S(1)} %fusion.64), channel_id=1, source_target_pairs={{0,4},{4,0},{1,5},{5,1},{2,6},{6,2},{3,7},{7,3},{8,12},{12,8},{9,1... | collective-permute-start | bytes 368648 | tf_op jit(solution)/shard_map/ppermute | solution.py:26
  286.3 6.8 %collective-permute-done.13 = bf16[80,768]{1,0:T(8,128)(2,1)S(1)} collective-permute-done((bf16[80,768]{1,0:T(8,128)(2,1)S(1)}, bf16[80,768]{1,0:T(8,128)(2,1)S(1)}, u32[]{:S(2)}, u32[]{:S(2)}) %collective-permute-start.13) | collective-permute-done | bytes 122912 | tf_op jit(solution)/shard_map/ppermute | solution.py:26
  293.2 12.1 %all_gather.3.h_ref = bf16[640,768]{1,0:T(8,128)(2,1)S(1)} all-gather(bf16[160,768]{1,0:T(8,128)(2,1)S(1)} %bitcast.84), channel_id=1, replica_groups=mesh['y'=4,'zl'=8,'core'=2,'zh'=2,'x'=4] {'x'}, dimensions={0}, use_global_device_ids=true | all-gather | bytes 1228800 | tf_op jit(solution)/shard_map/all_gather | solution.py:330
  305.3 2.3 down.1
  307.6 19.3 %all-to-all-start.6 = ((bf16[64,40,128]{2,1,0:T(8,128)(2,1)}), bf16[64,40,128]{2,1,0:T(8,128)(2,1)S(1)}, u32[]{:S(2)}, u32[]{:S(2)}) async-start(bf16[64,40,128]{2,1,0:T(8,128)(2,1)} %bitcast.34), calls=%async_computation.6 | async-start | bytes 1310720 | tf_op jit(solution)/shard_map/all_to_all | solution.py:332
  329.8 31.9 %all-to-all-done.6 = bf16[64,40,128]{2,1,0:T(8,128)(2,1)S(1)} async-done(((bf16[64,40,128]{2,1,0:T(8,128)(2,1)}), bf16[64,40,128]{2,1,0:T(8,128)(2,1)S(1)}, u32[]{:S(2)}, u32[]{:S(2)}) %all-to-all-start.6) | async-done | bytes 655392 | tf_op jit(solution)/shard_map/all_to_all | solution.py:332
  361.7 4.4 %fusion.140 = f32[1024,128]{0,1:T(8,128)S(1)} fusion(bf16[2560,1024]{0,1:T(8,128)(2,1)} %select_dynamic-update-slice_fusion, bf16[2560,128]{1,0:T(8,128)(2,1)S(1)} %bitcast.81), kind=kOutput, calls=%fused_computation.270 | convolution fusion | flops 671088640 | bytes 6422528 | tf_op jit(solution)/shard_map/dot_general | solution.py:333
  (110 shorter events, 22.7 us)
Async XLA Ops:
  0.6 56.3 %collective-permute-start = (bf16[512,128]{1,0:T(8,128)(2,1)}, bf16[512,128]{1,0:T(8,128)(2,1)S(1)}, u32[]{:S(2)}, u32[]{:S(2)}) collective-permute-start(bf16[512,128]{1,0:T(8,128)(2,1)} %bitcast.74), channel_id=1, source_target_pairs={{0,2},{1,3},{2,0},{3,1},{4,6},{5,7},{6,4},{7,5},{8,10},{9,11},{10,... | collective-permute-start | bytes 393224 | tf_op jit(solution)/shard_map/ppermute | solution.py:26
  6.1 50.8 %collective-permute-start.1 = (bf16[512,128]{1,0:T(8,128)(2,1)}, bf16[512,128]{1,0:T(8,128)(2,1)S(1)}, u32[]{:S(2)}, u32[]{:S(2)}) collective-permute-start(bf16[512,128]{1,0:T(8,128)(2,1)} %bitcast.75), channel_id=1, source_target_pairs={{0,1},{1,2},{2,3},{3,0},{4,5},{5,6},{6,7},{7,4},{8,9},{9,10},{10,1... | collective-permute-start | bytes 393224 | tf_op jit(solution)/shard_map/ppermute | solution.py:26
  8.4 48.6 %collective-permute-start.2 = (bf16[512,128]{1,0:T(8,128)(2,1)}, bf16[512,128]{1,0:T(8,128)(2,1)S(1)}, u32[]{:S(2)}, u32[]{:S(2)}) collective-permute-start(bf16[512,128]{1,0:T(8,128)(2,1)} %bitcast.76), channel_id=1, source_target_pairs={{0,3},{1,0},{2,1},{3,2},{4,7},{5,4},{6,5},{7,6},{8,11},{9,8},{10,9... | collective-permute-start | bytes 393224 | tf_op jit(solution)/shard_map/ppermute | solution.py:26
  14.2 40.0 %all-to-all-start = ((bf16[8,2,32,128]{3,2,1,0:T(8,128)(2,1)}), bf16[8,2,32,128]{3,2,1,0:T(8,128)(2,1)S(1)}, u32[]{:S(2)}, u32[]{:S(2)}) async-start(bf16[8,2,32,128]{3,2,1,0:T(8,128)(2,1)} %broadcast_in_dim.146), calls=%async_computation | async-start | bytes 262144 | tf_op jit(solution)/shard_map/all_to_all | solution.py:230
  27.4 17.3 %collective-permute-start.7 = (bf16[8,4096]{1,0:T(8,128)(2,1)S(1)}, bf16[8,4096]{1,0:T(8,128)(2,1)S(1)}, u32[]{:S(2)}, u32[]{:S(2)}) collective-permute-start(bf16[8,4096]{1,0:T(8,128)(2,1)S(1)} %reshape.117), channel_id=1, source_target_pairs={{0,64},{16,80},{32,96},{48,112},{64,0},{80,16},{96,32},{112,48},{1... | collective-permute-start | bytes 196616 | tf_op jit(solution)/shard_map/ppermute | solution.py:30
  44.7 9.6 %collective-permute-start.8 = (bf16[16,4096]{1,0:T(8,128)(2,1)S(1)}, bf16[16,4096]{1,0:T(8,128)(2,1)S(1)}, u32[]{:S(2)}, u32[]{:S(2)}) collective-permute-start(bf16[16,4096]{1,0:T(8,128)(2,1)S(1)} %pad_maximum_fusion.3), channel_id=1, source_target_pairs={{0,32},{16,48},{32,0},{48,16},{64,96},{80,112},{96,64},{112,80},{1... | collective-permute-start | bytes 393224 | tf_op jit(solution)/shard_map/ppermute | solution.py:30
  54.3 9.2 %collective-permute-start.9 = (bf16[32,4096]{1,0:T(8,128)(2,1)S(1)}, bf16[32,4096]{1,0:T(8,128)(2,1)S(1)}, u32[]{:S(2)}, u32[]{:S(2)}) collective-permute-start(bf16[32,4096]{1,0:T(8,128)(2,1)S(1)} %pad_maximum_fusion.2), channel_id=1, source_target_pairs={{0,16},{16,0},{32,48},{48,32},{64,80},{80,64},{96,112},{112,96},{1... | collective-permute-start | bytes 786440 | tf_op jit(solution)/shard_map/ppermute | solution.py:30
  56.9 21.5 %copy-start.4 = (bf16[512,128]{1,0:T(8,128)(2,1)}, bf16[512,128]{1,0:T(8,128)(2,1)S(1)}, u32[]{:S(2)}) copy-start(bf16[512,128]{1,0:T(8,128)(2,1)S(1)} %collective-permute-done.q_ref) | copy-start | bytes 393220
  57.0 21.5 %copy-start.2 = (bf16[512,128]{1,0:T(8,128)(2,1)}, bf16[512,128]{1,0:T(8,128)(2,1)S(1)}, u32[]{:S(2)}) copy-start(bf16[512,128]{1,0:T(8,128)(2,1)S(1)} %collective-permute-done.1.q_ref) | copy-start | bytes 393220
  57.9 12.9 %all-to-all-start.1 = ((bf16[4,8,2,32,128]{4,3,1,2,0:T(8,128)(2,1)}), bf16[4,8,2,32,128]{4,3,1,2,0:T(8,128)(2,1)S(1)}, u32[]{:S(2)}, u32[]{:S(2)}) async-start(bf16[4,8,2,32,128]{4,3,1,2,0:T(8,128)(2,1)} %broadcast_in_dim.147), calls=%async_computation.1 | async-start | bytes 1048576 | tf_op jit(solution)/shard_map/all_to_all | solution.py:235
  70.8 13.9 %copy-start.10 = (bf16[4,8,2,32,128]{4,3,1,2,0:T(8,128)(2,1)}, bf16[4,8,2,32,128]{4,3,1,2,0:T(8,128)(2,1)S(1)}, u32[]{:S(2)}) copy-start(bf16[4,8,2,32,128]{4,3,1,2,0:T(8,128)(2,1)S(1)} %all-to-all-done.1) | copy-start | bytes 1572868
  72.3 39.6 %all-to-all-start.2 = ((bf16[4,64,4096]{2,1,0:T(8,128)(2,1)}), bf16[4,64,4096]{2,1,0:T(8,128)(2,1)S(1)}, u32[]{:S(2)}, u32[]{:S(2)}) async-start(bf16[4,64,4096]{2,1,0:T(8,128)(2,1)} %broadcast_in_dim.150), calls=%async_computation.2 | async-start | bytes 4194304 | tf_op jit(solution)/shard_map/all_to_all | solution.py:48
  78.4 7.5 %copy-start.8 = (pred[2560,128]{0,1:T(8,128)(4,1)}, pred[2560,128]{0,1:T(8,128)(4,1)S(1)}, u32[]{:S(2)}) copy-start(pred[2560,128]{0,1:T(8,128)(4,1)S(1)} %get-tuple-element.31) | copy-start | bytes 983044
  78.4 6.3 %collective-permute-start.3 = (bf16[4,8,2,32,128]{4,3,1,2,0:T(8,128)(2,1)S(1)}, bf16[4,8,2,32,128]{4,3,1,2,0:T(8,128)(2,1)S(1)}, u32[]{:S(2)}, u32[]{:S(2)}) collective-permute-start(bf16[4,8,2,32,128]{4,3,1,2,0:T(8,128)(2,1)S(1)} %all-to-all-done.1), channel_id=1, source_target_pairs={{0,8},{8,0},{1,9},{9,1},{2,10},{10,2},{3,11},{11,3},{4,12},{12,4},... | collective-permute-start | bytes 1572872 | tf_op jit(solution)/shard_map/ppermute | solution.py:26
  82.1 10.1 %copy-start.3 = (bf16[512,128]{1,0:T(8,128)(2,1)S(1)}, bf16[512,128]{1,0:T(8,128)(2,1)}, u32[]{:S(2)}) copy-start(bf16[512,128]{1,0:T(8,128)(2,1)} %copy-done.2) | copy-start | bytes 393220
  84.7 34.9 %copy-start.17 = (s32[512]{0:T(512)S(1)}, s32[512]{0:T(512)}, u32[]{:S(2)}) copy-start(s32[512]{0:T(512)} %get-tuple-element.68) | copy-start | bytes 6148
  84.7 34.9 %copy-start.18 = (s32[512]{0:T(512)S(1)}, s32[512]{0:T(512)}, u32[]{:S(2)}) copy-start(s32[512]{0:T(512)} %get-tuple-element.69) | copy-start | bytes 6148
  84.7 34.9 %copy-start.19 = (s32[512]{0:T(512)S(1)}, s32[512]{0:T(512)}, u32[]{:S(2)}) copy-start(s32[512]{0:T(512)} %get-tuple-element.70) | copy-start | bytes 6148
  84.7 34.9 %copy-start.20 = (s32[512]{0:T(512)S(1)}, s32[512]{0:T(512)}, u32[]{:S(2)}) copy-start(s32[512]{0:T(512)} %get-tuple-element.71) | copy-start | bytes 6148
  85.9 0.9 copy-start.5
  90.2 21.7 %collective-permute-start.4 = (bf16[144,512]{1,0:T(8,128)(2,1)S(1)}, bf16[144,512]{1,0:T(8,128)(2,1)}, u32[]{:S(2)}, u32[]{:S(2)}) collective-permute-start(bf16[144,512]{1,0:T(8,128)(2,1)S(1)} %attend.4), channel_id=1, source_target_pairs={{0,2},{1,3},{2,0},{3,1},{4,6},{5,7},{6,4},{7,5},{8,10},{9,11},{10,... | collective-permute-start | bytes 442376 | tf_op jit(solution)/shard_map/ppermute | solution.py:26
  96.2 15.7 %collective-permute-start.5 = (bf16[144,512]{1,0:T(8,128)(2,1)}, bf16[144,512]{1,0:T(8,128)(2,1)}, u32[]{:S(2)}, u32[]{:S(2)}) collective-permute-start(bf16[144,512]{1,0:T(8,128)(2,1)} %attend.5), channel_id=1, source_target_pairs={{0,3},{1,0},{2,1},{3,2},{4,7},{5,4},{6,5},{7,6},{8,11},{9,8},{10,9... | collective-permute-start | bytes 442376 | tf_op jit(solution)/shard_map/ppermute | solution.py:26
  103.6 8.2 %collective-permute-start.6 = (bf16[144,512]{1,0:T(8,128)(2,1)}, bf16[144,512]{1,0:T(8,128)(2,1)}, u32[]{:S(2)}, u32[]{:S(2)}) collective-permute-start(bf16[144,512]{1,0:T(8,128)(2,1)} %attend.6), channel_id=1, source_target_pairs={{0,1},{1,2},{2,3},{3,0},{4,5},{5,6},{6,7},{7,4},{8,9},{9,10},{10,1... | collective-permute-start | bytes 442376 | tf_op jit(solution)/shard_map/ppermute | solution.py:26
  105.6 0.9 copy-start.1
  106.5 23.8 %copy-start.15 = (pred[2560]{0:T(1024)(128)(4,1)}, pred[2560]{0:T(1024)(128)(4,1)S(1)}, u32[]{:S(2)}) copy-start(pred[2560]{0:T(1024)(128)(4,1)S(1)} %get-tuple-element.64) | copy-start | bytes 7684
  111.9 8.4 %collective-permute-start.10 = (bf16[256,4096]{1,0:T(8,128)(2,1)S(1)}, bf16[256,4096]{1,0:T(8,128)(2,1)}, u32[]{:S(2)}, u32[]{:S(2)}) collective-permute-start(bf16[256,4096]{1,0:T(8,128)(2,1)S(1)} %bitcast.69), channel_id=1, source_target_pairs={{0,8},{8,0},{1,9},{9,1},{2,10},{10,2},{3,11},{11,3},{4,12},{12,4},... | collective-permute-start | bytes 6291464 | tf_op jit(solution)/shard_map/ppermute | solution.py:26
  119.5 0.8 copy-start.13
  120.3 10.1 %copy-start.7 = (bf16[2560,128]{0,1:T(8,128)(2,1)S(1)}, bf16[2560,128]{0,1:T(8,128)(2,1)}, u32[]{:S(2)}) copy-start(bf16[2560,128]{0,1:T(8,128)(2,1)} %get-tuple-element.35) | copy-start | bytes 1966084
  120.3 33.7 %copy-start.9 = (pred[2560,128]{0,1:T(8,128)(4,1)S(1)}, pred[2560,128]{0,1:T(8,128)(4,1)}, u32[]{:S(2)}) copy-start(pred[2560,128]{0,1:T(8,128)(4,1)} %copy-done.8) | copy-start | bytes 983044
  126.7 30.3 %copy-start.14 = (bf16[128,512]{1,0:T(8,128)(2,1)S(1)}, bf16[128,512]{1,0:T(8,128)(2,1)}, u32[]{:S(2)}) copy-start(bf16[128,512]{1,0:T(8,128)(2,1)} %param.13) | copy-start | bytes 393220
  126.7 18.9 %all-to-all-start.3 = ((bf16[4,2,128,512]{3,2,1,0:T(8,128)(2,1)}), bf16[4,2,128,512]{3,2,1,0:T(8,128)(2,1)S(1)}, u32[]{:S(2)}, u32[]{:S(2)}) async-start(bf16[4,2,128,512]{3,2,1,0:T(8,128)(2,1)} %project.1), calls=%async_computation.3 | async-start | bytes 2097152 | tf_op jit(solution)/shard_map/all_to_all | solution.py:267
  130.3 30.4 %copy-start.6 = (f32[512]{0:T(512)S(1)}, f32[512]{0:T(512)}, u32[]{:S(2)}) copy-start(f32[512]{0:T(512)} %param.14) | copy-start | bytes 6148
  145.9 14.9 %collective-permute-start.11 = (bf16[128,512]{0,1:T(8,128)(2,1)S(1)}, bf16[128,512]{0,1:T(8,128)(2,1)S(1)}, u32[]{:S(2)}, u32[]{:S(2)}) collective-permute-start(bf16[128,512]{0,1:T(8,128)(2,1)S(1)} %bitcast.87), channel_id=1, source_target_pairs={{0,4},{4,0},{1,5},{5,1},{2,6},{6,2},{3,7},{7,3},{8,12},{12,8},{9,1... | collective-permute-start | bytes 393224 | tf_op jit(solution)/shard_map/ppermute | solution.py:26
  160.8 3.4 copy-start.11
  164.1 53.0 %all-to-all-start.4 = ((bf16[64,40,128]{2,1,0:T(8,128)(2,1)}), bf16[64,40,128]{2,1,0:T(8,128)(2,1)S(1)}, u32[]{:S(2)}, u32[]{:S(2)}) async-start(bf16[64,40,128]{2,1,0:T(8,128)(2,1)} %bitcast.23), calls=%async_computation.4 | async-start | bytes 1310720 | tf_op jit(solution)/shard_map/all_to_all | solution.py:311
  218.8 86.5 %copy-start = (bf16[1,768,512]{2,1,0:T(8,128)(2,1)S(1)}, bf16[1,768,512]{2,1,0:T(8,128)(2,1)}, u32[]{:S(2)}) copy-start(bf16[1,768,512]{2,1,0:T(8,128)(2,1)} %param.18) | copy-start | bytes 2359300
  247.0 80.9 %copy-start.16 = (pred[2560]{0:T(1024)(128)(4,1)S(1)}, pred[2560]{0:T(1024)(128)(4,1)}, u32[]{:S(2)}) copy-start(pred[2560]{0:T(1024)(128)(4,1)} %copy-done.15) | copy-start | bytes 7684
  247.8 27.5 %collective-permute-start.12 = (bf16[80,1664]{1,0:T(8,128)(2,1)}, bf16[80,1664]{1,0:T(8,128)(2,1)S(1)}, u32[]{:S(2)}, u32[]{:S(2)}) collective-permute-start(bf16[80,1664]{1,0:T(8,128)(2,1)} %fusion.60), channel_id=1, source_target_pairs={{0,4},{4,0},{1,5},{5,1},{2,6},{6,2},{3,7},{7,3},{8,12},{12,8},{9,1... | collective-permute-start | bytes 798728 | tf_op jit(solution)/shard_map/ppermute | solution.py:26
  275.6 17.5 %collective-permute-start.13 = (bf16[80,768]{1,0:T(8,128)(2,1)S(1)}, bf16[80,768]{1,0:T(8,128)(2,1)S(1)}, u32[]{:S(2)}, u32[]{:S(2)}) collective-permute-start(bf16[80,768]{1,0:T(8,128)(2,1)S(1)} %fusion.64), channel_id=1, source_target_pairs={{0,4},{4,0},{1,5},{5,1},{2,6},{6,2},{3,7},{7,3},{8,12},{12,8},{9,1... | collective-permute-start | bytes 368648 | tf_op jit(solution)/shard_map/ppermute | solution.py:26
  307.6 54.1 %all-to-all-start.6 = ((bf16[64,40,128]{2,1,0:T(8,128)(2,1)}), bf16[64,40,128]{2,1,0:T(8,128)(2,1)S(1)}, u32[]{:S(2)}, u32[]{:S(2)}) async-start(bf16[64,40,128]{2,1,0:T(8,128)(2,1)} %bitcast.34), calls=%async_computation.6 | async-start | bytes 1310720 | tf_op jit(solution)/shard_map/all_to_all | solution.py:332
  361.7 4.4 %copy-start.12 = (bf16[128,512]{0,1:T(8,128)(2,1)S(1)}, bf16[128,512]{0,1:T(8,128)(2,1)}, u32[]{:S(2)}) copy-start(bf16[128,512]{0,1:T(8,128)(2,1)} %copy-done.11) | copy-start | bytes 393220

commit v4 on v3

--- a/solution.py
+++ b/solution.py
@@ -34,18 +34,9 @@
     return lax.optimization_barrier((value, earlier))[0]
 
 
-def gather_line(w_out):
-    rows = w_out.reshape(-1, D)
-    rows = jnp.concatenate([rows, partner(rows, "zl", 4)], axis=0)
-    return jnp.concatenate([rows, partner(rows, "zl", 2)], axis=0)
-
-
-def gather_rest(rows, first, second):
-    rows = after(rows, first)
-    rows = jnp.concatenate([rows, partner(rows, "zl", 1)], axis=0)
-    rows = after(rows, second)
-    rows = jnp.broadcast_to(rows[None], (4,) + rows.shape)
-    return lax.all_to_all(rows, "y", 0, 0, tiled=True).reshape(-1, D)
+def double(rows, bit, earlier):
+    rows = after(rows, earlier)
+    return jnp.concatenate([rows, partner(rows, "zl", bit)], axis=0)
 
 
 def feature_order(zl, core, heads, size):
@@ -60,29 +51,36 @@
     return (source == inner // 2 * size + block * 2 + inner % 2).astype(BF16)
 
 
-def project_kernel(c_ref, near_ref, far_ref, o_ref):
+def project_kernel(side, c_ref, near_ref, far_ref, o_ref):
     half = near_ref.shape[0]
     part = jnp.dot(c_ref[:, :half], near_ref[...], preferred_element_type=F32)
     part = part + jnp.dot(c_ref[:, half:], far_ref[...], preferred_element_type=F32)
-    o_ref[0, 0] = part.astype(BF16)
-
-
-def project(ordered, near, far):
+    o_ref[0] = part.astype(BF16)
+
+
+def project(side, ordered, near, far):
     tokens = ordered.shape[0]
     width = D // 8
     return pl.pallas_call(
         project_kernel,
-        out_shape=jax.ShapeDtypeStruct((4, 2, tokens, width), BF16),
-        grid=(4, 2),
-        in_specs=[
-            pl.BlockSpec(ordered.shape, lambda i, j: (0, 0)),
-            pl.BlockSpec((near.shape[0], width), lambda i, j: (0, j * 4 + i)),
-            pl.BlockSpec((near.shape[0], width), lambda i, j: (0, j * 4 + i)),
-        ],
-        out_specs=pl.BlockSpec((1, 1, tokens, width), lambda i, j: (i, j, 0, 0)),
+        out_shape=jax.ShapeDtypeStruct((4, tokens, width), BF16),
+        grid_spec=pltpu.PrefetchScalarGridSpec(
+            num_scalar_prefetch=1,
+            grid=(4,),
+            in_specs=[
+                pl.BlockSpec(ordered.shape, lambda i, side: (0, 0)),
+                pl.BlockSpec((near.shape[0], width), lambda i, side: (0, side[0] * 4 + i)),
+                pl.BlockSpec((near.shape[0], width), lambda i, side: (0, side[0] * 4 + i)),
+            ],
+            out_specs=pl.BlockSpec((1, tokens, width), lambda i, side: (i, 0, 0)),
+        ),
         compiler_params=pltpu.CompilerParams(vmem_limit_bytes=32 << 20),
         name="project",
-    )(ordered, near, far)
+    )(side, ordered, near, far)
+
+
+def sum_along_x(parts):
+    return jnp.sum(lax.all_to_all(parts, "x", 0, 0, tiled=True).astype(F32), axis=0)
 
 
 def swap_order():
@@ -93,13 +91,14 @@
     return (source == (inner * 4 + outer) * MOST + rank).astype(BF16)
 
 
-def gate_up_kernel(x_ref, order_ref, w_ref, gain_ref, o_ref, rows_ref):
+def gate_up_kernel(side, x_ref, order_ref, w_ref, gain_ref, o_ref, rows_ref):
     step = order_ref.shape[0]
+    begin = pl.multiple_of(side[0] * (x_ref.shape[0] // 2), 16)
     quarter = step // 4
     lanes = x_ref.shape[1]
-    for b in range(x_ref.shape[0] // step):
+    for b in range(x_ref.shape[0] // step // 2):
         moved = jnp.dot(
-            order_ref[...], x_ref[b * step : (b + 1) * step, :], preferred_element_type=F32
+            order_ref[...], x_ref[pl.ds(begin + b * step, step), :], preferred_element_type=F32
         ).astype(BF16)
         for c in range(4):
             rows_ref[b * quarter : (b + 1) * quarter, c * lanes : (c + 1) * lanes] = moved[
@@ -107,6 +106,7 @@
             ]
     wide = w_ref.shape[1]
     inverse = 1.0 / gain_ref[...]
+    step = step // 2
     for b in range(rows_ref.shape[0] // step):
         rows = rows_ref[b * step : (b + 1) * step, :]
         part = jnp.dot(rows, w_ref[...], preferred_element_type=F32)
@@ -119,15 +119,16 @@
         o_ref[b * step : (b + 1) * step, wide : wide + 128] = extra.astype(BF16)
 
 
-def gate_up(arrived, weights, gain):
-    slots = arrived.shape[0] // 4
+def gate_up(side, arrived, order, weights, gain):
+    slots = arrived.shape[0] // 8
     return pl.pallas_call(
         gate_up_kernel,
         out_shape=jax.ShapeDtypeStruct((slots, weights.shape[1] + 128), BF16),
+        in_specs=[pl.BlockSpec(memory_space=pltpu.SMEM)] + [pl.BlockSpec(memory_space=pltpu.VMEM)] * 4,
         scratch_shapes=[pltpu.VMEM((slots, weights.shape[0]), BF16)],
         compiler_params=pltpu.CompilerParams(vmem_limit_bytes=48 << 20),
         name="gate_up",
-    )(arrived, swap_order(), weights, gain[None, :])
+    )(side, arrived, order, weights, gain[None, :])
 
 
 def down_kernel(h_ref, order_ref, w_ref, o_ref):
@@ -139,7 +140,7 @@
             h_ref[a * step : (a + 1) * step, :], w_ref[...], preferred_element_type=F32
         )
         for e in range(4):
-            b = a * 4 + e
+            b = e // 2 * 8 + a * 2 + e % 2
             piece = found[e * quarter : (e + 1) * quarter]
             piece = jnp.concatenate(
                 [piece[:, c * lanes : (c + 1) * lanes] for c in range(4)], axis=0
@@ -149,14 +150,14 @@
             ).astype(BF16)
 
 
-def down(hidden, weights):
+def down(hidden, order, weights):
     lanes = weights.shape[1] // 4
     return pl.pallas_call(
         down_kernel,
         out_shape=jax.ShapeDtypeStruct((hidden.shape[0] * 4, lanes), BF16),
         compiler_params=pltpu.CompilerParams(vmem_limit_bytes=48 << 20),
         name="down",
-    )(hidden, swap_order(), weights)
+    )(hidden, order, weights)
 
 
 def attend_kernel(place, q_ref, k_ref, v_ref, o_ref, *, heads, piece, tokens):
@@ -226,14 +227,16 @@
     pair = lax.dynamic_index_in_dim(pair, zh, 2, keepdims=False)
     pair = lax.dynamic_slice_in_dim(pair, x * piece, piece, 1)
     pair = jnp.broadcast_to(pair[None], (8,) + pair.shape)
-    line = gather_line(w_out)
+    line = w_out.reshape(-1, D)
+    line = jnp.concatenate([line, partner(line, "zl", 4)], axis=0)
     pair = first = lax.all_to_all(pair, "zl", 0, 0, tiled=True)
     rows = queries.reshape(tokens * heads, size)
     asked = [shift(rows, "x", step) for step in (1, 2, 3)]
     pair = after(pair, asked)
     pair = jnp.broadcast_to(pair[None], (4,) + pair.shape)
     pair = second = lax.all_to_all(pair, "y", 0, 0, tiled=True)
-    near = gather_rest(line, first, second)
+    line = double(line, 2, first)
+    line = double(line, 1, second)
     pair = jnp.stack([pair, shift(pair, "core", 1)], axis=0)
     all_keys = pair[:, :, :, 0].reshape(-1, size)
     all_values = pair[:, :, :, 1].reshape(-1, size)
@@ -244,6 +247,10 @@
         theirs = after(asked[step - 1], found)
         found = attend(place, theirs, all_keys, all_values, heads, piece, tokens)
         parts.append(shift(found, "x", -step))
+        if step == 2:
+            line = after(line, found)
+            line = jnp.broadcast_to(line[None], (4,) + line.shape)
+            near = lax.all_to_all(line, "y", 0, 0, tiled=True).reshape(-1, D)
     rows = after(rows, found)
     parts.append(attend(place, rows, all_keys, all_values, heads, piece, tokens))
     near = after(near, parts)
@@ -263,12 +270,10 @@
     ordered = jnp.dot(
         context.reshape(tokens, heads * size), order, preferred_element_type=F32
     ).astype(BF16)
-    projected = project(ordered, near, far)
-    projected = lax.all_to_all(projected, "x", 0, 0, tiled=True)
-    half = jnp.sum(projected.astype(F32), axis=0)
-    theirs = lax.dynamic_index_in_dim(half, 1 - zh, 0, keepdims=False).astype(BF16)
-    mine = lax.dynamic_index_in_dim(half, zh, 0, keepdims=False)
-    attended = mine + shift(theirs, "zh", 1).astype(F32)
+    mine = jnp.stack([zh]).astype(jnp.int32)
+    half = sum_along_x(project(1 - mine, ordered, near, far)).astype(BF16)
+    own = after(project(mine, ordered, near, far), half)
+    attended = sum_along_x(own) + shift(half, "zh", 1).astype(F32)
     state = resid.astype(F32) + attended
     scaled = (state * gain[None, :]).astype(BF16)
 
@@ -311,13 +316,12 @@
     arrived = lax.all_to_all(outgoing, CTX, 0, 0, tiled=True).reshape(4 * slots, lanes)
 
     units = w_gate_up.shape[3]
-    part = gate_up(arrived, w_gate_up.reshape(width, 2 * units), gain)
-    part = part.reshape(4, slots // 4, 2 * units + 128)
-    part = lax.all_to_all(part, "x", 0, 0, tiled=True)
-    part = jnp.sum(part.astype(F32), axis=0).reshape(2, slots // 8, 2 * units + 128)
-    theirs = lax.dynamic_index_in_dim(part, 1 - zh, 0, keepdims=False).astype(BF16)
-    mine = lax.dynamic_index_in_dim(part, zh, 0, keepdims=False)
-    part = mine + shift(theirs, "zh", 1).astype(F32)
+    order = swap_order()
+    weights = w_gate_up.reshape(width, 2 * units)
+    shape = (4, slots // 8, 2 * units + 128)
+    half = sum_along_x(gate_up(1 - mine, arrived, order, weights, gain).reshape(shape)).astype(BF16)
+    own = after(gate_up(mine, arrived, order, weights, gain).reshape(shape), half)
+    part = sum_along_x(own) + shift(half, "zh", 1).astype(F32)
     square = part[:, 2 * units : 2 * units + 1] + part[:, 2 * units + 1 : 2 * units + 2]
     inverse = lax.rsqrt(square / D + EPSILON)
     hidden = (jax.nn.silu(part[:, :units] * inverse) * (part[:, units : 2 * units] * inverse)).astype(
@@ -326,9 +330,9 @@
     other = shift(hidden, "zh", 1)
     hidden = jnp.where(
         zh == 0, jnp.stack([hidden, other], axis=0), jnp.stack([other, hidden], axis=0)
-    ).reshape(slots // 4, units)
-    hidden = lax.all_gather(hidden, "x", axis=0, tiled=True)
-    result = down(hidden, w_down[0]).reshape(ctx_count, 4 * MOST, lanes)
+    )
+    hidden = lax.all_gather(hidden, "x", axis=0).reshape(slots, units)
+    result = down(hidden, order, w_down[0]).reshape(ctx_count, 4 * MOST, lanes)
     returned = lax.all_to_all(result, CTX, 0, 0, tiled=True).reshape(4 * slots, lanes)
     routed = lax.dot_general(
         combine, returned, (((0,), (0,)), ((), ())), preferred_element_type=F32

time: 369 us -> 363 us (0.984)
  blocking collectives: 40 us -> 12.2 us
  starting transfers between devices: 125 us -> 139 us
  Pallas kernels: 25.2 us -> 29.6 us
    all_to_all x1 -> x0, blocking collectives: 27.9 us -> none  [body(): part = lax.all_to_all(part, 'x', 0, 0, tiled=True)]
    all_to_all x2 -> x5, starting transfers between devices: 7.25 us -> 19.1 us  [the longest x4 15.5 us: sum_along_x(): lax.all_to_all(parts, 'x', 0, 0, tiled=True).astype(F32)]
    all_to_all x2 -> x5, waiting for transfers between devices: 13.3 us -> 21.3 us  [the longest x4 21.3 us: sum_along_x(): lax.all_to_all(parts, 'x', 0, 0, tiled=True).astype(F32)]
    ppermute x3, waiting for transfers between devices: 13.1 us -> 5.33 us  [partner(): return lax.ppermute(value, axis, [(i, i ^ bit) for i in range(SIZES[axis])])]
    pallas_call x1 -> x2, Pallas kernels: 6.37 us -> 7.59 us  [project(): pl.pallas_call(project_kernel, out_shape=jax.ShapeDtypeStruct((4, tokens,...]
  transfers between devices with their start and end apart: 20 -> 23, of which waited for: 11 -> 13; matrix products, arithmetic and copies ran while one was open for 9% -> 8% of each run, Pallas kernels for 4% -> 5%
where the time goes in v4:
time: 363 us; the launch traced here: 361 us
  starting transfers between devices  139 us (38%)
  waiting for transfers between devices  132 us (36%)
  Pallas kernels  29.6 us (8%)
  other arithmetic  24.3 us (7%)
  blocking collectives  12.2 us (3%)
  matrix products  11.2 us (3%)
  local copies, waits for them, and re-layouts  10.9 us (3%)
    ppermute x11, starting transfers between devices, shift(): lax.ppermute(value, axis, [(i, (i + step) % count) for i in range(count)])  53.3 us
    ppermute x11, waiting for transfers between devices, shift(): lax.ppermute(value, axis, [(i, (i + step) % count) for i in range(count)])  33.1 us
    all_to_all x1, waiting for transfers between devices, body(): lax.all_to_all(outgoing, CTX, 0, 0, tiled=True).reshape(4 * slots, lanes)  32.8 us
    all_to_all x1, waiting for transfers between devices, body(): lax.all_to_all(result, CTX, 0, 0, tiled=True).reshape(4 * slots, lanes)  31.9 us
    all_to_all x4, waiting for transfers between devices, sum_along_x(): lax.all_to_all(parts, 'x', 0, 0, tiled=True).astype(F32)  21.3 us
    all_to_all x1, starting transfers between devices, body(): lax.all_to_all(result, CTX, 0, 0, tiled=True).reshape(4 * slots, lanes)  19.6 us
    all_to_all x1, starting transfers between devices, body(): lax.all_to_all(outgoing, CTX, 0, 0, tiled=True).reshape(4 * slots, lanes)  19.3 us
    all_to_all x4, starting transfers between devices, sum_along_x(): lax.all_to_all(parts, 'x', 0, 0, tiled=True).astype(F32)  15.5 us
  transfers between devices with their start and end apart: 23, of which 13 were waited for; matrix products, arithmetic and copies ran while one was open for 8% of the time, Pallas kernels for 5%

profile of v4, /device:TPU:1, one launch (start us, length us, event | category | flops | bytes accessed | tf_op | source)
XLA Modules:
  0.0 360.8 jit_solution(10224536425231987997)
XLA Ops:
  0.6 5.5 %collective-permute-start = (bf16[512,128]{1,0:T(8,128)(2,1)}, bf16[512,128]{1,0:T(8,128)(2,1)S(1)}, u32[]{:S(2)}, u32[]{:S(2)}) collective-permute-start(bf16[512,128]{1,0:T(8,128)(2,1)} %bitcast.63), channel_id=1, source_target_pairs={{0,2},{1,3},{2,0},{3,1},{4,6},{5,7},{6,4},{7,5},{8,10},{9,11},{10,... | collective-permute-start | bytes 393224 | tf_op jit(solution)/shard_map/ppermute | solution.py:26
  6.1 2.2 collective-permute-start.1
  8.4 4.3 %collective-permute-start.2 = (bf16[512,128]{1,0:T(8,128)(2,1)}, bf16[512,128]{1,0:T(8,128)(2,1)S(1)}, u32[]{:S(2)}, u32[]{:S(2)}) collective-permute-start(bf16[512,128]{1,0:T(8,128)(2,1)} %bitcast.65), channel_id=1, source_target_pairs={{0,3},{1,0},{2,1},{3,2},{4,7},{5,4},{6,5},{7,6},{8,11},{9,8},{10,9... | collective-permute-start | bytes 393224 | tf_op jit(solution)/shard_map/ppermute | solution.py:26
  14.2 12.2 %all-to-all-start = ((bf16[8,2,32,128]{3,2,1,0:T(8,128)(2,1)}), bf16[8,2,32,128]{3,2,1,0:T(8,128)(2,1)S(1)}, u32[]{:S(2)}, u32[]{:S(2)}) async-start(bf16[8,2,32,128]{3,2,1,0:T(8,128)(2,1)} %broadcast_in_dim.147), calls=%async_computation | async-start | bytes 262144 | tf_op jit(solution)/shard_map/all_to_all | solution.py:232
  27.4 7.3 %collective-permute-start.7 = (bf16[8,4096]{1,0:T(8,128)(2,1)S(1)}, bf16[8,4096]{1,0:T(8,128)(2,1)S(1)}, u32[]{:S(2)}, u32[]{:S(2)}) collective-permute-start(bf16[8,4096]{1,0:T(8,128)(2,1)S(1)} %reshape.172), channel_id=1, source_target_pairs={{0,64},{16,80},{32,96},{48,112},{64,0},{80,16},{96,32},{112,48},{1... | collective-permute-start | bytes 196616 | tf_op jit(solution)/shard_map/ppermute | solution.py:30
  37.0 3.1 fusion.9
  40.1 4.6 %collective-permute-done.7 = bf16[8,4096]{1,0:T(8,128)(2,1)S(1)} collective-permute-done((bf16[8,4096]{1,0:T(8,128)(2,1)S(1)}, bf16[8,4096]{1,0:T(8,128)(2,1)S(1)}, u32[]{:S(2)}, u32[]{:S(2)}) %collective-permute-start.7) | collective-permute-done | bytes 65568 | tf_op jit(solution)/shard_map/ppermute | solution.py:30
  44.7 1.9 collective-permute-start.8
  46.6 2.6 convert_select_fusion.3
  50.1 4.2 %all-to-all-start.1 = ((bf16[4,8,2,32,128]{4,3,1,2,0:T(8,128)(2,1)}), bf16[4,8,2,32,128]{4,3,1,2,0:T(8,128)(2,1)S(1)}, u32[]{:S(2)}, u32[]{:S(2)}) async-start(bf16[4,8,2,32,128]{4,3,1,2,0:T(8,128)(2,1)} %broadcast_in_dim.148), calls=%async_computation.1 | async-start | bytes 1048576 | tf_op jit(solution)/shard_map/all_to_all | solution.py:237
  54.4 8.0 %all-to-all-done.1 = bf16[4,8,2,32,128]{4,3,1,2,0:T(8,128)(2,1)S(1)} async-done(((bf16[4,8,2,32,128]{4,3,1,2,0:T(8,128)(2,1)}), bf16[4,8,2,32,128]{4,3,1,2,0:T(8,128)(2,1)S(1)}, u32[]{:S(2)}, u32[]{:S(2)}) %all-to-all-start.1) | async-done | bytes 524320 | tf_op jit(solution)/shard_map/all_to_all | solution.py:237
  64.3 4.3 %collective-permute-start.3 = (bf16[4,8,2,32,128]{4,3,1,2,0:T(8,128)(2,1)S(1)}, bf16[4,8,2,32,128]{4,3,1,2,0:T(8,128)(2,1)S(1)}, u32[]{:S(2)}, u32[]{:S(2)}) collective-permute-start(bf16[4,8,2,32,128]{4,3,1,2,0:T(8,128)(2,1)S(1)} %all-to-all-done.1), channel_id=1, source_target_pairs={{0,8},{8,0},{1,9},{9,1},{2,10},{10,2},{3,11},{11,3},{4,12},{12,4},... | collective-permute-start | bytes 1572872 | tf_op jit(solution)/shard_map/ppermute | solution.py:26
  70.2 3.4 attend.4
  75.2 3.6 all-to-all-start.2
  78.8 2.5 select_dynamic-update-slice_fusion.7
  82.4 1.9 collective-permute-start.4
  85.2 4.0 %attend.5 = bf16[144,512]{1,0:T(8,128)(2,1)} custom-call(s32[3]{0:T(128)S(1)} %pad_add_fusion.place, bf16[512,128]{1,0:T(8,128)(2,1)S(1)} %copy-done.3, bf16[2048,128]{1,0:T(8,128)(2,1)S(1)} %bitcast.56, bf16[2048,128]{1,0:T(8,128)(2,1)S(1)} %bitcast.52), custom_call_target="tpu_custom_call" | custom-call | tf_op jit(solution)/shard_map/attend/pallas_call | solution.py:201
  89.2 3.4 collective-permute-start.5
  92.6 4.0 %attend.6 = bf16[144,512]{1,0:T(8,128)(2,1)} custom-call(s32[3]{0:T(128)S(1)} %pad_add_fusion.place, bf16[512,128]{1,0:T(8,128)(2,1)S(1)} %collective-permute-done.2.q_ref, bf16[2048,128]{1,0:T(8,128)(2,1)S(1)} %bitcast.57, bf16[2048,128]{1,0:T(8,128)(2,1)S(1)} %bitcast.53), custom_call_target="tpu_custom_call" | custom-call | tf_op jit(solution)/shard_map/attend/pallas_call | solution.py:201
  99.4 3.4 attend.7
  104.2 6.4 %collective-permute-start.10 = (bf16[256,4096]{1,0:T(8,128)(2,1)S(1)}, bf16[256,4096]{1,0:T(8,128)(2,1)}, u32[]{:S(2)}, u32[]{:S(2)}) collective-permute-start(bf16[256,4096]{1,0:T(8,128)(2,1)S(1)} %bitcast.46), channel_id=1, source_target_pairs={{0,8},{8,0},{1,9},{9,1},{2,10},{10,2},{3,11},{11,3},{4,12},{12,4},... | collective-permute-start | bytes 6291464 | tf_op jit(solution)/shard_map/ppermute | solution.py:26
  110.5 2.0 select_dynamic-update-slice_fusion.5
  116.1 3.8 %project.3 = bf16[4,128,512]{2,1,0:T(8,128)(2,1)} custom-call(s32[1]{0:T(128)S(6)} %sub.121.side, bf16[128,512]{1,0:T(8,128)(2,1)S(1)} %convolution_convert_fusion.1.c_ref, bf16[256,4096]{1,0:T(8,128)(2,1)S(1)} %bitcast.47, bf16[256,4096]{1,0:T(8,128)(2,1)} %collective-permute-done.10.far_ref), custom_call_target="tpu_custom_call" | custom-call | tf_op jit(solution)/shard_map/project/pallas_call | solution.py:64
  119.9 4.3 %all-to-all-start.3 = ((bf16[4,128,512]{2,1,0:T(8,128)(2,1)}), bf16[4,128,512]{2,1,0:T(8,128)(2,1)}, u32[]{:S(2)}, u32[]{:S(2)}) async-start(bf16[4,128,512]{2,1,0:T(8,128)(2,1)} %project.3), calls=%async_computation.3 | async-start | bytes 1048576 | tf_op jit(solution)/shard_map/all_to_all | solution.py:83
  125.1 3.8 %project.2 = bf16[4,128,512]{2,1,0:T(8,128)(2,1)} custom-call(s32[1]{0:T(128)} %bitcast.18.side, bf16[128,512]{1,0:T(8,128)(2,1)S(1)} %convolution_convert_fusion.1.c_ref, bf16[256,4096]{1,0:T(8,128)(2,1)S(1)} %bitcast.48, bf16[256,4096]{1,0:T(8,128)(2,1)} %collective-permute-done.10.far_ref), custom_call_target="tpu_custom_call" | custom-call | tf_op jit(solution)/shard_map/project/pallas_call | solution.py:64
  128.9 4.9 %all-to-all-done.3 = bf16[4,128,512]{2,1,0:T(8,128)(2,1)} async-done(((bf16[4,128,512]{2,1,0:T(8,128)(2,1)}), bf16[4,128,512]{2,1,0:T(8,128)(2,1)}, u32[]{:S(2)}, u32[]{:S(2)}) %all-to-all-start.3) | async-done | bytes 524320 | tf_op jit(solution)/shard_map/all_to_all | solution.py:83
  135.0 3.5 all-to-all-start.4
  138.5 3.0 convert_select_fusion.2
  142.3 8.1 %collective-permute-start.11 = (bf16[128,512]{0,1:T(8,128)(2,1)}, bf16[128,512]{0,1:T(8,128)(2,1)S(1)}, u32[]{:S(2)}, u32[]{:S(2)}) collective-permute-start(bf16[128,512]{0,1:T(8,128)(2,1)} %copy.49), channel_id=1, source_target_pairs={{0,4},{4,0},{1,5},{5,1},{2,6},{6,2},{3,7},{7,3},{8,12},{12,8},{9,1... | collective-permute-start | bytes 393224 | tf_op jit(solution)/shard_map/ppermute | solution.py:26
  150.7 6.9 %collective-permute-done.11 = bf16[128,512]{0,1:T(8,128)(2,1)S(1)} collective-permute-done((bf16[128,512]{0,1:T(8,128)(2,1)}, bf16[128,512]{0,1:T(8,128)(2,1)S(1)}, u32[]{:S(2)}, u32[]{:S(2)}) %collective-permute-start.11) | collective-permute-done | bytes 131104 | tf_op jit(solution)/shard_map/ppermute | solution.py:26
  157.8 3.0 convolution_convert_fusion
  160.8 19.3 %all-to-all-start.5 = ((bf16[64,40,128]{2,1,0:T(8,128)(2,1)}), bf16[64,40,128]{2,1,0:T(8,128)(2,1)S(1)}, u32[]{:S(2)}, u32[]{:S(2)}) async-start(bf16[64,40,128]{2,1,0:T(8,128)(2,1)} %bitcast.22), calls=%async_computation.5 | async-start | bytes 1310720 | tf_op jit(solution)/shard_map/all_to_all | solution.py:316
  182.2 32.8 %all-to-all-done.5 = bf16[64,40,128]{2,1,0:T(8,128)(2,1)S(1)} async-done(((bf16[64,40,128]{2,1,0:T(8,128)(2,1)}), bf16[64,40,128]{2,1,0:T(8,128)(2,1)S(1)}, u32[]{:S(2)}, u32[]{:S(2)}) %all-to-all-start.5) | async-done | bytes 655392 | tf_op jit(solution)/shard_map/all_to_all | solution.py:316
  214.9 2.5 gate_up.3
  217.4 4.2 %all-to-all-start.6 = ((bf16[4,80,1664]{2,1,0:T(8,128)(2,1)}), bf16[4,80,1664]{2,1,0:T(8,128)(2,1)}, u32[]{:S(2)}, u32[]{:S(2)}) async-start(bf16[4,80,1664]{2,1,0:T(8,128)(2,1)} %bitcast.26), calls=%async_computation.6 | async-start | bytes 2129920 | tf_op jit(solution)/shard_map/all_to_all | solution.py:83
  221.7 2.4 gate_up.2
  224.1 11.3 %all-to-all-done.6 = bf16[4,80,1664]{2,1,0:T(8,128)(2,1)} async-done(((bf16[4,80,1664]{2,1,0:T(8,128)(2,1)}), bf16[4,80,1664]{2,1,0:T(8,128)(2,1)}, u32[]{:S(2)}, u32[]{:S(2)}) %all-to-all-start.6) | async-done | bytes 1064992 | tf_op jit(solution)/shard_map/all_to_all | solution.py:83
  236.8 3.5 all-to-all-start.7
  240.4 7.3 %collective-permute-start.12 = (bf16[80,1664]{1,0:T(8,128)(2,1)S(1)}, bf16[80,1664]{1,0:T(8,128)(2,1)}, u32[]{:S(2)}, u32[]{:S(2)}) collective-permute-start(bf16[80,1664]{1,0:T(8,128)(2,1)S(1)} %reduce_sum.74), channel_id=1, source_target_pairs={{0,4},{4,0},{1,5},{5,1},{2,6},{6,2},{3,7},{7,3},{8,12},{12,8},{9,1... | collective-permute-start | bytes 798728 | tf_op jit(solution)/shard_map/ppermute | solution.py:26
  247.7 5.1 %all-to-all-done.7 = bf16[4,80,1664]{2,1,0:T(8,128)(2,1)S(1)} async-done(((bf16[4,80,1664]{2,1,0:T(8,128)(2,1)}), bf16[4,80,1664]{2,1,0:T(8,128)(2,1)S(1)}, u32[]{:S(2)}, u32[]{:S(2)}) %all-to-all-start.7) | async-done | bytes 1064992 | tf_op jit(solution)/shard_map/all_to_all | solution.py:83
  252.9 18.0 %collective-permute-done.12 = bf16[80,1664]{1,0:T(8,128)(2,1)} collective-permute-done((bf16[80,1664]{1,0:T(8,128)(2,1)S(1)}, bf16[80,1664]{1,0:T(8,128)(2,1)}, u32[]{:S(2)}, u32[]{:S(2)}) %collective-permute-start.12) | collective-permute-done | bytes 266272 | tf_op jit(solution)/shard_map/ppermute | solution.py:26
  272.2 8.0 %collective-permute-start.13 = (bf16[80,768]{1,0:T(8,128)(2,1)S(1)}, bf16[80,768]{1,0:T(8,128)(2,1)S(1)}, u32[]{:S(2)}, u32[]{:S(2)}) collective-permute-start(bf16[80,768]{1,0:T(8,128)(2,1)S(1)} %fusion.62), channel_id=1, source_target_pairs={{0,4},{4,0},{1,5},{5,1},{2,6},{6,2},{3,7},{7,3},{8,12},{12,8},{9,1... | collective-permute-start | bytes 368648 | tf_op jit(solution)/shard_map/ppermute | solution.py:26
  280.4 6.2 %collective-permute-done.13 = bf16[80,768]{1,0:T(8,128)(2,1)S(1)} collective-permute-done((bf16[80,768]{1,0:T(8,128)(2,1)S(1)}, bf16[80,768]{1,0:T(8,128)(2,1)S(1)}, u32[]{:S(2)}, u32[]{:S(2)}) %collective-permute-start.13) | collective-permute-done | bytes 122912 | tf_op jit(solution)/shard_map/ppermute | solution.py:26
  286.6 12.2 %all_gather.4 = bf16[4,2,80,768]{3,2,1,0:T(8,128)(2,1)S(1)} all-gather(bf16[1,2,80,768]{3,2,1,0:T(8,128)(2,1)S(1)} %maximum_select_fusion), channel_id=1, replica_groups=mesh['y'=4,'zl'=8,'core'=2,'zh'=2,'x'=4] {'x'}, dimensions={0}, use_global_device_ids=true | all-gather | bytes 1228800 | tf_op jit(solution)/shard_map/all_gather | solution.py:334
  298.8 2.3 down.1
  301.2 19.6 %all-to-all-start.8 = ((bf16[64,40,128]{2,1,0:T(8,128)(2,1)}), bf16[64,40,128]{2,1,0:T(8,128)(2,1)S(1)}, u32[]{:S(2)}, u32[]{:S(2)}) async-start(bf16[64,40,128]{2,1,0:T(8,128)(2,1)} %bitcast.31), calls=%async_computation.8 | async-start | bytes 1310720 | tf_op jit(solution)/shard_map/all_to_all | solution.py:336
  323.7 31.9 %all-to-all-done.8 = bf16[64,40,128]{2,1,0:T(8,128)(2,1)S(1)} async-done(((bf16[64,40,128]{2,1,0:T(8,128)(2,1)}), bf16[64,40,128]{2,1,0:T(8,128)(2,1)S(1)}, u32[]{:S(2)}, u32[]{:S(2)}) %all-to-all-start.8) | async-done | bytes 655392 | tf_op jit(solution)/shard_map/all_to_all | solution.py:336
  355.6 4.3 %fusion.138 = f32[1024,128]{0,1:T(8,128)S(1)} fusion(bf16[2560,1024]{0,1:T(8,128)(2,1)} %select_dynamic-update-slice_fusion, bf16[2560,128]{1,0:T(8,128)(2,1)S(1)} %bitcast.69), kind=kOutput, calls=%fused_computation.264 | convolution fusion | flops 671088640 | bytes 6422528 | tf_op jit(solution)/shard_map/dot_general | solution.py:337
  (96 shorter events, 32.5 us)
Async XLA Ops:
  0.6 48.6 %collective-permute-start = (bf16[512,128]{1,0:T(8,128)(2,1)}, bf16[512,128]{1,0:T(8,128)(2,1)S(1)}, u32[]{:S(2)}, u32[]{:S(2)}) collective-permute-start(bf16[512,128]{1,0:T(8,128)(2,1)} %bitcast.63), channel_id=1, source_target_pairs={{0,2},{1,3},{2,0},{3,1},{4,6},{5,7},{6,4},{7,5},{8,10},{9,11},{10,... | collective-permute-start | bytes 393224 | tf_op jit(solution)/shard_map/ppermute | solution.py:26
  6.1 43.1 %collective-permute-start.1 = (bf16[512,128]{1,0:T(8,128)(2,1)}, bf16[512,128]{1,0:T(8,128)(2,1)S(1)}, u32[]{:S(2)}, u32[]{:S(2)}) collective-permute-start(bf16[512,128]{1,0:T(8,128)(2,1)} %bitcast.64), channel_id=1, source_target_pairs={{0,1},{1,2},{2,3},{3,0},{4,5},{5,6},{6,7},{7,4},{8,9},{9,10},{10,1... | collective-permute-start | bytes 393224 | tf_op jit(solution)/shard_map/ppermute | solution.py:26
  8.4 40.9 %collective-permute-start.2 = (bf16[512,128]{1,0:T(8,128)(2,1)}, bf16[512,128]{1,0:T(8,128)(2,1)S(1)}, u32[]{:S(2)}, u32[]{:S(2)}) collective-permute-start(bf16[512,128]{1,0:T(8,128)(2,1)} %bitcast.65), channel_id=1, source_target_pairs={{0,3},{1,0},{2,1},{3,2},{4,7},{5,4},{6,5},{7,6},{8,11},{9,8},{10,9... | collective-permute-start | bytes 393224 | tf_op jit(solution)/shard_map/ppermute | solution.py:26
  14.2 30.5 %all-to-all-start = ((bf16[8,2,32,128]{3,2,1,0:T(8,128)(2,1)}), bf16[8,2,32,128]{3,2,1,0:T(8,128)(2,1)S(1)}, u32[]{:S(2)}, u32[]{:S(2)}) async-start(bf16[8,2,32,128]{3,2,1,0:T(8,128)(2,1)} %broadcast_in_dim.147), calls=%async_computation | async-start | bytes 262144 | tf_op jit(solution)/shard_map/all_to_all | solution.py:232
  27.4 17.3 %collective-permute-start.7 = (bf16[8,4096]{1,0:T(8,128)(2,1)S(1)}, bf16[8,4096]{1,0:T(8,128)(2,1)S(1)}, u32[]{:S(2)}, u32[]{:S(2)}) collective-permute-start(bf16[8,4096]{1,0:T(8,128)(2,1)S(1)} %reshape.172), channel_id=1, source_target_pairs={{0,64},{16,80},{32,96},{48,112},{64,0},{80,16},{96,32},{112,48},{1... | collective-permute-start | bytes 196616 | tf_op jit(solution)/shard_map/ppermute | solution.py:30
  44.7 9.6 %collective-permute-start.8 = (bf16[16,4096]{1,0:T(8,128)(2,1)S(1)}, bf16[16,4096]{1,0:T(8,128)(2,1)S(1)}, u32[]{:S(2)}, u32[]{:S(2)}) collective-permute-start(bf16[16,4096]{1,0:T(8,128)(2,1)S(1)} %pad_maximum_fusion.3), channel_id=1, source_target_pairs={{0,32},{16,48},{32,0},{48,16},{64,96},{80,112},{96,64},{112,80},{1... | collective-permute-start | bytes 393224 | tf_op jit(solution)/shard_map/ppermute | solution.py:30
  49.2 26.0 %copy-start.2 = (bf16[512,128]{1,0:T(8,128)(2,1)}, bf16[512,128]{1,0:T(8,128)(2,1)S(1)}, u32[]{:S(2)}) copy-start(bf16[512,128]{1,0:T(8,128)(2,1)S(1)} %collective-permute-done.1.q_ref) | copy-start | bytes 393220
  50.1 12.2 %all-to-all-start.1 = ((bf16[4,8,2,32,128]{4,3,1,2,0:T(8,128)(2,1)}), bf16[4,8,2,32,128]{4,3,1,2,0:T(8,128)(2,1)S(1)}, u32[]{:S(2)}, u32[]{:S(2)}) async-start(bf16[4,8,2,32,128]{4,3,1,2,0:T(8,128)(2,1)} %broadcast_in_dim.148), calls=%async_computation.1 | async-start | bytes 1048576 | tf_op jit(solution)/shard_map/all_to_all | solution.py:237
  62.3 7.1 %collective-permute-start.9 = (bf16[32,4096]{1,0:T(8,128)(2,1)S(1)}, bf16[32,4096]{1,0:T(8,128)(2,1)S(1)}, u32[]{:S(2)}, u32[]{:S(2)}) collective-permute-start(bf16[32,4096]{1,0:T(8,128)(2,1)S(1)} %pad_maximum_fusion.2), channel_id=1, source_target_pairs={{0,16},{16,0},{32,48},{48,32},{64,80},{80,64},{96,112},{112,96},{1... | collective-permute-start | bytes 786440 | tf_op jit(solution)/shard_map/ppermute | solution.py:30
  64.3 5.9 %collective-permute-start.3 = (bf16[4,8,2,32,128]{4,3,1,2,0:T(8,128)(2,1)S(1)}, bf16[4,8,2,32,128]{4,3,1,2,0:T(8,128)(2,1)S(1)}, u32[]{:S(2)}, u32[]{:S(2)}) collective-permute-start(bf16[4,8,2,32,128]{4,3,1,2,0:T(8,128)(2,1)S(1)} %all-to-all-done.1), channel_id=1, source_target_pairs={{0,8},{8,0},{1,9},{9,1},{2,10},{10,2},{3,11},{11,3},{4,12},{12,4},... | collective-permute-start | bytes 1572872 | tf_op jit(solution)/shard_map/ppermute | solution.py:26
  75.2 29.0 %all-to-all-start.2 = ((bf16[4,64,4096]{2,1,0:T(8,128)(2,1)}), bf16[4,64,4096]{2,1,0:T(8,128)(2,1)S(1)}, u32[]{:S(2)}, u32[]{:S(2)}) async-start(bf16[4,64,4096]{2,1,0:T(8,128)(2,1)} %broadcast_in_dim.151), calls=%async_computation.2 | async-start | bytes 4194304 | tf_op jit(solution)/shard_map/all_to_all | solution.py:253
  81.3 1.1 copy-start.5
  82.4 21.8 %collective-permute-start.4 = (bf16[144,512]{1,0:T(8,128)(2,1)S(1)}, bf16[144,512]{1,0:T(8,128)(2,1)}, u32[]{:S(2)}, u32[]{:S(2)}) collective-permute-start(bf16[144,512]{1,0:T(8,128)(2,1)S(1)} %attend.4), channel_id=1, source_target_pairs={{0,2},{1,3},{2,0},{3,1},{4,6},{5,7},{6,4},{7,5},{8,10},{9,11},{10,... | collective-permute-start | bytes 442376 | tf_op jit(solution)/shard_map/ppermute | solution.py:26
  84.3 0.9 copy-start.3
  89.2 15.0 %collective-permute-start.5 = (bf16[144,512]{1,0:T(8,128)(2,1)}, bf16[144,512]{1,0:T(8,128)(2,1)}, u32[]{:S(2)}, u32[]{:S(2)}) collective-permute-start(bf16[144,512]{1,0:T(8,128)(2,1)} %attend.5), channel_id=1, source_target_pairs={{0,3},{1,0},{2,1},{3,2},{4,7},{5,4},{6,5},{7,6},{8,11},{9,8},{10,9... | collective-permute-start | bytes 442376 | tf_op jit(solution)/shard_map/ppermute | solution.py:26
  96.6 7.6 %collective-permute-start.6 = (bf16[144,512]{1,0:T(8,128)(2,1)}, bf16[144,512]{1,0:T(8,128)(2,1)}, u32[]{:S(2)}, u32[]{:S(2)}) collective-permute-start(bf16[144,512]{1,0:T(8,128)(2,1)} %attend.6), channel_id=1, source_target_pairs={{0,1},{1,2},{2,3},{3,0},{4,5},{5,6},{6,7},{7,4},{8,9},{9,10},{10,1... | collective-permute-start | bytes 442376 | tf_op jit(solution)/shard_map/ppermute | solution.py:26
  98.5 0.9 copy-start.1
  104.2 11.9 %collective-permute-start.10 = (bf16[256,4096]{1,0:T(8,128)(2,1)S(1)}, bf16[256,4096]{1,0:T(8,128)(2,1)}, u32[]{:S(2)}, u32[]{:S(2)}) collective-permute-start(bf16[256,4096]{1,0:T(8,128)(2,1)S(1)} %bitcast.46), channel_id=1, source_target_pairs={{0,8},{8,0},{1,9},{9,1},{2,10},{10,2},{3,11},{11,3},{4,12},{12,4},... | collective-permute-start | bytes 6291464 | tf_op jit(solution)/shard_map/ppermute | solution.py:26
  114.8 0.7 copy-start.9
  116.0 8.1 %copy-start.6 = (bf16[2560,128]{0,1:T(8,128)(2,1)S(1)}, bf16[2560,128]{0,1:T(8,128)(2,1)}, u32[]{:S(2)}) copy-start(bf16[2560,128]{0,1:T(8,128)(2,1)} %copy-done.5) | copy-start | bytes 1966084
  119.9 18.6 %copy-start.7 = (pred[2560,128]{0,1:T(8,128)(4,1)S(1)}, pred[2560,128]{0,1:T(8,128)(4,1)}, u32[]{:S(2)}) copy-start(pred[2560,128]{0,1:T(8,128)(4,1)} %get-tuple-element.37) | copy-start | bytes 983044
  119.9 14.0 %all-to-all-start.3 = ((bf16[4,128,512]{2,1,0:T(8,128)(2,1)}), bf16[4,128,512]{2,1,0:T(8,128)(2,1)}, u32[]{:S(2)}, u32[]{:S(2)}) async-start(bf16[4,128,512]{2,1,0:T(8,128)(2,1)} %project.3), calls=%async_computation.3 | async-start | bytes 1048576 | tf_op jit(solution)/shard_map/all_to_all | solution.py:83
  125.1 16.3 %copy-start.10 = (bf16[128,512]{1,0:T(8,128)(2,1)S(1)}, bf16[128,512]{1,0:T(8,128)(2,1)}, u32[]{:S(2)}) copy-start(bf16[128,512]{1,0:T(8,128)(2,1)} %param.13) | copy-start | bytes 393220
  125.1 32.4 %copy-start.4 = (f32[512]{0:T(512)S(1)}, f32[512]{0:T(512)}, u32[]{:S(2)}) copy-start(f32[512]{0:T(512)} %param.14) | copy-start | bytes 6148
  128.9 28.8 %copy-start.8 = (bf16[2560,128]{0,1:T(8,128)(2,1)S(1)}, bf16[2560,128]{0,1:T(8,128)(2,1)}, u32[]{:S(2)}) copy-start(bf16[2560,128]{0,1:T(8,128)(2,1)} %get-tuple-element.36) | copy-start | bytes 1966084
  135.0 15.5 %all-to-all-start.4 = ((bf16[4,128,512]{2,1,0:T(8,128)(2,1)}), bf16[4,128,512]{2,1,0:T(8,128)(2,1)S(1)}, u32[]{:S(2)}, u32[]{:S(2)}) async-start(bf16[4,128,512]{2,1,0:T(8,128)(2,1)} %project.2), calls=%async_computation.4 | async-start | bytes 1048576 | tf_op jit(solution)/shard_map/all_to_all | solution.py:83
  142.3 15.2 %collective-permute-start.11 = (bf16[128,512]{0,1:T(8,128)(2,1)}, bf16[128,512]{0,1:T(8,128)(2,1)S(1)}, u32[]{:S(2)}, u32[]{:S(2)}) collective-permute-start(bf16[128,512]{0,1:T(8,128)(2,1)} %copy.49), channel_id=1, source_target_pairs={{0,4},{4,0},{1,5},{5,1},{2,6},{6,2},{3,7},{7,3},{8,12},{12,8},{9,1... | collective-permute-start | bytes 393224 | tf_op jit(solution)/shard_map/ppermute | solution.py:26
  160.8 54.1 %all-to-all-start.5 = ((bf16[64,40,128]{2,1,0:T(8,128)(2,1)}), bf16[64,40,128]{2,1,0:T(8,128)(2,1)S(1)}, u32[]{:S(2)}, u32[]{:S(2)}) async-start(bf16[64,40,128]{2,1,0:T(8,128)(2,1)} %bitcast.22), calls=%async_computation.5 | async-start | bytes 1310720 | tf_op jit(solution)/shard_map/all_to_all | solution.py:316
  217.4 18.0 %all-to-all-start.6 = ((bf16[4,80,1664]{2,1,0:T(8,128)(2,1)}), bf16[4,80,1664]{2,1,0:T(8,128)(2,1)}, u32[]{:S(2)}, u32[]{:S(2)}) async-start(bf16[4,80,1664]{2,1,0:T(8,128)(2,1)} %bitcast.26), calls=%async_computation.6 | async-start | bytes 2129920 | tf_op jit(solution)/shard_map/all_to_all | solution.py:83
  224.1 74.7 %copy-start = (bf16[1,768,512]{2,1,0:T(8,128)(2,1)S(1)}, bf16[1,768,512]{2,1,0:T(8,128)(2,1)}, u32[]{:S(2)}) copy-start(bf16[1,768,512]{2,1,0:T(8,128)(2,1)} %param.18) | copy-start | bytes 2359300
  236.8 15.9 %all-to-all-start.7 = ((bf16[4,80,1664]{2,1,0:T(8,128)(2,1)}), bf16[4,80,1664]{2,1,0:T(8,128)(2,1)S(1)}, u32[]{:S(2)}, u32[]{:S(2)}) async-start(bf16[4,80,1664]{2,1,0:T(8,128)(2,1)} %bitcast.25), calls=%async_computation.7 | async-start | bytes 2129920 | tf_op jit(solution)/shard_map/all_to_all | solution.py:83
  240.4 30.5 %collective-permute-start.12 = (bf16[80,1664]{1,0:T(8,128)(2,1)S(1)}, bf16[80,1664]{1,0:T(8,128)(2,1)}, u32[]{:S(2)}, u32[]{:S(2)}) collective-permute-start(bf16[80,1664]{1,0:T(8,128)(2,1)S(1)} %reduce_sum.74), channel_id=1, source_target_pairs={{0,4},{4,0},{1,5},{5,1},{2,6},{6,2},{3,7},{7,3},{8,12},{12,8},{9,1... | collective-permute-start | bytes 798728 | tf_op jit(solution)/shard_map/ppermute | solution.py:26
  272.2 14.3 %collective-permute-start.13 = (bf16[80,768]{1,0:T(8,128)(2,1)S(1)}, bf16[80,768]{1,0:T(8,128)(2,1)S(1)}, u32[]{:S(2)}, u32[]{:S(2)}) collective-permute-start(bf16[80,768]{1,0:T(8,128)(2,1)S(1)} %fusion.62), channel_id=1, source_target_pairs={{0,4},{4,0},{1,5},{5,1},{2,6},{6,2},{3,7},{7,3},{8,12},{12,8},{9,1... | collective-permute-start | bytes 368648 | tf_op jit(solution)/shard_map/ppermute | solution.py:26
  301.2 54.4 %all-to-all-start.8 = ((bf16[64,40,128]{2,1,0:T(8,128)(2,1)}), bf16[64,40,128]{2,1,0:T(8,128)(2,1)S(1)}, u32[]{:S(2)}, u32[]{:S(2)}) async-start(bf16[64,40,128]{2,1,0:T(8,128)(2,1)} %bitcast.31), calls=%async_computation.8 | async-start | bytes 1310720 | tf_op jit(solution)/shard_map/all_to_all | solution.py:336

commit v5 on v4

--- a/solution.py
+++ b/solution.py
@@ -131,7 +131,7 @@
     )(side, arrived, order, weights, gain[None, :])
 
 
-def down_kernel(h_ref, order_ref, w_ref, o_ref):
+def down_kernel(h_ref, order_ref, w_ref, o_ref, *, by_x):
     step = order_ref.shape[0]
     quarter = step // 4
     lanes = o_ref.shape[1]
@@ -140,7 +140,7 @@
             h_ref[a * step : (a + 1) * step, :], w_ref[...], preferred_element_type=F32
         )
         for e in range(4):
-            b = e // 2 * 8 + a * 2 + e % 2
+            b = e // 2 * 8 + a * 2 + e % 2 if by_x else a * 4 + e
             piece = found[e * quarter : (e + 1) * quarter]
             piece = jnp.concatenate(
                 [piece[:, c * lanes : (c + 1) * lanes] for c in range(4)], axis=0
@@ -150,14 +150,44 @@
             ).astype(BF16)
 
 
-def down(hidden, order, weights):
+def down(hidden, order, weights, by_x, name):
     lanes = weights.shape[1] // 4
     return pl.pallas_call(
-        down_kernel,
+        functools.partial(down_kernel, by_x=by_x),
         out_shape=jax.ShapeDtypeStruct((hidden.shape[0] * 4, lanes), BF16),
         compiler_params=pltpu.CompilerParams(vmem_limit_bytes=48 << 20),
-        name="down",
+        name=name,
     )(hidden, order, weights)
+
+
+def combine_kernel(x_ref, order_ref, w_ref, state_ref, o_ref, rows_ref):
+    step = order_ref.shape[0]
+    quarter = step // 4
+    lanes = x_ref.shape[1]
+    for b in range(x_ref.shape[0] // step):
+        moved = jnp.dot(
+            order_ref[...], x_ref[b * step : (b + 1) * step, :], preferred_element_type=F32
+        ).astype(BF16)
+        for c in range(4):
+            rows_ref[b * quarter : (b + 1) * quarter, c * lanes : (c + 1) * lanes] = moved[
+                c * quarter : (c + 1) * quarter
+            ]
+    routed = lax.dot_general(
+        w_ref[...], rows_ref[...], (((0,), (0,)), ((), ())), preferred_element_type=F32
+    )
+    tokens = state_ref.shape[0]
+    o_ref[...] = (state_ref[...] + routed[:tokens] + routed[tokens:]).astype(BF16)
+
+
+def combine(returned, order, weights, state):
+    slots = weights.shape[0]
+    return pl.pallas_call(
+        combine_kernel,
+        out_shape=jax.ShapeDtypeStruct(state.shape, BF16),
+        scratch_shapes=[pltpu.VMEM((slots, state.shape[1]), BF16)],
+        compiler_params=pltpu.CompilerParams(vmem_limit_bytes=48 << 20),
+        name="combine",
+    )(returned, order, weights, state)
 
 
 def attend_kernel(place, q_ref, k_ref, v_ref, o_ref, *, heads, piece, tokens):
@@ -278,7 +308,7 @@
     scaled = (state * gain[None, :]).astype(BF16)
 
     slots = ctx_count * MOST
-    ids = expert_ids.T
+    ids = after(expert_ids, ordered).T
     expert = jnp.arange(ctx_count, dtype=jnp.int32)
     named = (ids[:, None, :] == expert[None, :, None]).astype(F32)
     weight = (gate_scores / jnp.sum(gate_scores, axis=1, keepdims=True)).T
@@ -287,36 +317,23 @@
     token = jnp.arange(tokens, dtype=jnp.int32)
     before = (token[:, None] < token[None, :]).astype(BF16)
     rank = jnp.dot(named, before, preferred_element_type=F32)
-    line = jnp.arange(4 * slots, dtype=jnp.int32)
-    spread = (line[:, None] // (4 * MOST) == expert[None, :]).astype(BF16)
+    line = jnp.arange(slots, dtype=jnp.int32)
+    spread = (line[:, None] // MOST == expert[None, :]).astype(BF16)
     weight_high = weight.astype(BF16)
     weight_low = (weight - weight_high.astype(F32)).astype(BF16)
     rank = jnp.where(named > 0, rank, -1.0).astype(BF16)
     tables = jnp.concatenate([rank, weight_high, weight_low], axis=1)
     tables = jnp.dot(spread, tables, preferred_element_type=F32)
     live = tables[:, :tokens] == (line % MOST).astype(F32)[:, None]
-    chunk = line // MOST % 4
-
-    def by_chunk(table):
-        table = table.astype(BF16)
-        zero = jnp.zeros((), BF16)
-        return [jnp.where((chunk == c)[:, None], table, zero) for c in range(4)]
-
-    dispatch = jnp.concatenate(by_chunk(live), axis=1)
-    combine = jnp.concatenate(
-        by_chunk(jnp.where(live, tables[:, tokens : 2 * tokens], 0.0))
-        + by_chunk(jnp.where(live, tables[:, 2 * tokens :], 0.0)),
-        axis=1,
-    )
+    mixing = jnp.where(jnp.concatenate([live, live], axis=1), tables[:, tokens:], 0.0).astype(BF16)
 
     lanes = width // 4
-    stacked = jnp.concatenate([scaled[:, c * lanes : (c + 1) * lanes] for c in range(4)], axis=0)
-    outgoing = jnp.dot(dispatch, stacked, preferred_element_type=F32).astype(BF16)
+    order = swap_order()
+    outgoing = down(live.astype(BF16), order, scaled, False, "dispatch")
     outgoing = outgoing.reshape(ctx_count, 4 * MOST, lanes)
     arrived = lax.all_to_all(outgoing, CTX, 0, 0, tiled=True).reshape(4 * slots, lanes)
 
     units = w_gate_up.shape[3]
-    order = swap_order()
     weights = w_gate_up.reshape(width, 2 * units)
     shape = (4, slots // 8, 2 * units + 128)
     half = sum_along_x(gate_up(1 - mine, arrived, order, weights, gain).reshape(shape)).astype(BF16)
@@ -332,14 +349,9 @@
         zh == 0, jnp.stack([hidden, other], axis=0), jnp.stack([other, hidden], axis=0)
     )
     hidden = lax.all_gather(hidden, "x", axis=0).reshape(slots, units)
-    result = down(hidden, order, w_down[0]).reshape(ctx_count, 4 * MOST, lanes)
+    result = down(hidden, order, w_down[0], True, "down").reshape(ctx_count, 4 * MOST, lanes)
     returned = lax.all_to_all(result, CTX, 0, 0, tiled=True).reshape(4 * slots, lanes)
-    routed = lax.dot_general(
-        combine, returned, (((0,), (0,)), ((), ())), preferred_element_type=F32
-    )
-    routed = routed[: 4 * tokens] + routed[4 * tokens :]
-    routed = jnp.concatenate([routed[c * tokens : (c + 1) * tokens] for c in range(4)], axis=1)
-    mixed = (state + routed).astype(BF16)
+    mixed = combine(returned, order, mixing, state)
     return (context, mixed)
 
 

time: 363 us -> 333 us (0.917)
  other arithmetic: 24.3 us -> 6.37 us
  waiting for transfers between devices: 132 us -> 117 us
  starting transfers between devices: 139 us -> 153 us
  matrix products: 11.2 us -> 1.12 us
    ppermute x11, starting transfers between devices: 53.3 us -> 64.4 us  [shift(): lax.ppermute(value, axis, [(i, (i + step) % count) for i in range(count)])]
    ppermute x11, waiting for transfers between devices: 33.1 us -> 22.2 us  [shift(): lax.ppermute(value, axis, [(i, (i + step) % count) for i in range(count)])]
    unnamed x6 -> x0, other arithmetic: 8.52 us -> none
    dot_general x2 -> x0, matrix products: 7.36 us -> none  [the longest x1 4.33 us: body(): lax.dot_general(combine, returned, (((0,), (0,)), ((), ())), preferred_el...]
    all_to_all x1, starting transfers between devices: 12.2 us -> 5.62 us  [body(): pair = first = lax.all_to_all(pair, 'zl', 0, 0, tiled=True)]
    ppermute x3, starting transfers between devices: 11.1 us -> 17 us  [partner(): return lax.ppermute(value, axis, [(i, i ^ bit) for i in range(SIZES[axis])])]
    select_n x3 -> x1, other arithmetic: 5.53 us -> 0.01 us  [body(): spread = (line[:, None] // MOST == expert[None, :]).astype(BF16)]
    ppermute x3, waiting for transfers between devices: 5.33 us -> 0.01 us  [partner(): return lax.ppermute(value, axis, [(i, i ^ bit) for i in range(SIZES[axis])])]
  transfers between devices with their start and end apart: 23 -> 23, of which waited for: 13 -> 13; matrix products, arithmetic and copies ran while one was open for 8% -> 3% of each run, Pallas kernels for 5% -> 5%
where the time goes in v5:
time: 333 us; the launch traced here: 330 us
  starting transfers between devices  153 us (46%)
  waiting for transfers between devices  117 us (35%)
  Pallas kernels  32.7 us (10%)
  blocking collectives  10.8 us (3%)
  local copies, waits for them, and re-layouts  8.68 us (3%)
  other arithmetic  6.37 us (2%)
    ppermute x11, starting transfers between devices, shift(): lax.ppermute(value, axis, [(i, (i + step) % count) for i in range(count)])  64.4 us
    all_to_all x1, waiting for transfers between devices, body(): lax.all_to_all(result, CTX, 0, 0, tiled=True).reshape(4 * slots, lanes)  33.6 us
    all_to_all x1, waiting for transfers between devices, body(): lax.all_to_all(outgoing, CTX, 0, 0, tiled=True).reshape(4 * slots, lanes)  33.1 us
    all_to_all x1, starting transfers between devices, body(): lax.all_to_all(result, CTX, 0, 0, tiled=True).reshape(4 * slots, lanes)  23.6 us
    ppermute x11, waiting for transfers between devices, shift(): lax.ppermute(value, axis, [(i, (i + step) % count) for i in range(count)])  22.2 us
    all_to_all x1, starting transfers between devices, body(): lax.all_to_all(outgoing, CTX, 0, 0, tiled=True).reshape(4 * slots, lanes)  19.8 us
    all_to_all x4, waiting for transfers between devices, sum_along_x(): lax.all_to_all(parts, 'x', 0, 0, tiled=True).astype(F32)  18.1 us
    ppermute x3, starting transfers between devices, partner(): return lax.ppermute(value, axis, [(i, i ^ bit) for i in range(SIZES[axis])])  17 us
  transfers between devices with their start and end apart: 23, of which 13 were waited for; matrix products, arithmetic and copies ran while one was open for 3% of the time, Pallas kernels for 5%

profile of v5, /device:TPU:1, one launch (start us, length us, event | category | flops | bytes accessed | tf_op | source)
XLA Modules:
  0.0 330.5 jit_solution(7409417551772061760)
XLA Ops:
  1.5 9.6 %collective-permute-start.7 = (bf16[8,4096]{1,0:T(8,128)(2,1)S(1)}, bf16[8,4096]{1,0:T(8,128)(2,1)S(1)}, u32[]{:S(2)}, u32[]{:S(2)}) collective-permute-start(bf16[8,4096]{1,0:T(8,128)(2,1)S(1)} %reshape.140), channel_id=1, source_target_pairs={{0,64},{16,80},{32,96},{48,112},{64,0},{80,16},{96,32},{112,48},{1... | collective-permute-start | bytes 196616 | tf_op jit(solution)/shard_map/ppermute | solution.py:30
  12.8 5.6 %all-to-all-start = ((bf16[8,2,32,128]{3,2,1,0:T(8,128)(2,1)}), bf16[8,2,32,128]{3,2,1,0:T(8,128)(2,1)S(1)}, u32[]{:S(2)}, u32[]{:S(2)}) async-start(bf16[8,2,32,128]{3,2,1,0:T(8,128)(2,1)} %broadcast_in_dim.25), calls=%async_computation | async-start | bytes 262144 | tf_op jit(solution)/shard_map/all_to_all | solution.py:262
  18.4 4.6 %collective-permute-start = (bf16[512,128]{1,0:T(8,128)(2,1)}, bf16[512,128]{1,0:T(8,128)(2,1)S(1)}, u32[]{:S(2)}, u32[]{:S(2)}) collective-permute-start(bf16[512,128]{1,0:T(8,128)(2,1)} %bitcast.62), channel_id=1, source_target_pairs={{0,2},{1,3},{2,0},{3,1},{4,6},{5,7},{6,4},{7,5},{8,10},{9,11},{10,... | collective-permute-start | bytes 393224 | tf_op jit(solution)/shard_map/ppermute | solution.py:26
  23.0 2.2 collective-permute-start.1
  25.3 4.3 %collective-permute-start.2 = (bf16[512,128]{1,0:T(8,128)(2,1)}, bf16[512,128]{1,0:T(8,128)(2,1)S(1)}, u32[]{:S(2)}, u32[]{:S(2)}) collective-permute-start(bf16[512,128]{1,0:T(8,128)(2,1)} %bitcast.64), channel_id=1, source_target_pairs={{0,3},{1,0},{2,1},{3,2},{4,7},{5,4},{6,5},{7,6},{8,11},{9,8},{10,9... | collective-permute-start | bytes 393224 | tf_op jit(solution)/shard_map/ppermute | solution.py:26
  29.6 4.3 %collective-permute-start.8 = (bf16[16,4096]{1,0:T(8,128)(2,1)S(1)}, bf16[16,4096]{1,0:T(8,128)(2,1)S(1)}, u32[]{:S(2)}, u32[]{:S(2)}) collective-permute-start(bf16[16,4096]{1,0:T(8,128)(2,1)S(1)} %pad_maximum_fusion.3), channel_id=1, source_target_pairs={{0,32},{16,48},{32,0},{48,16},{64,96},{80,112},{96,64},{112,80},{1... | collective-permute-start | bytes 393224 | tf_op jit(solution)/shard_map/ppermute | solution.py:30
  34.8 4.2 %all-to-all-start.1 = ((bf16[4,8,2,32,128]{4,3,1,2,0:T(8,128)(2,1)}), bf16[4,8,2,32,128]{4,3,1,2,0:T(8,128)(2,1)S(1)}, u32[]{:S(2)}, u32[]{:S(2)}) async-start(bf16[4,8,2,32,128]{4,3,1,2,0:T(8,128)(2,1)} %broadcast_in_dim.26), calls=%async_computation.1 | async-start | bytes 1048576 | tf_op jit(solution)/shard_map/all_to_all | solution.py:267
  39.0 6.9 %all-to-all-done.1 = bf16[4,8,2,32,128]{4,3,1,2,0:T(8,128)(2,1)S(1)} async-done(((bf16[4,8,2,32,128]{4,3,1,2,0:T(8,128)(2,1)}), bf16[4,8,2,32,128]{4,3,1,2,0:T(8,128)(2,1)S(1)}, u32[]{:S(2)}, u32[]{:S(2)}) %all-to-all-start.1) | async-done | bytes 524320 | tf_op jit(solution)/shard_map/all_to_all | solution.py:267
  45.9 3.1 collective-permute-start.9
  49.0 6.3 %collective-permute-start.3 = (bf16[4,8,2,32,128]{4,3,1,2,0:T(8,128)(2,1)S(1)}, bf16[4,8,2,32,128]{4,3,1,2,0:T(8,128)(2,1)S(1)}, u32[]{:S(2)}, u32[]{:S(2)}) collective-permute-start(bf16[4,8,2,32,128]{4,3,1,2,0:T(8,128)(2,1)S(1)} %all-to-all-done.1), channel_id=1, source_target_pairs={{0,8},{8,0},{1,9},{9,1},{2,10},{10,2},{3,11},{11,3},{4,12},{12,4},... | collective-permute-start | bytes 1572872 | tf_op jit(solution)/shard_map/ppermute | solution.py:26
  56.9 3.4 %attend.4 = bf16[144,512]{1,0:T(8,128)(2,1)S(1)} custom-call(s32[3]{0:T(128)S(1)} %pad_add_fusion.place, bf16[512,128]{1,0:T(8,128)(2,1)S(1)} %collective-permute-done.q_ref, bf16[2048,128]{1,0:T(8,128)(2,1)S(1)} %bitcast.53, bf16[2048,128]{1,0:T(8,128)(2,1)S(1)} %bitcast.49), custom_call_target="tpu_custom_call" | custom-call | tf_op jit(solution)/shard_map/attend/pallas_call | solution.py:231
  60.3 1.6 broadcast_in_dim.30
  61.9 3.6 %all-to-all-start.2 = ((bf16[4,64,4096]{2,1,0:T(8,128)(2,1)}), bf16[4,64,4096]{2,1,0:T(8,128)(2,1)S(1)}, u32[]{:S(2)}, u32[]{:S(2)}) async-start(bf16[4,64,4096]{2,1,0:T(8,128)(2,1)} %broadcast_in_dim.30), calls=%async_computation.2 | async-start | bytes 4194304 | tf_op jit(solution)/shard_map/all_to_all | solution.py:283
  65.6 1.9 collective-permute-start.4
  68.5 4.0 %attend.5 = bf16[144,512]{1,0:T(8,128)(2,1)} custom-call(s32[3]{0:T(128)S(1)} %pad_add_fusion.place, bf16[512,128]{1,0:T(8,128)(2,1)S(1)} %copy-done.3, bf16[2048,128]{1,0:T(8,128)(2,1)S(1)} %bitcast.54, bf16[2048,128]{1,0:T(8,128)(2,1)S(1)} %bitcast.50), custom_call_target="tpu_custom_call" | custom-call | tf_op jit(solution)/shard_map/attend/pallas_call | solution.py:231
  72.4 3.6 %collective-permute-start.5 = (bf16[144,512]{1,0:T(8,128)(2,1)}, bf16[144,512]{1,0:T(8,128)(2,1)}, u32[]{:S(2)}, u32[]{:S(2)}) collective-permute-start(bf16[144,512]{1,0:T(8,128)(2,1)} %attend.5), channel_id=1, source_target_pairs={{0,3},{1,0},{2,1},{3,2},{4,7},{5,4},{6,5},{7,6},{8,11},{9,8},{10,9... | collective-permute-start | bytes 442376 | tf_op jit(solution)/shard_map/ppermute | solution.py:26
  76.1 4.0 %attend.6 = bf16[144,512]{1,0:T(8,128)(2,1)} custom-call(s32[3]{0:T(128)S(1)} %pad_add_fusion.place, bf16[512,128]{1,0:T(8,128)(2,1)S(1)} %collective-permute-done.2.q_ref, bf16[2048,128]{1,0:T(8,128)(2,1)S(1)} %bitcast.55, bf16[2048,128]{1,0:T(8,128)(2,1)S(1)} %bitcast.51), custom_call_target="tpu_custom_call" | custom-call | tf_op jit(solution)/shard_map/attend/pallas_call | solution.py:231
  80.1 2.5 collective-permute-start.6
  83.5 3.4 %attend.7 = bf16[144,512]{1,0:T(8,128)(2,1)S(1)} custom-call(s32[3]{0:T(128)S(1)} %pad_add_fusion.place, bf16[512,128]{1,0:T(8,128)(2,1)S(1)} %bitcast.65, bf16[2048,128]{1,0:T(8,128)(2,1)S(1)} %bitcast.56, bf16[2048,128]{1,0:T(8,128)(2,1)S(1)} %bitcast.52), custom_call_target="tpu_custom_call" | custom-call | tf_op jit(solution)/shard_map/attend/pallas_call | solution.py:231
  87.7 2.7 all-to-all-done.2
  90.4 4.3 %collective-permute-start.10 = (bf16[256,4096]{1,0:T(8,128)(2,1)S(1)}, bf16[256,4096]{1,0:T(8,128)(2,1)}, u32[]{:S(2)}, u32[]{:S(2)}) collective-permute-start(bf16[256,4096]{1,0:T(8,128)(2,1)S(1)} %bitcast.44), channel_id=1, source_target_pairs={{0,8},{8,0},{1,9},{9,1},{2,10},{10,2},{3,11},{11,3},{4,12},{12,4},... | collective-permute-start | bytes 6291464 | tf_op jit(solution)/shard_map/ppermute | solution.py:26
  98.6 3.7 %project.3 = bf16[4,128,512]{2,1,0:T(8,128)(2,1)} custom-call(s32[1]{0:T(128)S(6)} %sub.105.side, bf16[128,512]{1,0:T(8,128)(2,1)S(1)} %convolution_convert_fusion.c_ref, bf16[256,4096]{1,0:T(8,128)(2,1)S(1)} %bitcast.45, bf16[256,4096]{1,0:T(8,128)(2,1)} %collective-permute-done.10.far_ref), custom_call_target="tpu_custom_call" | custom-call | tf_op jit(solution)/shard_map/project/pallas_call | solution.py:64
  102.3 3.5 %all-to-all-start.3 = ((bf16[4,128,512]{2,1,0:T(8,128)(2,1)}), bf16[4,128,512]{2,1,0:T(8,128)(2,1)S(1)}, u32[]{:S(2)}, u32[]{:S(2)}) async-start(bf16[4,128,512]{2,1,0:T(8,128)(2,1)} %project.3), calls=%async_computation.3 | async-start | bytes 1048576 | tf_op jit(solution)/shard_map/all_to_all | solution.py:83
  105.9 3.8 %project.2 = bf16[4,128,512]{2,1,0:T(8,128)(2,1)} custom-call(s32[1]{0:T(128)} %bitcast.18.side, bf16[128,512]{1,0:T(8,128)(2,1)S(1)} %convolution_convert_fusion.c_ref, bf16[256,4096]{1,0:T(8,128)(2,1)S(1)} %bitcast.46, bf16[256,4096]{1,0:T(8,128)(2,1)} %collective-permute-done.10.far_ref), custom_call_target="tpu_custom_call" | custom-call | tf_op jit(solution)/shard_map/project/pallas_call | solution.py:64
  109.7 5.3 %all-to-all-done.3 = bf16[4,128,512]{2,1,0:T(8,128)(2,1)S(1)} async-done(((bf16[4,128,512]{2,1,0:T(8,128)(2,1)}), bf16[4,128,512]{2,1,0:T(8,128)(2,1)S(1)}, u32[]{:S(2)}, u32[]{:S(2)}) %all-to-all-start.3) | async-done | bytes 524320 | tf_op jit(solution)/shard_map/all_to_all | solution.py:83
  115.1 3.6 %all-to-all-start.4 = ((bf16[4,128,512]{2,1,0:T(8,128)(2,1)}), bf16[4,128,512]{2,1,0:T(8,128)(2,1)S(1)}, u32[]{:S(2)}, u32[]{:S(2)}) async-start(bf16[4,128,512]{2,1,0:T(8,128)(2,1)} %project.2), calls=%async_computation.4 | async-start | bytes 1048576 | tf_op jit(solution)/shard_map/all_to_all | solution.py:83
  119.2 10.9 %collective-permute-start.11 = (bf16[128,512]{1,0:T(8,128)(2,1)S(1)}, bf16[128,512]{1,0:T(8,128)(2,1)S(1)}, u32[]{:S(2)}, u32[]{:S(2)}) collective-permute-start(bf16[128,512]{1,0:T(8,128)(2,1)S(1)} %reduce_sum.72), channel_id=1, source_target_pairs={{0,4},{4,0},{1,5},{5,1},{2,6},{6,2},{3,7},{7,3},{8,12},{12,8},{9,1... | collective-permute-start | bytes 393224 | tf_op jit(solution)/shard_map/ppermute | solution.py:26
  130.2 3.7 %collective-permute-done.11 = bf16[128,512]{1,0:T(8,128)(2,1)S(1)} collective-permute-done((bf16[128,512]{1,0:T(8,128)(2,1)S(1)}, bf16[128,512]{1,0:T(8,128)(2,1)S(1)}, u32[]{:S(2)}, u32[]{:S(2)}) %collective-permute-start.11) | collective-permute-done | bytes 131104 | tf_op jit(solution)/shard_map/ppermute | solution.py:26
  134.0 1.9 dispatch.1
  136.0 19.8 %all-to-all-start.5 = ((bf16[64,40,128]{2,1,0:T(8,128)(2,1)}), bf16[64,40,128]{2,1,0:T(8,128)(2,1)S(1)}, u32[]{:S(2)}, u32[]{:S(2)}) async-start(bf16[64,40,128]{2,1,0:T(8,128)(2,1)} %bitcast.22), calls=%async_computation.5 | async-start | bytes 1310720 | tf_op jit(solution)/shard_map/all_to_all | solution.py:334
  155.8 1.7 copy.47
  157.5 33.1 %all-to-all-done.5 = bf16[64,40,128]{2,1,0:T(8,128)(2,1)S(1)} async-done(((bf16[64,40,128]{2,1,0:T(8,128)(2,1)}), bf16[64,40,128]{2,1,0:T(8,128)(2,1)S(1)}, u32[]{:S(2)}, u32[]{:S(2)}) %all-to-all-start.5) | async-done | bytes 655392 | tf_op jit(solution)/shard_map/all_to_all | solution.py:334
  190.6 2.4 gate_up.3
  193.0 4.2 %all-to-all-start.6 = ((bf16[4,80,1664]{2,1,0:T(8,128)(2,1)}), bf16[4,80,1664]{2,1,0:T(8,128)(2,1)}, u32[]{:S(2)}, u32[]{:S(2)}) async-start(bf16[4,80,1664]{2,1,0:T(8,128)(2,1)} %bitcast.26), calls=%async_computation.6 | async-start | bytes 2129920 | tf_op jit(solution)/shard_map/all_to_all | solution.py:83
  197.2 2.4 gate_up.2
  199.6 11.3 %all-to-all-done.6 = bf16[4,80,1664]{2,1,0:T(8,128)(2,1)} async-done(((bf16[4,80,1664]{2,1,0:T(8,128)(2,1)}), bf16[4,80,1664]{2,1,0:T(8,128)(2,1)}, u32[]{:S(2)}, u32[]{:S(2)}) %all-to-all-start.6) | async-done | bytes 1064992 | tf_op jit(solution)/shard_map/all_to_all | solution.py:83
  210.9 1.4 reduce_sum.74
  212.3 3.5 %all-to-all-start.7 = ((bf16[4,80,1664]{2,1,0:T(8,128)(2,1)}), bf16[4,80,1664]{2,1,0:T(8,128)(2,1)S(1)}, u32[]{:S(2)}, u32[]{:S(2)}) async-start(bf16[4,80,1664]{2,1,0:T(8,128)(2,1)} %bitcast.25), calls=%async_computation.7 | async-start | bytes 2129920 | tf_op jit(solution)/shard_map/all_to_all | solution.py:83
  215.9 10.9 %collective-permute-start.12 = (bf16[80,1664]{1,0:T(8,128)(2,1)S(1)}, bf16[80,1664]{1,0:T(8,128)(2,1)S(1)}, u32[]{:S(2)}, u32[]{:S(2)}) collective-permute-start(bf16[80,1664]{1,0:T(8,128)(2,1)S(1)} %reduce_sum.74), channel_id=1, source_target_pairs={{0,4},{4,0},{1,5},{5,1},{2,6},{6,2},{3,7},{7,3},{8,12},{12,8},{9,1... | collective-permute-start | bytes 798728 | tf_op jit(solution)/shard_map/ppermute | solution.py:26
  226.8 1.5 all-to-all-done.7
  228.4 4.0 %collective-permute-done.12 = bf16[80,1664]{1,0:T(8,128)(2,1)S(1)} collective-permute-done((bf16[80,1664]{1,0:T(8,128)(2,1)S(1)}, bf16[80,1664]{1,0:T(8,128)(2,1)S(1)}, u32[]{:S(2)}, u32[]{:S(2)}) %collective-permute-start.12) | collective-permute-done | bytes 266272 | tf_op jit(solution)/shard_map/ppermute | solution.py:26
  232.8 12.8 %collective-permute-start.13 = (bf16[80,768]{1,0:T(8,128)(2,1)S(1)}, bf16[80,768]{1,0:T(8,128)(2,1)S(1)}, u32[]{:S(2)}, u32[]{:S(2)}) collective-permute-start(bf16[80,768]{1,0:T(8,128)(2,1)S(1)} %fusion.52), channel_id=1, source_target_pairs={{0,4},{4,0},{1,5},{5,1},{2,6},{6,2},{3,7},{7,3},{8,12},{12,8},{9,1... | collective-permute-start | bytes 368648 | tf_op jit(solution)/shard_map/ppermute | solution.py:26
  245.8 11.8 %collective-permute-done.13 = bf16[80,768]{1,0:T(8,128)(2,1)S(1)} collective-permute-done((bf16[80,768]{1,0:T(8,128)(2,1)S(1)}, bf16[80,768]{1,0:T(8,128)(2,1)S(1)}, u32[]{:S(2)}, u32[]{:S(2)}) %collective-permute-start.13) | collective-permute-done | bytes 122912 | tf_op jit(solution)/shard_map/ppermute | solution.py:26
  257.6 10.8 %all_gather.4 = bf16[4,2,80,768]{3,2,1,0:T(8,128)(2,1)S(1)} all-gather(bf16[1,2,80,768]{3,2,1,0:T(8,128)(2,1)S(1)} %maximum_select_fusion), channel_id=1, replica_groups=mesh['y'=4,'zl'=8,'core'=2,'zh'=2,'x'=4] {'x'}, dimensions={0}, use_global_device_ids=true | all-gather | bytes 1228800 | tf_op jit(solution)/shard_map/all_gather | solution.py:351
  268.4 2.3 down.1
  270.7 23.6 %all-to-all-start.8 = ((bf16[64,40,128]{2,1,0:T(8,128)(2,1)}), bf16[64,40,128]{2,1,0:T(8,128)(2,1)S(1)}, u32[]{:S(2)}, u32[]{:S(2)}) async-start(bf16[64,40,128]{2,1,0:T(8,128)(2,1)} %bitcast.31), calls=%async_computation.8 | async-start | bytes 1310720 | tf_op jit(solution)/shard_map/all_to_all | solution.py:353
  295.5 33.6 %all-to-all-done.8 = bf16[64,40,128]{2,1,0:T(8,128)(2,1)S(1)} async-done(((bf16[64,40,128]{2,1,0:T(8,128)(2,1)}), bf16[64,40,128]{2,1,0:T(8,128)(2,1)S(1)}, u32[]{:S(2)}, u32[]{:S(2)}) %all-to-all-start.8) | async-done | bytes 655392 | tf_op jit(solution)/shard_map/all_to_all | solution.py:353
  329.1 1.4 combine.1
  (77 shorter events, 14.3 us)
Async XLA Ops:
  1.5 28.1 %collective-permute-start.7 = (bf16[8,4096]{1,0:T(8,128)(2,1)S(1)}, bf16[8,4096]{1,0:T(8,128)(2,1)S(1)}, u32[]{:S(2)}, u32[]{:S(2)}) collective-permute-start(bf16[8,4096]{1,0:T(8,128)(2,1)S(1)} %reshape.140), channel_id=1, source_target_pairs={{0,64},{16,80},{32,96},{48,112},{64,0},{80,16},{96,32},{112,48},{1... | collective-permute-start | bytes 196616 | tf_op jit(solution)/shard_map/ppermute | solution.py:30
  12.8 16.8 %all-to-all-start = ((bf16[8,2,32,128]{3,2,1,0:T(8,128)(2,1)}), bf16[8,2,32,128]{3,2,1,0:T(8,128)(2,1)S(1)}, u32[]{:S(2)}, u32[]{:S(2)}) async-start(bf16[8,2,32,128]{3,2,1,0:T(8,128)(2,1)} %broadcast_in_dim.25), calls=%async_computation | async-start | bytes 262144 | tf_op jit(solution)/shard_map/all_to_all | solution.py:262
  18.4 15.5 %collective-permute-start = (bf16[512,128]{1,0:T(8,128)(2,1)}, bf16[512,128]{1,0:T(8,128)(2,1)S(1)}, u32[]{:S(2)}, u32[]{:S(2)}) collective-permute-start(bf16[512,128]{1,0:T(8,128)(2,1)} %bitcast.62), channel_id=1, source_target_pairs={{0,2},{1,3},{2,0},{3,1},{4,6},{5,7},{6,4},{7,5},{8,10},{9,11},{10,... | collective-permute-start | bytes 393224 | tf_op jit(solution)/shard_map/ppermute | solution.py:26
  23.0 10.8 %collective-permute-start.1 = (bf16[512,128]{1,0:T(8,128)(2,1)}, bf16[512,128]{1,0:T(8,128)(2,1)S(1)}, u32[]{:S(2)}, u32[]{:S(2)}) collective-permute-start(bf16[512,128]{1,0:T(8,128)(2,1)} %bitcast.63), channel_id=1, source_target_pairs={{0,1},{1,2},{2,3},{3,0},{4,5},{5,6},{6,7},{7,4},{8,9},{9,10},{10,1... | collective-permute-start | bytes 393224 | tf_op jit(solution)/shard_map/ppermute | solution.py:26
  25.3 8.6 %collective-permute-start.2 = (bf16[512,128]{1,0:T(8,128)(2,1)}, bf16[512,128]{1,0:T(8,128)(2,1)S(1)}, u32[]{:S(2)}, u32[]{:S(2)}) collective-permute-start(bf16[512,128]{1,0:T(8,128)(2,1)} %bitcast.64), channel_id=1, source_target_pairs={{0,3},{1,0},{2,1},{3,2},{4,7},{5,4},{6,5},{7,6},{8,11},{9,8},{10,9... | collective-permute-start | bytes 393224 | tf_op jit(solution)/shard_map/ppermute | solution.py:26
  29.6 9.4 %collective-permute-start.8 = (bf16[16,4096]{1,0:T(8,128)(2,1)S(1)}, bf16[16,4096]{1,0:T(8,128)(2,1)S(1)}, u32[]{:S(2)}, u32[]{:S(2)}) collective-permute-start(bf16[16,4096]{1,0:T(8,128)(2,1)S(1)} %pad_maximum_fusion.3), channel_id=1, source_target_pairs={{0,32},{16,48},{32,0},{48,16},{64,96},{80,112},{96,64},{112,80},{1... | collective-permute-start | bytes 393224 | tf_op jit(solution)/shard_map/ppermute | solution.py:30
  33.9 21.5 %copy-start.2 = (bf16[512,128]{1,0:T(8,128)(2,1)}, bf16[512,128]{1,0:T(8,128)(2,1)S(1)}, u32[]{:S(2)}) copy-start(bf16[512,128]{1,0:T(8,128)(2,1)S(1)} %collective-permute-done.1.q_ref) | copy-start | bytes 393220
  34.8 11.1 %all-to-all-start.1 = ((bf16[4,8,2,32,128]{4,3,1,2,0:T(8,128)(2,1)}), bf16[4,8,2,32,128]{4,3,1,2,0:T(8,128)(2,1)S(1)}, u32[]{:S(2)}, u32[]{:S(2)}) async-start(bf16[4,8,2,32,128]{4,3,1,2,0:T(8,128)(2,1)} %broadcast_in_dim.26), calls=%async_computation.1 | async-start | bytes 1048576 | tf_op jit(solution)/shard_map/all_to_all | solution.py:267
  45.9 9.4 %collective-permute-start.9 = (bf16[32,4096]{1,0:T(8,128)(2,1)S(1)}, bf16[32,4096]{1,0:T(8,128)(2,1)S(1)}, u32[]{:S(2)}, u32[]{:S(2)}) collective-permute-start(bf16[32,4096]{1,0:T(8,128)(2,1)S(1)} %pad_maximum_fusion.2), channel_id=1, source_target_pairs={{0,16},{16,0},{32,48},{48,32},{64,80},{80,64},{96,112},{112,96},{1... | collective-permute-start | bytes 786440 | tf_op jit(solution)/shard_map/ppermute | solution.py:30
  49.0 7.8 %collective-permute-start.3 = (bf16[4,8,2,32,128]{4,3,1,2,0:T(8,128)(2,1)S(1)}, bf16[4,8,2,32,128]{4,3,1,2,0:T(8,128)(2,1)S(1)}, u32[]{:S(2)}, u32[]{:S(2)}) collective-permute-start(bf16[4,8,2,32,128]{4,3,1,2,0:T(8,128)(2,1)S(1)} %all-to-all-done.1), channel_id=1, source_target_pairs={{0,8},{8,0},{1,9},{9,1},{2,10},{10,2},{3,11},{11,3},{4,12},{12,4},... | collective-permute-start | bytes 1572872 | tf_op jit(solution)/shard_map/ppermute | solution.py:26
  61.9 28.4 %all-to-all-start.2 = ((bf16[4,64,4096]{2,1,0:T(8,128)(2,1)}), bf16[4,64,4096]{2,1,0:T(8,128)(2,1)S(1)}, u32[]{:S(2)}, u32[]{:S(2)}) async-start(bf16[4,64,4096]{2,1,0:T(8,128)(2,1)} %broadcast_in_dim.30), calls=%async_computation.2 | async-start | bytes 4194304 | tf_op jit(solution)/shard_map/all_to_all | solution.py:283
  65.5 17.0 %copy-start.8 = (f32[128,8]{0,1:T(8,128)S(1)}, f32[128,8]{0,1:T(8,128)}, u32[]{:S(2)}) copy-start(f32[128,8]{0,1:T(8,128)} %param.16) | copy-start | bytes 12292
  65.6 22.0 %collective-permute-start.4 = (bf16[144,512]{1,0:T(8,128)(2,1)S(1)}, bf16[144,512]{1,0:T(8,128)(2,1)}, u32[]{:S(2)}, u32[]{:S(2)}) collective-permute-start(bf16[144,512]{1,0:T(8,128)(2,1)S(1)} %attend.4), channel_id=1, source_target_pairs={{0,2},{1,3},{2,0},{3,1},{4,6},{5,7},{6,4},{7,5},{8,10},{9,11},{10,... | collective-permute-start | bytes 442376 | tf_op jit(solution)/shard_map/ppermute | solution.py:26
  67.6 0.9 copy-start.3
  72.4 15.2 %collective-permute-start.5 = (bf16[144,512]{1,0:T(8,128)(2,1)}, bf16[144,512]{1,0:T(8,128)(2,1)}, u32[]{:S(2)}, u32[]{:S(2)}) collective-permute-start(bf16[144,512]{1,0:T(8,128)(2,1)} %attend.5), channel_id=1, source_target_pairs={{0,3},{1,0},{2,1},{3,2},{4,7},{5,4},{6,5},{7,6},{8,11},{9,8},{10,9... | collective-permute-start | bytes 442376 | tf_op jit(solution)/shard_map/ppermute | solution.py:26
  80.1 7.6 %collective-permute-start.6 = (bf16[144,512]{1,0:T(8,128)(2,1)}, bf16[144,512]{1,0:T(8,128)(2,1)}, u32[]{:S(2)}, u32[]{:S(2)}) collective-permute-start(bf16[144,512]{1,0:T(8,128)(2,1)} %attend.6), channel_id=1, source_target_pairs={{0,1},{1,2},{2,3},{3,0},{4,5},{5,6},{6,7},{7,4},{8,9},{9,10},{10,1... | collective-permute-start | bytes 442376 | tf_op jit(solution)/shard_map/ppermute | solution.py:26
  82.6 0.9 copy-start.1
  90.4 8.2 %collective-permute-start.10 = (bf16[256,4096]{1,0:T(8,128)(2,1)S(1)}, bf16[256,4096]{1,0:T(8,128)(2,1)}, u32[]{:S(2)}, u32[]{:S(2)}) collective-permute-start(bf16[256,4096]{1,0:T(8,128)(2,1)S(1)} %bitcast.44), channel_id=1, source_target_pairs={{0,8},{8,0},{1,9},{9,1},{2,10},{10,2},{3,11},{11,3},{4,12},{12,4},... | collective-permute-start | bytes 6291464 | tf_op jit(solution)/shard_map/ppermute | solution.py:26
  97.2 0.8 copy-start.6
  97.3 0.7 copy-start.9
  102.3 12.7 %all-to-all-start.3 = ((bf16[4,128,512]{2,1,0:T(8,128)(2,1)}), bf16[4,128,512]{2,1,0:T(8,128)(2,1)S(1)}, u32[]{:S(2)}, u32[]{:S(2)}) async-start(bf16[4,128,512]{2,1,0:T(8,128)(2,1)} %project.3), calls=%async_computation.3 | async-start | bytes 1048576 | tf_op jit(solution)/shard_map/all_to_all | solution.py:83
  115.1 18.9 %copy-start.4 = (f32[512]{0:T(512)S(1)}, f32[512]{0:T(512)}, u32[]{:S(2)}) copy-start(f32[512]{0:T(512)} %param.14) | copy-start | bytes 6148
  115.1 18.9 %copy-start.7 = (bf16[128,512]{1,0:T(8,128)(2,1)S(1)}, bf16[128,512]{1,0:T(8,128)(2,1)}, u32[]{:S(2)}) copy-start(bf16[128,512]{1,0:T(8,128)(2,1)} %param.13) | copy-start | bytes 393220
  115.1 15.1 %all-to-all-start.4 = ((bf16[4,128,512]{2,1,0:T(8,128)(2,1)}), bf16[4,128,512]{2,1,0:T(8,128)(2,1)S(1)}, u32[]{:S(2)}, u32[]{:S(2)}) async-start(bf16[4,128,512]{2,1,0:T(8,128)(2,1)} %project.2), calls=%async_computation.4 | async-start | bytes 1048576 | tf_op jit(solution)/shard_map/all_to_all | solution.py:83
  119.1 16.9 %copy-start.5 = (f32[640,384]{1,0:T(8,128)}, f32[640,384]{1,0:T(8,128)S(1)}, u32[]{:S(2)}) copy-start(f32[640,384]{1,0:T(8,128)S(1)} %fusion.50) | copy-start | bytes 2949124
  119.2 14.7 %collective-permute-start.11 = (bf16[128,512]{1,0:T(8,128)(2,1)S(1)}, bf16[128,512]{1,0:T(8,128)(2,1)S(1)}, u32[]{:S(2)}, u32[]{:S(2)}) collective-permute-start(bf16[128,512]{1,0:T(8,128)(2,1)S(1)} %reduce_sum.72), channel_id=1, source_target_pairs={{0,4},{4,0},{1,5},{5,1},{2,6},{6,2},{3,7},{7,3},{8,12},{12,8},{9,1... | collective-permute-start | bytes 393224 | tf_op jit(solution)/shard_map/ppermute | solution.py:26
  136.0 54.6 %all-to-all-start.5 = ((bf16[64,40,128]{2,1,0:T(8,128)(2,1)}), bf16[64,40,128]{2,1,0:T(8,128)(2,1)S(1)}, u32[]{:S(2)}, u32[]{:S(2)}) async-start(bf16[64,40,128]{2,1,0:T(8,128)(2,1)} %bitcast.22), calls=%async_computation.5 | async-start | bytes 1310720 | tf_op jit(solution)/shard_map/all_to_all | solution.py:334
  193.0 18.0 %all-to-all-start.6 = ((bf16[4,80,1664]{2,1,0:T(8,128)(2,1)}), bf16[4,80,1664]{2,1,0:T(8,128)(2,1)}, u32[]{:S(2)}, u32[]{:S(2)}) async-start(bf16[4,80,1664]{2,1,0:T(8,128)(2,1)} %bitcast.26), calls=%async_computation.6 | async-start | bytes 2129920 | tf_op jit(solution)/shard_map/all_to_all | solution.py:83
  212.3 15.9 %all-to-all-start.7 = ((bf16[4,80,1664]{2,1,0:T(8,128)(2,1)}), bf16[4,80,1664]{2,1,0:T(8,128)(2,1)S(1)}, u32[]{:S(2)}, u32[]{:S(2)}) async-start(bf16[4,80,1664]{2,1,0:T(8,128)(2,1)} %bitcast.25), calls=%async_computation.7 | async-start | bytes 2129920 | tf_op jit(solution)/shard_map/all_to_all | solution.py:83
  215.9 16.5 %collective-permute-start.12 = (bf16[80,1664]{1,0:T(8,128)(2,1)S(1)}, bf16[80,1664]{1,0:T(8,128)(2,1)S(1)}, u32[]{:S(2)}, u32[]{:S(2)}) collective-permute-start(bf16[80,1664]{1,0:T(8,128)(2,1)S(1)} %reduce_sum.74), channel_id=1, source_target_pairs={{0,4},{4,0},{1,5},{5,1},{2,6},{6,2},{3,7},{7,3},{8,12},{12,8},{9,1... | collective-permute-start | bytes 798728 | tf_op jit(solution)/shard_map/ppermute | solution.py:26
  232.4 36.0 %copy-start = (bf16[1,768,512]{2,1,0:T(8,128)(2,1)S(1)}, bf16[1,768,512]{2,1,0:T(8,128)(2,1)}, u32[]{:S(2)}) copy-start(bf16[1,768,512]{2,1,0:T(8,128)(2,1)} %param.18) | copy-start | bytes 2359300
  232.8 24.8 %collective-permute-start.13 = (bf16[80,768]{1,0:T(8,128)(2,1)S(1)}, bf16[80,768]{1,0:T(8,128)(2,1)S(1)}, u32[]{:S(2)}, u32[]{:S(2)}) collective-permute-start(bf16[80,768]{1,0:T(8,128)(2,1)S(1)} %fusion.52), channel_id=1, source_target_pairs={{0,4},{4,0},{1,5},{5,1},{2,6},{6,2},{3,7},{7,3},{8,12},{12,8},{9,1... | collective-permute-start | bytes 368648 | tf_op jit(solution)/shard_map/ppermute | solution.py:26
  270.7 58.4 %all-to-all-start.8 = ((bf16[64,40,128]{2,1,0:T(8,128)(2,1)}), bf16[64,40,128]{2,1,0:T(8,128)(2,1)S(1)}, u32[]{:S(2)}, u32[]{:S(2)}) async-start(bf16[64,40,128]{2,1,0:T(8,128)(2,1)} %bitcast.31), calls=%async_computation.8 | async-start | bytes 1310720 | tf_op jit(solution)/shard_map/all_to_all | solution.py:353

commit v6 on v5

--- a/solution.py
+++ b/solution.py
@@ -35,8 +35,8 @@
 
 
 def double(rows, bit, earlier):
-    rows = after(rows, earlier)
-    return jnp.concatenate([rows, partner(rows, "zl", bit)], axis=0)
+    found = partner(rows, "zl", bit)
+    return jnp.concatenate([after(rows, earlier), found], axis=0)
 
 
 def feature_order(zl, core, heads, size):
@@ -197,14 +197,16 @@
     scores = lax.dot_general(
         k_ref[...], q_ref[...], (((1,), (1,)), ((), ())), preferred_element_type=F32
     )
-    key = lax.broadcasted_iota(jnp.int32, (keys, rows), 0)
-    row = lax.broadcasted_iota(jnp.int32, (keys, rows), 1) + pl.program_id(0) * rows
-    core = jnp.where(key >= half, 1 - place[1], place[1])
-    block = (key % half) // piece
-    key_pos = (block * 2 + core) * tokens + place[2] * piece + key % piece
-    row_pos = place[0] + row // heads
+    blocks = keys // piece
+    block = lax.broadcasted_iota(jnp.int32, (blocks, 1, rows), 0)
+    core = jnp.where(block >= blocks // 2, 1 - place[1], place[1])
+    begin = (block % (blocks // 2) * 2 + core) * tokens + place[2] * piece
+    row = lax.broadcasted_iota(jnp.int32, (blocks, 1, rows), 2) + pl.program_id(0) * rows
+    ahead = place[0] + row // heads - begin
+    inner = lax.broadcasted_iota(jnp.int32, (blocks, piece, rows), 1)
     factor = math.log2(math.e) / math.sqrt(q_ref.shape[1])
-    masked = jnp.where(key_pos <= row_pos, scores * factor, -1e30)
+    scores = (scores * factor).reshape(blocks, piece, rows)
+    masked = jnp.where(inner <= ahead, scores, -1e30).reshape(keys, rows)
     best = jnp.max(masked, axis=0, keepdims=True)
     best = jnp.maximum(best, FLOOR).astype(BF16)
     prob = jnp.exp2(masked - best.astype(F32))
@@ -261,26 +263,28 @@
     line = jnp.concatenate([line, partner(line, "zl", 4)], axis=0)
     pair = first = lax.all_to_all(pair, "zl", 0, 0, tiled=True)
     rows = queries.reshape(tokens * heads, size)
-    asked = [shift(rows, "x", step) for step in (1, 2, 3)]
-    pair = after(pair, asked)
+    beside = partner(rows, "x", 1)
+    pair = after(pair, beside)
     pair = jnp.broadcast_to(pair[None], (4,) + pair.shape)
     pair = second = lax.all_to_all(pair, "y", 0, 0, tiled=True)
+    across = partner(jnp.concatenate([beside, rows], axis=0), "x", 2)
     line = double(line, 2, first)
     line = double(line, 1, second)
+    pair = after(pair, across)
     pair = jnp.stack([pair, shift(pair, "core", 1)], axis=0)
     all_keys = pair[:, :, :, 0].reshape(-1, size)
     all_values = pair[:, :, :, 1].reshape(-1, size)
 
     place = jnp.stack([ctx_place * tokens, core, x]).astype(jnp.int32)
+    line = after(line, all_keys)
+    line = jnp.broadcast_to(line[None], (4,) + line.shape)
+    near = lax.all_to_all(line, "y", 0, 0, tiled=True).reshape(-1, D)
     parts, found = [], place
-    for step in (2, 1, 3):
-        theirs = after(asked[step - 1], found)
+    asked = [(1, beside), (3, across[: tokens * heads]), (2, across[tokens * heads :])]
+    for bit, theirs in asked:
+        theirs = after(theirs, found)
         found = attend(place, theirs, all_keys, all_values, heads, piece, tokens)
-        parts.append(shift(found, "x", -step))
-        if step == 2:
-            line = after(line, found)
-            line = jnp.broadcast_to(line[None], (4,) + line.shape)
-            near = lax.all_to_all(line, "y", 0, 0, tiled=True).reshape(-1, D)
+        parts.append(partner(found, "x", bit))
     rows = after(rows, found)
     parts.append(attend(place, rows, all_keys, all_values, heads, piece, tokens))
     near = after(near, parts)

time: 333 us -> 335 us (level)
  starting transfers between devices: 153 us -> 127 us
  waiting for transfers between devices: 117 us -> 140 us
    ppermute x11 -> x5, starting transfers between devices: 64.4 us -> 28.1 us  [shift(): lax.ppermute(value, axis, [(i, (i + step) % count) for i in range(count)])]
    ppermute x11 -> x5, waiting for transfers between devices: 22.2 us -> 36.8 us  [shift(): lax.ppermute(value, axis, [(i, (i + step) % count) for i in range(count)])]
    ppermute x3 -> x8, starting transfers between devices: 17 us -> 28 us  [partner(): return lax.ppermute(value, axis, [(i, i ^ bit) for i in range(SIZES[axis])])]
    all_to_all x1, starting transfers between devices: 5.62 us -> 13.1 us  [body(): pair = first = lax.all_to_all(pair, 'zl', 0, 0, tiled=True)]
    ppermute x3 -> x8, waiting for transfers between devices: 0.01 us -> 7.33 us  [partner(): return lax.ppermute(value, axis, [(i, i ^ bit) for i in range(SIZES[axis])])]
    all_to_all x1, starting transfers between devices: 23.6 us -> 16.5 us  [body(): lax.all_to_all(result, CTX, 0, 0, tiled=True).reshape(4 * slots, lanes)]
    all_to_all x4, waiting for transfers between devices: 18.1 us -> 23 us  [sum_along_x(): lax.all_to_all(parts, 'x', 0, 0, tiled=True).astype(F32)]
  transfers between devices with their start and end apart: 23 -> 22, of which waited for: 13 -> 12; matrix products, arithmetic and copies ran while one was open for 3% -> 4% of each run, Pallas kernels for 5% -> 6%
where the time goes in v6:
time: 335 us; the launch traced here: 333 us
  waiting for transfers between devices  140 us (42%)
  starting transfers between devices  127 us (38%)
  Pallas kernels  32.2 us (10%)
  blocking collectives  13.3 us (4%)
  other arithmetic  9.05 us (3%)
  local copies, waits for them, and re-layouts  8.8 us (3%)
    ppermute x5, waiting for transfers between devices, shift(): lax.ppermute(value, axis, [(i, (i + step) % count) for i in range(count)])  36.8 us
    all_to_all x1, waiting for transfers between devices, body(): lax.all_to_all(result, CTX, 0, 0, tiled=True).reshape(4 * slots, lanes)  33.6 us
    all_to_all x1, waiting for transfers between devices, body(): lax.all_to_all(outgoing, CTX, 0, 0, tiled=True).reshape(4 * slots, lanes)  33.1 us
    ppermute x5, starting transfers between devices, shift(): lax.ppermute(value, axis, [(i, (i + step) % count) for i in range(count)])  28.1 us
    ppermute x8, starting transfers between devices, partner(): return lax.ppermute(value, axis, [(i, i ^ bit) for i in range(SIZES[axis])])  28 us
    all_to_all x4, waiting for transfers between devices, sum_along_x(): lax.all_to_all(parts, 'x', 0, 0, tiled=True).astype(F32)  23 us
    all_to_all x1, starting transfers between devices, body(): lax.all_to_all(outgoing, CTX, 0, 0, tiled=True).reshape(4 * slots, lanes)  18.6 us
    all_to_all x1, starting transfers between devices, body(): lax.all_to_all(result, CTX, 0, 0, tiled=True).reshape(4 * slots, lanes)  16.5 us
  transfers between devices with their start and end apart: 22, of which 12 were waited for; matrix products, arithmetic and copies ran while one was open for 4% of the time, Pallas kernels for 6%

profile of v6, /device:TPU:1, one launch (start us, length us, event | category | flops | bytes accessed | tf_op | source)
XLA Modules:
  0.0 333.4 jit_solution(990819245602954992)
XLA Ops:
  2.2 13.1 %all-to-all-start = ((bf16[8,2,32,128]{3,2,1,0:T(8,128)(2,1)}), bf16[8,2,32,128]{3,2,1,0:T(8,128)(2,1)S(1)}, u32[]{:S(2)}, u32[]{:S(2)}) async-start(bf16[8,2,32,128]{3,2,1,0:T(8,128)(2,1)} %broadcast_in_dim.25), calls=%async_computation | async-start | bytes 262144 | tf_op jit(solution)/shard_map/all_to_all | solution.py:264
  16.2 7.3 %collective-permute-start.6 = (bf16[8,4096]{1,0:T(8,128)(2,1)S(1)}, bf16[8,4096]{1,0:T(8,128)(2,1)S(1)}, u32[]{:S(2)}, u32[]{:S(2)}) collective-permute-start(bf16[8,4096]{1,0:T(8,128)(2,1)S(1)} %reshape.140), channel_id=1, source_target_pairs={{0,64},{16,80},{32,96},{48,112},{64,0},{80,16},{96,32},{112,48},{1... | collective-permute-start | bytes 196616 | tf_op jit(solution)/shard_map/ppermute | solution.py:30
  23.5 3.1 collective-permute-start
  26.6 6.8 %collective-permute-done.6 = bf16[8,4096]{1,0:T(8,128)(2,1)S(1)} collective-permute-done((bf16[8,4096]{1,0:T(8,128)(2,1)S(1)}, bf16[8,4096]{1,0:T(8,128)(2,1)S(1)}, u32[]{:S(2)}, u32[]{:S(2)}) %collective-permute-start.6) | collective-permute-done | bytes 65568 | tf_op jit(solution)/shard_map/ppermute | solution.py:30
  33.5 1.9 collective-permute-start.7
  36.3 4.7 %collective-permute-start.1 = (bf16[1024,128]{1,0:T(8,128)(2,1)S(1)}, bf16[1024,128]{1,0:T(8,128)(2,1)S(1)}, u32[]{:S(2)}, u32[]{:S(2)}) collective-permute-start(bf16[1024,128]{1,0:T(8,128)(2,1)S(1)} %pad_maximum_fusion.2), channel_id=1, source_target_pairs={{0,2},{1,3},{2,0},{3,1},{4,6},{5,7},{6,4},{7,5},{8,10},{9,11},{10,... | collective-permute-start | bytes 786440 | tf_op jit(solution)/shard_map/ppermute | solution.py:30
  41.9 4.2 %all-to-all-start.1 = ((bf16[4,8,2,32,128]{4,3,1,2,0:T(8,128)(2,1)}), bf16[4,8,2,32,128]{4,3,1,2,0:T(8,128)(2,1)S(1)}, u32[]{:S(2)}, u32[]{:S(2)}) async-start(bf16[4,8,2,32,128]{4,3,1,2,0:T(8,128)(2,1)} %broadcast_in_dim.26), calls=%async_computation.1 | async-start | bytes 1048576 | tf_op jit(solution)/shard_map/all_to_all | solution.py:269
  46.1 1.9 collective-permute-start.8
  48.1 6.0 %all-to-all-done.1 = bf16[4,8,2,32,128]{4,3,1,2,0:T(8,128)(2,1)S(1)} async-done(((bf16[4,8,2,32,128]{4,3,1,2,0:T(8,128)(2,1)}), bf16[4,8,2,32,128]{4,3,1,2,0:T(8,128)(2,1)S(1)}, u32[]{:S(2)}, u32[]{:S(2)}) %all-to-all-start.1) | async-done | bytes 524320 | tf_op jit(solution)/shard_map/all_to_all | solution.py:269
  54.1 4.4 %collective-permute-start.2 = (bf16[4,8,2,32,128]{4,3,1,2,0:T(8,128)(2,1)S(1)}, bf16[4,8,2,32,128]{4,3,1,2,0:T(8,128)(2,1)S(1)}, u32[]{:S(2)}, u32[]{:S(2)}) collective-permute-start(bf16[4,8,2,32,128]{4,3,1,2,0:T(8,128)(2,1)S(1)} %all-to-all-done.1), channel_id=1, source_target_pairs={{0,8},{8,0},{1,9},{9,1},{2,10},{10,2},{3,11},{11,3},{4,12},{12,4},... | collective-permute-start | bytes 1572872 | tf_op jit(solution)/shard_map/ppermute | solution.py:26
  58.5 1.4 collective-permute-done.2
  60.0 1.6 broadcast_in_dim.30
  61.6 3.6 %all-to-all-start.2 = ((bf16[4,64,4096]{2,1,0:T(8,128)(2,1)}), bf16[4,64,4096]{2,1,0:T(8,128)(2,1)S(1)}, u32[]{:S(2)}, u32[]{:S(2)}) async-start(bf16[4,64,4096]{2,1,0:T(8,128)(2,1)} %broadcast_in_dim.30), calls=%async_computation.2 | async-start | bytes 4194304 | tf_op jit(solution)/shard_map/all_to_all | solution.py:281
  67.0 3.7 %attend.4 = bf16[144,512]{1,0:T(8,128)(2,1)} custom-call(s32[3]{0:T(128)S(1)} %pad_add_fusion.place, bf16[512,128]{1,0:T(8,128)(2,1)S(1)} %collective-permute-done.q_ref, bf16[2048,128]{1,0:T(8,128)(2,1)S(1)} %bitcast.53, bf16[2048,128]{1,0:T(8,128)(2,1)S(1)} %bitcast.49), custom_call_target="tpu_custom_call" | custom-call | tf_op jit(solution)/shard_map/attend/pallas_call | solution.py:233
  70.7 2.3 collective-permute-start.3
  73.1 3.7 %attend.5 = bf16[144,512]{1,0:T(8,128)(2,1)} custom-call(s32[3]{0:T(128)S(1)} %pad_add_fusion.place, bf16[512,128]{1,0:T(8,128)(2,1)S(1)} %get-tuple-element.18.q_ref, bf16[2048,128]{1,0:T(8,128)(2,1)S(1)} %bitcast.54, bf16[2048,128]{1,0:T(8,128)(2,1)S(1)} %bitcast.50), custom_call_target="tpu_custom_call" | custom-call | tf_op jit(solution)/shard_map/attend/pallas_call | solution.py:233
  76.8 2.5 collective-permute-start.4
  79.2 3.7 %attend.6 = bf16[144,512]{1,0:T(8,128)(2,1)} custom-call(s32[3]{0:T(128)S(1)} %pad_add_fusion.place, bf16[512,128]{1,0:T(8,128)(2,1)S(1)} %get-tuple-element.19.q_ref, bf16[2048,128]{1,0:T(8,128)(2,1)S(1)} %bitcast.55, bf16[2048,128]{1,0:T(8,128)(2,1)S(1)} %bitcast.51), custom_call_target="tpu_custom_call" | custom-call | tf_op jit(solution)/shard_map/attend/pallas_call | solution.py:233
  82.9 4.3 %collective-permute-start.5 = (bf16[144,512]{1,0:T(8,128)(2,1)}, bf16[144,512]{1,0:T(8,128)(2,1)}, u32[]{:S(2)}, u32[]{:S(2)}) collective-permute-start(bf16[144,512]{1,0:T(8,128)(2,1)} %attend.6), channel_id=1, source_target_pairs={{0,2},{1,3},{2,0},{3,1},{4,6},{5,7},{6,4},{7,5},{8,10},{9,11},{10,... | collective-permute-start | bytes 442376 | tf_op jit(solution)/shard_map/ppermute | solution.py:30
  87.8 3.1 attend.7
  91.4 3.4 %collective-permute-start.9 = (bf16[256,4096]{1,0:T(8,128)(2,1)S(1)}, bf16[256,4096]{1,0:T(8,128)(2,1)}, u32[]{:S(2)}, u32[]{:S(2)}) collective-permute-start(bf16[256,4096]{1,0:T(8,128)(2,1)S(1)} %bitcast.44), channel_id=1, source_target_pairs={{0,8},{8,0},{1,9},{9,1},{2,10},{10,2},{3,11},{11,3},{4,12},{12,4},... | collective-permute-start | bytes 6291464 | tf_op jit(solution)/shard_map/ppermute | solution.py:26
  99.5 3.7 %project.3 = bf16[4,128,512]{2,1,0:T(8,128)(2,1)} custom-call(s32[1]{0:T(128)S(6)} %sub.105.side, bf16[128,512]{1,0:T(8,128)(2,1)S(1)} %convolution_convert_fusion.c_ref, bf16[256,4096]{1,0:T(8,128)(2,1)S(1)} %bitcast.45, bf16[256,4096]{1,0:T(8,128)(2,1)} %collective-permute-done.9.far_ref), custom_call_target="tpu_custom_call" | custom-call | tf_op jit(solution)/shard_map/project/pallas_call | solution.py:64
  103.3 3.6 %all-to-all-start.3 = ((bf16[4,128,512]{2,1,0:T(8,128)(2,1)}), bf16[4,128,512]{2,1,0:T(8,128)(2,1)S(1)}, u32[]{:S(2)}, u32[]{:S(2)}) async-start(bf16[4,128,512]{2,1,0:T(8,128)(2,1)} %project.3), calls=%async_computation.3 | async-start | bytes 1048576 | tf_op jit(solution)/shard_map/all_to_all | solution.py:83
  107.1 3.7 %project.2 = bf16[4,128,512]{2,1,0:T(8,128)(2,1)} custom-call(s32[1]{0:T(128)} %bitcast.18.side, bf16[128,512]{1,0:T(8,128)(2,1)S(1)} %convolution_convert_fusion.c_ref, bf16[256,4096]{1,0:T(8,128)(2,1)S(1)} %bitcast.46, bf16[256,4096]{1,0:T(8,128)(2,1)} %collective-permute-done.9.far_ref), custom_call_target="tpu_custom_call" | custom-call | tf_op jit(solution)/shard_map/project/pallas_call | solution.py:64
  110.8 5.4 %all-to-all-done.3 = bf16[4,128,512]{2,1,0:T(8,128)(2,1)S(1)} async-done(((bf16[4,128,512]{2,1,0:T(8,128)(2,1)}), bf16[4,128,512]{2,1,0:T(8,128)(2,1)S(1)}, u32[]{:S(2)}, u32[]{:S(2)}) %all-to-all-start.3) | async-done | bytes 524320 | tf_op jit(solution)/shard_map/all_to_all | solution.py:83
  116.4 3.6 %all-to-all-start.4 = ((bf16[4,128,512]{2,1,0:T(8,128)(2,1)}), bf16[4,128,512]{2,1,0:T(8,128)(2,1)S(1)}, u32[]{:S(2)}, u32[]{:S(2)}) async-start(bf16[4,128,512]{2,1,0:T(8,128)(2,1)} %project.2), calls=%async_computation.4 | async-start | bytes 1048576 | tf_op jit(solution)/shard_map/all_to_all | solution.py:83
  121.4 7.9 %collective-permute-start.10 = (bf16[128,512]{1,0:T(8,128)(2,1)S(1)}, bf16[128,512]{1,0:T(8,128)(2,1)S(1)}, u32[]{:S(2)}, u32[]{:S(2)}) collective-permute-start(bf16[128,512]{1,0:T(8,128)(2,1)S(1)} %reduce_sum.72), channel_id=1, source_target_pairs={{0,4},{4,0},{1,5},{5,1},{2,6},{6,2},{3,7},{7,3},{8,12},{12,8},{9,1... | collective-permute-start | bytes 393224 | tf_op jit(solution)/shard_map/ppermute | solution.py:26
  129.5 8.0 %collective-permute-done.10 = bf16[128,512]{1,0:T(8,128)(2,1)S(1)} collective-permute-done((bf16[128,512]{1,0:T(8,128)(2,1)S(1)}, bf16[128,512]{1,0:T(8,128)(2,1)S(1)}, u32[]{:S(2)}, u32[]{:S(2)}) %collective-permute-start.10) | collective-permute-done | bytes 131104 | tf_op jit(solution)/shard_map/ppermute | solution.py:26
  137.5 1.9 dispatch.1
  139.5 18.6 %all-to-all-start.5 = ((bf16[64,40,128]{2,1,0:T(8,128)(2,1)}), bf16[64,40,128]{2,1,0:T(8,128)(2,1)S(1)}, u32[]{:S(2)}, u32[]{:S(2)}) async-start(bf16[64,40,128]{2,1,0:T(8,128)(2,1)} %bitcast.22), calls=%async_computation.5 | async-start | bytes 1310720 | tf_op jit(solution)/shard_map/all_to_all | solution.py:338
  158.1 1.7 copy.47
  159.8 33.1 %all-to-all-done.5 = bf16[64,40,128]{2,1,0:T(8,128)(2,1)S(1)} async-done(((bf16[64,40,128]{2,1,0:T(8,128)(2,1)}), bf16[64,40,128]{2,1,0:T(8,128)(2,1)S(1)}, u32[]{:S(2)}, u32[]{:S(2)}) %all-to-all-start.5) | async-done | bytes 655392 | tf_op jit(solution)/shard_map/all_to_all | solution.py:338
  192.9 2.4 gate_up.3
  195.3 4.4 %all-to-all-start.6 = ((bf16[4,80,1664]{2,1,0:T(8,128)(2,1)}), bf16[4,80,1664]{2,1,0:T(8,128)(2,1)}, u32[]{:S(2)}, u32[]{:S(2)}) async-start(bf16[4,80,1664]{2,1,0:T(8,128)(2,1)} %bitcast.26), calls=%async_computation.6 | async-start | bytes 2129920 | tf_op jit(solution)/shard_map/all_to_all | solution.py:83
  199.8 2.4 gate_up.2
  202.2 11.5 %all-to-all-done.6 = bf16[4,80,1664]{2,1,0:T(8,128)(2,1)} async-done(((bf16[4,80,1664]{2,1,0:T(8,128)(2,1)}), bf16[4,80,1664]{2,1,0:T(8,128)(2,1)}, u32[]{:S(2)}, u32[]{:S(2)}) %all-to-all-start.6) | async-done | bytes 1064992 | tf_op jit(solution)/shard_map/all_to_all | solution.py:83
  213.6 1.4 reduce_sum.74
  215.1 3.5 %all-to-all-start.7 = ((bf16[4,80,1664]{2,1,0:T(8,128)(2,1)}), bf16[4,80,1664]{2,1,0:T(8,128)(2,1)S(1)}, u32[]{:S(2)}, u32[]{:S(2)}) async-start(bf16[4,80,1664]{2,1,0:T(8,128)(2,1)} %bitcast.25), calls=%async_computation.7 | async-start | bytes 2129920 | tf_op jit(solution)/shard_map/all_to_all | solution.py:83
  218.6 6.5 %collective-permute-start.11 = (bf16[80,1664]{1,0:T(8,128)(2,1)S(1)}, bf16[80,1664]{1,0:T(8,128)(2,1)S(1)}, u32[]{:S(2)}, u32[]{:S(2)}) collective-permute-start(bf16[80,1664]{1,0:T(8,128)(2,1)S(1)} %reduce_sum.74), channel_id=1, source_target_pairs={{0,4},{4,0},{1,5},{5,1},{2,6},{6,2},{3,7},{7,3},{8,12},{12,8},{9,1... | collective-permute-start | bytes 798728 | tf_op jit(solution)/shard_map/ppermute | solution.py:26
  225.1 6.0 %all-to-all-done.7 = bf16[4,80,1664]{2,1,0:T(8,128)(2,1)S(1)} async-done(((bf16[4,80,1664]{2,1,0:T(8,128)(2,1)}), bf16[4,80,1664]{2,1,0:T(8,128)(2,1)S(1)}, u32[]{:S(2)}, u32[]{:S(2)}) %all-to-all-start.7) | async-done | bytes 1064992 | tf_op jit(solution)/shard_map/all_to_all | solution.py:83
  231.3 17.9 %collective-permute-done.11 = bf16[80,1664]{1,0:T(8,128)(2,1)S(1)} collective-permute-done((bf16[80,1664]{1,0:T(8,128)(2,1)S(1)}, bf16[80,1664]{1,0:T(8,128)(2,1)S(1)}, u32[]{:S(2)}, u32[]{:S(2)}) %collective-permute-start.11) | collective-permute-done | bytes 266272 | tf_op jit(solution)/shard_map/ppermute | solution.py:26
  249.7 5.8 %collective-permute-start.12 = (bf16[80,768]{1,0:T(8,128)(2,1)S(1)}, bf16[80,768]{1,0:T(8,128)(2,1)S(1)}, u32[]{:S(2)}, u32[]{:S(2)}) collective-permute-start(bf16[80,768]{1,0:T(8,128)(2,1)S(1)} %fusion.52), channel_id=1, source_target_pairs={{0,4},{4,0},{1,5},{5,1},{2,6},{6,2},{3,7},{7,3},{8,12},{12,8},{9,1... | collective-permute-start | bytes 368648 | tf_op jit(solution)/shard_map/ppermute | solution.py:26
  255.7 9.4 %collective-permute-done.12 = bf16[80,768]{1,0:T(8,128)(2,1)S(1)} collective-permute-done((bf16[80,768]{1,0:T(8,128)(2,1)S(1)}, bf16[80,768]{1,0:T(8,128)(2,1)S(1)}, u32[]{:S(2)}, u32[]{:S(2)}) %collective-permute-start.12) | collective-permute-done | bytes 122912 | tf_op jit(solution)/shard_map/ppermute | solution.py:26
  265.1 13.3 %all_gather.4 = bf16[4,2,80,768]{3,2,1,0:T(8,128)(2,1)S(1)} all-gather(bf16[1,2,80,768]{3,2,1,0:T(8,128)(2,1)S(1)} %maximum_select_fusion), channel_id=1, replica_groups=mesh['y'=4,'zl'=8,'core'=2,'zh'=2,'x'=4] {'x'}, dimensions={0}, use_global_device_ids=true | all-gather | bytes 1228800 | tf_op jit(solution)/shard_map/all_gather | solution.py:355
  278.4 2.3 down.1
  280.7 16.5 %all-to-all-start.8 = ((bf16[64,40,128]{2,1,0:T(8,128)(2,1)}), bf16[64,40,128]{2,1,0:T(8,128)(2,1)S(1)}, u32[]{:S(2)}, u32[]{:S(2)}) async-start(bf16[64,40,128]{2,1,0:T(8,128)(2,1)} %bitcast.31), calls=%async_computation.8 | async-start | bytes 1310720 | tf_op jit(solution)/shard_map/all_to_all | solution.py:357
  298.4 33.6 %all-to-all-done.8 = bf16[64,40,128]{2,1,0:T(8,128)(2,1)S(1)} async-done(((bf16[64,40,128]{2,1,0:T(8,128)(2,1)}), bf16[64,40,128]{2,1,0:T(8,128)(2,1)S(1)}, u32[]{:S(2)}, u32[]{:S(2)}) %all-to-all-start.8) | async-done | bytes 655392 | tf_op jit(solution)/shard_map/all_to_all | solution.py:357
  332.0 1.4 combine.1
  (77 shorter events, 15.5 us)
Async XLA Ops:
  2.2 38.7 %all-to-all-start = ((bf16[8,2,32,128]{3,2,1,0:T(8,128)(2,1)}), bf16[8,2,32,128]{3,2,1,0:T(8,128)(2,1)S(1)}, u32[]{:S(2)}, u32[]{:S(2)}) async-start(bf16[8,2,32,128]{3,2,1,0:T(8,128)(2,1)} %broadcast_in_dim.25), calls=%async_computation | async-start | bytes 262144 | tf_op jit(solution)/shard_map/all_to_all | solution.py:264
  16.2 17.3 %collective-permute-start.6 = (bf16[8,4096]{1,0:T(8,128)(2,1)S(1)}, bf16[8,4096]{1,0:T(8,128)(2,1)S(1)}, u32[]{:S(2)}, u32[]{:S(2)}) collective-permute-start(bf16[8,4096]{1,0:T(8,128)(2,1)S(1)} %reshape.140), channel_id=1, source_target_pairs={{0,64},{16,80},{32,96},{48,112},{64,0},{80,16},{96,32},{112,48},{1... | collective-permute-start | bytes 196616 | tf_op jit(solution)/shard_map/ppermute | solution.py:30
  23.5 11.9 %collective-permute-start = (bf16[512,128]{1,0:T(8,128)(2,1)}, bf16[512,128]{1,0:T(8,128)(2,1)S(1)}, u32[]{:S(2)}, u32[]{:S(2)}) collective-permute-start(bf16[512,128]{1,0:T(8,128)(2,1)} %bitcast.62), channel_id=1, source_target_pairs={{0,1},{1,0},{2,3},{3,2},{4,5},{5,4},{6,7},{7,6},{8,9},{9,8},{10,11... | collective-permute-start | bytes 393224 | tf_op jit(solution)/shard_map/ppermute | solution.py:30
  33.5 12.6 %collective-permute-start.7 = (bf16[16,4096]{1,0:T(8,128)(2,1)S(1)}, bf16[16,4096]{1,0:T(8,128)(2,1)S(1)}, u32[]{:S(2)}, u32[]{:S(2)}) collective-permute-start(bf16[16,4096]{1,0:T(8,128)(2,1)S(1)} %constant_dynamic-update-slice_fusion), channel_id=1, source_target_pairs={{0,32},{16,48},{32,0},{48,16},{64,96},{80,112},{96,64},{112,80},{1... | collective-permute-start | bytes 393224 | tf_op jit(solution)/shard_map/ppermute | solution.py:30
  36.3 11.7 %collective-permute-start.1 = (bf16[1024,128]{1,0:T(8,128)(2,1)S(1)}, bf16[1024,128]{1,0:T(8,128)(2,1)S(1)}, u32[]{:S(2)}, u32[]{:S(2)}) collective-permute-start(bf16[1024,128]{1,0:T(8,128)(2,1)S(1)} %pad_maximum_fusion.2), channel_id=1, source_target_pairs={{0,2},{1,3},{2,0},{3,1},{4,6},{5,7},{6,4},{7,5},{8,10},{9,11},{10,... | collective-permute-start | bytes 786440 | tf_op jit(solution)/shard_map/ppermute | solution.py:30
  41.9 12.1 %all-to-all-start.1 = ((bf16[4,8,2,32,128]{4,3,1,2,0:T(8,128)(2,1)}), bf16[4,8,2,32,128]{4,3,1,2,0:T(8,128)(2,1)S(1)}, u32[]{:S(2)}, u32[]{:S(2)}) async-start(bf16[4,8,2,32,128]{4,3,1,2,0:T(8,128)(2,1)} %broadcast_in_dim.26), calls=%async_computation.1 | async-start | bytes 1048576 | tf_op jit(solution)/shard_map/all_to_all | solution.py:269
  46.1 12.3 %collective-permute-start.8 = (bf16[32,4096]{1,0:T(8,128)(2,1)S(1)}, bf16[32,4096]{1,0:T(8,128)(2,1)S(1)}, u32[]{:S(2)}, u32[]{:S(2)}) collective-permute-start(bf16[32,4096]{1,0:T(8,128)(2,1)S(1)} %constant_dynamic-update-slice_fusion.2), channel_id=1, source_target_pairs={{0,16},{16,0},{32,48},{48,32},{64,80},{80,64},{96,112},{112,96},{1... | collective-permute-start | bytes 786440 | tf_op jit(solution)/shard_map/ppermute | solution.py:30
  48.1 10.4 %copy-start.5 = (bf16[1024,128]{1,0:T(8,128)(2,1)}, bf16[1024,128]{1,0:T(8,128)(2,1)S(1)}, u32[]{:S(2)}) copy-start(bf16[1024,128]{1,0:T(8,128)(2,1)S(1)} %collective-permute-done.1) | copy-start | bytes 786436
  54.1 5.9 %collective-permute-start.2 = (bf16[4,8,2,32,128]{4,3,1,2,0:T(8,128)(2,1)S(1)}, bf16[4,8,2,32,128]{4,3,1,2,0:T(8,128)(2,1)S(1)}, u32[]{:S(2)}, u32[]{:S(2)}) collective-permute-start(bf16[4,8,2,32,128]{4,3,1,2,0:T(8,128)(2,1)S(1)} %all-to-all-done.1), channel_id=1, source_target_pairs={{0,8},{8,0},{1,9},{9,1},{2,10},{10,2},{3,11},{11,3},{4,12},{12,4},... | collective-permute-start | bytes 1572872 | tf_op jit(solution)/shard_map/ppermute | solution.py:26
  61.6 29.8 %all-to-all-start.2 = ((bf16[4,64,4096]{2,1,0:T(8,128)(2,1)}), bf16[4,64,4096]{2,1,0:T(8,128)(2,1)S(1)}, u32[]{:S(2)}, u32[]{:S(2)}) async-start(bf16[4,64,4096]{2,1,0:T(8,128)(2,1)} %broadcast_in_dim.30), calls=%async_computation.2 | async-start | bytes 4194304 | tf_op jit(solution)/shard_map/all_to_all | solution.py:281
  70.7 17.1 %copy-start.7 = (f32[128,8]{0,1:T(8,128)S(1)}, f32[128,8]{0,1:T(8,128)}, u32[]{:S(2)}) copy-start(f32[128,8]{0,1:T(8,128)} %param.16) | copy-start | bytes 12292
  70.7 17.1 %copy-start.1 = (bf16[128,4,128]{2,1,0:T(4,128)(2,1)S(1)}, bf16[128,4,128]{2,1,0:T(4,128)(2,1)}, u32[]{:S(2)}) copy-start(bf16[128,4,128]{2,1,0:T(4,128)(2,1)} %param.10) | copy-start | bytes 393220
  70.7 20.7 %collective-permute-start.3 = (bf16[144,512]{1,0:T(8,128)(2,1)}, bf16[144,512]{1,0:T(8,128)(2,1)}, u32[]{:S(2)}, u32[]{:S(2)}) collective-permute-start(bf16[144,512]{1,0:T(8,128)(2,1)} %attend.4), channel_id=1, source_target_pairs={{0,1},{1,0},{2,3},{3,2},{4,5},{5,4},{6,7},{7,6},{8,9},{9,8},{10,11... | collective-permute-start | bytes 442376 | tf_op jit(solution)/shard_map/ppermute | solution.py:30
  76.8 14.6 %collective-permute-start.4 = (bf16[144,512]{1,0:T(8,128)(2,1)}, bf16[144,512]{1,0:T(8,128)(2,1)}, u32[]{:S(2)}, u32[]{:S(2)}) collective-permute-start(bf16[144,512]{1,0:T(8,128)(2,1)} %attend.5), channel_id=1, source_target_pairs={{0,3},{1,2},{2,1},{3,0},{4,7},{5,6},{6,5},{7,4},{8,11},{9,10},{10,... | collective-permute-start | bytes 442376 | tf_op jit(solution)/shard_map/ppermute | solution.py:30
  82.9 8.4 %collective-permute-start.5 = (bf16[144,512]{1,0:T(8,128)(2,1)}, bf16[144,512]{1,0:T(8,128)(2,1)}, u32[]{:S(2)}, u32[]{:S(2)}) collective-permute-start(bf16[144,512]{1,0:T(8,128)(2,1)} %attend.6), channel_id=1, source_target_pairs={{0,2},{1,3},{2,0},{3,1},{4,6},{5,7},{6,4},{7,5},{8,10},{9,11},{10,... | collective-permute-start | bytes 442376 | tf_op jit(solution)/shard_map/ppermute | solution.py:30
  91.4 8.1 %collective-permute-start.9 = (bf16[256,4096]{1,0:T(8,128)(2,1)S(1)}, bf16[256,4096]{1,0:T(8,128)(2,1)}, u32[]{:S(2)}, u32[]{:S(2)}) collective-permute-start(bf16[256,4096]{1,0:T(8,128)(2,1)S(1)} %bitcast.44), channel_id=1, source_target_pairs={{0,8},{8,0},{1,9},{9,1},{2,10},{10,2},{3,11},{11,3},{4,12},{12,4},... | collective-permute-start | bytes 6291464 | tf_op jit(solution)/shard_map/ppermute | solution.py:26
  98.0 1.5 copy-start.4
  98.1 1.4 copy-start.8
  103.3 13.0 %all-to-all-start.3 = ((bf16[4,128,512]{2,1,0:T(8,128)(2,1)}), bf16[4,128,512]{2,1,0:T(8,128)(2,1)S(1)}, u32[]{:S(2)}, u32[]{:S(2)}) async-start(bf16[4,128,512]{2,1,0:T(8,128)(2,1)} %project.3), calls=%async_computation.3 | async-start | bytes 1048576 | tf_op jit(solution)/shard_map/all_to_all | solution.py:83
  116.3 21.1 %copy-start.2 = (f32[512]{0:T(512)S(1)}, f32[512]{0:T(512)}, u32[]{:S(2)}) copy-start(f32[512]{0:T(512)} %param.14) | copy-start | bytes 6148
  116.4 21.1 %copy-start.6 = (bf16[128,512]{1,0:T(8,128)(2,1)S(1)}, bf16[128,512]{1,0:T(8,128)(2,1)}, u32[]{:S(2)}) copy-start(bf16[128,512]{1,0:T(8,128)(2,1)} %param.13) | copy-start | bytes 393220
  116.4 13.0 %all-to-all-start.4 = ((bf16[4,128,512]{2,1,0:T(8,128)(2,1)}), bf16[4,128,512]{2,1,0:T(8,128)(2,1)S(1)}, u32[]{:S(2)}, u32[]{:S(2)}) async-start(bf16[4,128,512]{2,1,0:T(8,128)(2,1)} %project.2), calls=%async_computation.4 | async-start | bytes 1048576 | tf_op jit(solution)/shard_map/all_to_all | solution.py:83
  120.3 0.9 copy-start.3
  121.4 16.0 %collective-permute-start.10 = (bf16[128,512]{1,0:T(8,128)(2,1)S(1)}, bf16[128,512]{1,0:T(8,128)(2,1)S(1)}, u32[]{:S(2)}, u32[]{:S(2)}) collective-permute-start(bf16[128,512]{1,0:T(8,128)(2,1)S(1)} %reduce_sum.72), channel_id=1, source_target_pairs={{0,4},{4,0},{1,5},{5,1},{2,6},{6,2},{3,7},{7,3},{8,12},{12,8},{9,1... | collective-permute-start | bytes 393224 | tf_op jit(solution)/shard_map/ppermute | solution.py:26
  139.5 53.4 %all-to-all-start.5 = ((bf16[64,40,128]{2,1,0:T(8,128)(2,1)}), bf16[64,40,128]{2,1,0:T(8,128)(2,1)S(1)}, u32[]{:S(2)}, u32[]{:S(2)}) async-start(bf16[64,40,128]{2,1,0:T(8,128)(2,1)} %bitcast.22), calls=%async_computation.5 | async-start | bytes 1310720 | tf_op jit(solution)/shard_map/all_to_all | solution.py:338
  195.3 18.3 %all-to-all-start.6 = ((bf16[4,80,1664]{2,1,0:T(8,128)(2,1)}), bf16[4,80,1664]{2,1,0:T(8,128)(2,1)}, u32[]{:S(2)}, u32[]{:S(2)}) async-start(bf16[4,80,1664]{2,1,0:T(8,128)(2,1)} %bitcast.26), calls=%async_computation.6 | async-start | bytes 2129920 | tf_op jit(solution)/shard_map/all_to_all | solution.py:83
  215.1 16.1 %all-to-all-start.7 = ((bf16[4,80,1664]{2,1,0:T(8,128)(2,1)}), bf16[4,80,1664]{2,1,0:T(8,128)(2,1)S(1)}, u32[]{:S(2)}, u32[]{:S(2)}) async-start(bf16[4,80,1664]{2,1,0:T(8,128)(2,1)} %bitcast.25), calls=%async_computation.7 | async-start | bytes 2129920 | tf_op jit(solution)/shard_map/all_to_all | solution.py:83
  218.6 30.7 %collective-permute-start.11 = (bf16[80,1664]{1,0:T(8,128)(2,1)S(1)}, bf16[80,1664]{1,0:T(8,128)(2,1)S(1)}, u32[]{:S(2)}, u32[]{:S(2)}) collective-permute-start(bf16[80,1664]{1,0:T(8,128)(2,1)S(1)} %reduce_sum.74), channel_id=1, source_target_pairs={{0,4},{4,0},{1,5},{5,1},{2,6},{6,2},{3,7},{7,3},{8,12},{12,8},{9,1... | collective-permute-start | bytes 798728 | tf_op jit(solution)/shard_map/ppermute | solution.py:26
  249.3 29.0 %copy-start = (bf16[1,768,512]{2,1,0:T(8,128)(2,1)S(1)}, bf16[1,768,512]{2,1,0:T(8,128)(2,1)}, u32[]{:S(2)}) copy-start(bf16[1,768,512]{2,1,0:T(8,128)(2,1)} %param.18) | copy-start | bytes 2359300
  249.7 15.4 %collective-permute-start.12 = (bf16[80,768]{1,0:T(8,128)(2,1)S(1)}, bf16[80,768]{1,0:T(8,128)(2,1)S(1)}, u32[]{:S(2)}, u32[]{:S(2)}) collective-permute-start(bf16[80,768]{1,0:T(8,128)(2,1)S(1)} %fusion.52), channel_id=1, source_target_pairs={{0,4},{4,0},{1,5},{5,1},{2,6},{6,2},{3,7},{7,3},{8,12},{12,8},{9,1... | collective-permute-start | bytes 368648 | tf_op jit(solution)/shard_map/ppermute | solution.py:26
  280.7 51.3 %all-to-all-start.8 = ((bf16[64,40,128]{2,1,0:T(8,128)(2,1)}), bf16[64,40,128]{2,1,0:T(8,128)(2,1)S(1)}, u32[]{:S(2)}, u32[]{:S(2)}) async-start(bf16[64,40,128]{2,1,0:T(8,128)(2,1)} %bitcast.31), calls=%async_computation.8 | async-start | bytes 1310720 | tf_op jit(solution)/shard_map/all_to_all | solution.py:357

commit v7 on v6

--- a/solution.py
+++ b/solution.py
@@ -35,8 +35,8 @@
 
 
 def double(rows, bit, earlier):
-    found = partner(rows, "zl", bit)
-    return jnp.concatenate([after(rows, earlier), found], axis=0)
+    rows = after(rows, earlier)
+    return jnp.concatenate([rows, partner(rows, "zl", bit)], axis=0)
 
 
 def feature_order(zl, core, heads, size):
@@ -191,56 +191,48 @@
 
 
 def attend_kernel(place, q_ref, k_ref, v_ref, o_ref, *, heads, piece, tokens):
-    rows = q_ref.shape[0]
-    keys = k_ref.shape[0]
-    half = keys // 2
-    scores = lax.dot_general(
-        k_ref[...], q_ref[...], (((1,), (1,)), ((), ())), preferred_element_type=F32
-    )
+    step = 256
+    keys, size = k_ref.shape
     blocks = keys // piece
-    block = lax.broadcasted_iota(jnp.int32, (blocks, 1, rows), 0)
+    factor = math.log2(math.e) / math.sqrt(size)
+    block = lax.broadcasted_iota(jnp.int32, (blocks, 1, step), 0)
     core = jnp.where(block >= blocks // 2, 1 - place[1], place[1])
-    begin = (block % (blocks // 2) * 2 + core) * tokens + place[2] * piece
-    row = lax.broadcasted_iota(jnp.int32, (blocks, 1, rows), 2) + pl.program_id(0) * rows
-    ahead = place[0] + row // heads - begin
-    inner = lax.broadcasted_iota(jnp.int32, (blocks, piece, rows), 1)
-    factor = math.log2(math.e) / math.sqrt(q_ref.shape[1])
-    scores = (scores * factor).reshape(blocks, piece, rows)
-    masked = jnp.where(inner <= ahead, scores, -1e30).reshape(keys, rows)
-    best = jnp.max(masked, axis=0, keepdims=True)
-    best = jnp.maximum(best, FLOOR).astype(BF16)
-    prob = jnp.exp2(masked - best.astype(F32))
-    total = jnp.sum(prob, axis=0, keepdims=True)
-    high = total.astype(BF16)
-    low = (total - high.astype(F32)).astype(BF16)
-    summed = lax.dot_general(
-        v_ref[...], prob.astype(BF16), (((0,), (0,)), ((), ())), preferred_element_type=F32
-    )
-    size = v_ref.shape[1]
-    o_ref[0:size, :] = summed.astype(BF16)
-    line = lax.broadcasted_iota(jnp.int32, (16, rows), 0)
-    extra = jnp.where(
-        line == 0,
-        best.astype(F32),
-        jnp.where(line == 1, high.astype(F32), jnp.where(line == 2, low.astype(F32), 0.0)),
-    )
-    o_ref[size : size + 16, :] = extra.astype(BF16)
+    begin = (block % (blocks // 2) * 2 + core) * tokens + place[2] * piece - place[0]
+    row = lax.broadcasted_iota(jnp.int32, (blocks, 1, step), 2) // heads
+    inner = lax.broadcasted_iota(jnp.int32, (blocks, piece, step), 1)
+    line = lax.broadcasted_iota(jnp.int32, (16, step), 0)
+    for i in range(q_ref.shape[0] // step):
+        scores = lax.dot_general(
+            k_ref[...],
+            q_ref[i * step : (i + 1) * step, :],
+            (((1,), (1,)), ((), ())),
+            preferred_element_type=F32,
+        )
+        ahead = row + i * step // heads - begin
+        scores = (scores * factor).reshape(blocks, piece, step)
+        masked = jnp.where(inner <= ahead, scores, -1e30).reshape(keys, step)
+        best = jnp.max(masked, axis=0, keepdims=True)
+        best = jnp.maximum(best, FLOOR).astype(BF16).astype(F32)
+        prob = jnp.exp2(masked - best)
+        total = jnp.sum(prob, axis=0, keepdims=True)
+        high = total.astype(BF16).astype(F32)
+        summed = move(v_ref[...], prob.astype(BF16))
+        o_ref[0:size, i * step : (i + 1) * step] = summed.astype(BF16)
+        extra = jnp.where(line == 1, high, jnp.where(line == 2, total - high, 0.0))
+        extra = jnp.where(line == 0, best, extra)
+        o_ref[size : size + 16, i * step : (i + 1) * step] = extra.astype(BF16)
+
+
+def move(matrix, rows):
+    return lax.dot_general(matrix, rows, (((0,), (0,)), ((), ())), preferred_element_type=F32)
 
 
 def attend(place, rows, keys, values, heads, piece, tokens):
     count, size = rows.shape
-    step = 256
     return pl.pallas_call(
         functools.partial(attend_kernel, heads=heads, piece=piece, tokens=tokens),
         out_shape=jax.ShapeDtypeStruct((size + 16, count), BF16),
-        grid=(count // step,),
-        in_specs=[
-            pl.BlockSpec(memory_space=pltpu.SMEM),
-            pl.BlockSpec((step, size), lambda i: (i, 0)),
-            pl.BlockSpec(keys.shape, lambda i: (0, 0)),
-            pl.BlockSpec(values.shape, lambda i: (0, 0)),
-        ],
-        out_specs=pl.BlockSpec((size + 16, step), lambda i: (0, i)),
+        in_specs=[pl.BlockSpec(memory_space=pltpu.SMEM)] + [pl.BlockSpec(memory_space=pltpu.VMEM)] * 3,
         compiler_params=pltpu.CompilerParams(vmem_limit_bytes=48 << 20),
         name="attend",
     )(place, rows, keys, values)
@@ -267,9 +259,10 @@
     pair = after(pair, beside)
     pair = jnp.broadcast_to(pair[None], (4,) + pair.shape)
     pair = second = lax.all_to_all(pair, "y", 0, 0, tiled=True)
-    across = partner(jnp.concatenate([beside, rows], axis=0), "x", 2)
+    across = partner(jnp.concatenate([beside, after(rows, first)], axis=0), "x", 2)
     line = double(line, 2, first)
-    line = double(line, 1, second)
+    found = partner(line, "zl", 1)
+    line = jnp.concatenate([after(line, second), found], axis=0)
     pair = after(pair, across)
     pair = jnp.stack([pair, shift(pair, "core", 1)], axis=0)
     all_keys = pair[:, :, :, 0].reshape(-1, size)

time: 335 us -> 329 us (0.982)
  waiting for transfers between devices: 140 us -> 124 us
  starting transfers between devices: 127 us -> 141 us
    ppermute x5, starting transfers between devices: 28.1 us -> 43.9 us  [shift(): lax.ppermute(value, axis, [(i, (i + step) % count) for i in range(count)])]
    ppermute x5, waiting for transfers between devices: 36.8 us -> 25.8 us  [shift(): lax.ppermute(value, axis, [(i, (i + step) % count) for i in range(count)])]
    all_to_all x1, starting transfers between devices: 13.1 us -> 5.62 us  [body(): pair = first = lax.all_to_all(pair, 'zl', 0, 0, tiled=True)]
    all_to_all x1, waiting for transfers between devices: 0.01 us -> 7.15 us  [body(): pair = first = lax.all_to_all(pair, 'zl', 0, 0, tiled=True)]
    all_to_all x1, waiting for transfers between devices: 6 us -> 0.01 us  [body(): pair = second = lax.all_to_all(pair, 'y', 0, 0, tiled=True)]
    ppermute x8, waiting for transfers between devices: 7.33 us -> 3.2 us  [partner(): return lax.ppermute(value, axis, [(i, i ^ bit) for i in range(SIZES[axis])])]
    ppermute x8, starting transfers between devices: 28 us -> 31.5 us  [partner(): return lax.ppermute(value, axis, [(i, i ^ bit) for i in range(SIZES[axis])])]
  transfers between devices with their start and end apart: 22 -> 22, of which waited for: 12 -> 13; matrix products, arithmetic and copies ran while one was open for 4% -> 3% of each run, Pallas kernels for 6% -> 6%
where the time goes in v7:
time: 329 us; the launch traced here: 327 us
  starting transfers between devices  141 us (43%)
  waiting for transfers between devices  124 us (38%)
  Pallas kernels  33 us (10%)
  blocking collectives  13.1 us (4%)
  local copies, waits for them, and re-layouts  7.9 us (2%)
  other arithmetic  6.36 us (2%)
    ppermute x5, starting transfers between devices, shift(): lax.ppermute(value, axis, [(i, (i + step) % count) for i in range(count)])  43.9 us
    all_to_all x1, waiting for transfers between devices, body(): lax.all_to_all(result, CTX, 0, 0, tiled=True).reshape(4 * slots, lanes)  33.6 us
    all_to_all x1, waiting for transfers between devices, body(): lax.all_to_all(outgoing, CTX, 0, 0, tiled=True).reshape(4 * slots, lanes)  33.1 us
    ppermute x8, starting transfers between devices, partner(): return lax.ppermute(value, axis, [(i, i ^ bit) for i in range(SIZES[axis])])  31.5 us
    ppermute x5, waiting for transfers between devices, shift(): lax.ppermute(value, axis, [(i, (i + step) % count) for i in range(count)])  25.8 us
    all_to_all x4, waiting for transfers between devices, sum_along_x(): lax.all_to_all(parts, 'x', 0, 0, tiled=True).astype(F32)  20.6 us
    all_to_all x1, starting transfers between devices, body(): lax.all_to_all(result, CTX, 0, 0, tiled=True).reshape(4 * slots, lanes)  18.6 us
    all_to_all x1, starting transfers between devices, body(): lax.all_to_all(outgoing, CTX, 0, 0, tiled=True).reshape(4 * slots, lanes)  17.6 us
  transfers between devices with their start and end apart: 22, of which 13 were waited for; matrix products, arithmetic and copies ran while one was open for 3% of the time, Pallas kernels for 6%

profile of v7, /device:TPU:1, one launch (start us, length us, event | category | flops | bytes accessed | tf_op | source)
XLA Modules:
  0.0 326.9 jit_solution(2701418935410519618)
XLA Ops:
  1.5 9.6 %collective-permute-start.6 = (bf16[8,4096]{1,0:T(8,128)(2,1)S(1)}, bf16[8,4096]{1,0:T(8,128)(2,1)S(1)}, u32[]{:S(2)}, u32[]{:S(2)}) collective-permute-start(bf16[8,4096]{1,0:T(8,128)(2,1)S(1)} %reshape.140), channel_id=1, source_target_pairs={{0,64},{16,80},{32,96},{48,112},{64,0},{80,16},{96,32},{112,48},{1... | collective-permute-start | bytes 196616 | tf_op jit(solution)/shard_map/ppermute | solution.py:30
  12.8 5.6 %all-to-all-start = ((bf16[8,2,32,128]{3,2,1,0:T(8,128)(2,1)}), bf16[8,2,32,128]{3,2,1,0:T(8,128)(2,1)S(1)}, u32[]{:S(2)}, u32[]{:S(2)}) async-start(bf16[8,2,32,128]{3,2,1,0:T(8,128)(2,1)} %broadcast_in_dim.25), calls=%async_computation | async-start | bytes 262144 | tf_op jit(solution)/shard_map/all_to_all | solution.py:256
  18.4 3.1 collective-permute-start
  21.5 7.2 %all-to-all-done = bf16[8,2,32,128]{3,2,1,0:T(8,128)(2,1)S(1)} async-done(((bf16[8,2,32,128]{3,2,1,0:T(8,128)(2,1)}), bf16[8,2,32,128]{3,2,1,0:T(8,128)(2,1)S(1)}, u32[]{:S(2)}, u32[]{:S(2)}) %all-to-all-start) | async-done | bytes 131104 | tf_op jit(solution)/shard_map/all_to_all | solution.py:256
  28.7 1.9 collective-permute-start.7
  31.6 4.2 %all-to-all-start.1 = ((bf16[4,8,2,32,128]{4,3,1,2,0:T(8,128)(2,1)}), bf16[4,8,2,32,128]{4,3,1,2,0:T(8,128)(2,1)S(1)}, u32[]{:S(2)}, u32[]{:S(2)}) async-start(bf16[4,8,2,32,128]{4,3,1,2,0:T(8,128)(2,1)} %broadcast_in_dim.26), calls=%async_computation.1 | async-start | bytes 1048576 | tf_op jit(solution)/shard_map/all_to_all | solution.py:261
  35.8 4.7 %collective-permute-start.1 = (bf16[1024,128]{1,0:T(8,128)(2,1)S(1)}, bf16[1024,128]{1,0:T(8,128)(2,1)}, u32[]{:S(2)}, u32[]{:S(2)}) collective-permute-start(bf16[1024,128]{1,0:T(8,128)(2,1)S(1)} %pad_maximum_fusion.2), channel_id=1, source_target_pairs={{0,2},{1,3},{2,0},{3,1},{4,6},{5,7},{6,4},{7,5},{8,10},{9,11},{10,... | collective-permute-start | bytes 786440 | tf_op jit(solution)/shard_map/ppermute | solution.py:30
  40.5 2.7 collective-permute-start.8
  44.5 7.0 %collective-permute-start.2 = (bf16[4,8,2,32,128]{4,3,1,2,0:T(8,128)(2,1)S(1)}, bf16[4,8,2,32,128]{4,3,1,2,0:T(8,128)(2,1)S(1)}, u32[]{:S(2)}, u32[]{:S(2)}) collective-permute-start(bf16[4,8,2,32,128]{4,3,1,2,0:T(8,128)(2,1)S(1)} %all-to-all-done.1), channel_id=1, source_target_pairs={{0,8},{8,0},{1,9},{9,1},{2,10},{10,2},{3,11},{11,3},{4,12},{12,4},... | collective-permute-start | bytes 1572872 | tf_op jit(solution)/shard_map/ppermute | solution.py:26
  51.6 1.5 collective-permute-done.2
  53.1 1.6 broadcast_in_dim.30
  54.7 4.5 %all-to-all-start.2 = ((bf16[4,64,4096]{2,1,0:T(8,128)(2,1)}), bf16[4,64,4096]{2,1,0:T(8,128)(2,1)S(1)}, u32[]{:S(2)}, u32[]{:S(2)}) async-start(bf16[4,64,4096]{2,1,0:T(8,128)(2,1)} %broadcast_in_dim.30), calls=%async_computation.2 | async-start | bytes 4194304 | tf_op jit(solution)/shard_map/all_to_all | solution.py:274
  60.4 3.9 %attend.4 = bf16[144,512]{1,0:T(8,128)(2,1)} custom-call(s32[3]{0:T(128)S(1)} %pad_add_fusion.place, bf16[512,128]{1,0:T(8,128)(2,1)S(1)} %collective-permute-done.q_ref, bf16[2048,128]{1,0:T(8,128)(2,1)S(1)} %bitcast.53, bf16[2048,128]{1,0:T(8,128)(2,1)S(1)} %bitcast.49), custom_call_target="tpu_custom_call" | custom-call | tf_op jit(solution)/shard_map/attend/pallas_call | solution.py:232
  64.3 3.2 collective-permute-start.3
  67.5 3.9 %attend.5 = bf16[144,512]{1,0:T(8,128)(2,1)} custom-call(s32[3]{0:T(128)S(1)} %pad_add_fusion.place, bf16[512,128]{1,0:T(8,128)(2,1)S(1)} %get-tuple-element.20.q_ref, bf16[2048,128]{1,0:T(8,128)(2,1)S(1)} %bitcast.54, bf16[2048,128]{1,0:T(8,128)(2,1)S(1)} %bitcast.50), custom_call_target="tpu_custom_call" | custom-call | tf_op jit(solution)/shard_map/attend/pallas_call | solution.py:232
  71.5 3.7 %collective-permute-start.4 = (bf16[144,512]{1,0:T(8,128)(2,1)}, bf16[144,512]{1,0:T(8,128)(2,1)}, u32[]{:S(2)}, u32[]{:S(2)}) collective-permute-start(bf16[144,512]{1,0:T(8,128)(2,1)} %attend.5), channel_id=1, source_target_pairs={{0,3},{1,2},{2,1},{3,0},{4,7},{5,6},{6,5},{7,4},{8,11},{9,10},{10,... | collective-permute-start | bytes 442376 | tf_op jit(solution)/shard_map/ppermute | solution.py:30
  75.2 3.9 %attend.6 = bf16[144,512]{1,0:T(8,128)(2,1)} custom-call(s32[3]{0:T(128)S(1)} %pad_add_fusion.place, bf16[512,128]{1,0:T(8,128)(2,1)S(1)} %get-tuple-element.21.q_ref, bf16[2048,128]{1,0:T(8,128)(2,1)S(1)} %bitcast.55, bf16[2048,128]{1,0:T(8,128)(2,1)S(1)} %bitcast.51), custom_call_target="tpu_custom_call" | custom-call | tf_op jit(solution)/shard_map/attend/pallas_call | solution.py:232
  79.1 2.5 collective-permute-start.5
  81.7 3.3 attend.7
  85.0 1.8 collective-permute-done.5
  86.8 4.5 %collective-permute-start.9 = (bf16[256,4096]{1,0:T(8,128)(2,1)S(1)}, bf16[256,4096]{1,0:T(8,128)(2,1)}, u32[]{:S(2)}, u32[]{:S(2)}) collective-permute-start(bf16[256,4096]{1,0:T(8,128)(2,1)S(1)} %bitcast.44), channel_id=1, source_target_pairs={{0,8},{8,0},{1,9},{9,1},{2,10},{10,2},{3,11},{11,3},{4,12},{12,4},... | collective-permute-start | bytes 6291464 | tf_op jit(solution)/shard_map/ppermute | solution.py:26
  95.0 3.7 %project.3 = bf16[4,128,512]{2,1,0:T(8,128)(2,1)} custom-call(s32[1]{0:T(128)S(6)} %sub.105.side, bf16[128,512]{1,0:T(8,128)(2,1)S(1)} %convolution_convert_fusion.c_ref, bf16[256,4096]{1,0:T(8,128)(2,1)S(1)} %bitcast.45, bf16[256,4096]{1,0:T(8,128)(2,1)} %collective-permute-done.9.far_ref), custom_call_target="tpu_custom_call" | custom-call | tf_op jit(solution)/shard_map/project/pallas_call | solution.py:64
  98.7 3.5 %all-to-all-start.3 = ((bf16[4,128,512]{2,1,0:T(8,128)(2,1)}), bf16[4,128,512]{2,1,0:T(8,128)(2,1)S(1)}, u32[]{:S(2)}, u32[]{:S(2)}) async-start(bf16[4,128,512]{2,1,0:T(8,128)(2,1)} %project.3), calls=%async_computation.3 | async-start | bytes 1048576 | tf_op jit(solution)/shard_map/all_to_all | solution.py:83
  102.4 3.8 %project.2 = bf16[4,128,512]{2,1,0:T(8,128)(2,1)} custom-call(s32[1]{0:T(128)} %bitcast.18.side, bf16[128,512]{1,0:T(8,128)(2,1)S(1)} %convolution_convert_fusion.c_ref, bf16[256,4096]{1,0:T(8,128)(2,1)S(1)} %bitcast.46, bf16[256,4096]{1,0:T(8,128)(2,1)} %collective-permute-done.9.far_ref), custom_call_target="tpu_custom_call" | custom-call | tf_op jit(solution)/shard_map/project/pallas_call | solution.py:64
  106.1 5.3 %all-to-all-done.3 = bf16[4,128,512]{2,1,0:T(8,128)(2,1)S(1)} async-done(((bf16[4,128,512]{2,1,0:T(8,128)(2,1)}), bf16[4,128,512]{2,1,0:T(8,128)(2,1)S(1)}, u32[]{:S(2)}, u32[]{:S(2)}) %all-to-all-start.3) | async-done | bytes 524320 | tf_op jit(solution)/shard_map/all_to_all | solution.py:83
  111.5 3.6 %all-to-all-start.4 = ((bf16[4,128,512]{2,1,0:T(8,128)(2,1)}), bf16[4,128,512]{2,1,0:T(8,128)(2,1)S(1)}, u32[]{:S(2)}, u32[]{:S(2)}) async-start(bf16[4,128,512]{2,1,0:T(8,128)(2,1)} %project.2), calls=%async_computation.4 | async-start | bytes 1048576 | tf_op jit(solution)/shard_map/all_to_all | solution.py:83
  115.7 10.9 %collective-permute-start.10 = (bf16[128,512]{1,0:T(8,128)(2,1)S(1)}, bf16[128,512]{1,0:T(8,128)(2,1)S(1)}, u32[]{:S(2)}, u32[]{:S(2)}) collective-permute-start(bf16[128,512]{1,0:T(8,128)(2,1)S(1)} %reduce_sum.72), channel_id=1, source_target_pairs={{0,4},{4,0},{1,5},{5,1},{2,6},{6,2},{3,7},{7,3},{8,12},{12,8},{9,1... | collective-permute-start | bytes 393224 | tf_op jit(solution)/shard_map/ppermute | solution.py:26
  126.7 3.7 %collective-permute-done.10 = bf16[128,512]{1,0:T(8,128)(2,1)S(1)} collective-permute-done((bf16[128,512]{1,0:T(8,128)(2,1)S(1)}, bf16[128,512]{1,0:T(8,128)(2,1)S(1)}, u32[]{:S(2)}, u32[]{:S(2)}) %collective-permute-start.10) | collective-permute-done | bytes 131104 | tf_op jit(solution)/shard_map/ppermute | solution.py:26
  130.4 2.0 dispatch.1
  132.4 17.6 %all-to-all-start.5 = ((bf16[64,40,128]{2,1,0:T(8,128)(2,1)}), bf16[64,40,128]{2,1,0:T(8,128)(2,1)S(1)}, u32[]{:S(2)}, u32[]{:S(2)}) async-start(bf16[64,40,128]{2,1,0:T(8,128)(2,1)} %bitcast.22), calls=%async_computation.5 | async-start | bytes 1310720 | tf_op jit(solution)/shard_map/all_to_all | solution.py:331
  150.0 1.7 copy.47
  151.7 33.1 %all-to-all-done.5 = bf16[64,40,128]{2,1,0:T(8,128)(2,1)S(1)} async-done(((bf16[64,40,128]{2,1,0:T(8,128)(2,1)}), bf16[64,40,128]{2,1,0:T(8,128)(2,1)S(1)}, u32[]{:S(2)}, u32[]{:S(2)}) %all-to-all-start.5) | async-done | bytes 655392 | tf_op jit(solution)/shard_map/all_to_all | solution.py:331
  184.8 2.4 gate_up.3
  187.2 4.3 %all-to-all-start.6 = ((bf16[4,80,1664]{2,1,0:T(8,128)(2,1)}), bf16[4,80,1664]{2,1,0:T(8,128)(2,1)}, u32[]{:S(2)}, u32[]{:S(2)}) async-start(bf16[4,80,1664]{2,1,0:T(8,128)(2,1)} %bitcast.26), calls=%async_computation.6 | async-start | bytes 2129920 | tf_op jit(solution)/shard_map/all_to_all | solution.py:83
  191.5 2.4 gate_up.2
  193.9 11.6 %all-to-all-done.6 = bf16[4,80,1664]{2,1,0:T(8,128)(2,1)} async-done(((bf16[4,80,1664]{2,1,0:T(8,128)(2,1)}), bf16[4,80,1664]{2,1,0:T(8,128)(2,1)}, u32[]{:S(2)}, u32[]{:S(2)}) %all-to-all-start.6) | async-done | bytes 1064992 | tf_op jit(solution)/shard_map/all_to_all | solution.py:83
  205.4 1.4 reduce_sum.74
  206.8 3.5 %all-to-all-start.7 = ((bf16[4,80,1664]{2,1,0:T(8,128)(2,1)}), bf16[4,80,1664]{2,1,0:T(8,128)(2,1)S(1)}, u32[]{:S(2)}, u32[]{:S(2)}) async-start(bf16[4,80,1664]{2,1,0:T(8,128)(2,1)} %bitcast.25), calls=%async_computation.7 | async-start | bytes 2129920 | tf_op jit(solution)/shard_map/all_to_all | solution.py:83
  210.4 9.2 %collective-permute-start.11 = (bf16[80,1664]{1,0:T(8,128)(2,1)S(1)}, bf16[80,1664]{1,0:T(8,128)(2,1)S(1)}, u32[]{:S(2)}, u32[]{:S(2)}) collective-permute-start(bf16[80,1664]{1,0:T(8,128)(2,1)S(1)} %reduce_sum.74), channel_id=1, source_target_pairs={{0,4},{4,0},{1,5},{5,1},{2,6},{6,2},{3,7},{7,3},{8,12},{12,8},{9,1... | collective-permute-start | bytes 798728 | tf_op jit(solution)/shard_map/ppermute | solution.py:26
  219.6 3.7 %all-to-all-done.7 = bf16[4,80,1664]{2,1,0:T(8,128)(2,1)S(1)} async-done(((bf16[4,80,1664]{2,1,0:T(8,128)(2,1)}), bf16[4,80,1664]{2,1,0:T(8,128)(2,1)S(1)}, u32[]{:S(2)}, u32[]{:S(2)}) %all-to-all-start.7) | async-done | bytes 1064992 | tf_op jit(solution)/shard_map/all_to_all | solution.py:83
  223.5 11.1 %collective-permute-done.11 = bf16[80,1664]{1,0:T(8,128)(2,1)S(1)} collective-permute-done((bf16[80,1664]{1,0:T(8,128)(2,1)S(1)}, bf16[80,1664]{1,0:T(8,128)(2,1)S(1)}, u32[]{:S(2)}, u32[]{:S(2)}) %collective-permute-start.11) | collective-permute-done | bytes 266272 | tf_op jit(solution)/shard_map/ppermute | solution.py:26
  235.0 12.3 %collective-permute-start.12 = (bf16[80,768]{1,0:T(8,128)(2,1)S(1)}, bf16[80,768]{1,0:T(8,128)(2,1)S(1)}, u32[]{:S(2)}, u32[]{:S(2)}) collective-permute-start(bf16[80,768]{1,0:T(8,128)(2,1)S(1)} %fusion.52), channel_id=1, source_target_pairs={{0,4},{4,0},{1,5},{5,1},{2,6},{6,2},{3,7},{7,3},{8,12},{12,8},{9,1... | collective-permute-start | bytes 368648 | tf_op jit(solution)/shard_map/ppermute | solution.py:26
  247.5 9.2 %collective-permute-done.12 = bf16[80,768]{1,0:T(8,128)(2,1)S(1)} collective-permute-done((bf16[80,768]{1,0:T(8,128)(2,1)S(1)}, bf16[80,768]{1,0:T(8,128)(2,1)S(1)}, u32[]{:S(2)}, u32[]{:S(2)}) %collective-permute-start.12) | collective-permute-done | bytes 122912 | tf_op jit(solution)/shard_map/ppermute | solution.py:26
  256.7 13.1 %all_gather.4 = bf16[4,2,80,768]{3,2,1,0:T(8,128)(2,1)S(1)} all-gather(bf16[1,2,80,768]{3,2,1,0:T(8,128)(2,1)S(1)} %maximum_select_fusion), channel_id=1, replica_groups=mesh['y'=4,'zl'=8,'core'=2,'zh'=2,'x'=4] {'x'}, dimensions={0}, use_global_device_ids=true | all-gather | bytes 1228800 | tf_op jit(solution)/shard_map/all_gather | solution.py:348
  269.8 2.3 down.1
  272.2 18.6 %all-to-all-start.8 = ((bf16[64,40,128]{2,1,0:T(8,128)(2,1)}), bf16[64,40,128]{2,1,0:T(8,128)(2,1)S(1)}, u32[]{:S(2)}, u32[]{:S(2)}) async-start(bf16[64,40,128]{2,1,0:T(8,128)(2,1)} %bitcast.31), calls=%async_computation.8 | async-start | bytes 1310720 | tf_op jit(solution)/shard_map/all_to_all | solution.py:350
  291.9 33.6 %all-to-all-done.8 = bf16[64,40,128]{2,1,0:T(8,128)(2,1)S(1)} async-done(((bf16[64,40,128]{2,1,0:T(8,128)(2,1)}), bf16[64,40,128]{2,1,0:T(8,128)(2,1)S(1)}, u32[]{:S(2)}, u32[]{:S(2)}) %all-to-all-start.8) | async-done | bytes 655392 | tf_op jit(solution)/shard_map/all_to_all | solution.py:350
  325.5 1.4 combine.1
  (74 shorter events, 12.5 us)
Async XLA Ops:
  1.5 20.0 %collective-permute-start.6 = (bf16[8,4096]{1,0:T(8,128)(2,1)S(1)}, bf16[8,4096]{1,0:T(8,128)(2,1)S(1)}, u32[]{:S(2)}, u32[]{:S(2)}) collective-permute-start(bf16[8,4096]{1,0:T(8,128)(2,1)S(1)} %reshape.140), channel_id=1, source_target_pairs={{0,64},{16,80},{32,96},{48,112},{64,0},{80,16},{96,32},{112,48},{1... | collective-permute-start | bytes 196616 | tf_op jit(solution)/shard_map/ppermute | solution.py:30
  12.1 23.7 %copy-start.1 = (bf16[128,4,128]{2,1,0:T(4,128)(2,1)S(1)}, bf16[128,4,128]{2,1,0:T(4,128)(2,1)}, u32[]{:S(2)}) copy-start(bf16[128,4,128]{2,1,0:T(4,128)(2,1)} %param.10) | copy-start | bytes 393220
  12.8 15.9 %all-to-all-start = ((bf16[8,2,32,128]{3,2,1,0:T(8,128)(2,1)}), bf16[8,2,32,128]{3,2,1,0:T(8,128)(2,1)S(1)}, u32[]{:S(2)}, u32[]{:S(2)}) async-start(bf16[8,2,32,128]{3,2,1,0:T(8,128)(2,1)} %broadcast_in_dim.25), calls=%async_computation | async-start | bytes 262144 | tf_op jit(solution)/shard_map/all_to_all | solution.py:256
  18.4 12.2 %collective-permute-start = (bf16[512,128]{1,0:T(8,128)(2,1)}, bf16[512,128]{1,0:T(8,128)(2,1)S(1)}, u32[]{:S(2)}, u32[]{:S(2)}) collective-permute-start(bf16[512,128]{1,0:T(8,128)(2,1)} %bitcast.62), channel_id=1, source_target_pairs={{0,1},{1,0},{2,3},{3,2},{4,5},{5,4},{6,7},{7,6},{8,9},{9,8},{10,11... | collective-permute-start | bytes 393224 | tf_op jit(solution)/shard_map/ppermute | solution.py:30
  28.7 11.7 %collective-permute-start.7 = (bf16[16,4096]{1,0:T(8,128)(2,1)S(1)}, bf16[16,4096]{1,0:T(8,128)(2,1)S(1)}, u32[]{:S(2)}, u32[]{:S(2)}) collective-permute-start(bf16[16,4096]{1,0:T(8,128)(2,1)S(1)} %pad_maximum_fusion.3), channel_id=1, source_target_pairs={{0,32},{16,48},{32,0},{48,16},{64,96},{80,112},{96,64},{112,80},{1... | collective-permute-start | bytes 393224 | tf_op jit(solution)/shard_map/ppermute | solution.py:30
  31.6 12.9 %all-to-all-start.1 = ((bf16[4,8,2,32,128]{4,3,1,2,0:T(8,128)(2,1)}), bf16[4,8,2,32,128]{4,3,1,2,0:T(8,128)(2,1)S(1)}, u32[]{:S(2)}, u32[]{:S(2)}) async-start(bf16[4,8,2,32,128]{4,3,1,2,0:T(8,128)(2,1)} %broadcast_in_dim.26), calls=%async_computation.1 | async-start | bytes 1048576 | tf_op jit(solution)/shard_map/all_to_all | solution.py:261
  35.8 8.7 %collective-permute-start.1 = (bf16[1024,128]{1,0:T(8,128)(2,1)S(1)}, bf16[1024,128]{1,0:T(8,128)(2,1)}, u32[]{:S(2)}, u32[]{:S(2)}) collective-permute-start(bf16[1024,128]{1,0:T(8,128)(2,1)S(1)} %pad_maximum_fusion.2), channel_id=1, source_target_pairs={{0,2},{1,3},{2,0},{3,1},{4,6},{5,7},{6,4},{7,5},{8,10},{9,11},{10,... | collective-permute-start | bytes 786440 | tf_op jit(solution)/shard_map/ppermute | solution.py:30
  40.5 11.0 %collective-permute-start.8 = (bf16[32,4096]{1,0:T(8,128)(2,1)S(1)}, bf16[32,4096]{1,0:T(8,128)(2,1)S(1)}, u32[]{:S(2)}, u32[]{:S(2)}) collective-permute-start(bf16[32,4096]{1,0:T(8,128)(2,1)S(1)} %constant_dynamic-update-slice_fusion), channel_id=1, source_target_pairs={{0,16},{16,0},{32,48},{48,32},{64,80},{80,64},{96,112},{112,96},{1... | collective-permute-start | bytes 786440 | tf_op jit(solution)/shard_map/ppermute | solution.py:30
  44.5 8.5 %collective-permute-start.2 = (bf16[4,8,2,32,128]{4,3,1,2,0:T(8,128)(2,1)S(1)}, bf16[4,8,2,32,128]{4,3,1,2,0:T(8,128)(2,1)S(1)}, u32[]{:S(2)}, u32[]{:S(2)}) collective-permute-start(bf16[4,8,2,32,128]{4,3,1,2,0:T(8,128)(2,1)S(1)} %all-to-all-done.1), channel_id=1, source_target_pairs={{0,8},{8,0},{1,9},{9,1},{2,10},{10,2},{3,11},{11,3},{4,12},{12,4},... | collective-permute-start | bytes 1572872 | tf_op jit(solution)/shard_map/ppermute | solution.py:26
  54.7 32.1 %all-to-all-start.2 = ((bf16[4,64,4096]{2,1,0:T(8,128)(2,1)}), bf16[4,64,4096]{2,1,0:T(8,128)(2,1)S(1)}, u32[]{:S(2)}, u32[]{:S(2)}) async-start(bf16[4,64,4096]{2,1,0:T(8,128)(2,1)} %broadcast_in_dim.30), calls=%async_computation.2 | async-start | bytes 4194304 | tf_op jit(solution)/shard_map/all_to_all | solution.py:274
  64.3 17.4 %copy-start.6 = (f32[128,8]{0,1:T(8,128)S(1)}, f32[128,8]{0,1:T(8,128)}, u32[]{:S(2)}) copy-start(f32[128,8]{0,1:T(8,128)} %param.16) | copy-start | bytes 12292
  64.3 22.5 %collective-permute-start.3 = (bf16[144,512]{1,0:T(8,128)(2,1)}, bf16[144,512]{1,0:T(8,128)(2,1)}, u32[]{:S(2)}, u32[]{:S(2)}) collective-permute-start(bf16[144,512]{1,0:T(8,128)(2,1)} %attend.4), channel_id=1, source_target_pairs={{0,1},{1,0},{2,3},{3,2},{4,5},{5,4},{6,7},{7,6},{8,9},{9,8},{10,11... | collective-permute-start | bytes 442376 | tf_op jit(solution)/shard_map/ppermute | solution.py:30
  71.5 15.3 %collective-permute-start.4 = (bf16[144,512]{1,0:T(8,128)(2,1)}, bf16[144,512]{1,0:T(8,128)(2,1)}, u32[]{:S(2)}, u32[]{:S(2)}) collective-permute-start(bf16[144,512]{1,0:T(8,128)(2,1)} %attend.5), channel_id=1, source_target_pairs={{0,3},{1,2},{2,1},{3,0},{4,7},{5,6},{6,5},{7,4},{8,11},{9,10},{10,... | collective-permute-start | bytes 442376 | tf_op jit(solution)/shard_map/ppermute | solution.py:30
  79.1 7.7 %collective-permute-start.5 = (bf16[144,512]{1,0:T(8,128)(2,1)}, bf16[144,512]{1,0:T(8,128)(2,1)}, u32[]{:S(2)}, u32[]{:S(2)}) collective-permute-start(bf16[144,512]{1,0:T(8,128)(2,1)} %attend.6), channel_id=1, source_target_pairs={{0,2},{1,3},{2,0},{3,1},{4,6},{5,7},{6,4},{7,5},{8,10},{9,11},{10,... | collective-permute-start | bytes 442376 | tf_op jit(solution)/shard_map/ppermute | solution.py:30
  86.8 8.2 %collective-permute-start.9 = (bf16[256,4096]{1,0:T(8,128)(2,1)S(1)}, bf16[256,4096]{1,0:T(8,128)(2,1)}, u32[]{:S(2)}, u32[]{:S(2)}) collective-permute-start(bf16[256,4096]{1,0:T(8,128)(2,1)S(1)} %bitcast.44), channel_id=1, source_target_pairs={{0,8},{8,0},{1,9},{9,1},{2,10},{10,2},{3,11},{11,3},{4,12},{12,4},... | collective-permute-start | bytes 6291464 | tf_op jit(solution)/shard_map/ppermute | solution.py:26
  93.8 0.8 copy-start.4
  93.9 0.7 copy-start.7
  98.7 12.7 %all-to-all-start.3 = ((bf16[4,128,512]{2,1,0:T(8,128)(2,1)}), bf16[4,128,512]{2,1,0:T(8,128)(2,1)S(1)}, u32[]{:S(2)}, u32[]{:S(2)}) async-start(bf16[4,128,512]{2,1,0:T(8,128)(2,1)} %project.3), calls=%async_computation.3 | async-start | bytes 1048576 | tf_op jit(solution)/shard_map/all_to_all | solution.py:83
  111.5 18.9 %copy-start.2 = (f32[512]{0:T(512)S(1)}, f32[512]{0:T(512)}, u32[]{:S(2)}) copy-start(f32[512]{0:T(512)} %param.14) | copy-start | bytes 6148
  111.5 18.9 %copy-start.5 = (bf16[128,512]{1,0:T(8,128)(2,1)S(1)}, bf16[128,512]{1,0:T(8,128)(2,1)}, u32[]{:S(2)}) copy-start(bf16[128,512]{1,0:T(8,128)(2,1)} %param.13) | copy-start | bytes 393220
  111.5 15.1 %all-to-all-start.4 = ((bf16[4,128,512]{2,1,0:T(8,128)(2,1)}), bf16[4,128,512]{2,1,0:T(8,128)(2,1)S(1)}, u32[]{:S(2)}, u32[]{:S(2)}) async-start(bf16[4,128,512]{2,1,0:T(8,128)(2,1)} %project.2), calls=%async_computation.4 | async-start | bytes 1048576 | tf_op jit(solution)/shard_map/all_to_all | solution.py:83
  115.5 16.9 %copy-start.3 = (f32[640,384]{1,0:T(8,128)}, f32[640,384]{1,0:T(8,128)S(1)}, u32[]{:S(2)}) copy-start(f32[640,384]{1,0:T(8,128)S(1)} %fusion.50) | copy-start | bytes 2949124
  115.7 14.7 %collective-permute-start.10 = (bf16[128,512]{1,0:T(8,128)(2,1)S(1)}, bf16[128,512]{1,0:T(8,128)(2,1)S(1)}, u32[]{:S(2)}, u32[]{:S(2)}) collective-permute-start(bf16[128,512]{1,0:T(8,128)(2,1)S(1)} %reduce_sum.72), channel_id=1, source_target_pairs={{0,4},{4,0},{1,5},{5,1},{2,6},{6,2},{3,7},{7,3},{8,12},{12,8},{9,1... | collective-permute-start | bytes 393224 | tf_op jit(solution)/shard_map/ppermute | solution.py:26
  132.4 52.4 %all-to-all-start.5 = ((bf16[64,40,128]{2,1,0:T(8,128)(2,1)}), bf16[64,40,128]{2,1,0:T(8,128)(2,1)S(1)}, u32[]{:S(2)}, u32[]{:S(2)}) async-start(bf16[64,40,128]{2,1,0:T(8,128)(2,1)} %bitcast.22), calls=%async_computation.5 | async-start | bytes 1310720 | tf_op jit(solution)/shard_map/all_to_all | solution.py:331
  187.2 18.2 %all-to-all-start.6 = ((bf16[4,80,1664]{2,1,0:T(8,128)(2,1)}), bf16[4,80,1664]{2,1,0:T(8,128)(2,1)}, u32[]{:S(2)}, u32[]{:S(2)}) async-start(bf16[4,80,1664]{2,1,0:T(8,128)(2,1)} %bitcast.26), calls=%async_computation.6 | async-start | bytes 2129920 | tf_op jit(solution)/shard_map/all_to_all | solution.py:83
  206.8 16.5 %all-to-all-start.7 = ((bf16[4,80,1664]{2,1,0:T(8,128)(2,1)}), bf16[4,80,1664]{2,1,0:T(8,128)(2,1)S(1)}, u32[]{:S(2)}, u32[]{:S(2)}) async-start(bf16[4,80,1664]{2,1,0:T(8,128)(2,1)} %bitcast.25), calls=%async_computation.7 | async-start | bytes 2129920 | tf_op jit(solution)/shard_map/all_to_all | solution.py:83
  210.4 24.2 %collective-permute-start.11 = (bf16[80,1664]{1,0:T(8,128)(2,1)S(1)}, bf16[80,1664]{1,0:T(8,128)(2,1)S(1)}, u32[]{:S(2)}, u32[]{:S(2)}) collective-permute-start(bf16[80,1664]{1,0:T(8,128)(2,1)S(1)} %reduce_sum.74), channel_id=1, source_target_pairs={{0,4},{4,0},{1,5},{5,1},{2,6},{6,2},{3,7},{7,3},{8,12},{12,8},{9,1... | collective-permute-start | bytes 798728 | tf_op jit(solution)/shard_map/ppermute | solution.py:26
  234.7 35.2 %copy-start = (bf16[1,768,512]{2,1,0:T(8,128)(2,1)S(1)}, bf16[1,768,512]{2,1,0:T(8,128)(2,1)}, u32[]{:S(2)}) copy-start(bf16[1,768,512]{2,1,0:T(8,128)(2,1)} %param.18) | copy-start | bytes 2359300
  235.0 21.7 %collective-permute-start.12 = (bf16[80,768]{1,0:T(8,128)(2,1)S(1)}, bf16[80,768]{1,0:T(8,128)(2,1)S(1)}, u32[]{:S(2)}, u32[]{:S(2)}) collective-permute-start(bf16[80,768]{1,0:T(8,128)(2,1)S(1)} %fusion.52), channel_id=1, source_target_pairs={{0,4},{4,0},{1,5},{5,1},{2,6},{6,2},{3,7},{7,3},{8,12},{12,8},{9,1... | collective-permute-start | bytes 368648 | tf_op jit(solution)/shard_map/ppermute | solution.py:26
  272.2 53.4 %all-to-all-start.8 = ((bf16[64,40,128]{2,1,0:T(8,128)(2,1)}), bf16[64,40,128]{2,1,0:T(8,128)(2,1)S(1)}, u32[]{:S(2)}, u32[]{:S(2)}) async-start(bf16[64,40,128]{2,1,0:T(8,128)(2,1)} %bitcast.31), calls=%async_computation.8 | async-start | bytes 1310720 | tf_op jit(solution)/shard_map/all_to_all | solution.py:350

commit v8 on v7

--- a/solution.py
+++ b/solution.py
@@ -53,9 +53,11 @@
 
 def project_kernel(side, c_ref, near_ref, far_ref, o_ref):
     half = near_ref.shape[0]
+    width = o_ref.shape[2]
     part = jnp.dot(c_ref[:, :half], near_ref[...], preferred_element_type=F32)
     part = part + jnp.dot(c_ref[:, half:], far_ref[...], preferred_element_type=F32)
-    o_ref[0] = part.astype(BF16)
+    for i in range(o_ref.shape[0]):
+        o_ref[i] = part[:, i * width : (i + 1) * width].astype(BF16)
 
 
 def project(side, ordered, near, far):
@@ -66,13 +68,13 @@
         out_shape=jax.ShapeDtypeStruct((4, tokens, width), BF16),
         grid_spec=pltpu.PrefetchScalarGridSpec(
             num_scalar_prefetch=1,
-            grid=(4,),
+            grid=(2,),
             in_specs=[
                 pl.BlockSpec(ordered.shape, lambda i, side: (0, 0)),
-                pl.BlockSpec((near.shape[0], width), lambda i, side: (0, side[0] * 4 + i)),
-                pl.BlockSpec((near.shape[0], width), lambda i, side: (0, side[0] * 4 + i)),
+                pl.BlockSpec((near.shape[0], 2 * width), lambda i, side: (0, side[0] * 2 + i)),
+                pl.BlockSpec((near.shape[0], 2 * width), lambda i, side: (0, side[0] * 2 + i)),
             ],
-            out_specs=pl.BlockSpec((1, tokens, width), lambda i, side: (i, 0, 0)),
+            out_specs=pl.BlockSpec((2, tokens, width), lambda i, side: (i, 0, 0)),
         ),
         compiler_params=pltpu.CompilerParams(vmem_limit_bytes=32 << 20),
         name="project",
@@ -191,7 +193,7 @@
 
 
 def attend_kernel(place, q_ref, k_ref, v_ref, o_ref, *, heads, piece, tokens):
-    step = 256
+    step = 512
     keys, size = k_ref.shape
     blocks = keys // piece
     factor = math.log2(math.e) / math.sqrt(size)

time: 329 us -> 325 us (0.988)
  Pallas kernels: 33 us -> 26.7 us
    pallas_call x4, Pallas kernels: 15.1 us -> 11.3 us  [attend(): pl.pallas_call(functools.partial(attend_kernel, heads=heads, piece=piece,...]
  transfers between devices with their start and end apart: 22 -> 22, of which waited for: 13 -> 14; matrix products, arithmetic and copies ran while one was open for 3% -> 3% of each run, Pallas kernels for 6% -> 5%
where the time goes in v8:
time: 325 us; the launch traced here: 323 us
  starting transfers between devices  140 us (43%)
  waiting for transfers between devices  127 us (39%)
  Pallas kernels  26.7 us (8%)
  blocking collectives  13.1 us (4%)
  local copies, waits for them, and re-layouts  7.9 us (2%)
  other arithmetic  6.36 us (2%)
    ppermute x5, starting transfers between devices, shift(): lax.ppermute(value, axis, [(i, (i + step) % count) for i in range(count)])  42.8 us
    all_to_all x1, waiting for transfers between devices, body(): lax.all_to_all(result, CTX, 0, 0, tiled=True).reshape(4 * slots, lanes)  33.6 us
    all_to_all x1, waiting for transfers between devices, body(): lax.all_to_all(outgoing, CTX, 0, 0, tiled=True).reshape(4 * slots, lanes)  33.1 us
    ppermute x8, starting transfers between devices, partner(): return lax.ppermute(value, axis, [(i, i ^ bit) for i in range(SIZES[axis])])  31.5 us
    ppermute x5, waiting for transfers between devices, shift(): lax.ppermute(value, axis, [(i, (i + step) % count) for i in range(count)])  26.3 us
    all_to_all x4, waiting for transfers between devices, sum_along_x(): lax.all_to_all(parts, 'x', 0, 0, tiled=True).astype(F32)  21.6 us
    all_to_all x1, starting transfers between devices, body(): lax.all_to_all(result, CTX, 0, 0, tiled=True).reshape(4 * slots, lanes)  18.7 us
    all_to_all x1, starting transfers between devices, body(): lax.all_to_all(outgoing, CTX, 0, 0, tiled=True).reshape(4 * slots, lanes)  17.2 us
  transfers between devices with their start and end apart: 22, of which 14 were waited for; matrix products, arithmetic and copies ran while one was open for 3% of the time, Pallas kernels for 5%

profile of v8, /device:TPU:1, one launch (start us, length us, event | category | flops | bytes accessed | tf_op | source)
XLA Modules:
  0.0 323.1 jit_solution(11466568279726640322)
XLA Ops:
  1.5 9.6 %collective-permute-start.6 = (bf16[8,4096]{1,0:T(8,128)(2,1)S(1)}, bf16[8,4096]{1,0:T(8,128)(2,1)S(1)}, u32[]{:S(2)}, u32[]{:S(2)}) collective-permute-start(bf16[8,4096]{1,0:T(8,128)(2,1)S(1)} %reshape.140), channel_id=1, source_target_pairs={{0,64},{16,80},{32,96},{48,112},{64,0},{80,16},{96,32},{112,48},{1... | collective-permute-start | bytes 196616 | tf_op jit(solution)/shard_map/ppermute | solution.py:30
  12.8 5.6 %all-to-all-start = ((bf16[8,2,32,128]{3,2,1,0:T(8,128)(2,1)}), bf16[8,2,32,128]{3,2,1,0:T(8,128)(2,1)S(1)}, u32[]{:S(2)}, u32[]{:S(2)}) async-start(bf16[8,2,32,128]{3,2,1,0:T(8,128)(2,1)} %broadcast_in_dim.25), calls=%async_computation | async-start | bytes 262144 | tf_op jit(solution)/shard_map/all_to_all | solution.py:258
  18.4 3.1 collective-permute-start
  21.5 7.2 %all-to-all-done = bf16[8,2,32,128]{3,2,1,0:T(8,128)(2,1)S(1)} async-done(((bf16[8,2,32,128]{3,2,1,0:T(8,128)(2,1)}), bf16[8,2,32,128]{3,2,1,0:T(8,128)(2,1)S(1)}, u32[]{:S(2)}, u32[]{:S(2)}) %all-to-all-start) | async-done | bytes 131104 | tf_op jit(solution)/shard_map/all_to_all | solution.py:258
  28.7 1.9 collective-permute-start.7
  31.6 4.2 %all-to-all-start.1 = ((bf16[4,8,2,32,128]{4,3,1,2,0:T(8,128)(2,1)}), bf16[4,8,2,32,128]{4,3,1,2,0:T(8,128)(2,1)S(1)}, u32[]{:S(2)}, u32[]{:S(2)}) async-start(bf16[4,8,2,32,128]{4,3,1,2,0:T(8,128)(2,1)} %broadcast_in_dim.26), calls=%async_computation.1 | async-start | bytes 1048576 | tf_op jit(solution)/shard_map/all_to_all | solution.py:263
  35.8 4.7 %collective-permute-start.1 = (bf16[1024,128]{1,0:T(8,128)(2,1)S(1)}, bf16[1024,128]{1,0:T(8,128)(2,1)}, u32[]{:S(2)}, u32[]{:S(2)}) collective-permute-start(bf16[1024,128]{1,0:T(8,128)(2,1)S(1)} %pad_maximum_fusion.2), channel_id=1, source_target_pairs={{0,2},{1,3},{2,0},{3,1},{4,6},{5,7},{6,4},{7,5},{8,10},{9,11},{10,... | collective-permute-start | bytes 786440 | tf_op jit(solution)/shard_map/ppermute | solution.py:30
  40.5 2.7 collective-permute-start.8
  44.5 7.0 %collective-permute-start.2 = (bf16[4,8,2,32,128]{4,3,1,2,0:T(8,128)(2,1)S(1)}, bf16[4,8,2,32,128]{4,3,1,2,0:T(8,128)(2,1)S(1)}, u32[]{:S(2)}, u32[]{:S(2)}) collective-permute-start(bf16[4,8,2,32,128]{4,3,1,2,0:T(8,128)(2,1)S(1)} %all-to-all-done.1), channel_id=1, source_target_pairs={{0,8},{8,0},{1,9},{9,1},{2,10},{10,2},{3,11},{11,3},{4,12},{12,4},... | collective-permute-start | bytes 1572872 | tf_op jit(solution)/shard_map/ppermute | solution.py:26
  51.6 1.5 collective-permute-done.2
  53.1 1.6 broadcast_in_dim.30
  54.7 4.5 %all-to-all-start.2 = ((bf16[4,64,4096]{2,1,0:T(8,128)(2,1)}), bf16[4,64,4096]{2,1,0:T(8,128)(2,1)S(1)}, u32[]{:S(2)}, u32[]{:S(2)}) async-start(bf16[4,64,4096]{2,1,0:T(8,128)(2,1)} %broadcast_in_dim.30), calls=%async_computation.2 | async-start | bytes 4194304 | tf_op jit(solution)/shard_map/all_to_all | solution.py:276
  60.4 3.0 attend.4
  63.4 3.2 %collective-permute-start.3 = (bf16[144,512]{1,0:T(8,128)(2,1)}, bf16[144,512]{1,0:T(8,128)(2,1)}, u32[]{:S(2)}, u32[]{:S(2)}) collective-permute-start(bf16[144,512]{1,0:T(8,128)(2,1)} %attend.4), channel_id=1, source_target_pairs={{0,1},{1,0},{2,3},{3,2},{4,5},{5,4},{6,7},{7,6},{8,9},{9,8},{10,11... | collective-permute-start | bytes 442376 | tf_op jit(solution)/shard_map/ppermute | solution.py:30
  66.6 3.0 attend.5
  69.6 3.7 %collective-permute-start.4 = (bf16[144,512]{1,0:T(8,128)(2,1)}, bf16[144,512]{1,0:T(8,128)(2,1)}, u32[]{:S(2)}, u32[]{:S(2)}) collective-permute-start(bf16[144,512]{1,0:T(8,128)(2,1)} %attend.5), channel_id=1, source_target_pairs={{0,3},{1,2},{2,1},{3,0},{4,7},{5,6},{6,5},{7,4},{8,11},{9,10},{10,... | collective-permute-start | bytes 442376 | tf_op jit(solution)/shard_map/ppermute | solution.py:30
  73.3 3.0 attend.6
  76.3 2.5 collective-permute-start.5
  78.9 2.3 attend.7
  81.3 2.9 collective-permute-done.5
  85.1 3.3 %collective-permute-start.9 = (bf16[256,4096]{1,0:T(8,128)(2,1)S(1)}, bf16[256,4096]{1,0:T(8,128)(2,1)}, u32[]{:S(2)}, u32[]{:S(2)}) collective-permute-start(bf16[256,4096]{1,0:T(8,128)(2,1)S(1)} %bitcast.44), channel_id=1, source_target_pairs={{0,8},{8,0},{1,9},{9,1},{2,10},{10,2},{3,11},{11,3},{4,12},{12,4},... | collective-permute-start | bytes 6291464 | tf_op jit(solution)/shard_map/ppermute | solution.py:26
  92.3 2.4 project.3
  94.7 4.0 %all-to-all-start.3 = ((bf16[4,128,512]{2,1,0:T(8,128)(2,1)}), bf16[4,128,512]{2,1,0:T(8,128)(2,1)S(1)}, u32[]{:S(2)}, u32[]{:S(2)}) async-start(bf16[4,128,512]{2,1,0:T(8,128)(2,1)} %project.3), calls=%async_computation.3 | async-start | bytes 1048576 | tf_op jit(solution)/shard_map/all_to_all | solution.py:85
  98.9 2.5 project.2
  101.4 6.3 %all-to-all-done.3 = bf16[4,128,512]{2,1,0:T(8,128)(2,1)S(1)} async-done(((bf16[4,128,512]{2,1,0:T(8,128)(2,1)}), bf16[4,128,512]{2,1,0:T(8,128)(2,1)S(1)}, u32[]{:S(2)}, u32[]{:S(2)}) %all-to-all-start.3) | async-done | bytes 524320 | tf_op jit(solution)/shard_map/all_to_all | solution.py:85
  107.8 3.6 %all-to-all-start.4 = ((bf16[4,128,512]{2,1,0:T(8,128)(2,1)}), bf16[4,128,512]{2,1,0:T(8,128)(2,1)S(1)}, u32[]{:S(2)}, u32[]{:S(2)}) async-start(bf16[4,128,512]{2,1,0:T(8,128)(2,1)} %project.2), calls=%async_computation.4 | async-start | bytes 1048576 | tf_op jit(solution)/shard_map/all_to_all | solution.py:85
  111.9 10.9 %collective-permute-start.10 = (bf16[128,512]{1,0:T(8,128)(2,1)S(1)}, bf16[128,512]{1,0:T(8,128)(2,1)S(1)}, u32[]{:S(2)}, u32[]{:S(2)}) collective-permute-start(bf16[128,512]{1,0:T(8,128)(2,1)S(1)} %reduce_sum.72), channel_id=1, source_target_pairs={{0,4},{4,0},{1,5},{5,1},{2,6},{6,2},{3,7},{7,3},{8,12},{12,8},{9,1... | collective-permute-start | bytes 393224 | tf_op jit(solution)/shard_map/ppermute | solution.py:26
  122.9 4.0 %collective-permute-done.10 = bf16[128,512]{1,0:T(8,128)(2,1)S(1)} collective-permute-done((bf16[128,512]{1,0:T(8,128)(2,1)S(1)}, bf16[128,512]{1,0:T(8,128)(2,1)S(1)}, u32[]{:S(2)}, u32[]{:S(2)}) %collective-permute-start.10) | collective-permute-done | bytes 131104 | tf_op jit(solution)/shard_map/ppermute | solution.py:26
  126.9 2.0 dispatch.1
  128.9 17.2 %all-to-all-start.5 = ((bf16[64,40,128]{2,1,0:T(8,128)(2,1)}), bf16[64,40,128]{2,1,0:T(8,128)(2,1)S(1)}, u32[]{:S(2)}, u32[]{:S(2)}) async-start(bf16[64,40,128]{2,1,0:T(8,128)(2,1)} %bitcast.22), calls=%async_computation.5 | async-start | bytes 1310720 | tf_op jit(solution)/shard_map/all_to_all | solution.py:333
  146.1 1.7 copy.47
  147.7 33.1 %all-to-all-done.5 = bf16[64,40,128]{2,1,0:T(8,128)(2,1)S(1)} async-done(((bf16[64,40,128]{2,1,0:T(8,128)(2,1)}), bf16[64,40,128]{2,1,0:T(8,128)(2,1)S(1)}, u32[]{:S(2)}, u32[]{:S(2)}) %all-to-all-start.5) | async-done | bytes 655392 | tf_op jit(solution)/shard_map/all_to_all | solution.py:333
  180.9 2.4 gate_up.3
  183.3 4.3 %all-to-all-start.6 = ((bf16[4,80,1664]{2,1,0:T(8,128)(2,1)}), bf16[4,80,1664]{2,1,0:T(8,128)(2,1)}, u32[]{:S(2)}, u32[]{:S(2)}) async-start(bf16[4,80,1664]{2,1,0:T(8,128)(2,1)} %bitcast.26), calls=%async_computation.6 | async-start | bytes 2129920 | tf_op jit(solution)/shard_map/all_to_all | solution.py:85
  187.5 2.4 gate_up.2
  189.9 11.6 %all-to-all-done.6 = bf16[4,80,1664]{2,1,0:T(8,128)(2,1)} async-done(((bf16[4,80,1664]{2,1,0:T(8,128)(2,1)}), bf16[4,80,1664]{2,1,0:T(8,128)(2,1)}, u32[]{:S(2)}, u32[]{:S(2)}) %all-to-all-start.6) | async-done | bytes 1064992 | tf_op jit(solution)/shard_map/all_to_all | solution.py:85
  201.5 1.4 reduce_sum.74
  202.9 3.5 %all-to-all-start.7 = ((bf16[4,80,1664]{2,1,0:T(8,128)(2,1)}), bf16[4,80,1664]{2,1,0:T(8,128)(2,1)S(1)}, u32[]{:S(2)}, u32[]{:S(2)}) async-start(bf16[4,80,1664]{2,1,0:T(8,128)(2,1)} %bitcast.25), calls=%async_computation.7 | async-start | bytes 2129920 | tf_op jit(solution)/shard_map/all_to_all | solution.py:85
  206.4 9.2 %collective-permute-start.11 = (bf16[80,1664]{1,0:T(8,128)(2,1)S(1)}, bf16[80,1664]{1,0:T(8,128)(2,1)S(1)}, u32[]{:S(2)}, u32[]{:S(2)}) collective-permute-start(bf16[80,1664]{1,0:T(8,128)(2,1)S(1)} %reduce_sum.74), channel_id=1, source_target_pairs={{0,4},{4,0},{1,5},{5,1},{2,6},{6,2},{3,7},{7,3},{8,12},{12,8},{9,1... | collective-permute-start | bytes 798728 | tf_op jit(solution)/shard_map/ppermute | solution.py:26
  215.7 3.7 %all-to-all-done.7 = bf16[4,80,1664]{2,1,0:T(8,128)(2,1)S(1)} async-done(((bf16[4,80,1664]{2,1,0:T(8,128)(2,1)}), bf16[4,80,1664]{2,1,0:T(8,128)(2,1)S(1)}, u32[]{:S(2)}, u32[]{:S(2)}) %all-to-all-start.7) | async-done | bytes 1064992 | tf_op jit(solution)/shard_map/all_to_all | solution.py:85
  219.5 11.1 %collective-permute-done.11 = bf16[80,1664]{1,0:T(8,128)(2,1)S(1)} collective-permute-done((bf16[80,1664]{1,0:T(8,128)(2,1)S(1)}, bf16[80,1664]{1,0:T(8,128)(2,1)S(1)}, u32[]{:S(2)}, u32[]{:S(2)}) %collective-permute-start.11) | collective-permute-done | bytes 266272 | tf_op jit(solution)/shard_map/ppermute | solution.py:26
  231.1 12.4 %collective-permute-start.12 = (bf16[80,768]{1,0:T(8,128)(2,1)S(1)}, bf16[80,768]{1,0:T(8,128)(2,1)S(1)}, u32[]{:S(2)}, u32[]{:S(2)}) collective-permute-start(bf16[80,768]{1,0:T(8,128)(2,1)S(1)} %fusion.52), channel_id=1, source_target_pairs={{0,4},{4,0},{1,5},{5,1},{2,6},{6,2},{3,7},{7,3},{8,12},{12,8},{9,1... | collective-permute-start | bytes 368648 | tf_op jit(solution)/shard_map/ppermute | solution.py:26
  243.6 9.2 %collective-permute-done.12 = bf16[80,768]{1,0:T(8,128)(2,1)S(1)} collective-permute-done((bf16[80,768]{1,0:T(8,128)(2,1)S(1)}, bf16[80,768]{1,0:T(8,128)(2,1)S(1)}, u32[]{:S(2)}, u32[]{:S(2)}) %collective-permute-start.12) | collective-permute-done | bytes 122912 | tf_op jit(solution)/shard_map/ppermute | solution.py:26
  252.8 13.1 %all_gather.4 = bf16[4,2,80,768]{3,2,1,0:T(8,128)(2,1)S(1)} all-gather(bf16[1,2,80,768]{3,2,1,0:T(8,128)(2,1)S(1)} %maximum_select_fusion), channel_id=1, replica_groups=mesh['y'=4,'zl'=8,'core'=2,'zh'=2,'x'=4] {'x'}, dimensions={0}, use_global_device_ids=true | all-gather | bytes 1228800 | tf_op jit(solution)/shard_map/all_gather | solution.py:350
  265.9 2.3 down.1
  268.2 18.7 %all-to-all-start.8 = ((bf16[64,40,128]{2,1,0:T(8,128)(2,1)}), bf16[64,40,128]{2,1,0:T(8,128)(2,1)S(1)}, u32[]{:S(2)}, u32[]{:S(2)}) async-start(bf16[64,40,128]{2,1,0:T(8,128)(2,1)} %bitcast.31), calls=%async_computation.8 | async-start | bytes 1310720 | tf_op jit(solution)/shard_map/all_to_all | solution.py:352
  288.1 33.6 %all-to-all-done.8 = bf16[64,40,128]{2,1,0:T(8,128)(2,1)S(1)} async-done(((bf16[64,40,128]{2,1,0:T(8,128)(2,1)}), bf16[64,40,128]{2,1,0:T(8,128)(2,1)S(1)}, u32[]{:S(2)}, u32[]{:S(2)}) %all-to-all-start.8) | async-done | bytes 655392 | tf_op jit(solution)/shard_map/all_to_all | solution.py:352
  321.7 1.4 combine.1
  (74 shorter events, 13.6 us)
Async XLA Ops:
  1.5 20.0 %collective-permute-start.6 = (bf16[8,4096]{1,0:T(8,128)(2,1)S(1)}, bf16[8,4096]{1,0:T(8,128)(2,1)S(1)}, u32[]{:S(2)}, u32[]{:S(2)}) collective-permute-start(bf16[8,4096]{1,0:T(8,128)(2,1)S(1)} %reshape.140), channel_id=1, source_target_pairs={{0,64},{16,80},{32,96},{48,112},{64,0},{80,16},{96,32},{112,48},{1... | collective-permute-start | bytes 196616 | tf_op jit(solution)/shard_map/ppermute | solution.py:30
  12.1 23.7 %copy-start.1 = (bf16[128,4,128]{2,1,0:T(4,128)(2,1)S(1)}, bf16[128,4,128]{2,1,0:T(4,128)(2,1)}, u32[]{:S(2)}) copy-start(bf16[128,4,128]{2,1,0:T(4,128)(2,1)} %param.10) | copy-start | bytes 393220
  12.8 15.9 %all-to-all-start = ((bf16[8,2,32,128]{3,2,1,0:T(8,128)(2,1)}), bf16[8,2,32,128]{3,2,1,0:T(8,128)(2,1)S(1)}, u32[]{:S(2)}, u32[]{:S(2)}) async-start(bf16[8,2,32,128]{3,2,1,0:T(8,128)(2,1)} %broadcast_in_dim.25), calls=%async_computation | async-start | bytes 262144 | tf_op jit(solution)/shard_map/all_to_all | solution.py:258
  18.4 12.2 %collective-permute-start = (bf16[512,128]{1,0:T(8,128)(2,1)}, bf16[512,128]{1,0:T(8,128)(2,1)S(1)}, u32[]{:S(2)}, u32[]{:S(2)}) collective-permute-start(bf16[512,128]{1,0:T(8,128)(2,1)} %bitcast.62), channel_id=1, source_target_pairs={{0,1},{1,0},{2,3},{3,2},{4,5},{5,4},{6,7},{7,6},{8,9},{9,8},{10,11... | collective-permute-start | bytes 393224 | tf_op jit(solution)/shard_map/ppermute | solution.py:30
  28.7 11.7 %collective-permute-start.7 = (bf16[16,4096]{1,0:T(8,128)(2,1)S(1)}, bf16[16,4096]{1,0:T(8,128)(2,1)S(1)}, u32[]{:S(2)}, u32[]{:S(2)}) collective-permute-start(bf16[16,4096]{1,0:T(8,128)(2,1)S(1)} %pad_maximum_fusion.3), channel_id=1, source_target_pairs={{0,32},{16,48},{32,0},{48,16},{64,96},{80,112},{96,64},{112,80},{1... | collective-permute-start | bytes 393224 | tf_op jit(solution)/shard_map/ppermute | solution.py:30
  31.6 12.9 %all-to-all-start.1 = ((bf16[4,8,2,32,128]{4,3,1,2,0:T(8,128)(2,1)}), bf16[4,8,2,32,128]{4,3,1,2,0:T(8,128)(2,1)S(1)}, u32[]{:S(2)}, u32[]{:S(2)}) async-start(bf16[4,8,2,32,128]{4,3,1,2,0:T(8,128)(2,1)} %broadcast_in_dim.26), calls=%async_computation.1 | async-start | bytes 1048576 | tf_op jit(solution)/shard_map/all_to_all | solution.py:263
  35.8 8.7 %collective-permute-start.1 = (bf16[1024,128]{1,0:T(8,128)(2,1)S(1)}, bf16[1024,128]{1,0:T(8,128)(2,1)}, u32[]{:S(2)}, u32[]{:S(2)}) collective-permute-start(bf16[1024,128]{1,0:T(8,128)(2,1)S(1)} %pad_maximum_fusion.2), channel_id=1, source_target_pairs={{0,2},{1,3},{2,0},{3,1},{4,6},{5,7},{6,4},{7,5},{8,10},{9,11},{10,... | collective-permute-start | bytes 786440 | tf_op jit(solution)/shard_map/ppermute | solution.py:30
  40.5 11.0 %collective-permute-start.8 = (bf16[32,4096]{1,0:T(8,128)(2,1)S(1)}, bf16[32,4096]{1,0:T(8,128)(2,1)S(1)}, u32[]{:S(2)}, u32[]{:S(2)}) collective-permute-start(bf16[32,4096]{1,0:T(8,128)(2,1)S(1)} %constant_dynamic-update-slice_fusion), channel_id=1, source_target_pairs={{0,16},{16,0},{32,48},{48,32},{64,80},{80,64},{96,112},{112,96},{1... | collective-permute-start | bytes 786440 | tf_op jit(solution)/shard_map/ppermute | solution.py:30
  44.5 8.5 %collective-permute-start.2 = (bf16[4,8,2,32,128]{4,3,1,2,0:T(8,128)(2,1)S(1)}, bf16[4,8,2,32,128]{4,3,1,2,0:T(8,128)(2,1)S(1)}, u32[]{:S(2)}, u32[]{:S(2)}) collective-permute-start(bf16[4,8,2,32,128]{4,3,1,2,0:T(8,128)(2,1)S(1)} %all-to-all-done.1), channel_id=1, source_target_pairs={{0,8},{8,0},{1,9},{9,1},{2,10},{10,2},{3,11},{11,3},{4,12},{12,4},... | collective-permute-start | bytes 1572872 | tf_op jit(solution)/shard_map/ppermute | solution.py:26
  54.7 30.4 %all-to-all-start.2 = ((bf16[4,64,4096]{2,1,0:T(8,128)(2,1)}), bf16[4,64,4096]{2,1,0:T(8,128)(2,1)S(1)}, u32[]{:S(2)}, u32[]{:S(2)}) async-start(bf16[4,64,4096]{2,1,0:T(8,128)(2,1)} %broadcast_in_dim.30), calls=%async_computation.2 | async-start | bytes 4194304 | tf_op jit(solution)/shard_map/all_to_all | solution.py:276
  63.4 15.5 %copy-start.6 = (f32[128,8]{0,1:T(8,128)S(1)}, f32[128,8]{0,1:T(8,128)}, u32[]{:S(2)}) copy-start(f32[128,8]{0,1:T(8,128)} %param.16) | copy-start | bytes 12292
  63.4 20.8 %collective-permute-start.3 = (bf16[144,512]{1,0:T(8,128)(2,1)}, bf16[144,512]{1,0:T(8,128)(2,1)}, u32[]{:S(2)}, u32[]{:S(2)}) collective-permute-start(bf16[144,512]{1,0:T(8,128)(2,1)} %attend.4), channel_id=1, source_target_pairs={{0,1},{1,0},{2,3},{3,2},{4,5},{5,4},{6,7},{7,6},{8,9},{9,8},{10,11... | collective-permute-start | bytes 442376 | tf_op jit(solution)/shard_map/ppermute | solution.py:30
  69.6 14.6 %collective-permute-start.4 = (bf16[144,512]{1,0:T(8,128)(2,1)}, bf16[144,512]{1,0:T(8,128)(2,1)}, u32[]{:S(2)}, u32[]{:S(2)}) collective-permute-start(bf16[144,512]{1,0:T(8,128)(2,1)} %attend.5), channel_id=1, source_target_pairs={{0,3},{1,2},{2,1},{3,0},{4,7},{5,6},{6,5},{7,4},{8,11},{9,10},{10,... | collective-permute-start | bytes 442376 | tf_op jit(solution)/shard_map/ppermute | solution.py:30
  76.3 7.9 %collective-permute-start.5 = (bf16[144,512]{1,0:T(8,128)(2,1)}, bf16[144,512]{1,0:T(8,128)(2,1)}, u32[]{:S(2)}, u32[]{:S(2)}) collective-permute-start(bf16[144,512]{1,0:T(8,128)(2,1)} %attend.6), channel_id=1, source_target_pairs={{0,2},{1,3},{2,0},{3,1},{4,6},{5,7},{6,4},{7,5},{8,10},{9,11},{10,... | collective-permute-start | bytes 442376 | tf_op jit(solution)/shard_map/ppermute | solution.py:30
  85.1 7.2 %collective-permute-start.9 = (bf16[256,4096]{1,0:T(8,128)(2,1)S(1)}, bf16[256,4096]{1,0:T(8,128)(2,1)}, u32[]{:S(2)}, u32[]{:S(2)}) collective-permute-start(bf16[256,4096]{1,0:T(8,128)(2,1)S(1)} %bitcast.44), channel_id=1, source_target_pairs={{0,8},{8,0},{1,9},{9,1},{2,10},{10,2},{3,11},{11,3},{4,12},{12,4},... | collective-permute-start | bytes 6291464 | tf_op jit(solution)/shard_map/ppermute | solution.py:26
  90.9 0.8 copy-start.4
  91.0 0.7 copy-start.7
  94.7 12.9 %all-to-all-start.3 = ((bf16[4,128,512]{2,1,0:T(8,128)(2,1)}), bf16[4,128,512]{2,1,0:T(8,128)(2,1)S(1)}, u32[]{:S(2)}, u32[]{:S(2)}) async-start(bf16[4,128,512]{2,1,0:T(8,128)(2,1)} %project.3), calls=%async_computation.3 | async-start | bytes 1048576 | tf_op jit(solution)/shard_map/all_to_all | solution.py:85
  107.7 19.1 %copy-start.2 = (f32[512]{0:T(512)S(1)}, f32[512]{0:T(512)}, u32[]{:S(2)}) copy-start(f32[512]{0:T(512)} %param.14) | copy-start | bytes 6148
  107.7 19.1 %copy-start.5 = (bf16[128,512]{1,0:T(8,128)(2,1)S(1)}, bf16[128,512]{1,0:T(8,128)(2,1)}, u32[]{:S(2)}) copy-start(bf16[128,512]{1,0:T(8,128)(2,1)} %param.13) | copy-start | bytes 393220
  107.8 15.1 %all-to-all-start.4 = ((bf16[4,128,512]{2,1,0:T(8,128)(2,1)}), bf16[4,128,512]{2,1,0:T(8,128)(2,1)S(1)}, u32[]{:S(2)}, u32[]{:S(2)}) async-start(bf16[4,128,512]{2,1,0:T(8,128)(2,1)} %project.2), calls=%async_computation.4 | async-start | bytes 1048576 | tf_op jit(solution)/shard_map/all_to_all | solution.py:85
  111.7 17.2 %copy-start.3 = (f32[640,384]{1,0:T(8,128)}, f32[640,384]{1,0:T(8,128)S(1)}, u32[]{:S(2)}) copy-start(f32[640,384]{1,0:T(8,128)S(1)} %fusion.50) | copy-start | bytes 2949124
  111.9 15.0 %collective-permute-start.10 = (bf16[128,512]{1,0:T(8,128)(2,1)S(1)}, bf16[128,512]{1,0:T(8,128)(2,1)S(1)}, u32[]{:S(2)}, u32[]{:S(2)}) collective-permute-start(bf16[128,512]{1,0:T(8,128)(2,1)S(1)} %reduce_sum.72), channel_id=1, source_target_pairs={{0,4},{4,0},{1,5},{5,1},{2,6},{6,2},{3,7},{7,3},{8,12},{12,8},{9,1... | collective-permute-start | bytes 393224 | tf_op jit(solution)/shard_map/ppermute | solution.py:26
  128.9 52.0 %all-to-all-start.5 = ((bf16[64,40,128]{2,1,0:T(8,128)(2,1)}), bf16[64,40,128]{2,1,0:T(8,128)(2,1)S(1)}, u32[]{:S(2)}, u32[]{:S(2)}) async-start(bf16[64,40,128]{2,1,0:T(8,128)(2,1)} %bitcast.22), calls=%async_computation.5 | async-start | bytes 1310720 | tf_op jit(solution)/shard_map/all_to_all | solution.py:333
  183.3 18.2 %all-to-all-start.6 = ((bf16[4,80,1664]{2,1,0:T(8,128)(2,1)}), bf16[4,80,1664]{2,1,0:T(8,128)(2,1)}, u32[]{:S(2)}, u32[]{:S(2)}) async-start(bf16[4,80,1664]{2,1,0:T(8,128)(2,1)} %bitcast.26), calls=%async_computation.6 | async-start | bytes 2129920 | tf_op jit(solution)/shard_map/all_to_all | solution.py:85
  202.9 16.5 %all-to-all-start.7 = ((bf16[4,80,1664]{2,1,0:T(8,128)(2,1)}), bf16[4,80,1664]{2,1,0:T(8,128)(2,1)S(1)}, u32[]{:S(2)}, u32[]{:S(2)}) async-start(bf16[4,80,1664]{2,1,0:T(8,128)(2,1)} %bitcast.25), calls=%async_computation.7 | async-start | bytes 2129920 | tf_op jit(solution)/shard_map/all_to_all | solution.py:85
  206.4 24.2 %collective-permute-start.11 = (bf16[80,1664]{1,0:T(8,128)(2,1)S(1)}, bf16[80,1664]{1,0:T(8,128)(2,1)S(1)}, u32[]{:S(2)}, u32[]{:S(2)}) collective-permute-start(bf16[80,1664]{1,0:T(8,128)(2,1)S(1)} %reduce_sum.74), channel_id=1, source_target_pairs={{0,4},{4,0},{1,5},{5,1},{2,6},{6,2},{3,7},{7,3},{8,12},{12,8},{9,1... | collective-permute-start | bytes 798728 | tf_op jit(solution)/shard_map/ppermute | solution.py:26
  230.7 35.2 %copy-start = (bf16[1,768,512]{2,1,0:T(8,128)(2,1)S(1)}, bf16[1,768,512]{2,1,0:T(8,128)(2,1)}, u32[]{:S(2)}) copy-start(bf16[1,768,512]{2,1,0:T(8,128)(2,1)} %param.18) | copy-start | bytes 2359300
  231.1 21.7 %collective-permute-start.12 = (bf16[80,768]{1,0:T(8,128)(2,1)S(1)}, bf16[80,768]{1,0:T(8,128)(2,1)S(1)}, u32[]{:S(2)}, u32[]{:S(2)}) collective-permute-start(bf16[80,768]{1,0:T(8,128)(2,1)S(1)} %fusion.52), channel_id=1, source_target_pairs={{0,4},{4,0},{1,5},{5,1},{2,6},{6,2},{3,7},{7,3},{8,12},{12,8},{9,1... | collective-permute-start | bytes 368648 | tf_op jit(solution)/shard_map/ppermute | solution.py:26
  268.2 53.5 %all-to-all-start.8 = ((bf16[64,40,128]{2,1,0:T(8,128)(2,1)}), bf16[64,40,128]{2,1,0:T(8,128)(2,1)S(1)}, u32[]{:S(2)}, u32[]{:S(2)}) async-start(bf16[64,40,128]{2,1,0:T(8,128)(2,1)} %bitcast.31), calls=%async_computation.8 | async-start | bytes 1310720 | tf_op jit(solution)/shard_map/all_to_all | solution.py:352

commit v9 on v8

--- a/solution.py
+++ b/solution.py
@@ -257,11 +257,11 @@
     line = jnp.concatenate([line, partner(line, "zl", 4)], axis=0)
     pair = first = lax.all_to_all(pair, "zl", 0, 0, tiled=True)
     rows = queries.reshape(tokens * heads, size)
-    beside = partner(rows, "x", 1)
+    beside = partner(rows, "x", 2)
     pair = after(pair, beside)
     pair = jnp.broadcast_to(pair[None], (4,) + pair.shape)
     pair = second = lax.all_to_all(pair, "y", 0, 0, tiled=True)
-    across = partner(jnp.concatenate([beside, after(rows, first)], axis=0), "x", 2)
+    across = partner(jnp.concatenate([beside, after(rows, first)], axis=0), "x", 1)
     line = double(line, 2, first)
     found = partner(line, "zl", 1)
     line = jnp.concatenate([after(line, second), found], axis=0)
@@ -275,7 +275,7 @@
     line = jnp.broadcast_to(line[None], (4,) + line.shape)
     near = lax.all_to_all(line, "y", 0, 0, tiled=True).reshape(-1, D)
     parts, found = [], place
-    asked = [(1, beside), (3, across[: tokens * heads]), (2, across[tokens * heads :])]
+    asked = [(2, beside), (3, across[: tokens * heads]), (1, across[tokens * heads :])]
     for bit, theirs in asked:
         theirs = after(theirs, found)
         found = attend(place, theirs, all_keys, all_values, heads, piece, tokens)

time: 325 us -> 322 us (level)
  no operation moved by 1% of the time
where the time goes in v9:
time: 322 us; the launch traced here: 321 us
  starting transfers between devices  139 us (43%)
  waiting for transfers between devices  126 us (39%)
  Pallas kernels  26.7 us (8%)
  blocking collectives  13.1 us (4%)
  local copies, waits for them, and re-layouts  7.9 us (2%)
  other arithmetic  6.36 us (2%)
    ppermute x5, starting transfers between devices, shift(): lax.ppermute(value, axis, [(i, (i + step) % count) for i in range(count)])  42.8 us
    all_to_all x1, waiting for transfers between devices, body(): lax.all_to_all(result, CTX, 0, 0, tiled=True).reshape(4 * slots, lanes)  33.6 us
    all_to_all x1, waiting for transfers between devices, body(): lax.all_to_all(outgoing, CTX, 0, 0, tiled=True).reshape(4 * slots, lanes)  33.1 us
    ppermute x8, starting transfers between devices, partner(): return lax.ppermute(value, axis, [(i, i ^ bit) for i in range(SIZES[axis])])  31.4 us
    ppermute x5, waiting for transfers between devices, shift(): lax.ppermute(value, axis, [(i, (i + step) % count) for i in range(count)])  26.2 us
    all_to_all x4, waiting for transfers between devices, sum_along_x(): lax.all_to_all(parts, 'x', 0, 0, tiled=True).astype(F32)  21.6 us
    all_to_all x1, starting transfers between devices, body(): lax.all_to_all(result, CTX, 0, 0, tiled=True).reshape(4 * slots, lanes)  18.5 us
    all_to_all x1, starting transfers between devices, body(): lax.all_to_all(outgoing, CTX, 0, 0, tiled=True).reshape(4 * slots, lanes)  16.2 us
  transfers between devices with their start and end apart: 22, of which 14 were waited for; matrix products, arithmetic and copies ran while one was open for 3% of the time, Pallas kernels for 5%

profile of v9, /device:TPU:1, one launch (start us, length us, event | category | flops | bytes accessed | tf_op | source)
XLA Modules:
  0.0 320.5 jit_solution(6708218819726503064)
XLA Ops:
  1.5 9.6 %collective-permute-start.6 = (bf16[8,4096]{1,0:T(8,128)(2,1)S(1)}, bf16[8,4096]{1,0:T(8,128)(2,1)S(1)}, u32[]{:S(2)}, u32[]{:S(2)}) collective-permute-start(bf16[8,4096]{1,0:T(8,128)(2,1)S(1)} %reshape.140), channel_id=1, source_target_pairs={{0,64},{16,80},{32,96},{48,112},{64,0},{80,16},{96,32},{112,48},{1... | collective-permute-start | bytes 196616 | tf_op jit(solution)/shard_map/ppermute | solution.py:30
  12.8 5.6 %all-to-all-start = ((bf16[8,2,32,128]{3,2,1,0:T(8,128)(2,1)}), bf16[8,2,32,128]{3,2,1,0:T(8,128)(2,1)S(1)}, u32[]{:S(2)}, u32[]{:S(2)}) async-start(bf16[8,2,32,128]{3,2,1,0:T(8,128)(2,1)} %broadcast_in_dim.25), calls=%async_computation | async-start | bytes 262144 | tf_op jit(solution)/shard_map/all_to_all | solution.py:258
  18.4 4.6 %collective-permute-start = (bf16[512,128]{1,0:T(8,128)(2,1)}, bf16[512,128]{1,0:T(8,128)(2,1)S(1)}, u32[]{:S(2)}, u32[]{:S(2)}) collective-permute-start(bf16[512,128]{1,0:T(8,128)(2,1)} %bitcast.62), channel_id=1, source_target_pairs={{0,2},{1,3},{2,0},{3,1},{4,6},{5,7},{6,4},{7,5},{8,10},{9,11},{10,... | collective-permute-start | bytes 393224 | tf_op jit(solution)/shard_map/ppermute | solution.py:30
  23.1 5.6 %all-to-all-done = bf16[8,2,32,128]{3,2,1,0:T(8,128)(2,1)S(1)} async-done(((bf16[8,2,32,128]{3,2,1,0:T(8,128)(2,1)}), bf16[8,2,32,128]{3,2,1,0:T(8,128)(2,1)S(1)}, u32[]{:S(2)}, u32[]{:S(2)}) %all-to-all-start) | async-done | bytes 131104 | tf_op jit(solution)/shard_map/all_to_all | solution.py:258
  28.7 1.9 collective-permute-start.7
  31.6 4.2 %all-to-all-start.1 = ((bf16[4,8,2,32,128]{4,3,1,2,0:T(8,128)(2,1)}), bf16[4,8,2,32,128]{4,3,1,2,0:T(8,128)(2,1)S(1)}, u32[]{:S(2)}, u32[]{:S(2)}) async-start(bf16[4,8,2,32,128]{4,3,1,2,0:T(8,128)(2,1)} %broadcast_in_dim.26), calls=%async_computation.1 | async-start | bytes 1048576 | tf_op jit(solution)/shard_map/all_to_all | solution.py:263
  35.8 3.1 collective-permute-start.1
  38.9 2.7 collective-permute-start.8
  41.6 1.6 collective-permute-done.1
  43.2 6.8 %collective-permute-start.2 = (bf16[4,8,2,32,128]{4,3,1,2,0:T(8,128)(2,1)S(1)}, bf16[4,8,2,32,128]{4,3,1,2,0:T(8,128)(2,1)S(1)}, u32[]{:S(2)}, u32[]{:S(2)}) collective-permute-start(bf16[4,8,2,32,128]{4,3,1,2,0:T(8,128)(2,1)S(1)} %all-to-all-done.1), channel_id=1, source_target_pairs={{0,8},{8,0},{1,9},{9,1},{2,10},{10,2},{3,11},{11,3},{4,12},{12,4},... | collective-permute-start | bytes 1572872 | tf_op jit(solution)/shard_map/ppermute | solution.py:26
  50.1 1.5 collective-permute-done.2
  51.6 1.6 broadcast_in_dim.30
  53.2 4.5 %all-to-all-start.2 = ((bf16[4,64,4096]{2,1,0:T(8,128)(2,1)}), bf16[4,64,4096]{2,1,0:T(8,128)(2,1)S(1)}, u32[]{:S(2)}, u32[]{:S(2)}) async-start(bf16[4,64,4096]{2,1,0:T(8,128)(2,1)} %broadcast_in_dim.30), calls=%async_computation.2 | async-start | bytes 4194304 | tf_op jit(solution)/shard_map/all_to_all | solution.py:276
  58.9 3.0 attend.4
  61.9 4.8 %collective-permute-start.3 = (bf16[144,512]{1,0:T(8,128)(2,1)}, bf16[144,512]{1,0:T(8,128)(2,1)}, u32[]{:S(2)}, u32[]{:S(2)}) collective-permute-start(bf16[144,512]{1,0:T(8,128)(2,1)} %attend.4), channel_id=1, source_target_pairs={{0,2},{1,3},{2,0},{3,1},{4,6},{5,7},{6,4},{7,5},{8,10},{9,11},{10,... | collective-permute-start | bytes 442376 | tf_op jit(solution)/shard_map/ppermute | solution.py:30
  66.6 3.0 attend.5
  69.6 2.8 collective-permute-start.4
  72.4 3.0 attend.6
  75.4 1.9 collective-permute-start.5
  77.4 2.3 attend.7
  79.7 2.1 collective-permute-done.5
  81.8 1.7 all-to-all-done.2
  83.5 3.4 %collective-permute-start.9 = (bf16[256,4096]{1,0:T(8,128)(2,1)S(1)}, bf16[256,4096]{1,0:T(8,128)(2,1)}, u32[]{:S(2)}, u32[]{:S(2)}) collective-permute-start(bf16[256,4096]{1,0:T(8,128)(2,1)S(1)} %bitcast.44), channel_id=1, source_target_pairs={{0,8},{8,0},{1,9},{9,1},{2,10},{10,2},{3,11},{11,3},{4,12},{12,4},... | collective-permute-start | bytes 6291464 | tf_op jit(solution)/shard_map/ppermute | solution.py:26
  90.8 2.4 project.3
  93.2 4.0 %all-to-all-start.3 = ((bf16[4,128,512]{2,1,0:T(8,128)(2,1)}), bf16[4,128,512]{2,1,0:T(8,128)(2,1)S(1)}, u32[]{:S(2)}, u32[]{:S(2)}) async-start(bf16[4,128,512]{2,1,0:T(8,128)(2,1)} %project.3), calls=%async_computation.3 | async-start | bytes 1048576 | tf_op jit(solution)/shard_map/all_to_all | solution.py:85
  97.4 2.5 project.2
  99.9 6.3 %all-to-all-done.3 = bf16[4,128,512]{2,1,0:T(8,128)(2,1)S(1)} async-done(((bf16[4,128,512]{2,1,0:T(8,128)(2,1)}), bf16[4,128,512]{2,1,0:T(8,128)(2,1)S(1)}, u32[]{:S(2)}, u32[]{:S(2)}) %all-to-all-start.3) | async-done | bytes 524320 | tf_op jit(solution)/shard_map/all_to_all | solution.py:85
  106.3 3.6 %all-to-all-start.4 = ((bf16[4,128,512]{2,1,0:T(8,128)(2,1)}), bf16[4,128,512]{2,1,0:T(8,128)(2,1)S(1)}, u32[]{:S(2)}, u32[]{:S(2)}) async-start(bf16[4,128,512]{2,1,0:T(8,128)(2,1)} %project.2), calls=%async_computation.4 | async-start | bytes 1048576 | tf_op jit(solution)/shard_map/all_to_all | solution.py:85
  110.4 10.9 %collective-permute-start.10 = (bf16[128,512]{1,0:T(8,128)(2,1)S(1)}, bf16[128,512]{1,0:T(8,128)(2,1)S(1)}, u32[]{:S(2)}, u32[]{:S(2)}) collective-permute-start(bf16[128,512]{1,0:T(8,128)(2,1)S(1)} %reduce_sum.72), channel_id=1, source_target_pairs={{0,4},{4,0},{1,5},{5,1},{2,6},{6,2},{3,7},{7,3},{8,12},{12,8},{9,1... | collective-permute-start | bytes 393224 | tf_op jit(solution)/shard_map/ppermute | solution.py:26
  121.4 3.9 %collective-permute-done.10 = bf16[128,512]{1,0:T(8,128)(2,1)S(1)} collective-permute-done((bf16[128,512]{1,0:T(8,128)(2,1)S(1)}, bf16[128,512]{1,0:T(8,128)(2,1)S(1)}, u32[]{:S(2)}, u32[]{:S(2)}) %collective-permute-start.10) | collective-permute-done | bytes 131104 | tf_op jit(solution)/shard_map/ppermute | solution.py:26
  125.4 2.0 dispatch.1
  127.4 16.2 %all-to-all-start.5 = ((bf16[64,40,128]{2,1,0:T(8,128)(2,1)}), bf16[64,40,128]{2,1,0:T(8,128)(2,1)S(1)}, u32[]{:S(2)}, u32[]{:S(2)}) async-start(bf16[64,40,128]{2,1,0:T(8,128)(2,1)} %bitcast.22), calls=%async_computation.5 | async-start | bytes 1310720 | tf_op jit(solution)/shard_map/all_to_all | solution.py:333
  143.7 1.7 copy.47
  145.3 33.1 %all-to-all-done.5 = bf16[64,40,128]{2,1,0:T(8,128)(2,1)S(1)} async-done(((bf16[64,40,128]{2,1,0:T(8,128)(2,1)}), bf16[64,40,128]{2,1,0:T(8,128)(2,1)S(1)}, u32[]{:S(2)}, u32[]{:S(2)}) %all-to-all-start.5) | async-done | bytes 655392 | tf_op jit(solution)/shard_map/all_to_all | solution.py:333
  178.4 2.4 gate_up.3
  180.8 4.3 %all-to-all-start.6 = ((bf16[4,80,1664]{2,1,0:T(8,128)(2,1)}), bf16[4,80,1664]{2,1,0:T(8,128)(2,1)}, u32[]{:S(2)}, u32[]{:S(2)}) async-start(bf16[4,80,1664]{2,1,0:T(8,128)(2,1)} %bitcast.26), calls=%async_computation.6 | async-start | bytes 2129920 | tf_op jit(solution)/shard_map/all_to_all | solution.py:85
  185.1 2.4 gate_up.2
  187.5 11.6 %all-to-all-done.6 = bf16[4,80,1664]{2,1,0:T(8,128)(2,1)} async-done(((bf16[4,80,1664]{2,1,0:T(8,128)(2,1)}), bf16[4,80,1664]{2,1,0:T(8,128)(2,1)}, u32[]{:S(2)}, u32[]{:S(2)}) %all-to-all-start.6) | async-done | bytes 1064992 | tf_op jit(solution)/shard_map/all_to_all | solution.py:85
  200.5 3.5 %all-to-all-start.7 = ((bf16[4,80,1664]{2,1,0:T(8,128)(2,1)}), bf16[4,80,1664]{2,1,0:T(8,128)(2,1)S(1)}, u32[]{:S(2)}, u32[]{:S(2)}) async-start(bf16[4,80,1664]{2,1,0:T(8,128)(2,1)} %bitcast.25), calls=%async_computation.7 | async-start | bytes 2129920 | tf_op jit(solution)/shard_map/all_to_all | solution.py:85
  204.0 9.3 %collective-permute-start.11 = (bf16[80,1664]{1,0:T(8,128)(2,1)S(1)}, bf16[80,1664]{1,0:T(8,128)(2,1)S(1)}, u32[]{:S(2)}, u32[]{:S(2)}) collective-permute-start(bf16[80,1664]{1,0:T(8,128)(2,1)S(1)} %reduce_sum.74), channel_id=1, source_target_pairs={{0,4},{4,0},{1,5},{5,1},{2,6},{6,2},{3,7},{7,3},{8,12},{12,8},{9,1... | collective-permute-start | bytes 798728 | tf_op jit(solution)/shard_map/ppermute | solution.py:26
  213.3 3.7 %all-to-all-done.7 = bf16[4,80,1664]{2,1,0:T(8,128)(2,1)S(1)} async-done(((bf16[4,80,1664]{2,1,0:T(8,128)(2,1)}), bf16[4,80,1664]{2,1,0:T(8,128)(2,1)S(1)}, u32[]{:S(2)}, u32[]{:S(2)}) %all-to-all-start.7) | async-done | bytes 1064992 | tf_op jit(solution)/shard_map/all_to_all | solution.py:85
  217.1 11.0 %collective-permute-done.11 = bf16[80,1664]{1,0:T(8,128)(2,1)S(1)} collective-permute-done((bf16[80,1664]{1,0:T(8,128)(2,1)S(1)}, bf16[80,1664]{1,0:T(8,128)(2,1)S(1)}, u32[]{:S(2)}, u32[]{:S(2)}) %collective-permute-start.11) | collective-permute-done | bytes 266272 | tf_op jit(solution)/shard_map/ppermute | solution.py:26
  228.6 12.4 %collective-permute-start.12 = (bf16[80,768]{1,0:T(8,128)(2,1)S(1)}, bf16[80,768]{1,0:T(8,128)(2,1)S(1)}, u32[]{:S(2)}, u32[]{:S(2)}) collective-permute-start(bf16[80,768]{1,0:T(8,128)(2,1)S(1)} %fusion.52), channel_id=1, source_target_pairs={{0,4},{4,0},{1,5},{5,1},{2,6},{6,2},{3,7},{7,3},{8,12},{12,8},{9,1... | collective-permute-start | bytes 368648 | tf_op jit(solution)/shard_map/ppermute | solution.py:26
  241.1 9.2 %collective-permute-done.12 = bf16[80,768]{1,0:T(8,128)(2,1)S(1)} collective-permute-done((bf16[80,768]{1,0:T(8,128)(2,1)S(1)}, bf16[80,768]{1,0:T(8,128)(2,1)S(1)}, u32[]{:S(2)}, u32[]{:S(2)}) %collective-permute-start.12) | collective-permute-done | bytes 122912 | tf_op jit(solution)/shard_map/ppermute | solution.py:26
  250.4 13.1 %all_gather.4 = bf16[4,2,80,768]{3,2,1,0:T(8,128)(2,1)S(1)} all-gather(bf16[1,2,80,768]{3,2,1,0:T(8,128)(2,1)S(1)} %maximum_select_fusion), channel_id=1, replica_groups=mesh['y'=4,'zl'=8,'core'=2,'zh'=2,'x'=4] {'x'}, dimensions={0}, use_global_device_ids=true | all-gather | bytes 1228800 | tf_op jit(solution)/shard_map/all_gather | solution.py:350
  263.5 2.3 down.1
  265.8 18.5 %all-to-all-start.8 = ((bf16[64,40,128]{2,1,0:T(8,128)(2,1)}), bf16[64,40,128]{2,1,0:T(8,128)(2,1)S(1)}, u32[]{:S(2)}, u32[]{:S(2)}) async-start(bf16[64,40,128]{2,1,0:T(8,128)(2,1)} %bitcast.31), calls=%async_computation.8 | async-start | bytes 1310720 | tf_op jit(solution)/shard_map/all_to_all | solution.py:352
  285.5 33.6 %all-to-all-done.8 = bf16[64,40,128]{2,1,0:T(8,128)(2,1)S(1)} async-done(((bf16[64,40,128]{2,1,0:T(8,128)(2,1)}), bf16[64,40,128]{2,1,0:T(8,128)(2,1)S(1)}, u32[]{:S(2)}, u32[]{:S(2)}) %all-to-all-start.8) | async-done | bytes 655392 | tf_op jit(solution)/shard_map/all_to_all | solution.py:352
  (74 shorter events, 14.1 us)
Async XLA Ops:
  1.5 21.6 %collective-permute-start.6 = (bf16[8,4096]{1,0:T(8,128)(2,1)S(1)}, bf16[8,4096]{1,0:T(8,128)(2,1)S(1)}, u32[]{:S(2)}, u32[]{:S(2)}) collective-permute-start(bf16[8,4096]{1,0:T(8,128)(2,1)S(1)} %reshape.140), channel_id=1, source_target_pairs={{0,64},{16,80},{32,96},{48,112},{64,0},{80,16},{96,32},{112,48},{1... | collective-permute-start | bytes 196616 | tf_op jit(solution)/shard_map/ppermute | solution.py:30
  12.1 23.7 %copy-start.1 = (bf16[128,4,128]{2,1,0:T(4,128)(2,1)S(1)}, bf16[128,4,128]{2,1,0:T(4,128)(2,1)}, u32[]{:S(2)}) copy-start(bf16[128,4,128]{2,1,0:T(4,128)(2,1)} %param.10) | copy-start | bytes 393220
  12.8 15.9 %all-to-all-start = ((bf16[8,2,32,128]{3,2,1,0:T(8,128)(2,1)}), bf16[8,2,32,128]{3,2,1,0:T(8,128)(2,1)S(1)}, u32[]{:S(2)}, u32[]{:S(2)}) async-start(bf16[8,2,32,128]{3,2,1,0:T(8,128)(2,1)} %broadcast_in_dim.25), calls=%async_computation | async-start | bytes 262144 | tf_op jit(solution)/shard_map/all_to_all | solution.py:258
  18.4 12.2 %collective-permute-start = (bf16[512,128]{1,0:T(8,128)(2,1)}, bf16[512,128]{1,0:T(8,128)(2,1)S(1)}, u32[]{:S(2)}, u32[]{:S(2)}) collective-permute-start(bf16[512,128]{1,0:T(8,128)(2,1)} %bitcast.62), channel_id=1, source_target_pairs={{0,2},{1,3},{2,0},{3,1},{4,6},{5,7},{6,4},{7,5},{8,10},{9,11},{10,... | collective-permute-start | bytes 393224 | tf_op jit(solution)/shard_map/ppermute | solution.py:30
  28.7 10.2 %collective-permute-start.7 = (bf16[16,4096]{1,0:T(8,128)(2,1)S(1)}, bf16[16,4096]{1,0:T(8,128)(2,1)S(1)}, u32[]{:S(2)}, u32[]{:S(2)}) collective-permute-start(bf16[16,4096]{1,0:T(8,128)(2,1)S(1)} %pad_maximum_fusion.3), channel_id=1, source_target_pairs={{0,32},{16,48},{32,0},{48,16},{64,96},{80,112},{96,64},{112,80},{1... | collective-permute-start | bytes 393224 | tf_op jit(solution)/shard_map/ppermute | solution.py:30
  31.6 11.6 %all-to-all-start.1 = ((bf16[4,8,2,32,128]{4,3,1,2,0:T(8,128)(2,1)}), bf16[4,8,2,32,128]{4,3,1,2,0:T(8,128)(2,1)S(1)}, u32[]{:S(2)}, u32[]{:S(2)}) async-start(bf16[4,8,2,32,128]{4,3,1,2,0:T(8,128)(2,1)} %broadcast_in_dim.26), calls=%async_computation.1 | async-start | bytes 1048576 | tf_op jit(solution)/shard_map/all_to_all | solution.py:263
  35.8 7.4 %collective-permute-start.1 = (bf16[1024,128]{1,0:T(8,128)(2,1)S(1)}, bf16[1024,128]{1,0:T(8,128)(2,1)}, u32[]{:S(2)}, u32[]{:S(2)}) collective-permute-start(bf16[1024,128]{1,0:T(8,128)(2,1)S(1)} %pad_maximum_fusion.2), channel_id=1, source_target_pairs={{0,1},{1,0},{2,3},{3,2},{4,5},{5,4},{6,7},{7,6},{8,9},{9,8},{10,11... | collective-permute-start | bytes 786440 | tf_op jit(solution)/shard_map/ppermute | solution.py:30
  38.9 11.1 %collective-permute-start.8 = (bf16[32,4096]{1,0:T(8,128)(2,1)S(1)}, bf16[32,4096]{1,0:T(8,128)(2,1)S(1)}, u32[]{:S(2)}, u32[]{:S(2)}) collective-permute-start(bf16[32,4096]{1,0:T(8,128)(2,1)S(1)} %constant_dynamic-update-slice_fusion), channel_id=1, source_target_pairs={{0,16},{16,0},{32,48},{48,32},{64,80},{80,64},{96,112},{112,96},{1... | collective-permute-start | bytes 786440 | tf_op jit(solution)/shard_map/ppermute | solution.py:30
  43.2 8.3 %collective-permute-start.2 = (bf16[4,8,2,32,128]{4,3,1,2,0:T(8,128)(2,1)S(1)}, bf16[4,8,2,32,128]{4,3,1,2,0:T(8,128)(2,1)S(1)}, u32[]{:S(2)}, u32[]{:S(2)}) collective-permute-start(bf16[4,8,2,32,128]{4,3,1,2,0:T(8,128)(2,1)S(1)} %all-to-all-done.1), channel_id=1, source_target_pairs={{0,8},{8,0},{1,9},{9,1},{2,10},{10,2},{3,11},{11,3},{4,12},{12,4},... | collective-permute-start | bytes 1572872 | tf_op jit(solution)/shard_map/ppermute | solution.py:26
  53.2 30.3 %all-to-all-start.2 = ((bf16[4,64,4096]{2,1,0:T(8,128)(2,1)}), bf16[4,64,4096]{2,1,0:T(8,128)(2,1)S(1)}, u32[]{:S(2)}, u32[]{:S(2)}) async-start(bf16[4,64,4096]{2,1,0:T(8,128)(2,1)} %broadcast_in_dim.30), calls=%async_computation.2 | async-start | bytes 4194304 | tf_op jit(solution)/shard_map/all_to_all | solution.py:276
  61.9 15.5 %copy-start.6 = (f32[128,8]{0,1:T(8,128)S(1)}, f32[128,8]{0,1:T(8,128)}, u32[]{:S(2)}) copy-start(f32[128,8]{0,1:T(8,128)} %param.16) | copy-start | bytes 12292
  61.9 19.9 %collective-permute-start.3 = (bf16[144,512]{1,0:T(8,128)(2,1)}, bf16[144,512]{1,0:T(8,128)(2,1)}, u32[]{:S(2)}, u32[]{:S(2)}) collective-permute-start(bf16[144,512]{1,0:T(8,128)(2,1)} %attend.4), channel_id=1, source_target_pairs={{0,2},{1,3},{2,0},{3,1},{4,6},{5,7},{6,4},{7,5},{8,10},{9,11},{10,... | collective-permute-start | bytes 442376 | tf_op jit(solution)/shard_map/ppermute | solution.py:30
  69.6 12.1 %collective-permute-start.4 = (bf16[144,512]{1,0:T(8,128)(2,1)}, bf16[144,512]{1,0:T(8,128)(2,1)}, u32[]{:S(2)}, u32[]{:S(2)}) collective-permute-start(bf16[144,512]{1,0:T(8,128)(2,1)} %attend.5), channel_id=1, source_target_pairs={{0,3},{1,2},{2,1},{3,0},{4,7},{5,6},{6,5},{7,4},{8,11},{9,10},{10,... | collective-permute-start | bytes 442376 | tf_op jit(solution)/shard_map/ppermute | solution.py:30
  75.4 6.4 %collective-permute-start.5 = (bf16[144,512]{1,0:T(8,128)(2,1)}, bf16[144,512]{1,0:T(8,128)(2,1)}, u32[]{:S(2)}, u32[]{:S(2)}) collective-permute-start(bf16[144,512]{1,0:T(8,128)(2,1)} %attend.6), channel_id=1, source_target_pairs={{0,1},{1,0},{2,3},{3,2},{4,5},{5,4},{6,7},{7,6},{8,9},{9,8},{10,11... | collective-permute-start | bytes 442376 | tf_op jit(solution)/shard_map/ppermute | solution.py:30
  83.5 7.3 %collective-permute-start.9 = (bf16[256,4096]{1,0:T(8,128)(2,1)S(1)}, bf16[256,4096]{1,0:T(8,128)(2,1)}, u32[]{:S(2)}, u32[]{:S(2)}) collective-permute-start(bf16[256,4096]{1,0:T(8,128)(2,1)S(1)} %bitcast.44), channel_id=1, source_target_pairs={{0,8},{8,0},{1,9},{9,1},{2,10},{10,2},{3,11},{11,3},{4,12},{12,4},... | collective-permute-start | bytes 6291464 | tf_op jit(solution)/shard_map/ppermute | solution.py:26
  89.4 0.8 copy-start.4
  89.5 0.7 copy-start.7
  93.2 12.9 %all-to-all-start.3 = ((bf16[4,128,512]{2,1,0:T(8,128)(2,1)}), bf16[4,128,512]{2,1,0:T(8,128)(2,1)S(1)}, u32[]{:S(2)}, u32[]{:S(2)}) async-start(bf16[4,128,512]{2,1,0:T(8,128)(2,1)} %project.3), calls=%async_computation.3 | async-start | bytes 1048576 | tf_op jit(solution)/shard_map/all_to_all | solution.py:85
  106.2 19.1 %copy-start.2 = (f32[512]{0:T(512)S(1)}, f32[512]{0:T(512)}, u32[]{:S(2)}) copy-start(f32[512]{0:T(512)} %param.14) | copy-start | bytes 6148
  106.3 19.1 %copy-start.5 = (bf16[128,512]{1,0:T(8,128)(2,1)S(1)}, bf16[128,512]{1,0:T(8,128)(2,1)}, u32[]{:S(2)}) copy-start(bf16[128,512]{1,0:T(8,128)(2,1)} %param.13) | copy-start | bytes 393220
  106.3 15.1 %all-to-all-start.4 = ((bf16[4,128,512]{2,1,0:T(8,128)(2,1)}), bf16[4,128,512]{2,1,0:T(8,128)(2,1)S(1)}, u32[]{:S(2)}, u32[]{:S(2)}) async-start(bf16[4,128,512]{2,1,0:T(8,128)(2,1)} %project.2), calls=%async_computation.4 | async-start | bytes 1048576 | tf_op jit(solution)/shard_map/all_to_all | solution.py:85
  110.2 17.2 %copy-start.3 = (f32[640,384]{1,0:T(8,128)}, f32[640,384]{1,0:T(8,128)S(1)}, u32[]{:S(2)}) copy-start(f32[640,384]{1,0:T(8,128)S(1)} %fusion.50) | copy-start | bytes 2949124
  110.4 15.0 %collective-permute-start.10 = (bf16[128,512]{1,0:T(8,128)(2,1)S(1)}, bf16[128,512]{1,0:T(8,128)(2,1)S(1)}, u32[]{:S(2)}, u32[]{:S(2)}) collective-permute-start(bf16[128,512]{1,0:T(8,128)(2,1)S(1)} %reduce_sum.72), channel_id=1, source_target_pairs={{0,4},{4,0},{1,5},{5,1},{2,6},{6,2},{3,7},{7,3},{8,12},{12,8},{9,1... | collective-permute-start | bytes 393224 | tf_op jit(solution)/shard_map/ppermute | solution.py:26
  127.4 51.0 %all-to-all-start.5 = ((bf16[64,40,128]{2,1,0:T(8,128)(2,1)}), bf16[64,40,128]{2,1,0:T(8,128)(2,1)S(1)}, u32[]{:S(2)}, u32[]{:S(2)}) async-start(bf16[64,40,128]{2,1,0:T(8,128)(2,1)} %bitcast.22), calls=%async_computation.5 | async-start | bytes 1310720 | tf_op jit(solution)/shard_map/all_to_all | solution.py:333
  180.8 18.2 %all-to-all-start.6 = ((bf16[4,80,1664]{2,1,0:T(8,128)(2,1)}), bf16[4,80,1664]{2,1,0:T(8,128)(2,1)}, u32[]{:S(2)}, u32[]{:S(2)}) async-start(bf16[4,80,1664]{2,1,0:T(8,128)(2,1)} %bitcast.26), calls=%async_computation.6 | async-start | bytes 2129920 | tf_op jit(solution)/shard_map/all_to_all | solution.py:85
  200.5 16.5 %all-to-all-start.7 = ((bf16[4,80,1664]{2,1,0:T(8,128)(2,1)}), bf16[4,80,1664]{2,1,0:T(8,128)(2,1)S(1)}, u32[]{:S(2)}, u32[]{:S(2)}) async-start(bf16[4,80,1664]{2,1,0:T(8,128)(2,1)} %bitcast.25), calls=%async_computation.7 | async-start | bytes 2129920 | tf_op jit(solution)/shard_map/all_to_all | solution.py:85
  204.0 24.1 %collective-permute-start.11 = (bf16[80,1664]{1,0:T(8,128)(2,1)S(1)}, bf16[80,1664]{1,0:T(8,128)(2,1)S(1)}, u32[]{:S(2)}, u32[]{:S(2)}) collective-permute-start(bf16[80,1664]{1,0:T(8,128)(2,1)S(1)} %reduce_sum.74), channel_id=1, source_target_pairs={{0,4},{4,0},{1,5},{5,1},{2,6},{6,2},{3,7},{7,3},{8,12},{12,8},{9,1... | collective-permute-start | bytes 798728 | tf_op jit(solution)/shard_map/ppermute | solution.py:26
  228.2 35.3 %copy-start = (bf16[1,768,512]{2,1,0:T(8,128)(2,1)S(1)}, bf16[1,768,512]{2,1,0:T(8,128)(2,1)}, u32[]{:S(2)}) copy-start(bf16[1,768,512]{2,1,0:T(8,128)(2,1)} %param.18) | copy-start | bytes 2359300
  228.6 21.8 %collective-permute-start.12 = (bf16[80,768]{1,0:T(8,128)(2,1)S(1)}, bf16[80,768]{1,0:T(8,128)(2,1)S(1)}, u32[]{:S(2)}, u32[]{:S(2)}) collective-permute-start(bf16[80,768]{1,0:T(8,128)(2,1)S(1)} %fusion.52), channel_id=1, source_target_pairs={{0,4},{4,0},{1,5},{5,1},{2,6},{6,2},{3,7},{7,3},{8,12},{12,8},{9,1... | collective-permute-start | bytes 368648 | tf_op jit(solution)/shard_map/ppermute | solution.py:26
  265.8 53.3 %all-to-all-start.8 = ((bf16[64,40,128]{2,1,0:T(8,128)(2,1)}), bf16[64,40,128]{2,1,0:T(8,128)(2,1)S(1)}, u32[]{:S(2)}, u32[]{:S(2)}) async-start(bf16[64,40,128]{2,1,0:T(8,128)(2,1)} %bitcast.31), calls=%async_computation.8 | async-start | bytes 1310720 | tf_op jit(solution)/shard_map/all_to_all | solution.py:352

commit v10 on v9

--- a/solution.py
+++ b/solution.py
@@ -98,17 +98,22 @@
     begin = pl.multiple_of(side[0] * (x_ref.shape[0] // 2), 16)
     quarter = step // 4
     lanes = x_ref.shape[1]
-    for b in range(x_ref.shape[0] // step // 2):
+    for b in range(0, x_ref.shape[0] // step // 2, 2):
+        first = x_ref[pl.ds(begin + b * step, step), :]
+        second = x_ref[pl.ds(begin + (b + 1) * step, step), :]
         moved = jnp.dot(
-            order_ref[...], x_ref[pl.ds(begin + b * step, step), :], preferred_element_type=F32
+            order_ref[...],
+            jnp.concatenate([first, second], axis=1),
+            preferred_element_type=F32,
         ).astype(BF16)
-        for c in range(4):
-            rows_ref[b * quarter : (b + 1) * quarter, c * lanes : (c + 1) * lanes] = moved[
-                c * quarter : (c + 1) * quarter
-            ]
+        for k in range(2):
+            for c in range(4):
+                rows_ref[
+                    (b + k) * quarter : (b + k + 1) * quarter, c * lanes : (c + 1) * lanes
+                ] = moved[c * quarter : (c + 1) * quarter, k * lanes : (k + 1) * lanes]
     wide = w_ref.shape[1]
     inverse = 1.0 / gain_ref[...]
-    step = step // 2
+    step = rows_ref.shape[0]
     for b in range(rows_ref.shape[0] // step):
         rows = rows_ref[b * step : (b + 1) * step, :]
         part = jnp.dot(rows, w_ref[...], preferred_element_type=F32)
@@ -137,19 +142,28 @@
     step = order_ref.shape[0]
     quarter = step // 4
     lanes = o_ref.shape[1]
+    found = jnp.dot(h_ref[...], w_ref[...], preferred_element_type=F32)
     for a in range(h_ref.shape[0] // step):
-        found = jnp.dot(
-            h_ref[a * step : (a + 1) * step, :], w_ref[...], preferred_element_type=F32
-        )
-        for e in range(4):
-            b = e // 2 * 8 + a * 2 + e % 2 if by_x else a * 4 + e
-            piece = found[e * quarter : (e + 1) * quarter]
-            piece = jnp.concatenate(
-                [piece[:, c * lanes : (c + 1) * lanes] for c in range(4)], axis=0
+        for e in range(0, 4, 2):
+            b = e // 2 * 8 + a * 2 if by_x else a * 4 + e
+            begin = a * step + e * quarter
+            pieces = [
+                jnp.concatenate(
+                    [
+                        found[begin + k * quarter : begin + (k + 1) * quarter, c * lanes : (c + 1) * lanes]
+                        for c in range(4)
+                    ],
+                    axis=0,
+                )
+                for k in range(2)
+            ]
+            moved = jnp.dot(
+                order_ref[...],
+                jnp.concatenate(pieces, axis=1).astype(BF16),
+                preferred_element_type=F32,
             ).astype(BF16)
-            o_ref[b * step : (b + 1) * step, :] = jnp.dot(
-                order_ref[...], piece, preferred_element_type=F32
-            ).astype(BF16)
+            o_ref[b * step : (b + 1) * step, :] = moved[:, :lanes]
+            o_ref[(b + 1) * step : (b + 2) * step, :] = moved[:, lanes:]
 
 
 def down(hidden, order, weights, by_x, name):
@@ -295,7 +309,7 @@
         below = below + (part[size + 1].astype(F32) + part[size + 2].astype(F32)) * scale
     context = (above / below[None, :]).astype(BF16).T.reshape(tokens, heads, size)
 
-    order = feature_order(zl, core, heads, size)
+    order = feature_order(after(zl, parts[3]), after(core, parts[3]), heads, size)
     ordered = jnp.dot(
         context.reshape(tokens, heads * size), order, preferred_element_type=F32
     ).astype(BF16)

time: 322 us -> 320 us (level)
  no operation moved by 1% of the time
where the time goes in v10:
time: 320 us; the launch traced here: 319 us
  starting transfers between devices  139 us (43%)
  waiting for transfers between devices  126 us (39%)
  Pallas kernels  24.3 us (8%)
  blocking collectives  13.1 us (4%)
  local copies, waits for them, and re-layouts  7.9 us (2%)
  other arithmetic  6.36 us (2%)
    ppermute x5, starting transfers between devices, shift(): lax.ppermute(value, axis, [(i, (i + step) % count) for i in range(count)])  42.7 us
    all_to_all x1, waiting for transfers between devices, body(): lax.all_to_all(result, CTX, 0, 0, tiled=True).reshape(4 * slots, lanes)  33.6 us
    all_to_all x1, waiting for transfers between devices, body(): lax.all_to_all(outgoing, CTX, 0, 0, tiled=True).reshape(4 * slots, lanes)  33.1 us
    ppermute x8, starting transfers between devices, partner(): return lax.ppermute(value, axis, [(i, i ^ bit) for i in range(SIZES[axis])])  31.4 us
    ppermute x5, waiting for transfers between devices, shift(): lax.ppermute(value, axis, [(i, (i + step) % count) for i in range(count)])  26.2 us
    all_to_all x4, waiting for transfers between devices, sum_along_x(): lax.all_to_all(parts, 'x', 0, 0, tiled=True).astype(F32)  22.2 us
    all_to_all x1, starting transfers between devices, body(): lax.all_to_all(result, CTX, 0, 0, tiled=True).reshape(4 * slots, lanes)  18.7 us
    all_to_all x1, starting transfers between devices, body(): lax.all_to_all(outgoing, CTX, 0, 0, tiled=True).reshape(4 * slots, lanes)  16.1 us
  transfers between devices with their start and end apart: 22, of which 14 were waited for; matrix products, arithmetic and copies ran while one was open for 3% of the time, Pallas kernels for 5%

profile of v10, /device:TPU:1, one launch (start us, length us, event | category | flops | bytes accessed | tf_op | source)
XLA Modules:
  0.0 318.6 jit_solution(2377490250839433073)
XLA Ops:
  1.5 9.6 %collective-permute-start.6 = (bf16[8,4096]{1,0:T(8,128)(2,1)S(1)}, bf16[8,4096]{1,0:T(8,128)(2,1)S(1)}, u32[]{:S(2)}, u32[]{:S(2)}) collective-permute-start(bf16[8,4096]{1,0:T(8,128)(2,1)S(1)} %reshape.140), channel_id=1, source_target_pairs={{0,64},{16,80},{32,96},{48,112},{64,0},{80,16},{96,32},{112,48},{1... | collective-permute-start | bytes 196616 | tf_op jit(solution)/shard_map/ppermute | solution.py:30
  12.8 5.6 %all-to-all-start = ((bf16[8,2,32,128]{3,2,1,0:T(8,128)(2,1)}), bf16[8,2,32,128]{3,2,1,0:T(8,128)(2,1)S(1)}, u32[]{:S(2)}, u32[]{:S(2)}) async-start(bf16[8,2,32,128]{3,2,1,0:T(8,128)(2,1)} %broadcast_in_dim.25), calls=%async_computation | async-start | bytes 262144 | tf_op jit(solution)/shard_map/all_to_all | solution.py:272
  18.4 4.6 %collective-permute-start = (bf16[512,128]{1,0:T(8,128)(2,1)}, bf16[512,128]{1,0:T(8,128)(2,1)S(1)}, u32[]{:S(2)}, u32[]{:S(2)}) collective-permute-start(bf16[512,128]{1,0:T(8,128)(2,1)} %bitcast.62), channel_id=1, source_target_pairs={{0,2},{1,3},{2,0},{3,1},{4,6},{5,7},{6,4},{7,5},{8,10},{9,11},{10,... | collective-permute-start | bytes 393224 | tf_op jit(solution)/shard_map/ppermute | solution.py:30
  23.1 5.6 %all-to-all-done = bf16[8,2,32,128]{3,2,1,0:T(8,128)(2,1)S(1)} async-done(((bf16[8,2,32,128]{3,2,1,0:T(8,128)(2,1)}), bf16[8,2,32,128]{3,2,1,0:T(8,128)(2,1)S(1)}, u32[]{:S(2)}, u32[]{:S(2)}) %all-to-all-start) | async-done | bytes 131104 | tf_op jit(solution)/shard_map/all_to_all | solution.py:272
  28.7 1.9 collective-permute-start.7
  31.6 4.2 %all-to-all-start.1 = ((bf16[4,8,2,32,128]{4,3,1,2,0:T(8,128)(2,1)}), bf16[4,8,2,32,128]{4,3,1,2,0:T(8,128)(2,1)S(1)}, u32[]{:S(2)}, u32[]{:S(2)}) async-start(bf16[4,8,2,32,128]{4,3,1,2,0:T(8,128)(2,1)} %broadcast_in_dim.26), calls=%async_computation.1 | async-start | bytes 1048576 | tf_op jit(solution)/shard_map/all_to_all | solution.py:277
  35.8 3.1 collective-permute-start.1
  38.9 2.7 collective-permute-start.8
  41.6 1.6 collective-permute-done.1
  43.2 6.8 %collective-permute-start.2 = (bf16[4,8,2,32,128]{4,3,1,2,0:T(8,128)(2,1)S(1)}, bf16[4,8,2,32,128]{4,3,1,2,0:T(8,128)(2,1)S(1)}, u32[]{:S(2)}, u32[]{:S(2)}) collective-permute-start(bf16[4,8,2,32,128]{4,3,1,2,0:T(8,128)(2,1)S(1)} %all-to-all-done.1), channel_id=1, source_target_pairs={{0,8},{8,0},{1,9},{9,1},{2,10},{10,2},{3,11},{11,3},{4,12},{12,4},... | collective-permute-start | bytes 1572872 | tf_op jit(solution)/shard_map/ppermute | solution.py:26
  50.1 1.5 collective-permute-done.2
  51.6 1.6 broadcast_in_dim.30
  53.2 4.5 %all-to-all-start.2 = ((bf16[4,64,4096]{2,1,0:T(8,128)(2,1)}), bf16[4,64,4096]{2,1,0:T(8,128)(2,1)S(1)}, u32[]{:S(2)}, u32[]{:S(2)}) async-start(bf16[4,64,4096]{2,1,0:T(8,128)(2,1)} %broadcast_in_dim.30), calls=%async_computation.2 | async-start | bytes 4194304 | tf_op jit(solution)/shard_map/all_to_all | solution.py:290
  58.9 3.0 attend.4
  61.9 4.8 %collective-permute-start.3 = (bf16[144,512]{1,0:T(8,128)(2,1)}, bf16[144,512]{1,0:T(8,128)(2,1)}, u32[]{:S(2)}, u32[]{:S(2)}) collective-permute-start(bf16[144,512]{1,0:T(8,128)(2,1)} %attend.4), channel_id=1, source_target_pairs={{0,2},{1,3},{2,0},{3,1},{4,6},{5,7},{6,4},{7,5},{8,10},{9,11},{10,... | collective-permute-start | bytes 442376 | tf_op jit(solution)/shard_map/ppermute | solution.py:30
  66.6 3.0 attend.5
  69.6 2.8 collective-permute-start.4
  72.4 3.0 attend.6
  75.4 1.9 collective-permute-start.5
  77.4 2.3 attend.7
  79.7 2.1 collective-permute-done.5
  81.8 1.7 all-to-all-done.2
  83.5 3.4 %collective-permute-start.9 = (bf16[256,4096]{1,0:T(8,128)(2,1)S(1)}, bf16[256,4096]{1,0:T(8,128)(2,1)}, u32[]{:S(2)}, u32[]{:S(2)}) collective-permute-start(bf16[256,4096]{1,0:T(8,128)(2,1)S(1)} %bitcast.44), channel_id=1, source_target_pairs={{0,8},{8,0},{1,9},{9,1},{2,10},{10,2},{3,11},{11,3},{4,12},{12,4},... | collective-permute-start | bytes 6291464 | tf_op jit(solution)/shard_map/ppermute | solution.py:26
  90.8 2.4 project.3
  93.2 4.0 %all-to-all-start.3 = ((bf16[4,128,512]{2,1,0:T(8,128)(2,1)}), bf16[4,128,512]{2,1,0:T(8,128)(2,1)S(1)}, u32[]{:S(2)}, u32[]{:S(2)}) async-start(bf16[4,128,512]{2,1,0:T(8,128)(2,1)} %project.3), calls=%async_computation.3 | async-start | bytes 1048576 | tf_op jit(solution)/shard_map/all_to_all | solution.py:85
  97.4 2.5 project.2
  99.9 6.3 %all-to-all-done.3 = bf16[4,128,512]{2,1,0:T(8,128)(2,1)S(1)} async-done(((bf16[4,128,512]{2,1,0:T(8,128)(2,1)}), bf16[4,128,512]{2,1,0:T(8,128)(2,1)S(1)}, u32[]{:S(2)}, u32[]{:S(2)}) %all-to-all-start.3) | async-done | bytes 524320 | tf_op jit(solution)/shard_map/all_to_all | solution.py:85
  106.3 3.6 %all-to-all-start.4 = ((bf16[4,128,512]{2,1,0:T(8,128)(2,1)}), bf16[4,128,512]{2,1,0:T(8,128)(2,1)S(1)}, u32[]{:S(2)}, u32[]{:S(2)}) async-start(bf16[4,128,512]{2,1,0:T(8,128)(2,1)} %project.2), calls=%async_computation.4 | async-start | bytes 1048576 | tf_op jit(solution)/shard_map/all_to_all | solution.py:85
  110.4 10.9 %collective-permute-start.10 = (bf16[128,512]{1,0:T(8,128)(2,1)S(1)}, bf16[128,512]{1,0:T(8,128)(2,1)S(1)}, u32[]{:S(2)}, u32[]{:S(2)}) collective-permute-start(bf16[128,512]{1,0:T(8,128)(2,1)S(1)} %reduce_sum.72), channel_id=1, source_target_pairs={{0,4},{4,0},{1,5},{5,1},{2,6},{6,2},{3,7},{7,3},{8,12},{12,8},{9,1... | collective-permute-start | bytes 393224 | tf_op jit(solution)/shard_map/ppermute | solution.py:26
  121.4 3.9 %collective-permute-done.10 = bf16[128,512]{1,0:T(8,128)(2,1)S(1)} collective-permute-done((bf16[128,512]{1,0:T(8,128)(2,1)S(1)}, bf16[128,512]{1,0:T(8,128)(2,1)S(1)}, u32[]{:S(2)}, u32[]{:S(2)}) %collective-permute-start.10) | collective-permute-done | bytes 131104 | tf_op jit(solution)/shard_map/ppermute | solution.py:26
  126.8 16.1 %all-to-all-start.5 = ((bf16[64,40,128]{2,1,0:T(8,128)(2,1)}), bf16[64,40,128]{2,1,0:T(8,128)(2,1)S(1)}, u32[]{:S(2)}, u32[]{:S(2)}) async-start(bf16[64,40,128]{2,1,0:T(8,128)(2,1)} %bitcast.22), calls=%async_computation.5 | async-start | bytes 1310720 | tf_op jit(solution)/shard_map/all_to_all | solution.py:347
  142.9 1.7 copy.47
  144.5 33.1 %all-to-all-done.5 = bf16[64,40,128]{2,1,0:T(8,128)(2,1)S(1)} async-done(((bf16[64,40,128]{2,1,0:T(8,128)(2,1)}), bf16[64,40,128]{2,1,0:T(8,128)(2,1)S(1)}, u32[]{:S(2)}, u32[]{:S(2)}) %all-to-all-start.5) | async-done | bytes 655392 | tf_op jit(solution)/shard_map/all_to_all | solution.py:347
  177.7 1.8 gate_up.3
  179.5 4.3 %all-to-all-start.6 = ((bf16[4,80,1664]{2,1,0:T(8,128)(2,1)}), bf16[4,80,1664]{2,1,0:T(8,128)(2,1)}, u32[]{:S(2)}, u32[]{:S(2)}) async-start(bf16[4,80,1664]{2,1,0:T(8,128)(2,1)} %bitcast.26), calls=%async_computation.6 | async-start | bytes 2129920 | tf_op jit(solution)/shard_map/all_to_all | solution.py:85
  183.8 1.9 gate_up.2
  185.6 12.1 %all-to-all-done.6 = bf16[4,80,1664]{2,1,0:T(8,128)(2,1)} async-done(((bf16[4,80,1664]{2,1,0:T(8,128)(2,1)}), bf16[4,80,1664]{2,1,0:T(8,128)(2,1)}, u32[]{:S(2)}, u32[]{:S(2)}) %all-to-all-start.6) | async-done | bytes 1064992 | tf_op jit(solution)/shard_map/all_to_all | solution.py:85
  197.7 1.4 reduce_sum.74
  199.1 3.5 %all-to-all-start.7 = ((bf16[4,80,1664]{2,1,0:T(8,128)(2,1)}), bf16[4,80,1664]{2,1,0:T(8,128)(2,1)S(1)}, u32[]{:S(2)}, u32[]{:S(2)}) async-start(bf16[4,80,1664]{2,1,0:T(8,128)(2,1)} %bitcast.25), calls=%async_computation.7 | async-start | bytes 2129920 | tf_op jit(solution)/shard_map/all_to_all | solution.py:85
  202.7 9.2 %collective-permute-start.11 = (bf16[80,1664]{1,0:T(8,128)(2,1)S(1)}, bf16[80,1664]{1,0:T(8,128)(2,1)S(1)}, u32[]{:S(2)}, u32[]{:S(2)}) collective-permute-start(bf16[80,1664]{1,0:T(8,128)(2,1)S(1)} %reduce_sum.74), channel_id=1, source_target_pairs={{0,4},{4,0},{1,5},{5,1},{2,6},{6,2},{3,7},{7,3},{8,12},{12,8},{9,1... | collective-permute-start | bytes 798728 | tf_op jit(solution)/shard_map/ppermute | solution.py:26
  211.9 3.7 %all-to-all-done.7 = bf16[4,80,1664]{2,1,0:T(8,128)(2,1)S(1)} async-done(((bf16[4,80,1664]{2,1,0:T(8,128)(2,1)}), bf16[4,80,1664]{2,1,0:T(8,128)(2,1)S(1)}, u32[]{:S(2)}, u32[]{:S(2)}) %all-to-all-start.7) | async-done | bytes 1064992 | tf_op jit(solution)/shard_map/all_to_all | solution.py:85
  215.8 11.2 %collective-permute-done.11 = bf16[80,1664]{1,0:T(8,128)(2,1)S(1)} collective-permute-done((bf16[80,1664]{1,0:T(8,128)(2,1)S(1)}, bf16[80,1664]{1,0:T(8,128)(2,1)S(1)}, u32[]{:S(2)}, u32[]{:S(2)}) %collective-permute-start.11) | collective-permute-done | bytes 266272 | tf_op jit(solution)/shard_map/ppermute | solution.py:26
  227.4 12.4 %collective-permute-start.12 = (bf16[80,768]{1,0:T(8,128)(2,1)S(1)}, bf16[80,768]{1,0:T(8,128)(2,1)S(1)}, u32[]{:S(2)}, u32[]{:S(2)}) collective-permute-start(bf16[80,768]{1,0:T(8,128)(2,1)S(1)} %fusion.52), channel_id=1, source_target_pairs={{0,4},{4,0},{1,5},{5,1},{2,6},{6,2},{3,7},{7,3},{8,12},{12,8},{9,1... | collective-permute-start | bytes 368648 | tf_op jit(solution)/shard_map/ppermute | solution.py:26
  239.9 9.1 %collective-permute-done.12 = bf16[80,768]{1,0:T(8,128)(2,1)S(1)} collective-permute-done((bf16[80,768]{1,0:T(8,128)(2,1)S(1)}, bf16[80,768]{1,0:T(8,128)(2,1)S(1)}, u32[]{:S(2)}, u32[]{:S(2)}) %collective-permute-start.12) | collective-permute-done | bytes 122912 | tf_op jit(solution)/shard_map/ppermute | solution.py:26
  249.0 13.1 %all_gather.4 = bf16[4,2,80,768]{3,2,1,0:T(8,128)(2,1)S(1)} all-gather(bf16[1,2,80,768]{3,2,1,0:T(8,128)(2,1)S(1)} %maximum_select_fusion), channel_id=1, replica_groups=mesh['y'=4,'zl'=8,'core'=2,'zh'=2,'x'=4] {'x'}, dimensions={0}, use_global_device_ids=true | all-gather | bytes 1228800 | tf_op jit(solution)/shard_map/all_gather | solution.py:364
  262.1 1.7 down.1
  263.8 18.7 %all-to-all-start.8 = ((bf16[64,40,128]{2,1,0:T(8,128)(2,1)}), bf16[64,40,128]{2,1,0:T(8,128)(2,1)S(1)}, u32[]{:S(2)}, u32[]{:S(2)}) async-start(bf16[64,40,128]{2,1,0:T(8,128)(2,1)} %bitcast.31), calls=%async_computation.8 | async-start | bytes 1310720 | tf_op jit(solution)/shard_map/all_to_all | solution.py:366
  283.6 33.6 %all-to-all-done.8 = bf16[64,40,128]{2,1,0:T(8,128)(2,1)S(1)} async-done(((bf16[64,40,128]{2,1,0:T(8,128)(2,1)}), bf16[64,40,128]{2,1,0:T(8,128)(2,1)S(1)}, u32[]{:S(2)}, u32[]{:S(2)}) %all-to-all-start.8) | async-done | bytes 655392 | tf_op jit(solution)/shard_map/all_to_all | solution.py:366
  (74 shorter events, 14.0 us)
Async XLA Ops:
  1.5 21.6 %collective-permute-start.6 = (bf16[8,4096]{1,0:T(8,128)(2,1)S(1)}, bf16[8,4096]{1,0:T(8,128)(2,1)S(1)}, u32[]{:S(2)}, u32[]{:S(2)}) collective-permute-start(bf16[8,4096]{1,0:T(8,128)(2,1)S(1)} %reshape.140), channel_id=1, source_target_pairs={{0,64},{16,80},{32,96},{48,112},{64,0},{80,16},{96,32},{112,48},{1... | collective-permute-start | bytes 196616 | tf_op jit(solution)/shard_map/ppermute | solution.py:30
  12.1 23.7 %copy-start.1 = (bf16[128,4,128]{2,1,0:T(4,128)(2,1)S(1)}, bf16[128,4,128]{2,1,0:T(4,128)(2,1)}, u32[]{:S(2)}) copy-start(bf16[128,4,128]{2,1,0:T(4,128)(2,1)} %param.10) | copy-start | bytes 393220
  12.8 15.9 %all-to-all-start = ((bf16[8,2,32,128]{3,2,1,0:T(8,128)(2,1)}), bf16[8,2,32,128]{3,2,1,0:T(8,128)(2,1)S(1)}, u32[]{:S(2)}, u32[]{:S(2)}) async-start(bf16[8,2,32,128]{3,2,1,0:T(8,128)(2,1)} %broadcast_in_dim.25), calls=%async_computation | async-start | bytes 262144 | tf_op jit(solution)/shard_map/all_to_all | solution.py:272
  18.4 12.2 %collective-permute-start = (bf16[512,128]{1,0:T(8,128)(2,1)}, bf16[512,128]{1,0:T(8,128)(2,1)S(1)}, u32[]{:S(2)}, u32[]{:S(2)}) collective-permute-start(bf16[512,128]{1,0:T(8,128)(2,1)} %bitcast.62), channel_id=1, source_target_pairs={{0,2},{1,3},{2,0},{3,1},{4,6},{5,7},{6,4},{7,5},{8,10},{9,11},{10,... | collective-permute-start | bytes 393224 | tf_op jit(solution)/shard_map/ppermute | solution.py:30
  28.7 10.2 %collective-permute-start.7 = (bf16[16,4096]{1,0:T(8,128)(2,1)S(1)}, bf16[16,4096]{1,0:T(8,128)(2,1)S(1)}, u32[]{:S(2)}, u32[]{:S(2)}) collective-permute-start(bf16[16,4096]{1,0:T(8,128)(2,1)S(1)} %pad_maximum_fusion.3), channel_id=1, source_target_pairs={{0,32},{16,48},{32,0},{48,16},{64,96},{80,112},{96,64},{112,80},{1... | collective-permute-start | bytes 393224 | tf_op jit(solution)/shard_map/ppermute | solution.py:30
  31.6 11.6 %all-to-all-start.1 = ((bf16[4,8,2,32,128]{4,3,1,2,0:T(8,128)(2,1)}), bf16[4,8,2,32,128]{4,3,1,2,0:T(8,128)(2,1)S(1)}, u32[]{:S(2)}, u32[]{:S(2)}) async-start(bf16[4,8,2,32,128]{4,3,1,2,0:T(8,128)(2,1)} %broadcast_in_dim.26), calls=%async_computation.1 | async-start | bytes 1048576 | tf_op jit(solution)/shard_map/all_to_all | solution.py:277
  35.8 7.4 %collective-permute-start.1 = (bf16[1024,128]{1,0:T(8,128)(2,1)S(1)}, bf16[1024,128]{1,0:T(8,128)(2,1)}, u32[]{:S(2)}, u32[]{:S(2)}) collective-permute-start(bf16[1024,128]{1,0:T(8,128)(2,1)S(1)} %pad_maximum_fusion.2), channel_id=1, source_target_pairs={{0,1},{1,0},{2,3},{3,2},{4,5},{5,4},{6,7},{7,6},{8,9},{9,8},{10,11... | collective-permute-start | bytes 786440 | tf_op jit(solution)/shard_map/ppermute | solution.py:30
  38.9 11.1 %collective-permute-start.8 = (bf16[32,4096]{1,0:T(8,128)(2,1)S(1)}, bf16[32,4096]{1,0:T(8,128)(2,1)S(1)}, u32[]{:S(2)}, u32[]{:S(2)}) collective-permute-start(bf16[32,4096]{1,0:T(8,128)(2,1)S(1)} %constant_dynamic-update-slice_fusion), channel_id=1, source_target_pairs={{0,16},{16,0},{32,48},{48,32},{64,80},{80,64},{96,112},{112,96},{1... | collective-permute-start | bytes 786440 | tf_op jit(solution)/shard_map/ppermute | solution.py:30
  43.2 8.3 %collective-permute-start.2 = (bf16[4,8,2,32,128]{4,3,1,2,0:T(8,128)(2,1)S(1)}, bf16[4,8,2,32,128]{4,3,1,2,0:T(8,128)(2,1)S(1)}, u32[]{:S(2)}, u32[]{:S(2)}) collective-permute-start(bf16[4,8,2,32,128]{4,3,1,2,0:T(8,128)(2,1)S(1)} %all-to-all-done.1), channel_id=1, source_target_pairs={{0,8},{8,0},{1,9},{9,1},{2,10},{10,2},{3,11},{11,3},{4,12},{12,4},... | collective-permute-start | bytes 1572872 | tf_op jit(solution)/shard_map/ppermute | solution.py:26
  53.2 30.3 %all-to-all-start.2 = ((bf16[4,64,4096]{2,1,0:T(8,128)(2,1)}), bf16[4,64,4096]{2,1,0:T(8,128)(2,1)S(1)}, u32[]{:S(2)}, u32[]{:S(2)}) async-start(bf16[4,64,4096]{2,1,0:T(8,128)(2,1)} %broadcast_in_dim.30), calls=%async_computation.2 | async-start | bytes 4194304 | tf_op jit(solution)/shard_map/all_to_all | solution.py:290
  61.9 15.5 %copy-start.6 = (f32[128,8]{0,1:T(8,128)S(1)}, f32[128,8]{0,1:T(8,128)}, u32[]{:S(2)}) copy-start(f32[128,8]{0,1:T(8,128)} %param.16) | copy-start | bytes 12292
  61.9 19.9 %collective-permute-start.3 = (bf16[144,512]{1,0:T(8,128)(2,1)}, bf16[144,512]{1,0:T(8,128)(2,1)}, u32[]{:S(2)}, u32[]{:S(2)}) collective-permute-start(bf16[144,512]{1,0:T(8,128)(2,1)} %attend.4), channel_id=1, source_target_pairs={{0,2},{1,3},{2,0},{3,1},{4,6},{5,7},{6,4},{7,5},{8,10},{9,11},{10,... | collective-permute-start | bytes 442376 | tf_op jit(solution)/shard_map/ppermute | solution.py:30
  69.6 12.1 %collective-permute-start.4 = (bf16[144,512]{1,0:T(8,128)(2,1)}, bf16[144,512]{1,0:T(8,128)(2,1)}, u32[]{:S(2)}, u32[]{:S(2)}) collective-permute-start(bf16[144,512]{1,0:T(8,128)(2,1)} %attend.5), channel_id=1, source_target_pairs={{0,3},{1,2},{2,1},{3,0},{4,7},{5,6},{6,5},{7,4},{8,11},{9,10},{10,... | collective-permute-start | bytes 442376 | tf_op jit(solution)/shard_map/ppermute | solution.py:30
  75.4 6.4 %collective-permute-start.5 = (bf16[144,512]{1,0:T(8,128)(2,1)}, bf16[144,512]{1,0:T(8,128)(2,1)}, u32[]{:S(2)}, u32[]{:S(2)}) collective-permute-start(bf16[144,512]{1,0:T(8,128)(2,1)} %attend.6), channel_id=1, source_target_pairs={{0,1},{1,0},{2,3},{3,2},{4,5},{5,4},{6,7},{7,6},{8,9},{9,8},{10,11... | collective-permute-start | bytes 442376 | tf_op jit(solution)/shard_map/ppermute | solution.py:30
  83.5 7.3 %collective-permute-start.9 = (bf16[256,4096]{1,0:T(8,128)(2,1)S(1)}, bf16[256,4096]{1,0:T(8,128)(2,1)}, u32[]{:S(2)}, u32[]{:S(2)}) collective-permute-start(bf16[256,4096]{1,0:T(8,128)(2,1)S(1)} %bitcast.44), channel_id=1, source_target_pairs={{0,8},{8,0},{1,9},{9,1},{2,10},{10,2},{3,11},{11,3},{4,12},{12,4},... | collective-permute-start | bytes 6291464 | tf_op jit(solution)/shard_map/ppermute | solution.py:26
  89.4 0.8 copy-start.4
  89.5 0.7 copy-start.7
  93.2 12.9 %all-to-all-start.3 = ((bf16[4,128,512]{2,1,0:T(8,128)(2,1)}), bf16[4,128,512]{2,1,0:T(8,128)(2,1)S(1)}, u32[]{:S(2)}, u32[]{:S(2)}) async-start(bf16[4,128,512]{2,1,0:T(8,128)(2,1)} %project.3), calls=%async_computation.3 | async-start | bytes 1048576 | tf_op jit(solution)/shard_map/all_to_all | solution.py:85
  106.2 19.1 %copy-start.2 = (f32[512]{0:T(512)S(1)}, f32[512]{0:T(512)}, u32[]{:S(2)}) copy-start(f32[512]{0:T(512)} %param.14) | copy-start | bytes 6148
  106.3 19.1 %copy-start.5 = (bf16[128,512]{1,0:T(8,128)(2,1)S(1)}, bf16[128,512]{1,0:T(8,128)(2,1)}, u32[]{:S(2)}) copy-start(bf16[128,512]{1,0:T(8,128)(2,1)} %param.13) | copy-start | bytes 393220
  106.3 15.1 %all-to-all-start.4 = ((bf16[4,128,512]{2,1,0:T(8,128)(2,1)}), bf16[4,128,512]{2,1,0:T(8,128)(2,1)S(1)}, u32[]{:S(2)}, u32[]{:S(2)}) async-start(bf16[4,128,512]{2,1,0:T(8,128)(2,1)} %project.2), calls=%async_computation.4 | async-start | bytes 1048576 | tf_op jit(solution)/shard_map/all_to_all | solution.py:85
  110.2 16.5 %copy-start.3 = (f32[640,384]{1,0:T(8,128)}, f32[640,384]{1,0:T(8,128)S(1)}, u32[]{:S(2)}) copy-start(f32[640,384]{1,0:T(8,128)S(1)} %fusion.50) | copy-start | bytes 2949124
  110.4 15.0 %collective-permute-start.10 = (bf16[128,512]{1,0:T(8,128)(2,1)S(1)}, bf16[128,512]{1,0:T(8,128)(2,1)S(1)}, u32[]{:S(2)}, u32[]{:S(2)}) collective-permute-start(bf16[128,512]{1,0:T(8,128)(2,1)S(1)} %reduce_sum.72), channel_id=1, source_target_pairs={{0,4},{4,0},{1,5},{5,1},{2,6},{6,2},{3,7},{7,3},{8,12},{12,8},{9,1... | collective-permute-start | bytes 393224 | tf_op jit(solution)/shard_map/ppermute | solution.py:26
  126.8 50.9 %all-to-all-start.5 = ((bf16[64,40,128]{2,1,0:T(8,128)(2,1)}), bf16[64,40,128]{2,1,0:T(8,128)(2,1)S(1)}, u32[]{:S(2)}, u32[]{:S(2)}) async-start(bf16[64,40,128]{2,1,0:T(8,128)(2,1)} %bitcast.22), calls=%async_computation.5 | async-start | bytes 1310720 | tf_op jit(solution)/shard_map/all_to_all | solution.py:347
  179.5 18.2 %all-to-all-start.6 = ((bf16[4,80,1664]{2,1,0:T(8,128)(2,1)}), bf16[4,80,1664]{2,1,0:T(8,128)(2,1)}, u32[]{:S(2)}, u32[]{:S(2)}) async-start(bf16[4,80,1664]{2,1,0:T(8,128)(2,1)} %bitcast.26), calls=%async_computation.6 | async-start | bytes 2129920 | tf_op jit(solution)/shard_map/all_to_all | solution.py:85
  199.1 16.5 %all-to-all-start.7 = ((bf16[4,80,1664]{2,1,0:T(8,128)(2,1)}), bf16[4,80,1664]{2,1,0:T(8,128)(2,1)S(1)}, u32[]{:S(2)}, u32[]{:S(2)}) async-start(bf16[4,80,1664]{2,1,0:T(8,128)(2,1)} %bitcast.25), calls=%async_computation.7 | async-start | bytes 2129920 | tf_op jit(solution)/shard_map/all_to_all | solution.py:85
  202.7 24.3 %collective-permute-start.11 = (bf16[80,1664]{1,0:T(8,128)(2,1)S(1)}, bf16[80,1664]{1,0:T(8,128)(2,1)S(1)}, u32[]{:S(2)}, u32[]{:S(2)}) collective-permute-start(bf16[80,1664]{1,0:T(8,128)(2,1)S(1)} %reduce_sum.74), channel_id=1, source_target_pairs={{0,4},{4,0},{1,5},{5,1},{2,6},{6,2},{3,7},{7,3},{8,12},{12,8},{9,1... | collective-permute-start | bytes 798728 | tf_op jit(solution)/shard_map/ppermute | solution.py:26
  227.0 35.1 %copy-start = (bf16[1,768,512]{2,1,0:T(8,128)(2,1)S(1)}, bf16[1,768,512]{2,1,0:T(8,128)(2,1)}, u32[]{:S(2)}) copy-start(bf16[1,768,512]{2,1,0:T(8,128)(2,1)} %param.18) | copy-start | bytes 2359300
  227.4 21.6 %collective-permute-start.12 = (bf16[80,768]{1,0:T(8,128)(2,1)S(1)}, bf16[80,768]{1,0:T(8,128)(2,1)S(1)}, u32[]{:S(2)}, u32[]{:S(2)}) collective-permute-start(bf16[80,768]{1,0:T(8,128)(2,1)S(1)} %fusion.52), channel_id=1, source_target_pairs={{0,4},{4,0},{1,5},{5,1},{2,6},{6,2},{3,7},{7,3},{8,12},{12,8},{9,1... | collective-permute-start | bytes 368648 | tf_op jit(solution)/shard_map/ppermute | solution.py:26
  263.8 53.5 %all-to-all-start.8 = ((bf16[64,40,128]{2,1,0:T(8,128)(2,1)}), bf16[64,40,128]{2,1,0:T(8,128)(2,1)S(1)}, u32[]{:S(2)}, u32[]{:S(2)}) async-start(bf16[64,40,128]{2,1,0:T(8,128)(2,1)} %bitcast.31), calls=%async_computation.8 | async-start | bytes 1310720 | tf_op jit(solution)/shard_map/all_to_all | solution.py:366
